TPU v7x, 256 devices: a whole 4x4x8 slice. The times are simulated.
256 devices in a mesh: seq: 8 (over y, core), factor: 32 (over z, x).
Axes of the slice: x: 4, y: 4, z: 8, core: 2. Of those that a mesh axis runs over, the one named last changes fastest.
Arguments:
- out_grads: bfloat16 [16384, 28672], P('seq', 'factor'), may hold values from -6 to 6
- in_acts: bfloat16 [16384, 8192], P('seq', 'factor'), may hold values from -6 to 6
- query_grads: bfloat16 [2048, 28672], P('seq', 'factor'), may hold values from -6 to 6
- query_acts: bfloat16 [2048, 8192], P('seq', 'factor'), may hold values from -6 to 6
- output_basis: float32 [1024, 28672], P('factor'), may hold values from -0.03125 to 0.03125
- input_basis: float32 [128, 8192], replicated, may hold values from -0.0625 to 0.0625
- eigenvalues: float32 [1024, 128], P('factor'), may hold values from 0.001 to 50
- doc_ids: int32 [16384], P('seq'), may hold values from 0 to 3, as said below
- doc_lengths: int32 [32], P('seq'), may hold values from 256 to 768, as said below
Outputs:
- scores: float32 [64, 32], P('factor', 'seq')
Inputs may be any that keep to these rules, and one draw needn't show every extreme that they name: doc_ids never decrease along the tokens of a group of 2048 consecutive tokens, and document k of group g holds exactly doc_lengths[g * 4 + k] of them. `doc_lengths`: the lengths of each group's 4 documents sum to 2048.
All inputs are finite; a program needn't handle non-finite values.
Results may differ from a plain program's by a relative error of at most 0.0003.
Values sent between devices are 32-bit elements; how exact they have to be, the bound alone decides.
No kernel may reach another device: no remote copies, remote signals or barrier semaphores. Data moves between devices by JAX's collectives and lax.ppermute only.
A program may use at most 64 MiB of HBM per device.

v0:
```python
import jax
import jax.numpy as jnp
from jax import lax
from jax.experimental import pallas as pl
from jax.experimental.pallas import tpu as pltpu
from jax.sharding import Mesh, PartitionSpec as P


QLEN = 32
DAMPING = 1.0
ZX = ("z", "x")

HALF = 512
VMEM = pl.BlockSpec(memory_space=pltpu.VMEM)
SMEM = pl.BlockSpec(memory_space=pltpu.SMEM)


def exchange(blocks, axis):
    return lax.all_to_all(blocks, axis, 0, 0, tiled=True)


def shifted(shard, axis, hops):
    n = lax.axis_size(axis)
    return lax.ppermute(shard, axis, [(i, (i + hops) % n) for i in range(n)])


def call(kernel, outs, in_specs, me, *args, grid=1, scratch=()):
    out_shape = [jax.ShapeDtypeStruct(*o) for o in outs]
    return pl.pallas_call(
        kernel,
        out_shape=out_shape,
        grid_spec=pltpu.PrefetchScalarGridSpec(
            num_scalar_prefetch=1,
            grid=(grid,),
            in_specs=in_specs,
            out_specs=[VMEM] * len(out_shape),
            scratch_shapes=list(scratch),
        ),
    )(me, *args)


def place(me_ref):
    me = me_ref[0]
    return me // 64, (me // 32) % 2, (me // 4) % 8, me % 4


def split(value):
    high = value.astype(jnp.bfloat16)
    return high, (value - high.astype(jnp.float32)).astype(jnp.bfloat16)


def dot_nt(left, right):
    return lax.dot_general(
        left, right, (((1,), (1,)), ((), ())), preferred_element_type=jnp.float32
    )


def dot_nn(left, right):
    return lax.dot_general(
        left, right, (((1,), (0,)), ((), ())), preferred_element_type=jnp.float32
    )


def input_rotation_kernel(me_ref, acts_ref, query_ref, basis_ref, *out_refs):
    _, _, _, x = place(me_ref)
    high, low = split(basis_ref[...])
    for k, out_ref in enumerate(out_refs):
        target = lax.rem(x + k, 4)
        acts = acts_ref[pl.ds(pl.multiple_of(target * 512, 512), 512), :]
        query = query_ref[pl.ds(pl.multiple_of(target * 64, 64), 64), :]
        out_ref[:, :64, :] = (dot_nt(acts, high) + dot_nt(acts, low)).reshape(8, 64, 128)
        out_ref[:, 64:, :] = (dot_nt(query, high) + dot_nt(query, low)).reshape(8, 8, 128)


def basis_pick_kernel(me_ref, basis_ref, out_ref):
    _, core, _, _ = place(me_ref)
    cols = basis_ref.shape[1] // 32
    for f in range(32):
        start = pl.multiple_of(f * cols + core * (cols - HALF), 128)
        out_ref[f] = basis_ref[:, pl.ds(start, HALF)]


def query_kernel(me_ref, grads_ref, *refs):
    slabs, out_ref, halves_ref = refs[:8], refs[8], refs[9]
    _, core, _, _ = place(me_ref)
    cols = grads_ref.shape[1]
    halves_ref[0] = grads_ref[:, :HALF]
    halves_ref[1, :, : 2 * HALF - cols] = jnp.zeros((grads_ref.shape[0], 2 * HALF - cols), jnp.bfloat16)
    halves_ref[1, :, 2 * HALF - cols :] = grads_ref[:, HALF:]
    own, other = halves_ref[core], halves_ref[1 - core]
    for slot in range(4):
        total = None
        for half, ref in ((own, slabs[slot]), (other, slabs[4 + slot])):
            high, low = split(ref[...].reshape(256, HALF))
            part = dot_nt(high, half) + dot_nt(low, half)
            total = part if total is None else total + part
        out_ref[:, :, slot] = total.reshape(8, 4, 8, total.shape[1])


def query_sum_kernel(me_ref, blocks_ref, *out_refs):
    _, _, _, x = place(me_ref)
    for k, out_ref in enumerate(out_refs):
        target = lax.rem(x + k, 4)
        total = blocks_ref[0, target]
        for sender in range(1, 8):
            total = total + blocks_ref[sender, target]
        out_ref[...] = total


def precond_kernel(me_ref, eig_ref, *refs):
    parts, blocks, out_ref, rot_in_ref = refs[:4], refs[4:8], refs[8], refs[9]
    y, _, _, x = place(me_ref)
    for k in range(4):
        source = lax.rem(x + 4 - k, 4)
        rot_in_ref[pl.ds(pl.multiple_of(source * 64, 64), 64), :] = blocks[k][:, 64:, :].reshape(64, 128)
    rot = parts[0][...] + parts[1][...] + parts[2][...] + parts[3][...]
    rot = rot.reshape(32, rot.shape[-1])
    lane_query = lax.broadcasted_iota(jnp.int32, rot.shape, 1) // QLEN
    count = rot.shape[1] // QLEN
    masked = jnp.concatenate([jnp.where(lane_query == q, rot, 0.0) for q in range(count)], 0)
    both = lax.dot_general(
        masked,
        rot_in_ref[...],
        (((1,), (0,)), ((), ())),
        precision=lax.Precision.HIGHEST,
        preferred_element_type=jnp.float32,
    ) * (1.0 / QLEN)
    for slot in range(4):
        rows = pl.ds(pl.multiple_of(8 * lax.rem(y + slot, 4), 8), 8)
        eig = eig_ref[rows, :] + DAMPING
        for q in range(count):
            out_ref[rows, q, :] = both[32 * q + 8 * slot : 32 * q + 8 * slot + 8] / eig


def hops_of(step):
    return jnp.where(step < 3, 2 + (step == 2).astype(jnp.int32) - (step == 1).astype(jnp.int32), 0)


def train_kernel(me_ref, len_ref, grads_ref, *refs):
    blocks, slabs, out_refs, (high_ref, low_ref, total_ref) = refs[:4], refs[4:12], refs[12:16], refs[16:]
    _, core, _, x = place(me_ref)
    step = pl.program_id(0)
    cols = grads_ref.shape[1]

    @pl.when(step == 0)
    def _():
        total_ref[...] = jnp.zeros_like(total_ref)

    for k in range(4):

        @pl.when(step == k)
        def _(k=k):
            first = lax.rem(x + 4 - k, 4) * 512
            high, low = split(blocks[k][:, :64, :].reshape(512, 128).T)
            pair = jnp.concatenate([high, low], 0)
            token = first + lax.broadcasted_iota(jnp.int32, pair.shape, 1)
            begin = jnp.int32(0)
            for doc in range(4):
                end = begin + len_ref[doc]

                @pl.when((begin < first + 512) & (end > first))
                def _(begin=begin, end=end, doc=doc):
                    masked = jnp.where((token >= begin) & (token < end), pair, jnp.zeros_like(pair))
                    both = dot_nn(masked, grads_ref[...])
                    total_ref[doc] += both[:128] + both[128:]

                begin = end

    @pl.when(step == 3)
    def _():
        for doc in range(4):
            length = jnp.full((128, cols), len_ref[doc], jnp.int32).astype(jnp.float32)
            high, low = split(total_ref[doc] / length)
            rows = slice(128 * doc, 128 * doc + 128)
            for ref, value in ((high_ref, high), (low_ref, low)):
                ref[0, rows, :] = value[:, :HALF]
                ref[1, rows, : 2 * HALF - cols] = jnp.zeros((128, 2 * HALF - cols), jnp.bfloat16)
                ref[1, rows, 2 * HALF - cols :] = value[:, HALF:]

    @pl.when(step >= 4)
    def _():
        total = None
        for half, group in ((core, slabs[:4]), (1 - core, slabs[4:])):
            value = jnp.concatenate([ref[...].reshape(64, HALF) for ref in group], 0)
            high, low = split(value)
            part = dot_nt(high, high_ref[half]) + dot_nt(high, low_ref[half]) + dot_nt(low, high_ref[half])
            total = part if total is None else total + part
        for at, out_ref in zip((4, 5, 6, 7), out_refs):

            @pl.when(step == at)
            def _(out_ref=out_ref):
                for slot in range(4):
                    out_ref[:, 8 * slot : 8 * slot + 8, :] = total[64 * slot : 64 * slot + 64].reshape(8, 8, 512)


def score_kernel(me_ref, blocks_ref, *refs):
    preconds, out_ref = refs[:8], refs[8]
    y, core, _, _ = place(me_ref)
    train = blocks_ref[0]
    for sender in range(1, 8):
        train = train + blocks_ref[sender]
    for index, ref in enumerate(preconds):
        other, k = divmod(index, 4)
        owner = 2 * lax.rem(y + 4 - k, 4) + lax.rem(core + other, 2)
        sums = [None] * 4
        for slot in range(4):
            base = 8 * lax.rem(y + slot, 4)
            for r in range(8):
                value = ref[base + r]
                row = train[8 * slot + r : 8 * slot + r + 1]
                for doc in range(4):
                    product = value * row[:, 128 * doc : 128 * doc + 128]
                    sums[doc] = product if sums[doc] is None else sums[doc] + product
        for q in range(8):
            for doc in range(4):
                out_ref[4 * owner + q // 2, 4 * (q % 2) + doc : 4 * (q % 2) + doc + 1, :] = sums[doc][q : q + 1]


def local(
    out_grads,
    in_acts,
    query_grads,
    query_acts,
    output_basis,
    input_basis,
    eigenvalues,
    doc_ids,
    doc_lengths,
):
    f32, bf16 = jnp.float32, jnp.bfloat16
    me = lax.axis_index(("y", "core", "z", "x")).astype(jnp.int32).reshape(1)
    queries = query_grads.shape[0]

    parts = call(
        input_rotation_kernel,
        [((8, 72, 128), f32)] * 4,
        [VMEM, VMEM, pl.BlockSpec((128, in_acts.shape[1]), lambda i, me: (0, me[0] % 32))],
        me, in_acts, query_acts, input_basis,
    )
    arrived = [parts[0]]
    for k in (2, 1, 3):
        arrived.append(shifted(parts[k], "x", k))
    part = arrived[0] + arrived[1] + arrived[2] + arrived[3]
    part = jnp.sum(exchange(part, "z"), axis=0)
    block = exchange(jnp.broadcast_to(part[None], (8, 72, 128)), "z")
    blocks = [block] + [None] * 3
    for k in (2, 1, 3):
        blocks[k] = shifted(block, "x", k)

    (picked,) = call(
        basis_pick_kernel,
        [((32, 8, HALF), f32)],
        [pl.BlockSpec((8, output_basis.shape[1]), lambda i, me: (me[0] // 64, 0))],
        me, output_basis,
    )
    slab = exchange(picked, ZX).reshape(8, 4, 8, HALF)
    slabs = [slab] + [shifted(slab, "y", 4 - k) for k in (1, 2, 3)]
    slabs = slabs + [shifted(s, "core", 1) for s in slabs]

    (rot,) = call(
        query_kernel,
        [((8, 4, 4, 8, queries), f32)],
        [VMEM] * 9,
        me, query_grads, *slabs,
        scratch=[pltpu.VMEM((2, queries, HALF), bf16)],
    )
    rot = exchange(rot, "z")
    rots = call(query_sum_kernel, [((4, 8, queries), f32)] * 4, [VMEM], me, rot)
    rots = [rots[0]] + [shifted(rots[k], "x", k) for k in (1, 2, 3)]
    (precond,) = call(
        precond_kernel,
        [((32, 8, 128), f32)],
        [VMEM] * 9,
        me, eigenvalues, *rots, *blocks,
        scratch=[pltpu.VMEM((queries, 128), f32)],
    )
    preconds = [precond]
    for k in (1, 2, 3):
        preconds.append(shifted(precond, "y", k))
    preconds = preconds + [shifted(p, "core", 1) for p in preconds]

    def slab_index(step, me):
        return (0, lax.rem(me[0] % 4 + hops_of(jnp.maximum(step - 4, 0)), 4), 0, 0)

    sent = call(
        train_kernel,
        [((8, 32, 512), f32)] * 4,
        [
            SMEM,
            pl.BlockSpec((512, out_grads.shape[1]), lambda i, me: (lax.rem(me[0] % 4 + 4 - jnp.minimum(i, 3), 4), 0)),
            *[VMEM] * 4,
            *[pl.BlockSpec((8, 1, 8, HALF), slab_index)] * 8,
        ],
        me, doc_lengths, out_grads, *blocks, *slabs,
        grid=8,
        scratch=[
            pltpu.VMEM((2, 512, HALF), bf16),
            pltpu.VMEM((2, 512, HALF), bf16),
            pltpu.VMEM((4, 128, out_grads.shape[1]), f32),
        ],
    )
    arrived = [sent[3]]
    for n, k in enumerate((2, 1, 3)):
        arrived.append(shifted(sent[n], "x", k))
    train = arrived[0] + arrived[1] + arrived[2] + arrived[3]
    train = exchange(train, "z")

    (partial_scores,) = call(score_kernel, [((32, 8, 128), f32)], [VMEM] * 9, me, train, *preconds)
    return jnp.sum(exchange(partial_scores, ZX), axis=(0, 2)).reshape(2, 4)


def solution(mesh):
    fine = Mesh(mesh.devices.reshape(4, 2, 8, 4), ("y", "core", "z", "x"))
    seq, factor = ("y", "core"), ("z", "x")
    in_specs = (
        P(seq, factor),
        P(seq, factor),
        P(seq, factor),
        P(seq, factor),
        P(factor, None),
        P(),
        P(factor, None),
        P(seq),
        P(seq),
    )

    return jax.shard_map(local, mesh=fine, in_specs=in_specs, out_specs=P(factor, seq), check_vma=False)
```

profile of v0, /device:TPU:8, one launch (start us, length us, event | category | flops | bytes accessed | tf_op | source)
XLA Modules:
  0.0 192.0 jit_solution(4443499781558163362)
XLA Ops:
  0.0 2.0 %shard_map.83 = f32[32,8,512]{2,1,0:T(8,128)} custom-call(s32[1]{0:T(128)} %bitcast.me_ref, f32[32,28672]{1,0:T(8,128)} %basis_ref.3), custom_call_target="tpu_custom_call" | custom-call | tf_op jit(solution)/shard_map/pallas_call | solution.py:29
  2.0 11.3 %all-to-all-start.2 = ((f32[32,8,512]{2,1,0:T(8,128)}), f32[32,8,512]{2,1,0:T(8,128)S(1)}, u32[]{:S(2)}, u32[]{:S(2)}) async-start(f32[32,8,512]{2,1,0:T(8,128)} %shard_map.83), calls=%async_computation.2 | async-start | bytes 1048576 | tf_op jit(solution)/shard_map/all_to_all | solution.py:19
  13.3 2.9 %shard_map.82 = (f32[8,72,128]{2,1,0:T(8,128)}, f32[8,72,128]{2,1,0:T(8,128)}, f32[8,72,128]{2,1,0:T(8,128)}, f32[8,72,128]{2,1,0:T(8,128)}) custom-call(s32[1]{0:T(128)} %bitcast.me_ref, bf16[2048,256]{1,0:T(8,128)(2,1)} %acts_ref.1, bf16[256,256]{1,0:T(8,128)(2,1)} %query_ref.1, f32[128,8192]{1,0:T(8,128)} %basis_ref.2), custom_call_target="tpu_custom_call" | custom-call | tf_op jit(solution)/shard_map/pallas_call | solution.py:29
  16.3 3.3 %collective-permute-start = (f32[8,72,128]{2,1,0:T(8,128)}, f32[8,72,128]{2,1,0:T(8,128)S(1)}, u32[]{:S(2)}, u32[]{:S(2)}) collective-permute-start(f32[8,72,128]{2,1,0:T(8,128)} %get-tuple-element.18), channel_id=1, source_target_pairs={{0,2},{1,3},{2,0},{3,1},{4,6},{5,7},{6,4},{7,5},{8,10},{9,11},{10,... | collective-permute-start | bytes 884744 | tf_op jit(solution)/shard_map/ppermute | solution.py:24
  20.1 2.7 %collective-permute-start.2 = (f32[8,72,128]{2,1,0:T(8,128)}, f32[8,72,128]{2,1,0:T(8,128)S(1)}, u32[]{:S(2)}, u32[]{:S(2)}) collective-permute-start(f32[8,72,128]{2,1,0:T(8,128)} %get-tuple-element.20), channel_id=1, source_target_pairs={{0,3},{1,0},{2,1},{3,2},{4,7},{5,4},{6,5},{7,6},{8,11},{9,8},{10,9... | collective-permute-start | bytes 884744 | tf_op jit(solution)/shard_map/ppermute | solution.py:24
  22.8 8.4 %all-to-all-done.2 = f32[32,8,512]{2,1,0:T(8,128)S(1)} async-done(((f32[32,8,512]{2,1,0:T(8,128)}), f32[32,8,512]{2,1,0:T(8,128)S(1)}, u32[]{:S(2)}, u32[]{:S(2)}) %all-to-all-start.2) | async-done | bytes 524320 | tf_op jit(solution)/shard_map/all_to_all | solution.py:19
  31.2 1.6 collective-permute-start.8
  32.7 0.9 collective-permute-start.7
  33.7 2.4 %collective-permute-start.6 = (f32[8,4,8,512]{3,2,1,0:T(8,128)S(1)}, f32[8,4,8,512]{3,2,1,0:T(8,128)S(1)}, u32[]{:S(2)}, u32[]{:S(2)}) collective-permute-start(f32[8,4,8,512]{3,2,1,0:T(8,128)S(1)} %bitcast.4), channel_id=1, source_target_pairs={{0,192},{64,0},{128,64},{192,128},{1,193},{65,1},{129,65},{193,129... | collective-permute-start | bytes 1572872 | tf_op jit(solution)/shard_map/ppermute | solution.py:24
  36.1 1.1 collective-permute-done.1
  37.2 1.7 add_add_fusion.1
  38.9 5.6 %all-to-all-start = ((f32[8,72,128]{2,1,0:T(8,128)}), f32[8,72,128]{2,1,0:T(8,128)S(1)}, u32[]{:S(2)}, u32[]{:S(2)}) async-start(f32[8,72,128]{2,1,0:T(8,128)} %add_add_fusion.1), calls=%async_computation | async-start | bytes 589824 | tf_op jit(solution)/shard_map/all_to_all | solution.py:19
  44.6 1.4 collective-permute-done.8.refs_7_.refs_3_
  46.0 3.1 %collective-permute-done.7.refs_6_.refs_2_ = f32[8,4,8,512]{3,2,1,0:T(8,128)S(1)} collective-permute-done((f32[8,4,8,512]{3,2,1,0:T(8,128)S(1)}, f32[8,4,8,512]{3,2,1,0:T(8,128)S(1)}, u32[]{:S(2)}, u32[]{:S(2)}) %collective-permute-start.7) | collective-permute-done | bytes 524320 | tf_op jit(solution)/shard_map/ppermute | solution.py:24
  49.1 7.3 %collective-permute-done.6.refs_5_.refs_1_ = f32[8,4,8,512]{3,2,1,0:T(8,128)S(1)} collective-permute-done((f32[8,4,8,512]{3,2,1,0:T(8,128)S(1)}, f32[8,4,8,512]{3,2,1,0:T(8,128)S(1)}, u32[]{:S(2)}, u32[]{:S(2)}) %collective-permute-start.6) | collective-permute-done | bytes 524320 | tf_op jit(solution)/shard_map/ppermute | solution.py:24
  56.3 1.0 all-to-all-done
  57.4 0.7 broadcast_in_dim.2
  58.1 3.4 %all-to-all-start.1 = ((f32[8,72,128]{2,1,0:T(8,128)}), f32[8,72,128]{2,1,0:T(8,128)S(1)}, u32[]{:S(2)}, u32[]{:S(2)}) async-start(f32[8,72,128]{2,1,0:T(8,128)} %broadcast_in_dim.2), calls=%async_computation.1 | async-start | bytes 589824 | tf_op jit(solution)/shard_map/all_to_all | solution.py:19
  61.6 0.7 copy-done.6
  62.5 4.6 %shard_map.85 = f32[8,4,4,8,256]{4,3,2,1,0:T(8,128)} custom-call(s32[1]{0:T(128)} %bitcast.me_ref, bf16[256,896]{1,0:T(8,128)(2,1)} %grads_ref.3, f32[8,4,8,512]{3,2,1,0:T(8,128)} %bitcast.6, f32[8,4,8,512]{3,2,1,0:T(8,128)} %copy-done.5, f32[8,4,8,512]{3,2,1,0:T(8,128)} %copy-done.4, f32[8,4,8,512]{3,2,1,0:T(8,128)} %copy-done.3, ...), custom_call_target="tpu_custom_call" | custom-call | tf_op jit(solution)/shard_map/pallas_call | solution.py:29
  67.1 7.3 %all-to-all-done.1.refs_0_.refs_4_ = f32[8,72,128]{2,1,0:T(8,128)S(1)} async-done(((f32[8,72,128]{2,1,0:T(8,128)}), f32[8,72,128]{2,1,0:T(8,128)S(1)}, u32[]{:S(2)}, u32[]{:S(2)}) %all-to-all-start.1) | async-done | bytes 294944 | tf_op jit(solution)/shard_map/all_to_all | solution.py:19
  74.4 3.6 %all-to-all-start.4 = ((f32[8,4,4,8,256]{4,3,2,1,0:T(8,128)}), f32[8,4,4,8,256]{4,3,2,1,0:T(8,128)S(1)}, u32[]{:S(2)}, u32[]{:S(2)}) async-start(f32[8,4,4,8,256]{4,3,2,1,0:T(8,128)} %shard_map.85), calls=%async_computation.4 | async-start | bytes 2097152 | tf_op jit(solution)/shard_map/all_to_all | solution.py:19
  78.0 1.9 collective-permute-start.5
  79.9 1.1 collective-permute-start.4
  81.7 11.1 %collective-permute-done.5.refs_3_.refs_7_ = f32[8,72,128]{2,1,0:T(8,128)S(1)} collective-permute-done((f32[8,72,128]{2,1,0:T(8,128)S(1)}, f32[8,72,128]{2,1,0:T(8,128)S(1)}, u32[]{:S(2)}, u32[]{:S(2)}) %collective-permute-start.5) | collective-permute-done | bytes 294944 | tf_op jit(solution)/shard_map/ppermute | solution.py:24
  92.7 3.7 %collective-permute-done.3.refs_1_.refs_5_ = f32[8,72,128]{2,1,0:T(8,128)S(1)} collective-permute-done((f32[8,72,128]{2,1,0:T(8,128)S(1)}, f32[8,72,128]{2,1,0:T(8,128)S(1)}, u32[]{:S(2)}, u32[]{:S(2)}) %collective-permute-start.3) | collective-permute-done | bytes 294944 | tf_op jit(solution)/shard_map/ppermute | solution.py:24
  96.4 0.7 copy-done.11
  97.2 13.1 %shard_map.84 = (f32[8,32,512]{2,1,0:T(8,128)}, f32[8,32,512]{2,1,0:T(8,128)}, f32[8,32,512]{2,1,0:T(8,128)}, f32[8,32,512]{2,1,0:T(8,128)}) custom-call(s32[1]{0:T(128)} %bitcast.me_ref, s32[4]{0:T(128)} %len_ref.1, bf16[2048,896]{1,0:T(8,128)(2,1)} %grads_ref.2, f32[8,72,128]{2,1,0:T(8,128)} %copy-done.2, f32[8,72,128]{2,1,0:T(8,128)} %copy-done.11, ...), custom_call_target="tpu_custom_call" | custom-call | tf_op jit(solution)/shard_map/pallas_call | solution.py:29
  110.3 1.2 collective-permute-start.13
  112.1 2.6 %collective-permute-start.15 = (f32[8,32,512]{2,1,0:T(8,128)}, f32[8,32,512]{2,1,0:T(8,128)S(1)}, u32[]{:S(2)}, u32[]{:S(2)}) collective-permute-start(f32[8,32,512]{2,1,0:T(8,128)} %get-tuple-element.24), channel_id=1, source_target_pairs={{0,3},{1,0},{2,1},{3,2},{4,7},{5,4},{6,5},{7,6},{8,11},{9,8},{10,9... | collective-permute-start | bytes 1572872 | tf_op jit(solution)/shard_map/ppermute | solution.py:24
  114.7 12.2 %collective-permute-done.13 = f32[8,32,512]{2,1,0:T(8,128)S(1)} collective-permute-done((f32[8,32,512]{2,1,0:T(8,128)}, f32[8,32,512]{2,1,0:T(8,128)S(1)}, u32[]{:S(2)}, u32[]{:S(2)}) %collective-permute-start.13) | collective-permute-done | bytes 524320 | tf_op jit(solution)/shard_map/ppermute | solution.py:24
  126.9 10.2 %collective-permute-done.14 = f32[8,32,512]{2,1,0:T(8,128)S(1)} collective-permute-done((f32[8,32,512]{2,1,0:T(8,128)}, f32[8,32,512]{2,1,0:T(8,128)S(1)}, u32[]{:S(2)}, u32[]{:S(2)}) %collective-permute-start.14) | collective-permute-done | bytes 524320 | tf_op jit(solution)/shard_map/ppermute | solution.py:24
  137.2 2.1 %add_add_fusion = f32[8,32,512]{2,1,0:T(8,128)} fusion(f32[8,32,512]{2,1,0:T(8,128)S(1)} %collective-permute-done.15, f32[8,32,512]{2,1,0:T(8,128)S(1)} %collective-permute-done.14, f32[8,32,512]{2,1,0:T(8,128)} %get-tuple-element.21, f32[8,32,512]{2,1,0:T(8,128)S(1)} %collective-permute-done.13), kind=kLoop, calls=%fused_computation | loop fusion | flops 393216 | bytes 2621440 | tf_op jit(solution)/shard_map/add | solution.py:305
  139.3 6.8 %all-to-all-start.3 = ((f32[8,32,512]{2,1,0:T(8,128)}), f32[8,32,512]{2,1,0:T(8,128)S(1)}, u32[]{:S(2)}, u32[]{:S(2)}) async-start(f32[8,32,512]{2,1,0:T(8,128)} %add_add_fusion), calls=%async_computation.3 | async-start | bytes 1048576 | tf_op jit(solution)/shard_map/all_to_all | solution.py:19
  146.0 1.9 %shard_map.86 = (f32[4,8,256]{2,1,0:T(8,128)}, f32[4,8,256]{2,1,0:T(8,128)}, f32[4,8,256]{2,1,0:T(8,128)}, f32[4,8,256]{2,1,0:T(8,128)}) custom-call(s32[1]{0:T(128)} %bitcast.me_ref, f32[8,4,4,8,256]{4,3,2,1,0:T(8,128)} %copy-done.1), custom_call_target="tpu_custom_call" | custom-call | tf_op jit(solution)/shard_map/pallas_call | solution.py:29
  148.0 2.1 %collective-permute-start.17 = (f32[4,8,256]{2,1,0:T(8,128)}, f32[4,8,256]{2,1,0:T(8,128)S(1)}, u32[]{:S(2)}, u32[]{:S(2)}) collective-permute-start(f32[4,8,256]{2,1,0:T(8,128)} %get-tuple-element.27), channel_id=1, source_target_pairs={{0,2},{1,3},{2,0},{3,1},{4,6},{5,7},{6,4},{7,5},{8,10},{9,11},{10,... | collective-permute-start | bytes 98312 | tf_op jit(solution)/shard_map/ppermute | solution.py:24
  150.0 1.6 collective-permute-start.18
  151.7 1.6 collective-permute-done.16.refs_1_
  153.6 0.9 collective-permute-done.18.refs_3_
  155.1 2.4 %shard_map.87.refs_0_ = f32[32,8,128]{2,1,0:T(8,128)} custom-call(s32[1]{0:T(128)} %bitcast.me_ref, f32[32,128]{1,0:T(8,128)} %eig_ref.1, f32[4,8,256]{2,1,0:T(8,128)} %get-tuple-element.25.refs_0_, f32[4,8,256]{2,1,0:T(8,128)} %copy-done.19, f32[4,8,256]{2,1,0:T(8,128)} %copy-done.20, f32[4,8,256]{2,1,0:T(8,128)} %copy-done.21, f32[8,72,128]{2,1,0:T(8,128)} %copy-done.2, ...), custom_call_target="tpu_custom_call" | custom-call | tf_op jit(solution)/shard_map/pallas_call | solution.py:29
  157.5 1.0 collective-permute-start.21
  158.5 1.2 collective-permute-start.20
  160.0 4.0 %collective-permute-done.21.refs_3_ = f32[32,8,128]{2,1,0:T(8,128)S(1)} collective-permute-done((f32[32,8,128]{2,1,0:T(8,128)}, f32[32,8,128]{2,1,0:T(8,128)S(1)}, u32[]{:S(2)}, u32[]{:S(2)}) %collective-permute-start.21) | collective-permute-done | bytes 131104 | tf_op jit(solution)/shard_map/ppermute | solution.py:24
  164.0 1.4 collective-permute-done.20.refs_2_
  165.4 1.0 collective-permute-done.19.refs_1_
  166.7 1.0 collective-permute-done.23.refs_5_
  168.5 2.4 %shard_map.88 = f32[32,8,128]{2,1,0:T(8,128)} custom-call(s32[1]{0:T(128)} %bitcast.me_ref, f32[8,32,512]{2,1,0:T(8,128)} %copy-done.8, f32[32,8,128]{2,1,0:T(8,128)} %shard_map.87.refs_0_, f32[32,8,128]{2,1,0:T(8,128)} %copy-done.14, f32[32,8,128]{2,1,0:T(8,128)} %copy-done.13, f32[32,8,128]{2,1,0:T(8,128)} %copy-done.12, f32[32,8,128]{2,1,0:T(8,128)} %copy-done.15, ...), custom_call_target="tpu_custom_call" | custom-call | tf_op jit(solution)/shard_map/pallas_call | solution.py:29
  170.9 20.3 %all_to_all.30 = f32[32,8,128]{2,1,0:T(8,128)S(1)} all-to-all(f32[32,8,128]{2,1,0:T(8,128)} %shard_map.88), channel_id=1, replica_groups=mesh['y'=4,'core'=2,'z'=8,'x'=4] {'z','x'}, dimensions={0} | all-to-all | bytes 262144 | tf_op jit(solution)/shard_map/all_to_all | solution.py:19
  (72 shorter events, 5.1 us)
Async XLA Ops:
  2.0 29.2 %all-to-all-start.2 = ((f32[32,8,512]{2,1,0:T(8,128)}), f32[32,8,512]{2,1,0:T(8,128)S(1)}, u32[]{:S(2)}, u32[]{:S(2)}) async-start(f32[32,8,512]{2,1,0:T(8,128)} %shard_map.83), calls=%async_computation.2 | async-start | bytes 1048576 | tf_op jit(solution)/shard_map/all_to_all | solution.py:19
  16.3 17.4 %collective-permute-start = (f32[8,72,128]{2,1,0:T(8,128)}, f32[8,72,128]{2,1,0:T(8,128)S(1)}, u32[]{:S(2)}, u32[]{:S(2)}) collective-permute-start(f32[8,72,128]{2,1,0:T(8,128)} %get-tuple-element.18), channel_id=1, source_target_pairs={{0,2},{1,3},{2,0},{3,1},{4,6},{5,7},{6,4},{7,5},{8,10},{9,11},{10,... | collective-permute-start | bytes 884744 | tf_op jit(solution)/shard_map/ppermute | solution.py:24
  19.6 17.6 %collective-permute-start.1 = (f32[8,72,128]{2,1,0:T(8,128)}, f32[8,72,128]{2,1,0:T(8,128)S(1)}, u32[]{:S(2)}, u32[]{:S(2)}) collective-permute-start(f32[8,72,128]{2,1,0:T(8,128)} %get-tuple-element.19), channel_id=1, source_target_pairs={{0,1},{1,2},{2,3},{3,0},{4,5},{5,6},{6,7},{7,4},{8,9},{9,10},{10,1... | collective-permute-start | bytes 884744 | tf_op jit(solution)/shard_map/ppermute | solution.py:24
  20.1 17.1 %collective-permute-start.2 = (f32[8,72,128]{2,1,0:T(8,128)}, f32[8,72,128]{2,1,0:T(8,128)S(1)}, u32[]{:S(2)}, u32[]{:S(2)}) collective-permute-start(f32[8,72,128]{2,1,0:T(8,128)} %get-tuple-element.20), channel_id=1, source_target_pairs={{0,3},{1,0},{2,1},{3,2},{4,7},{5,4},{6,5},{7,6},{8,11},{9,8},{10,9... | collective-permute-start | bytes 884744 | tf_op jit(solution)/shard_map/ppermute | solution.py:24
  31.2 30.4 %copy-start = (f32[32,8,512]{2,1,0:T(8,128)}, f32[32,8,512]{2,1,0:T(8,128)S(1)}, u32[]{:S(2)}) copy-start(f32[32,8,512]{2,1,0:T(8,128)S(1)} %all-to-all-done.2) | copy-start | bytes 1572868
  31.2 14.8 %collective-permute-start.8 = (f32[8,4,8,512]{3,2,1,0:T(8,128)S(1)}, f32[8,4,8,512]{3,2,1,0:T(8,128)S(1)}, u32[]{:S(2)}, u32[]{:S(2)}) collective-permute-start(f32[8,4,8,512]{3,2,1,0:T(8,128)S(1)} %bitcast.2), channel_id=1, source_target_pairs={{0,64},{64,128},{128,192},{192,0},{1,65},{65,129},{129,193},{193,1... | collective-permute-start | bytes 1572872 | tf_op jit(solution)/shard_map/ppermute | solution.py:24
  32.7 16.3 %collective-permute-start.7 = (f32[8,4,8,512]{3,2,1,0:T(8,128)S(1)}, f32[8,4,8,512]{3,2,1,0:T(8,128)S(1)}, u32[]{:S(2)}, u32[]{:S(2)}) collective-permute-start(f32[8,4,8,512]{3,2,1,0:T(8,128)S(1)} %bitcast.3), channel_id=1, source_target_pairs={{0,128},{64,192},{128,0},{192,64},{1,129},{65,193},{129,1},{193,65... | collective-permute-start | bytes 1572872 | tf_op jit(solution)/shard_map/ppermute | solution.py:24
  33.7 22.6 %collective-permute-start.6 = (f32[8,4,8,512]{3,2,1,0:T(8,128)S(1)}, f32[8,4,8,512]{3,2,1,0:T(8,128)S(1)}, u32[]{:S(2)}, u32[]{:S(2)}) collective-permute-start(f32[8,4,8,512]{3,2,1,0:T(8,128)S(1)} %bitcast.4), channel_id=1, source_target_pairs={{0,192},{64,0},{128,64},{192,128},{1,193},{65,1},{129,65},{193,129... | collective-permute-start | bytes 1572872 | tf_op jit(solution)/shard_map/ppermute | solution.py:24
  38.9 18.4 %all-to-all-start = ((f32[8,72,128]{2,1,0:T(8,128)}), f32[8,72,128]{2,1,0:T(8,128)S(1)}, u32[]{:S(2)}, u32[]{:S(2)}) async-start(f32[8,72,128]{2,1,0:T(8,128)} %add_add_fusion.1), calls=%async_computation | async-start | bytes 589824 | tf_op jit(solution)/shard_map/all_to_all | solution.py:19
  44.6 16.9 %collective-permute-start.9 = (f32[8,4,8,512]{3,2,1,0:T(8,128)S(1)}, f32[8,4,8,512]{3,2,1,0:T(8,128)S(1)}, u32[]{:S(2)}, u32[]{:S(2)}) collective-permute-start(f32[8,4,8,512]{3,2,1,0:T(8,128)S(1)} %bitcast.5), channel_id=1, source_target_pairs={{0,32},{32,0},{1,33},{33,1},{2,34},{34,2},{3,35},{35,3},{4,36},{36... | collective-permute-start | bytes 1572872 | tf_op jit(solution)/shard_map/ppermute | solution.py:24
  46.0 15.6 %copy-start.3 = (f32[8,4,8,512]{3,2,1,0:T(8,128)}, f32[8,4,8,512]{3,2,1,0:T(8,128)S(1)}, u32[]{:S(2)}) copy-start(f32[8,4,8,512]{3,2,1,0:T(8,128)S(1)} %collective-permute-done.8.refs_7_.refs_3_) | copy-start | bytes 1572868
  46.0 15.6 %collective-permute-start.12 = (f32[8,4,8,512]{3,2,1,0:T(8,128)S(1)}, f32[8,4,8,512]{3,2,1,0:T(8,128)S(1)}, u32[]{:S(2)}, u32[]{:S(2)}) collective-permute-start(f32[8,4,8,512]{3,2,1,0:T(8,128)S(1)} %collective-permute-done.8.refs_7_.refs_3_), channel_id=1, source_target_pairs={{0,32},{32,0},{1,33},{33,1},{2,34},{34,2},{3,35},{35,3},{4,36},{36... | collective-permute-start | bytes 1572872 | tf_op jit(solution)/shard_map/ppermute | solution.py:24
  49.0 12.6 %copy-start.4 = (f32[8,4,8,512]{3,2,1,0:T(8,128)}, f32[8,4,8,512]{3,2,1,0:T(8,128)S(1)}, u32[]{:S(2)}) copy-start(f32[8,4,8,512]{3,2,1,0:T(8,128)S(1)} %collective-permute-done.7.refs_6_.refs_2_) | copy-start | bytes 1572868
  49.0 12.5 %collective-permute-start.11 = (f32[8,4,8,512]{3,2,1,0:T(8,128)S(1)}, f32[8,4,8,512]{3,2,1,0:T(8,128)}, u32[]{:S(2)}, u32[]{:S(2)}) collective-permute-start(f32[8,4,8,512]{3,2,1,0:T(8,128)S(1)} %collective-permute-done.7.refs_6_.refs_2_), channel_id=1, source_target_pairs={{0,32},{32,0},{1,33},{33,1},{2,34},{34,2},{3,35},{35,3},{4,36},{36... | collective-permute-start | bytes 1572872 | tf_op jit(solution)/shard_map/ppermute | solution.py:24
  56.3 5.3 %copy-start.5 = (f32[8,4,8,512]{3,2,1,0:T(8,128)}, f32[8,4,8,512]{3,2,1,0:T(8,128)S(1)}, u32[]{:S(2)}) copy-start(f32[8,4,8,512]{3,2,1,0:T(8,128)S(1)} %collective-permute-done.6.refs_5_.refs_1_) | copy-start | bytes 1572868
  56.3 5.2 %collective-permute-start.10 = (f32[8,4,8,512]{3,2,1,0:T(8,128)S(1)}, f32[8,4,8,512]{3,2,1,0:T(8,128)}, u32[]{:S(2)}, u32[]{:S(2)}) collective-permute-start(f32[8,4,8,512]{3,2,1,0:T(8,128)S(1)} %collective-permute-done.6.refs_5_.refs_1_), channel_id=1, source_target_pairs={{0,32},{32,0},{1,33},{33,1},{2,34},{34,2},{3,35},{35,3},{4,36},{36... | collective-permute-start | bytes 1572872 | tf_op jit(solution)/shard_map/ppermute | solution.py:24
  58.1 16.3 %all-to-all-start.1 = ((f32[8,72,128]{2,1,0:T(8,128)}), f32[8,72,128]{2,1,0:T(8,128)S(1)}, u32[]{:S(2)}, u32[]{:S(2)}) async-start(f32[8,72,128]{2,1,0:T(8,128)} %broadcast_in_dim.2), calls=%async_computation.1 | async-start | bytes 589824 | tf_op jit(solution)/shard_map/all_to_all | solution.py:19
  61.6 1.0 copy-start.7
  74.4 21.9 %copy-start.2 = (f32[8,72,128]{2,1,0:T(8,128)}, f32[8,72,128]{2,1,0:T(8,128)S(1)}, u32[]{:S(2)}) copy-start(f32[8,72,128]{2,1,0:T(8,128)S(1)} %all-to-all-done.1.refs_0_.refs_4_) | copy-start | bytes 884740
  74.4 64.8 %all-to-all-start.4 = ((f32[8,4,4,8,256]{4,3,2,1,0:T(8,128)}), f32[8,4,4,8,256]{4,3,2,1,0:T(8,128)S(1)}, u32[]{:S(2)}, u32[]{:S(2)}) async-start(f32[8,4,4,8,256]{4,3,2,1,0:T(8,128)} %shard_map.85), calls=%async_computation.4 | async-start | bytes 2097152 | tf_op jit(solution)/shard_map/all_to_all | solution.py:19
  78.0 14.7 %collective-permute-start.5 = (f32[8,72,128]{2,1,0:T(8,128)S(1)}, f32[8,72,128]{2,1,0:T(8,128)S(1)}, u32[]{:S(2)}, u32[]{:S(2)}) collective-permute-start(f32[8,72,128]{2,1,0:T(8,128)S(1)} %all-to-all-done.1.refs_0_.refs_4_), channel_id=1, source_target_pairs={{0,3},{1,0},{2,1},{3,2},{4,7},{5,4},{6,5},{7,6},{8,11},{9,8},{10,9... | collective-permute-start | bytes 884744 | tf_op jit(solution)/shard_map/ppermute | solution.py:24
  79.9 12.8 %collective-permute-start.4 = (f32[8,72,128]{2,1,0:T(8,128)S(1)}, f32[8,72,128]{2,1,0:T(8,128)S(1)}, u32[]{:S(2)}, u32[]{:S(2)}) collective-permute-start(f32[8,72,128]{2,1,0:T(8,128)S(1)} %all-to-all-done.1.refs_0_.refs_4_), channel_id=1, source_target_pairs={{0,2},{1,3},{2,0},{3,1},{4,6},{5,7},{6,4},{7,5},{8,10},{9,11},{10,... | collective-permute-start | bytes 884744 | tf_op jit(solution)/shard_map/ppermute | solution.py:24
  81.0 15.4 %collective-permute-start.3 = (f32[8,72,128]{2,1,0:T(8,128)S(1)}, f32[8,72,128]{2,1,0:T(8,128)S(1)}, u32[]{:S(2)}, u32[]{:S(2)}) collective-permute-start(f32[8,72,128]{2,1,0:T(8,128)S(1)} %all-to-all-done.1.refs_0_.refs_4_), channel_id=1, source_target_pairs={{0,1},{1,2},{2,3},{3,0},{4,5},{5,6},{6,7},{7,4},{8,9},{9,10},{10,1... | collective-permute-start | bytes 884744 | tf_op jit(solution)/shard_map/ppermute | solution.py:24
  92.7 3.7 %copy-start.9 = (f32[8,72,128]{2,1,0:T(8,128)}, f32[8,72,128]{2,1,0:T(8,128)S(1)}, u32[]{:S(2)}) copy-start(f32[8,72,128]{2,1,0:T(8,128)S(1)} %collective-permute-done.5.refs_3_.refs_7_) | copy-start | bytes 884740
  92.7 3.7 %copy-start.10 = (f32[8,72,128]{2,1,0:T(8,128)}, f32[8,72,128]{2,1,0:T(8,128)S(1)}, u32[]{:S(2)}) copy-start(f32[8,72,128]{2,1,0:T(8,128)S(1)} %collective-permute-done.4.refs_2_.refs_6_) | copy-start | bytes 884740
  110.3 16.6 %collective-permute-start.13 = (f32[8,32,512]{2,1,0:T(8,128)}, f32[8,32,512]{2,1,0:T(8,128)S(1)}, u32[]{:S(2)}, u32[]{:S(2)}) collective-permute-start(f32[8,32,512]{2,1,0:T(8,128)} %get-tuple-element.22), channel_id=1, source_target_pairs={{0,2},{1,3},{2,0},{3,1},{4,6},{5,7},{6,4},{7,5},{8,10},{9,11},{10,... | collective-permute-start | bytes 1572872 | tf_op jit(solution)/shard_map/ppermute | solution.py:24
  111.5 25.7 %collective-permute-start.14 = (f32[8,32,512]{2,1,0:T(8,128)}, f32[8,32,512]{2,1,0:T(8,128)S(1)}, u32[]{:S(2)}, u32[]{:S(2)}) collective-permute-start(f32[8,32,512]{2,1,0:T(8,128)} %get-tuple-element.23), channel_id=1, source_target_pairs={{0,1},{1,2},{2,3},{3,0},{4,5},{5,6},{6,7},{7,4},{8,9},{9,10},{10,1... | collective-permute-start | bytes 1572872 | tf_op jit(solution)/shard_map/ppermute | solution.py:24
  112.1 25.1 %collective-permute-start.15 = (f32[8,32,512]{2,1,0:T(8,128)}, f32[8,32,512]{2,1,0:T(8,128)S(1)}, u32[]{:S(2)}, u32[]{:S(2)}) collective-permute-start(f32[8,32,512]{2,1,0:T(8,128)} %get-tuple-element.24), channel_id=1, source_target_pairs={{0,3},{1,0},{2,1},{3,2},{4,7},{5,4},{6,5},{7,6},{8,11},{9,8},{10,9... | collective-permute-start | bytes 1572872 | tf_op jit(solution)/shard_map/ppermute | solution.py:24
  139.3 6.8 %copy-start.1 = (f32[8,4,4,8,256]{4,3,2,1,0:T(8,128)}, f32[8,4,4,8,256]{4,3,2,1,0:T(8,128)S(1)}, u32[]{:S(2)}) copy-start(f32[8,4,4,8,256]{4,3,2,1,0:T(8,128)S(1)} %all-to-all-done.4.blocks_ref) | copy-start | bytes 3145732
  139.3 27.2 %all-to-all-start.3 = ((f32[8,32,512]{2,1,0:T(8,128)}), f32[8,32,512]{2,1,0:T(8,128)S(1)}, u32[]{:S(2)}, u32[]{:S(2)}) async-start(f32[8,32,512]{2,1,0:T(8,128)} %add_add_fusion), calls=%async_computation.3 | async-start | bytes 1048576 | tf_op jit(solution)/shard_map/all_to_all | solution.py:19
  148.0 5.3 %collective-permute-start.16 = (f32[4,8,256]{2,1,0:T(8,128)}, f32[4,8,256]{2,1,0:T(8,128)S(1)}, u32[]{:S(2)}, u32[]{:S(2)}) collective-permute-start(f32[4,8,256]{2,1,0:T(8,128)} %get-tuple-element.26), channel_id=1, source_target_pairs={{0,1},{1,2},{2,3},{3,0},{4,5},{5,6},{6,7},{7,4},{8,9},{9,10},{10,1... | collective-permute-start | bytes 98312 | tf_op jit(solution)/shard_map/ppermute | solution.py:24
  148.0 5.7 %collective-permute-start.17 = (f32[4,8,256]{2,1,0:T(8,128)}, f32[4,8,256]{2,1,0:T(8,128)S(1)}, u32[]{:S(2)}, u32[]{:S(2)}) collective-permute-start(f32[4,8,256]{2,1,0:T(8,128)} %get-tuple-element.27), channel_id=1, source_target_pairs={{0,2},{1,3},{2,0},{3,1},{4,6},{5,7},{6,4},{7,5},{8,10},{9,11},{10,... | collective-permute-start | bytes 98312 | tf_op jit(solution)/shard_map/ppermute | solution.py:24
  150.0 4.5 %collective-permute-start.18 = (f32[4,8,256]{2,1,0:T(8,128)}, f32[4,8,256]{2,1,0:T(8,128)S(1)}, u32[]{:S(2)}, u32[]{:S(2)}) collective-permute-start(f32[4,8,256]{2,1,0:T(8,128)} %get-tuple-element.28), channel_id=1, source_target_pairs={{0,3},{1,0},{2,1},{3,2},{4,7},{5,4},{6,5},{7,6},{8,11},{9,8},{10,9... | collective-permute-start | bytes 98312 | tf_op jit(solution)/shard_map/ppermute | solution.py:24
  153.3 1.2 copy-start.19
  157.5 6.5 %collective-permute-start.21 = (f32[32,8,128]{2,1,0:T(8,128)}, f32[32,8,128]{2,1,0:T(8,128)S(1)}, u32[]{:S(2)}, u32[]{:S(2)}) collective-permute-start(f32[32,8,128]{2,1,0:T(8,128)} %shard_map.87.refs_0_), channel_id=1, source_target_pairs={{0,192},{64,0},{128,64},{192,128},{1,193},{65,1},{129,65},{193,129... | collective-permute-start | bytes 393224 | tf_op jit(solution)/shard_map/ppermute | solution.py:24
  158.5 6.8 %collective-permute-start.20 = (f32[32,8,128]{2,1,0:T(8,128)}, f32[32,8,128]{2,1,0:T(8,128)S(1)}, u32[]{:S(2)}, u32[]{:S(2)}) collective-permute-start(f32[32,8,128]{2,1,0:T(8,128)} %shard_map.87.refs_0_), channel_id=1, source_target_pairs={{0,128},{64,192},{128,0},{192,64},{1,129},{65,193},{129,1},{193,65... | collective-permute-start | bytes 393224 | tf_op jit(solution)/shard_map/ppermute | solution.py:24
  159.7 6.7 %collective-permute-start.19 = (f32[32,8,128]{2,1,0:T(8,128)}, f32[32,8,128]{2,1,0:T(8,128)S(1)}, u32[]{:S(2)}, u32[]{:S(2)}) collective-permute-start(f32[32,8,128]{2,1,0:T(8,128)} %shard_map.87.refs_0_), channel_id=1, source_target_pairs={{0,64},{64,128},{128,192},{192,0},{1,65},{65,129},{129,193},{193,1... | collective-permute-start | bytes 393224 | tf_op jit(solution)/shard_map/ppermute | solution.py:24
  160.0 6.4 %collective-permute-start.22 = (f32[32,8,128]{2,1,0:T(8,128)}, f32[32,8,128]{2,1,0:T(8,128)S(1)}, u32[]{:S(2)}, u32[]{:S(2)}) collective-permute-start(f32[32,8,128]{2,1,0:T(8,128)} %shard_map.87.refs_0_), channel_id=1, source_target_pairs={{0,32},{32,0},{1,33},{33,1},{2,34},{34,2},{3,35},{35,3},{4,36},{36... | collective-permute-start | bytes 393224 | tf_op jit(solution)/shard_map/ppermute | solution.py:24
  164.0 3.8 %copy-start.12 = (f32[32,8,128]{2,1,0:T(8,128)}, f32[32,8,128]{2,1,0:T(8,128)S(1)}, u32[]{:S(2)}) copy-start(f32[32,8,128]{2,1,0:T(8,128)S(1)} %collective-permute-done.21.refs_3_) | copy-start | bytes 393220
  164.0 2.5 %collective-permute-start.25 = (f32[32,8,128]{2,1,0:T(8,128)S(1)}, f32[32,8,128]{2,1,0:T(8,128)S(1)}, u32[]{:S(2)}, u32[]{:S(2)}) collective-permute-start(f32[32,8,128]{2,1,0:T(8,128)S(1)} %collective-permute-done.21.refs_3_), channel_id=1, source_target_pairs={{0,32},{32,0},{1,33},{33,1},{2,34},{34,2},{3,35},{35,3},{4,36},{36... | collective-permute-start | bytes 393224 | tf_op jit(solution)/shard_map/ppermute | solution.py:24
  165.4 2.4 %copy-start.13 = (f32[32,8,128]{2,1,0:T(8,128)}, f32[32,8,128]{2,1,0:T(8,128)S(1)}, u32[]{:S(2)}) copy-start(f32[32,8,128]{2,1,0:T(8,128)S(1)} %collective-permute-done.20.refs_2_) | copy-start | bytes 393220
  165.4 1.3 collective-permute-start.24
  166.4 1.4 copy-start.14
  166.4 1.3 collective-permute-start.23
  166.4 1.4 copy-start.8
  166.4 1.3 copy-start.15
  166.5 1.3 copy-start.16
  166.7 1.1 copy-start.17
  (5 other events, 3.7 us)
where the time goes:
time: 194 us; the launch traced here: 192 us
  waiting for transfers between devices  77.3 us (40%)
  starting transfers between devices  56.4 us (29%)
  Pallas kernels  29.5 us (15%)
  blocking collectives  20.3 us (10%)
  local copies, waits for them, and re-layouts  4.33 us (2%)
  other arithmetic  3.95 us (2%)
    ppermute x26, waiting for transfers between devices, shifted(): return lax.ppermute(shard, axis, [(i, (i + hops) % n) for i in range(n)])  60.6 us
    all_to_all x5, starting transfers between devices, exchange(): return lax.all_to_all(blocks, axis, 0, 0, tiled=True)  30.7 us
    pallas_call x7, Pallas kernels, call(): pl.pallas_call(kernel, out_shape=out_shape, grid_spec=pltpu.PrefetchScala...  29.5 us
    ppermute x26, starting transfers between devices, shifted(): return lax.ppermute(shard, axis, [(i, (i + hops) % n) for i in range(n)])  25.7 us
    all_to_all x1, blocking collectives, exchange(): return lax.all_to_all(blocks, axis, 0, 0, tiled=True)  20.3 us
    all_to_all x5, waiting for transfers between devices, exchange(): return lax.all_to_all(blocks, axis, 0, 0, tiled=True)  16.7 us
  transfers between devices with their start and end apart: 31, of which 19 were waited for; matrix products, arithmetic and copies ran while one was open for 2% of the time, Pallas kernels for 13%

commit v1 on v0

--- a/solution.py
+++ b/solution.py
@@ -1,3 +1,5 @@
+import functools
+
 import jax
 import jax.numpy as jnp
 from jax import lax
@@ -24,7 +26,7 @@
     return lax.ppermute(shard, axis, [(i, (i + hops) % n) for i in range(n)])
 
 
-def call(kernel, outs, in_specs, me, *args, grid=1, scratch=()):
+def call(kernel, outs, in_specs, me, *, args, grid=1, scratch=()):
     out_shape = [jax.ShapeDtypeStruct(*o) for o in outs]
     return pl.pallas_call(
         kernel,
@@ -80,21 +82,34 @@
         out_ref[f] = basis_ref[:, pl.ds(start, HALF)]
 
 
-def query_kernel(me_ref, grads_ref, *refs):
-    slabs, out_ref, halves_ref = refs[:8], refs[8], refs[9]
+def block_sum_kernel(me_ref, blocks_ref, out_ref):
+    total = blocks_ref[0]
+    for sender in range(1, 8):
+        total = total + blocks_ref[sender]
+    for target in range(8):
+        out_ref[target] = total
+
+
+def query_kernel(own, me_ref, grads_ref, *refs):
+    so_far = None if own else refs[0]
+    slabs, out_ref, half_ref = refs[-6:-2], refs[-2], refs[-1]
     _, core, _, _ = place(me_ref)
     cols = grads_ref.shape[1]
-    halves_ref[0] = grads_ref[:, :HALF]
-    halves_ref[1, :, : 2 * HALF - cols] = jnp.zeros((grads_ref.shape[0], 2 * HALF - cols), jnp.bfloat16)
-    halves_ref[1, :, 2 * HALF - cols :] = grads_ref[:, HALF:]
-    own, other = halves_ref[core], halves_ref[1 - core]
+    half = core if own else 1 - core
+
+    @pl.when(half == 0)
+    def _():
+        half_ref[...] = grads_ref[:, :HALF]
+
+    @pl.when(half == 1)
+    def _():
+        half_ref[:, : 2 * HALF - cols] = jnp.zeros((grads_ref.shape[0], 2 * HALF - cols), jnp.bfloat16)
+        half_ref[:, 2 * HALF - cols :] = grads_ref[:, HALF:]
+
     for slot in range(4):
-        total = None
-        for half, ref in ((own, slabs[slot]), (other, slabs[4 + slot])):
-            high, low = split(ref[...].reshape(256, HALF))
-            part = dot_nt(high, half) + dot_nt(low, half)
-            total = part if total is None else total + part
-        out_ref[:, :, slot] = total.reshape(8, 4, 8, total.shape[1])
+        high, low = split(slabs[slot][...].reshape(256, HALF))
+        total = (dot_nt(high, half_ref[...]) + dot_nt(low, half_ref[...])).reshape(8, 4, 8, half_ref.shape[0])
+        out_ref[:, :, slot] = total if own else so_far[:, :, slot] + total
 
 
 def query_sum_kernel(me_ref, blocks_ref, *out_refs):
@@ -132,12 +147,19 @@
             out_ref[rows, q, :] = both[32 * q + 8 * slot : 32 * q + 8 * slot + 8] / eig
 
 
-def hops_of(step):
-    return jnp.where(step < 3, 2 + (step == 2).astype(jnp.int32) - (step == 1).astype(jnp.int32), 0)
+def basis_product(core, slabs, high_ref, low_ref, out_ref):
+    total = None
+    for half, group in ((core, slabs[:4]), (1 - core, slabs[4:])):
+        value = jnp.concatenate([ref[...].reshape(64, HALF) for ref in group], 0)
+        high, low = split(value)
+        part = dot_nt(high, high_ref[half]) + dot_nt(high, low_ref[half]) + dot_nt(low, high_ref[half])
+        total = part if total is None else total + part
+    for slot in range(4):
+        out_ref[:, 8 * slot : 8 * slot + 8, :] = total[64 * slot : 64 * slot + 64].reshape(8, 8, 512)
 
 
 def train_kernel(me_ref, len_ref, grads_ref, *refs):
-    blocks, slabs, out_refs, (high_ref, low_ref, total_ref) = refs[:4], refs[4:12], refs[12:16], refs[16:]
+    blocks, slabs, (out_ref, high_ref, low_ref, total_ref) = refs[:4], refs[4:12], refs[12:]
     _, core, _, x = place(me_ref)
     step = pl.program_id(0)
     cols = grads_ref.shape[1]
@@ -177,20 +199,19 @@
                 ref[1, rows, : 2 * HALF - cols] = jnp.zeros((128, 2 * HALF - cols), jnp.bfloat16)
                 ref[1, rows, 2 * HALF - cols :] = value[:, HALF:]
 
-    @pl.when(step >= 4)
-    def _():
-        total = None
-        for half, group in ((core, slabs[:4]), (1 - core, slabs[4:])):
-            value = jnp.concatenate([ref[...].reshape(64, HALF) for ref in group], 0)
-            high, low = split(value)
-            part = dot_nt(high, high_ref[half]) + dot_nt(high, low_ref[half]) + dot_nt(low, high_ref[half])
-            total = part if total is None else total + part
-        for at, out_ref in zip((4, 5, 6, 7), out_refs):
-
-            @pl.when(step == at)
-            def _(out_ref=out_ref):
-                for slot in range(4):
-                    out_ref[:, 8 * slot : 8 * slot + 8, :] = total[64 * slot : 64 * slot + 64].reshape(8, 8, 512)
+    @pl.when(step == 4)
+    def _():
+        basis_product(core, slabs, high_ref, low_ref, out_ref)
+
+
+def product_kernel(me_ref, high_ref, low_ref, *refs):
+    slabs, out_refs = refs[:8], refs[8:]
+    _, core, _, _ = place(me_ref)
+    for at, out_ref in enumerate(out_refs):
+
+        @pl.when(pl.program_id(0) == at)
+        def _(out_ref=out_ref):
+            basis_product(core, slabs, high_ref, low_ref, out_ref)
 
 
 def score_kernel(me_ref, blocks_ref, *refs):
@@ -235,14 +256,15 @@
         input_rotation_kernel,
         [((8, 72, 128), f32)] * 4,
         [VMEM, VMEM, pl.BlockSpec((128, in_acts.shape[1]), lambda i, me: (0, me[0] % 32))],
-        me, in_acts, query_acts, input_basis,
+        me, args=(in_acts, query_acts, input_basis),
     )
     arrived = [parts[0]]
     for k in (2, 1, 3):
         arrived.append(shifted(parts[k], "x", k))
     part = arrived[0] + arrived[1] + arrived[2] + arrived[3]
-    part = jnp.sum(exchange(part, "z"), axis=0)
-    block = exchange(jnp.broadcast_to(part[None], (8, 72, 128)), "z")
+    part = exchange(part, "z")
+    (part,) = call(block_sum_kernel, [((8, 72, 128), f32)], [VMEM], me, args=(part,))
+    block = exchange(part, "z")
     blocks = [block] + [None] * 3
     for k in (2, 1, 3):
         blocks[k] = shifted(block, "x", k)
@@ -251,27 +273,30 @@
         basis_pick_kernel,
         [((32, 8, HALF), f32)],
         [pl.BlockSpec((8, output_basis.shape[1]), lambda i, me: (me[0] // 64, 0))],
-        me, output_basis,
+        me, args=(output_basis,),
     )
     slab = exchange(picked, ZX).reshape(8, 4, 8, HALF)
-    slabs = [slab] + [shifted(slab, "y", 4 - k) for k in (1, 2, 3)]
-    slabs = slabs + [shifted(s, "core", 1) for s in slabs]
-
-    (rot,) = call(
-        query_kernel,
-        [((8, 4, 4, 8, queries), f32)],
-        [VMEM] * 9,
-        me, query_grads, *slabs,
-        scratch=[pltpu.VMEM((2, queries, HALF), bf16)],
+    slabs = [slab]
+    for k in (1, 2, 3):
+        slabs.append(shifted(slab, "y", 4 - k))
+    for k in range(4):
+        slabs.append(shifted(slabs[k], "core", 1))
+
+    query_call = functools.partial(
+        call, outs=[((8, 4, 4, 8, queries), f32)], me=me, scratch=[pltpu.VMEM((queries, HALF), bf16)]
+    )
+    (rot,) = query_call(functools.partial(query_kernel, True), in_specs=[VMEM] * 5, args=(query_grads, *slabs[:4]))
+    (rot,) = query_call(
+        functools.partial(query_kernel, False), in_specs=[VMEM] * 6, args=(query_grads, rot, *slabs[4:])
     )
     rot = exchange(rot, "z")
-    rots = call(query_sum_kernel, [((4, 8, queries), f32)] * 4, [VMEM], me, rot)
+    rots = call(query_sum_kernel, [((4, 8, queries), f32)] * 4, [VMEM], me, args=(rot,))
     rots = [rots[0]] + [shifted(rots[k], "x", k) for k in (1, 2, 3)]
     (precond,) = call(
         precond_kernel,
         [((32, 8, 128), f32)],
         [VMEM] * 9,
-        me, eigenvalues, *rots, *blocks,
+        me, args=(eigenvalues, *rots, *blocks),
         scratch=[pltpu.VMEM((queries, 128), f32)],
     )
     preconds = [precond]
@@ -279,33 +304,40 @@
         preconds.append(shifted(precond, "y", k))
     preconds = preconds + [shifted(p, "core", 1) for p in preconds]
 
-    def slab_index(step, me):
-        return (0, lax.rem(me[0] % 4 + hops_of(jnp.maximum(step - 4, 0)), 4), 0, 0)
-
-    sent = call(
+    def slab_specs(first, stride=0):
+        return [
+            pl.BlockSpec((8, 1, 8, HALF), lambda i, me: (0, lax.rem(me[0] % 4 + first + stride * i, 4), 0, 0))
+        ] * 8
+
+    block_shape, sum_shape = ((8, 32, 512), f32), ((2, 512, HALF), bf16)
+    sent = [None] * 4
+    sent[2], high, low = call(
         train_kernel,
-        [((8, 32, 512), f32)] * 4,
+        [block_shape, sum_shape, sum_shape],
         [
             SMEM,
             pl.BlockSpec((512, out_grads.shape[1]), lambda i, me: (lax.rem(me[0] % 4 + 4 - jnp.minimum(i, 3), 4), 0)),
             *[VMEM] * 4,
-            *[pl.BlockSpec((8, 1, 8, HALF), slab_index)] * 8,
+            *slab_specs(2),
         ],
-        me, doc_lengths, out_grads, *blocks, *slabs,
-        grid=8,
-        scratch=[
-            pltpu.VMEM((2, 512, HALF), bf16),
-            pltpu.VMEM((2, 512, HALF), bf16),
-            pltpu.VMEM((4, 128, out_grads.shape[1]), f32),
-        ],
-    )
-    arrived = [sent[3]]
-    for n, k in enumerate((2, 1, 3)):
-        arrived.append(shifted(sent[n], "x", k))
-    train = arrived[0] + arrived[1] + arrived[2] + arrived[3]
+        me,
+        args=(doc_lengths, out_grads, *blocks, *slabs),
+        grid=5,
+        scratch=[pltpu.VMEM((4, 128, out_grads.shape[1]), f32)],
+    )
+    sent[1], sent[3] = call(
+        product_kernel, [block_shape] * 2, [VMEM, VMEM, *slab_specs(1, 2)], me, args=(high, low, *slabs), grid=2
+    )
+    sent[2] = shifted(sent[2], "x", 2)
+    (sent[0],) = call(
+        product_kernel, [block_shape], [VMEM, VMEM, *slab_specs(0)], me, args=(high, low, *slabs)
+    )
+    for k in (1, 3):
+        sent[k] = shifted(sent[k], "x", k)
+    train = sent[0] + sent[1] + sent[2] + sent[3]
     train = exchange(train, "z")
 
-    (partial_scores,) = call(score_kernel, [((32, 8, 128), f32)], [VMEM] * 9, me, train, *preconds)
+    (partial_scores,) = call(score_kernel, [((32, 8, 128), f32)], [VMEM] * 9, me, args=(train, *preconds))
     return jnp.sum(exchange(partial_scores, ZX), axis=(0, 2)).reshape(2, 4)
 
 

time: 194 us -> 197 us (1.015)
  Pallas kernels: 29.5 us -> 38.7 us
  waiting for transfers between devices: 77.3 us -> 70.3 us
    pallas_call x7 -> x11, Pallas kernels: 29.5 us -> 38.7 us  [call(): pl.pallas_call(kernel, out_shape=out_shape, grid_spec=pltpu.PrefetchScala...]
    all_to_all x5, waiting for transfers between devices: 16.7 us -> 13 us  [exchange(): return lax.all_to_all(blocks, axis, 0, 0, tiled=True)]
    ppermute x26, waiting for transfers between devices: 60.6 us -> 57.3 us  [shifted(): return lax.ppermute(shard, axis, [(i, (i + hops) % n) for i in range(n)])]
    unnamed x44 -> x48, local copies, waits for them, and re-layouts: 2.95 us -> 4.66 us
  transfers between devices with their start and end apart: 31 -> 31, of which waited for: 19 -> 18; matrix products, arithmetic and copies ran while one was open for 2% -> 2% of each run, Pallas kernels for 13% -> 18%
where the time goes in v1:
time: 197 us; the launch traced here: 195 us
  waiting for transfers between devices  70.3 us (36%)
  starting transfers between devices  57.6 us (29%)
  Pallas kernels  38.7 us (20%)
  blocking collectives  19.3 us (10%)
  local copies, waits for them, and re-layouts  5.31 us (3%)
  other arithmetic  3.94 us (2%)
    ppermute x26, waiting for transfers between devices, shifted(): return lax.ppermute(shard, axis, [(i, (i + hops) % n) for i in range(n)])  57.3 us
    pallas_call x11, Pallas kernels, call(): pl.pallas_call(kernel, out_shape=out_shape, grid_spec=pltpu.PrefetchScala...  38.7 us
    all_to_all x5, starting transfers between devices, exchange(): return lax.all_to_all(blocks, axis, 0, 0, tiled=True)  30.7 us
    ppermute x26, starting transfers between devices, shifted(): return lax.ppermute(shard, axis, [(i, (i + hops) % n) for i in range(n)])  26.9 us
    all_to_all x1, blocking collectives, exchange(): return lax.all_to_all(blocks, axis, 0, 0, tiled=True)  19.3 us
    all_to_all x5, waiting for transfers between devices, exchange(): return lax.all_to_all(blocks, axis, 0, 0, tiled=True)  13 us
    unnamed x48, local copies, waits for them, and re-layouts  4.66 us
  transfers between devices with their start and end apart: 31, of which 18 were waited for; matrix products, arithmetic and copies ran while one was open for 2% of the time, Pallas kernels for 18%

profile of v1, /device:TPU:8, one launch (start us, length us, event | category | flops | bytes accessed | tf_op | source)
XLA Modules:
  0.0 195.4 jit_solution(25765745276485821)
XLA Ops:
  0.0 2.0 %shard_map.84 = f32[32,8,512]{2,1,0:T(8,128)} custom-call(s32[1]{0:T(128)} %bitcast.me_ref, f32[32,28672]{1,0:T(8,128)} %basis_ref.3), custom_call_target="tpu_custom_call" | custom-call | tf_op jit(solution)/shard_map/pallas_call | solution.py:31
  2.0 11.3 %all-to-all-start.2 = ((f32[32,8,512]{2,1,0:T(8,128)}), f32[32,8,512]{2,1,0:T(8,128)S(1)}, u32[]{:S(2)}, u32[]{:S(2)}) async-start(f32[32,8,512]{2,1,0:T(8,128)} %shard_map.84), calls=%async_computation.2 | async-start | bytes 1048576 | tf_op jit(solution)/shard_map/all_to_all | solution.py:21
  13.4 3.0 %shard_map.82 = (f32[8,72,128]{2,1,0:T(8,128)}, f32[8,72,128]{2,1,0:T(8,128)}, f32[8,72,128]{2,1,0:T(8,128)}, f32[8,72,128]{2,1,0:T(8,128)}) custom-call(s32[1]{0:T(128)} %bitcast.me_ref, bf16[2048,256]{1,0:T(8,128)(2,1)} %acts_ref.1, bf16[256,256]{1,0:T(8,128)(2,1)} %query_ref.1, f32[128,8192]{1,0:T(8,128)} %basis_ref.2), custom_call_target="tpu_custom_call" | custom-call | tf_op jit(solution)/shard_map/pallas_call | solution.py:31
  16.3 3.3 %collective-permute-start = (f32[8,72,128]{2,1,0:T(8,128)}, f32[8,72,128]{2,1,0:T(8,128)S(1)}, u32[]{:S(2)}, u32[]{:S(2)}) collective-permute-start(f32[8,72,128]{2,1,0:T(8,128)} %get-tuple-element.19), channel_id=1, source_target_pairs={{0,2},{1,3},{2,0},{3,1},{4,6},{5,7},{6,4},{7,5},{8,10},{9,11},{10,... | collective-permute-start | bytes 884744 | tf_op jit(solution)/shard_map/ppermute | solution.py:26
  20.2 2.7 %collective-permute-start.2 = (f32[8,72,128]{2,1,0:T(8,128)}, f32[8,72,128]{2,1,0:T(8,128)S(1)}, u32[]{:S(2)}, u32[]{:S(2)}) collective-permute-start(f32[8,72,128]{2,1,0:T(8,128)} %get-tuple-element.21), channel_id=1, source_target_pairs={{0,3},{1,0},{2,1},{3,2},{4,7},{5,4},{6,5},{7,6},{8,11},{9,8},{10,9... | collective-permute-start | bytes 884744 | tf_op jit(solution)/shard_map/ppermute | solution.py:26
  22.9 8.3 %all-to-all-done.2 = f32[32,8,512]{2,1,0:T(8,128)S(1)} async-done(((f32[32,8,512]{2,1,0:T(8,128)}), f32[32,8,512]{2,1,0:T(8,128)S(1)}, u32[]{:S(2)}, u32[]{:S(2)}) %all-to-all-start.2) | async-done | bytes 524320 | tf_op jit(solution)/shard_map/all_to_all | solution.py:21
  31.2 1.6 collective-permute-start.8
  32.8 0.9 collective-permute-start.7
  33.7 2.4 %collective-permute-start.6 = (f32[8,4,8,512]{3,2,1,0:T(8,128)S(1)}, f32[8,4,8,512]{3,2,1,0:T(8,128)}, u32[]{:S(2)}, u32[]{:S(2)}) collective-permute-start(f32[8,4,8,512]{3,2,1,0:T(8,128)S(1)} %bitcast.4), channel_id=1, source_target_pairs={{0,192},{64,0},{128,64},{192,128},{1,193},{65,1},{129,65},{193,129... | collective-permute-start | bytes 1572872 | tf_op jit(solution)/shard_map/ppermute | solution.py:26
  36.1 1.1 collective-permute-done.1
  37.3 1.7 add_add_fusion.1
  39.0 5.6 %all-to-all-start = ((f32[8,72,128]{2,1,0:T(8,128)}), f32[8,72,128]{2,1,0:T(8,128)S(1)}, u32[]{:S(2)}, u32[]{:S(2)}) async-start(f32[8,72,128]{2,1,0:T(8,128)} %add_add_fusion.1), calls=%async_computation | async-start | bytes 589824 | tf_op jit(solution)/shard_map/all_to_all | solution.py:21
  44.6 1.4 collective-permute-done.8.refs_7_.refs_3_
  46.0 3.2 %collective-permute-done.7.refs_6_.refs_2_ = f32[8,4,8,512]{3,2,1,0:T(8,128)} collective-permute-done((f32[8,4,8,512]{3,2,1,0:T(8,128)S(1)}, f32[8,4,8,512]{3,2,1,0:T(8,128)}, u32[]{:S(2)}, u32[]{:S(2)}) %collective-permute-start.7) | collective-permute-done | bytes 524320 | tf_op jit(solution)/shard_map/ppermute | solution.py:26
  49.2 7.3 %collective-permute-done.6.refs_5_.refs_1_ = f32[8,4,8,512]{3,2,1,0:T(8,128)} collective-permute-done((f32[8,4,8,512]{3,2,1,0:T(8,128)S(1)}, f32[8,4,8,512]{3,2,1,0:T(8,128)}, u32[]{:S(2)}, u32[]{:S(2)}) %collective-permute-start.6) | collective-permute-done | bytes 524320 | tf_op jit(solution)/shard_map/ppermute | solution.py:26
  56.5 0.9 all-to-all-done.blocks_ref
  58.1 1.7 shard_map.83
  59.8 3.4 %all-to-all-start.1 = ((f32[8,72,128]{2,1,0:T(8,128)}), f32[8,72,128]{2,1,0:T(8,128)S(1)}, u32[]{:S(2)}, u32[]{:S(2)}) async-start(f32[8,72,128]{2,1,0:T(8,128)} %shard_map.83), calls=%async_computation.1 | async-start | bytes 589824 | tf_op jit(solution)/shard_map/all_to_all | solution.py:21
  63.3 3.4 %shard_map.88.refs_0_ = f32[8,4,4,8,256]{4,3,2,1,0:T(8,128)} custom-call(s32[1]{0:T(128)} %bitcast.me_ref, bf16[256,896]{1,0:T(8,128)(2,1)} %grads_ref.5, f32[8,4,8,512]{3,2,1,0:T(8,128)} %bitcast.6, f32[8,4,8,512]{3,2,1,0:T(8,128)} %collective-permute-done.6.refs_5_.refs_1_, f32[8,4,8,512]{3,2,1,0:T(8,128)} %collective-permute-done.7.refs_6_.refs_2_, ...), custom_call_target="tpu_custom_call" | custom-call | tf_op jit(solution)/shard_map/pallas_call | solution.py:31
  68.7 3.8 %shard_map.89 = f32[8,4,4,8,256]{4,3,2,1,0:T(8,128)} custom-call(s32[1]{0:T(128)} %bitcast.me_ref, bf16[256,896]{1,0:T(8,128)(2,1)} %grads_ref.5, f32[8,4,4,8,256]{4,3,2,1,0:T(8,128)} %shard_map.88.refs_0_, f32[8,4,8,512]{3,2,1,0:T(8,128)} %copy-done.1, f32[8,4,8,512]{3,2,1,0:T(8,128)} %copy-done.4, f32[8,4,8,512]{3,2,1,0:T(8,128)} %copy-done.3, ...), custom_call_target="tpu_custom_call" | custom-call | tf_op jit(solution)/shard_map/pallas_call | solution.py:31
  72.5 3.8 %all-to-all-done.1.refs_0_.refs_4_ = f32[8,72,128]{2,1,0:T(8,128)S(1)} async-done(((f32[8,72,128]{2,1,0:T(8,128)}), f32[8,72,128]{2,1,0:T(8,128)S(1)}, u32[]{:S(2)}, u32[]{:S(2)}) %all-to-all-start.1) | async-done | bytes 294944 | tf_op jit(solution)/shard_map/all_to_all | solution.py:21
  76.3 3.6 %all-to-all-start.4 = ((f32[8,4,4,8,256]{4,3,2,1,0:T(8,128)}), f32[8,4,4,8,256]{4,3,2,1,0:T(8,128)S(1)}, u32[]{:S(2)}, u32[]{:S(2)}) async-start(f32[8,4,4,8,256]{4,3,2,1,0:T(8,128)} %shard_map.89), calls=%async_computation.4 | async-start | bytes 2097152 | tf_op jit(solution)/shard_map/all_to_all | solution.py:21
  79.8 1.9 collective-permute-start.5
  81.7 1.1 collective-permute-start.4
  83.5 11.1 %collective-permute-done.5.refs_3_.refs_7_ = f32[8,72,128]{2,1,0:T(8,128)S(1)} collective-permute-done((f32[8,72,128]{2,1,0:T(8,128)S(1)}, f32[8,72,128]{2,1,0:T(8,128)S(1)}, u32[]{:S(2)}, u32[]{:S(2)}) %collective-permute-start.5) | collective-permute-done | bytes 294944 | tf_op jit(solution)/shard_map/ppermute | solution.py:26
  94.5 3.7 %collective-permute-done.3.refs_1_.refs_5_ = f32[8,72,128]{2,1,0:T(8,128)S(1)} collective-permute-done((f32[8,72,128]{2,1,0:T(8,128)S(1)}, f32[8,72,128]{2,1,0:T(8,128)S(1)}, u32[]{:S(2)}, u32[]{:S(2)}) %collective-permute-start.3) | collective-permute-done | bytes 294944 | tf_op jit(solution)/shard_map/ppermute | solution.py:26
  98.9 9.1 %shard_map.85 = (f32[8,32,512]{2,1,0:T(8,128)}, bf16[2,512,512]{2,1,0:T(8,128)(2,1)}, bf16[2,512,512]{2,1,0:T(8,128)(2,1)}) custom-call(s32[1]{0:T(128)} %bitcast.me_ref, s32[4]{0:T(128)} %len_ref.1, bf16[2048,896]{1,0:T(8,128)(2,1)} %grads_ref.3, f32[8,72,128]{2,1,0:T(8,128)} %copy-done.7, f32[8,72,128]{2,1,0:T(8,128)} %copy-done.11, ...), custom_call_target="tpu_custom_call" | custom-call | tf_op jit(solution)/shard_map/pallas_call | solution.py:31
  108.0 5.3 %shard_map.87 = (f32[8,32,512]{2,1,0:T(8,128)}, f32[8,32,512]{2,1,0:T(8,128)}) custom-call(s32[1]{0:T(128)} %bitcast.me_ref, bf16[2,512,512]{2,1,0:T(8,128)(2,1)} %get-tuple-element.22.high_ref, bf16[2,512,512]{2,1,0:T(8,128)(2,1)} %get-tuple-element.23.low_ref, f32[8,4,8,512]{3,2,1,0:T(8,128)} %bitcast.8, ...), custom_call_target="tpu_custom_call" | custom-call | tf_op jit(solution)/shard_map/pallas_call | solution.py:31
  113.3 3.2 %collective-permute-start.15 = (f32[8,32,512]{2,1,0:T(8,128)}, f32[8,32,512]{2,1,0:T(8,128)S(1)}, u32[]{:S(2)}, u32[]{:S(2)}) collective-permute-start(f32[8,32,512]{2,1,0:T(8,128)} %get-tuple-element.26), channel_id=1, source_target_pairs={{0,3},{1,0},{2,1},{3,2},{4,7},{5,4},{6,5},{7,6},{8,11},{9,8},{10,9... | collective-permute-start | bytes 1572872 | tf_op jit(solution)/shard_map/ppermute | solution.py:26
  116.6 3.6 %shard_map.86 = f32[8,32,512]{2,1,0:T(8,128)} custom-call(s32[1]{0:T(128)} %bitcast.me_ref, bf16[2,512,512]{2,1,0:T(8,128)(2,1)} %get-tuple-element.22.high_ref, bf16[2,512,512]{2,1,0:T(8,128)(2,1)} %get-tuple-element.23.low_ref, f32[8,4,8,512]{3,2,1,0:T(8,128)} %bitcast.9, f32[8,4,8,512]{3,2,1,0:T(8,128)} %collective-permute-done.6.refs_5_.refs_1_, ...), custom_call_target="tpu_custom_call" | custom-call | tf_op jit(solution)/shard_map/pallas_call | solution.py:31
  120.2 19.6 %collective-permute-done.13 = f32[8,32,512]{2,1,0:T(8,128)S(1)} collective-permute-done((f32[8,32,512]{2,1,0:T(8,128)}, f32[8,32,512]{2,1,0:T(8,128)S(1)}, u32[]{:S(2)}, u32[]{:S(2)}) %collective-permute-start.13) | collective-permute-done | bytes 524320 | tf_op jit(solution)/shard_map/ppermute | solution.py:26
  139.8 2.0 %add_add_fusion = f32[8,32,512]{2,1,0:T(8,128)} fusion(f32[8,32,512]{2,1,0:T(8,128)S(1)} %collective-permute-done.15, f32[8,32,512]{2,1,0:T(8,128)S(1)} %collective-permute-done.14, f32[8,32,512]{2,1,0:T(8,128)} %shard_map.86, f32[8,32,512]{2,1,0:T(8,128)S(1)} %collective-permute-done.13), kind=kLoop, calls=%fused_computation | loop fusion | flops 393216 | bytes 2621440 | tf_op jit(solution)/shard_map/add | solution.py:337
  141.9 6.8 %all-to-all-start.3 = ((f32[8,32,512]{2,1,0:T(8,128)}), f32[8,32,512]{2,1,0:T(8,128)S(1)}, u32[]{:S(2)}, u32[]{:S(2)}) async-start(f32[8,32,512]{2,1,0:T(8,128)} %add_add_fusion), calls=%async_computation.3 | async-start | bytes 1048576 | tf_op jit(solution)/shard_map/all_to_all | solution.py:21
  148.7 1.9 shard_map.90
  150.6 0.9 collective-permute-start.16
  151.5 3.6 %collective-permute-start.17 = (f32[4,8,256]{2,1,0:T(8,128)}, f32[4,8,256]{2,1,0:T(8,128)S(1)}, u32[]{:S(2)}, u32[]{:S(2)}) collective-permute-start(f32[4,8,256]{2,1,0:T(8,128)} %get-tuple-element.29), channel_id=1, source_target_pairs={{0,2},{1,3},{2,0},{3,1},{4,6},{5,7},{6,4},{7,5},{8,10},{9,11},{10,... | collective-permute-start | bytes 98312 | tf_op jit(solution)/shard_map/ppermute | solution.py:26
  155.0 0.9 collective-permute-done.16.refs_1_
  155.9 1.5 collective-permute-done.17.refs_2_
  157.5 1.7 collective-permute-done.18.refs_3_
  159.8 2.4 %shard_map.91.refs_0_ = f32[32,8,128]{2,1,0:T(8,128)} custom-call(s32[1]{0:T(128)} %bitcast.me_ref, f32[32,128]{1,0:T(8,128)} %eig_ref.1, f32[4,8,256]{2,1,0:T(8,128)} %get-tuple-element.27.refs_0_, f32[4,8,256]{2,1,0:T(8,128)} %copy-done.20, f32[4,8,256]{2,1,0:T(8,128)} %copy-done.21, f32[4,8,256]{2,1,0:T(8,128)} %copy-done.22, f32[8,72,128]{2,1,0:T(8,128)} %copy-done.7, ...), custom_call_target="tpu_custom_call" | custom-call | tf_op jit(solution)/shard_map/pallas_call | solution.py:31
  162.9 1.9 collective-permute-start.20
  164.9 1.4 collective-permute-start.19
  166.3 1.1 collective-permute-done.21.refs_3_
  167.3 2.3 %collective-permute-done.20.refs_2_ = f32[32,8,128]{2,1,0:T(8,128)S(1)} collective-permute-done((f32[32,8,128]{2,1,0:T(8,128)}, f32[32,8,128]{2,1,0:T(8,128)S(1)}, u32[]{:S(2)}, u32[]{:S(2)}) %collective-permute-start.20) | collective-permute-done | bytes 131104 | tf_op jit(solution)/shard_map/ppermute | solution.py:26
  169.6 1.2 collective-permute-done.19.refs_1_
  171.0 1.2 collective-permute-done.23.refs_5_
  172.8 2.4 %shard_map.92 = f32[32,8,128]{2,1,0:T(8,128)} custom-call(s32[1]{0:T(128)} %bitcast.me_ref, f32[8,32,512]{2,1,0:T(8,128)} %copy-done.8, f32[32,8,128]{2,1,0:T(8,128)} %shard_map.91.refs_0_, f32[32,8,128]{2,1,0:T(8,128)} %copy-done.15, f32[32,8,128]{2,1,0:T(8,128)} %copy-done.14, f32[32,8,128]{2,1,0:T(8,128)} %copy-done.13, f32[32,8,128]{2,1,0:T(8,128)} %copy-done.16, ...), custom_call_target="tpu_custom_call" | custom-call | tf_op jit(solution)/shard_map/pallas_call | solution.py:31
  175.3 19.3 %all_to_all.30 = f32[32,8,128]{2,1,0:T(8,128)S(1)} all-to-all(f32[32,8,128]{2,1,0:T(8,128)} %shard_map.92), channel_id=1, replica_groups=mesh['y'=4,'core'=2,'z'=8,'x'=4] {'z','x'}, dimensions={0} | all-to-all | bytes 262144 | tf_op jit(solution)/shard_map/all_to_all | solution.py:21
  (78 shorter events, 7.6 us)
Async XLA Ops:
  2.0 29.2 %all-to-all-start.2 = ((f32[32,8,512]{2,1,0:T(8,128)}), f32[32,8,512]{2,1,0:T(8,128)S(1)}, u32[]{:S(2)}, u32[]{:S(2)}) async-start(f32[32,8,512]{2,1,0:T(8,128)} %shard_map.84), calls=%async_computation.2 | async-start | bytes 1048576 | tf_op jit(solution)/shard_map/all_to_all | solution.py:21
  16.3 17.4 %collective-permute-start = (f32[8,72,128]{2,1,0:T(8,128)}, f32[8,72,128]{2,1,0:T(8,128)S(1)}, u32[]{:S(2)}, u32[]{:S(2)}) collective-permute-start(f32[8,72,128]{2,1,0:T(8,128)} %get-tuple-element.19), channel_id=1, source_target_pairs={{0,2},{1,3},{2,0},{3,1},{4,6},{5,7},{6,4},{7,5},{8,10},{9,11},{10,... | collective-permute-start | bytes 884744 | tf_op jit(solution)/shard_map/ppermute | solution.py:26
  19.6 17.6 %collective-permute-start.1 = (f32[8,72,128]{2,1,0:T(8,128)}, f32[8,72,128]{2,1,0:T(8,128)S(1)}, u32[]{:S(2)}, u32[]{:S(2)}) collective-permute-start(f32[8,72,128]{2,1,0:T(8,128)} %get-tuple-element.20), channel_id=1, source_target_pairs={{0,1},{1,2},{2,3},{3,0},{4,5},{5,6},{6,7},{7,4},{8,9},{9,10},{10,1... | collective-permute-start | bytes 884744 | tf_op jit(solution)/shard_map/ppermute | solution.py:26
  20.2 17.1 %collective-permute-start.2 = (f32[8,72,128]{2,1,0:T(8,128)}, f32[8,72,128]{2,1,0:T(8,128)S(1)}, u32[]{:S(2)}, u32[]{:S(2)}) collective-permute-start(f32[8,72,128]{2,1,0:T(8,128)} %get-tuple-element.21), channel_id=1, source_target_pairs={{0,3},{1,0},{2,1},{3,2},{4,7},{5,4},{6,5},{7,6},{8,11},{9,8},{10,9... | collective-permute-start | bytes 884744 | tf_op jit(solution)/shard_map/ppermute | solution.py:26
  31.2 32.1 %copy-start = (f32[32,8,512]{2,1,0:T(8,128)}, f32[32,8,512]{2,1,0:T(8,128)S(1)}, u32[]{:S(2)}) copy-start(f32[32,8,512]{2,1,0:T(8,128)S(1)} %all-to-all-done.2) | copy-start | bytes 1572868
  31.2 14.8 %collective-permute-start.8 = (f32[8,4,8,512]{3,2,1,0:T(8,128)S(1)}, f32[8,4,8,512]{3,2,1,0:T(8,128)S(1)}, u32[]{:S(2)}, u32[]{:S(2)}) collective-permute-start(f32[8,4,8,512]{3,2,1,0:T(8,128)S(1)} %bitcast.2), channel_id=1, source_target_pairs={{0,64},{64,128},{128,192},{192,0},{1,65},{65,129},{129,193},{193,1... | collective-permute-start | bytes 1572872 | tf_op jit(solution)/shard_map/ppermute | solution.py:26
  32.8 16.4 %collective-permute-start.7 = (f32[8,4,8,512]{3,2,1,0:T(8,128)S(1)}, f32[8,4,8,512]{3,2,1,0:T(8,128)}, u32[]{:S(2)}, u32[]{:S(2)}) collective-permute-start(f32[8,4,8,512]{3,2,1,0:T(8,128)S(1)} %bitcast.3), channel_id=1, source_target_pairs={{0,128},{64,192},{128,0},{192,64},{1,129},{65,193},{129,1},{193,65... | collective-permute-start | bytes 1572872 | tf_op jit(solution)/shard_map/ppermute | solution.py:26
  33.7 22.8 %collective-permute-start.6 = (f32[8,4,8,512]{3,2,1,0:T(8,128)S(1)}, f32[8,4,8,512]{3,2,1,0:T(8,128)}, u32[]{:S(2)}, u32[]{:S(2)}) collective-permute-start(f32[8,4,8,512]{3,2,1,0:T(8,128)S(1)} %bitcast.4), channel_id=1, source_target_pairs={{0,192},{64,0},{128,64},{192,128},{1,193},{65,1},{129,65},{193,129... | collective-permute-start | bytes 1572872 | tf_op jit(solution)/shard_map/ppermute | solution.py:26
  39.0 18.4 %all-to-all-start = ((f32[8,72,128]{2,1,0:T(8,128)}), f32[8,72,128]{2,1,0:T(8,128)S(1)}, u32[]{:S(2)}, u32[]{:S(2)}) async-start(f32[8,72,128]{2,1,0:T(8,128)} %add_add_fusion.1), calls=%async_computation | async-start | bytes 589824 | tf_op jit(solution)/shard_map/all_to_all | solution.py:21
  44.6 22.1 %collective-permute-start.9 = (f32[8,4,8,512]{3,2,1,0:T(8,128)S(1)}, f32[8,4,8,512]{3,2,1,0:T(8,128)S(1)}, u32[]{:S(2)}, u32[]{:S(2)}) collective-permute-start(f32[8,4,8,512]{3,2,1,0:T(8,128)S(1)} %bitcast.5), channel_id=1, source_target_pairs={{0,32},{32,0},{1,33},{33,1},{2,34},{34,2},{3,35},{35,3},{4,36},{36... | collective-permute-start | bytes 1572872 | tf_op jit(solution)/shard_map/ppermute | solution.py:26
  46.0 17.3 %copy-start.5 = (f32[8,4,8,512]{3,2,1,0:T(8,128)}, f32[8,4,8,512]{3,2,1,0:T(8,128)S(1)}, u32[]{:S(2)}) copy-start(f32[8,4,8,512]{3,2,1,0:T(8,128)S(1)} %collective-permute-done.8.refs_7_.refs_3_) | copy-start | bytes 1572868
  46.0 20.7 %collective-permute-start.12 = (f32[8,4,8,512]{3,2,1,0:T(8,128)S(1)}, f32[8,4,8,512]{3,2,1,0:T(8,128)S(1)}, u32[]{:S(2)}, u32[]{:S(2)}) collective-permute-start(f32[8,4,8,512]{3,2,1,0:T(8,128)S(1)} %collective-permute-done.8.refs_7_.refs_3_), channel_id=1, source_target_pairs={{0,32},{32,0},{1,33},{33,1},{2,34},{34,2},{3,35},{35,3},{4,36},{36... | collective-permute-start | bytes 1572872 | tf_op jit(solution)/shard_map/ppermute | solution.py:26
  49.2 17.5 %collective-permute-start.11 = (f32[8,4,8,512]{3,2,1,0:T(8,128)}, f32[8,4,8,512]{3,2,1,0:T(8,128)S(1)}, u32[]{:S(2)}, u32[]{:S(2)}) collective-permute-start(f32[8,4,8,512]{3,2,1,0:T(8,128)} %collective-permute-done.7.refs_6_.refs_2_), channel_id=1, source_target_pairs={{0,32},{32,0},{1,33},{33,1},{2,34},{34,2},{3,35},{35,3},{4,36},{36... | collective-permute-start | bytes 1572872 | tf_op jit(solution)/shard_map/ppermute | solution.py:26
  56.5 10.3 %collective-permute-start.10 = (f32[8,4,8,512]{3,2,1,0:T(8,128)}, f32[8,4,8,512]{3,2,1,0:T(8,128)S(1)}, u32[]{:S(2)}, u32[]{:S(2)}) collective-permute-start(f32[8,4,8,512]{3,2,1,0:T(8,128)} %collective-permute-done.6.refs_5_.refs_1_), channel_id=1, source_target_pairs={{0,32},{32,0},{1,33},{33,1},{2,34},{34,2},{3,35},{35,3},{4,36},{36... | collective-permute-start | bytes 1572872 | tf_op jit(solution)/shard_map/ppermute | solution.py:26
  59.8 16.4 %all-to-all-start.1 = ((f32[8,72,128]{2,1,0:T(8,128)}), f32[8,72,128]{2,1,0:T(8,128)S(1)}, u32[]{:S(2)}, u32[]{:S(2)}) async-start(f32[8,72,128]{2,1,0:T(8,128)} %shard_map.83), calls=%async_computation.1 | async-start | bytes 589824 | tf_op jit(solution)/shard_map/all_to_all | solution.py:21
  66.7 1.2 copy-start.3
  76.2 22.0 %copy-start.7 = (f32[8,72,128]{2,1,0:T(8,128)}, f32[8,72,128]{2,1,0:T(8,128)S(1)}, u32[]{:S(2)}) copy-start(f32[8,72,128]{2,1,0:T(8,128)S(1)} %all-to-all-done.1.refs_0_.refs_4_) | copy-start | bytes 884740
  76.3 65.6 %all-to-all-start.4 = ((f32[8,4,4,8,256]{4,3,2,1,0:T(8,128)}), f32[8,4,4,8,256]{4,3,2,1,0:T(8,128)S(1)}, u32[]{:S(2)}, u32[]{:S(2)}) async-start(f32[8,4,4,8,256]{4,3,2,1,0:T(8,128)} %shard_map.89), calls=%async_computation.4 | async-start | bytes 2097152 | tf_op jit(solution)/shard_map/all_to_all | solution.py:21
  79.8 14.7 %collective-permute-start.5 = (f32[8,72,128]{2,1,0:T(8,128)S(1)}, f32[8,72,128]{2,1,0:T(8,128)S(1)}, u32[]{:S(2)}, u32[]{:S(2)}) collective-permute-start(f32[8,72,128]{2,1,0:T(8,128)S(1)} %all-to-all-done.1.refs_0_.refs_4_), channel_id=1, source_target_pairs={{0,3},{1,0},{2,1},{3,2},{4,7},{5,4},{6,5},{7,6},{8,11},{9,8},{10,9... | collective-permute-start | bytes 884744 | tf_op jit(solution)/shard_map/ppermute | solution.py:26
  81.7 12.8 %collective-permute-start.4 = (f32[8,72,128]{2,1,0:T(8,128)S(1)}, f32[8,72,128]{2,1,0:T(8,128)S(1)}, u32[]{:S(2)}, u32[]{:S(2)}) collective-permute-start(f32[8,72,128]{2,1,0:T(8,128)S(1)} %all-to-all-done.1.refs_0_.refs_4_), channel_id=1, source_target_pairs={{0,2},{1,3},{2,0},{3,1},{4,6},{5,7},{6,4},{7,5},{8,10},{9,11},{10,... | collective-permute-start | bytes 884744 | tf_op jit(solution)/shard_map/ppermute | solution.py:26
  82.8 15.4 %collective-permute-start.3 = (f32[8,72,128]{2,1,0:T(8,128)S(1)}, f32[8,72,128]{2,1,0:T(8,128)S(1)}, u32[]{:S(2)}, u32[]{:S(2)}) collective-permute-start(f32[8,72,128]{2,1,0:T(8,128)S(1)} %all-to-all-done.1.refs_0_.refs_4_), channel_id=1, source_target_pairs={{0,1},{1,2},{2,3},{3,0},{4,5},{5,6},{6,7},{7,4},{8,9},{9,10},{10,1... | collective-permute-start | bytes 884744 | tf_op jit(solution)/shard_map/ppermute | solution.py:26
  94.5 3.7 %copy-start.9 = (f32[8,72,128]{2,1,0:T(8,128)}, f32[8,72,128]{2,1,0:T(8,128)S(1)}, u32[]{:S(2)}) copy-start(f32[8,72,128]{2,1,0:T(8,128)S(1)} %collective-permute-done.5.refs_3_.refs_7_) | copy-start | bytes 884740
  94.5 3.7 %copy-start.10 = (f32[8,72,128]{2,1,0:T(8,128)}, f32[8,72,128]{2,1,0:T(8,128)S(1)}, u32[]{:S(2)}) copy-start(f32[8,72,128]{2,1,0:T(8,128)S(1)} %collective-permute-done.4.refs_2_.refs_6_) | copy-start | bytes 884740
  108.0 8.6 %copy-start.23 = (f32[8,32,512]{2,1,0:T(8,128)S(1)}, f32[8,32,512]{2,1,0:T(8,128)}, u32[]{:S(2)}) copy-start(f32[8,32,512]{2,1,0:T(8,128)} %get-tuple-element.25) | copy-start | bytes 1572868
  113.3 26.5 %collective-permute-start.13 = (f32[8,32,512]{2,1,0:T(8,128)}, f32[8,32,512]{2,1,0:T(8,128)S(1)}, u32[]{:S(2)}, u32[]{:S(2)}) collective-permute-start(f32[8,32,512]{2,1,0:T(8,128)} %get-tuple-element.24), channel_id=1, source_target_pairs={{0,1},{1,2},{2,3},{3,0},{4,5},{5,6},{6,7},{7,4},{8,9},{9,10},{10,1... | collective-permute-start | bytes 1572872 | tf_op jit(solution)/shard_map/ppermute | solution.py:26
  113.3 26.5 %collective-permute-start.15 = (f32[8,32,512]{2,1,0:T(8,128)}, f32[8,32,512]{2,1,0:T(8,128)S(1)}, u32[]{:S(2)}, u32[]{:S(2)}) collective-permute-start(f32[8,32,512]{2,1,0:T(8,128)} %get-tuple-element.26), channel_id=1, source_target_pairs={{0,3},{1,0},{2,1},{3,2},{4,7},{5,4},{6,5},{7,6},{8,11},{9,8},{10,9... | collective-permute-start | bytes 1572872 | tf_op jit(solution)/shard_map/ppermute | solution.py:26
  116.6 23.3 %collective-permute-start.14 = (f32[8,32,512]{2,1,0:T(8,128)S(1)}, f32[8,32,512]{2,1,0:T(8,128)S(1)}, u32[]{:S(2)}, u32[]{:S(2)}) collective-permute-start(f32[8,32,512]{2,1,0:T(8,128)S(1)} %copy-done.23), channel_id=1, source_target_pairs={{0,2},{1,3},{2,0},{3,1},{4,6},{5,7},{6,4},{7,5},{8,10},{9,11},{10,... | collective-permute-start | bytes 1572872 | tf_op jit(solution)/shard_map/ppermute | solution.py:26
  141.9 6.8 %copy-start.6 = (f32[8,4,4,8,256]{4,3,2,1,0:T(8,128)}, f32[8,4,4,8,256]{4,3,2,1,0:T(8,128)S(1)}, u32[]{:S(2)}) copy-start(f32[8,4,4,8,256]{4,3,2,1,0:T(8,128)S(1)} %all-to-all-done.4.blocks_ref) | copy-start | bytes 3145732
  141.9 28.9 %all-to-all-start.3 = ((f32[8,32,512]{2,1,0:T(8,128)}), f32[8,32,512]{2,1,0:T(8,128)S(1)}, u32[]{:S(2)}, u32[]{:S(2)}) async-start(f32[8,32,512]{2,1,0:T(8,128)} %add_add_fusion), calls=%async_computation.3 | async-start | bytes 1048576 | tf_op jit(solution)/shard_map/all_to_all | solution.py:21
  150.6 5.3 %collective-permute-start.16 = (f32[4,8,256]{2,1,0:T(8,128)}, f32[4,8,256]{2,1,0:T(8,128)S(1)}, u32[]{:S(2)}, u32[]{:S(2)}) collective-permute-start(f32[4,8,256]{2,1,0:T(8,128)} %get-tuple-element.28), channel_id=1, source_target_pairs={{0,1},{1,2},{2,3},{3,0},{4,5},{5,6},{6,7},{7,4},{8,9},{9,10},{10,1... | collective-permute-start | bytes 98312 | tf_op jit(solution)/shard_map/ppermute | solution.py:26
  151.5 6.0 %collective-permute-start.17 = (f32[4,8,256]{2,1,0:T(8,128)}, f32[4,8,256]{2,1,0:T(8,128)S(1)}, u32[]{:S(2)}, u32[]{:S(2)}) collective-permute-start(f32[4,8,256]{2,1,0:T(8,128)} %get-tuple-element.29), channel_id=1, source_target_pairs={{0,2},{1,3},{2,0},{3,1},{4,6},{5,7},{6,4},{7,5},{8,10},{9,11},{10,... | collective-permute-start | bytes 98312 | tf_op jit(solution)/shard_map/ppermute | solution.py:26
  155.0 4.1 %collective-permute-start.18 = (f32[4,8,256]{2,1,0:T(8,128)}, f32[4,8,256]{2,1,0:T(8,128)S(1)}, u32[]{:S(2)}, u32[]{:S(2)}) collective-permute-start(f32[4,8,256]{2,1,0:T(8,128)} %get-tuple-element.30), channel_id=1, source_target_pairs={{0,3},{1,0},{2,1},{3,2},{4,7},{5,4},{6,5},{7,6},{8,11},{9,8},{10,9... | collective-permute-start | bytes 98312 | tf_op jit(solution)/shard_map/ppermute | solution.py:26
  155.9 3.2 %copy-start.20 = (f32[4,8,256]{2,1,0:T(8,128)}, f32[4,8,256]{2,1,0:T(8,128)S(1)}, u32[]{:S(2)}) copy-start(f32[4,8,256]{2,1,0:T(8,128)S(1)} %collective-permute-done.16.refs_1_) | copy-start | bytes 98308
  157.5 1.7 copy-start.21
  162.1 5.2 %collective-permute-start.21 = (f32[32,8,128]{2,1,0:T(8,128)}, f32[32,8,128]{2,1,0:T(8,128)S(1)}, u32[]{:S(2)}, u32[]{:S(2)}) collective-permute-start(f32[32,8,128]{2,1,0:T(8,128)} %shard_map.91.refs_0_), channel_id=1, source_target_pairs={{0,192},{64,0},{128,64},{192,128},{1,193},{65,1},{129,65},{193,129... | collective-permute-start | bytes 393224 | tf_op jit(solution)/shard_map/ppermute | solution.py:26
  162.9 6.7 %collective-permute-start.20 = (f32[32,8,128]{2,1,0:T(8,128)}, f32[32,8,128]{2,1,0:T(8,128)S(1)}, u32[]{:S(2)}, u32[]{:S(2)}) collective-permute-start(f32[32,8,128]{2,1,0:T(8,128)} %shard_map.91.refs_0_), channel_id=1, source_target_pairs={{0,128},{64,192},{128,0},{192,64},{1,129},{65,193},{129,1},{193,65... | collective-permute-start | bytes 393224 | tf_op jit(solution)/shard_map/ppermute | solution.py:26
  164.9 5.9 %collective-permute-start.19 = (f32[32,8,128]{2,1,0:T(8,128)}, f32[32,8,128]{2,1,0:T(8,128)S(1)}, u32[]{:S(2)}, u32[]{:S(2)}) collective-permute-start(f32[32,8,128]{2,1,0:T(8,128)} %shard_map.91.refs_0_), channel_id=1, source_target_pairs={{0,64},{64,128},{128,192},{192,0},{1,65},{65,129},{129,193},{193,1... | collective-permute-start | bytes 393224 | tf_op jit(solution)/shard_map/ppermute | solution.py:26
  166.3 4.6 %collective-permute-start.22 = (f32[32,8,128]{2,1,0:T(8,128)}, f32[32,8,128]{2,1,0:T(8,128)S(1)}, u32[]{:S(2)}, u32[]{:S(2)}) collective-permute-start(f32[32,8,128]{2,1,0:T(8,128)} %shard_map.91.refs_0_), channel_id=1, source_target_pairs={{0,32},{32,0},{1,33},{33,1},{2,34},{34,2},{3,35},{35,3},{4,36},{36... | collective-permute-start | bytes 393224 | tf_op jit(solution)/shard_map/ppermute | solution.py:26
  167.3 4.8 %copy-start.13 = (f32[32,8,128]{2,1,0:T(8,128)}, f32[32,8,128]{2,1,0:T(8,128)S(1)}, u32[]{:S(2)}) copy-start(f32[32,8,128]{2,1,0:T(8,128)S(1)} %collective-permute-done.21.refs_3_) | copy-start | bytes 393220
  167.3 3.5 %collective-permute-start.25 = (f32[32,8,128]{2,1,0:T(8,128)S(1)}, f32[32,8,128]{2,1,0:T(8,128)S(1)}, u32[]{:S(2)}, u32[]{:S(2)}) collective-permute-start(f32[32,8,128]{2,1,0:T(8,128)S(1)} %collective-permute-done.21.refs_3_), channel_id=1, source_target_pairs={{0,32},{32,0},{1,33},{33,1},{2,34},{34,2},{3,35},{35,3},{4,36},{36... | collective-permute-start | bytes 393224 | tf_op jit(solution)/shard_map/ppermute | solution.py:26
  169.6 2.5 %copy-start.14 = (f32[32,8,128]{2,1,0:T(8,128)}, f32[32,8,128]{2,1,0:T(8,128)S(1)}, u32[]{:S(2)}) copy-start(f32[32,8,128]{2,1,0:T(8,128)S(1)} %collective-permute-done.20.refs_2_) | copy-start | bytes 393220
  169.6 1.3 collective-permute-start.24
  170.8 1.4 copy-start.15
  170.8 1.3 collective-permute-start.23
  170.8 1.4 copy-start.8
  170.8 1.3 copy-start.16
  170.8 1.3 copy-start.17
  171.0 1.2 copy-start.18
  (7 other events, 5.3 us)

commit v2 on v1

--- a/solution.py
+++ b/solution.py
@@ -80,14 +80,6 @@
     for f in range(32):
         start = pl.multiple_of(f * cols + core * (cols - HALF), 128)
         out_ref[f] = basis_ref[:, pl.ds(start, HALF)]
-
-
-def block_sum_kernel(me_ref, blocks_ref, out_ref):
-    total = blocks_ref[0]
-    for sender in range(1, 8):
-        total = total + blocks_ref[sender]
-    for target in range(8):
-        out_ref[target] = total
 
 
 def query_kernel(own, me_ref, grads_ref, *refs):
@@ -263,7 +255,7 @@
         arrived.append(shifted(parts[k], "x", k))
     part = arrived[0] + arrived[1] + arrived[2] + arrived[3]
     part = exchange(part, "z")
-    (part,) = call(block_sum_kernel, [((8, 72, 128), f32)], [VMEM], me, args=(part,))
+    part = jnp.broadcast_to(jnp.sum(part, axis=0)[None], (8, 72, 128))
     block = exchange(part, "z")
     blocks = [block] + [None] * 3
     for k in (2, 1, 3):

time: 197 us -> 196 us (level)
    pallas_call x11 -> x10, Pallas kernels: 38.7 us -> 36.9 us  [call(): pl.pallas_call(kernel, out_shape=out_shape, grid_spec=pltpu.PrefetchScala...]
    unnamed x48 -> x46, local copies, waits for them, and re-layouts: 4.66 us -> 3.94 us
  transfers between devices with their start and end apart: 31 -> 31, of which waited for: 18 -> 18; matrix products, arithmetic and copies ran while one was open for 2% -> 2% of each run, Pallas kernels for 18% -> 17%
where the time goes in v2:
time: 196 us; the launch traced here: 194 us
  waiting for transfers between devices  70.4 us (36%)
  starting transfers between devices  57.6 us (29%)
  Pallas kernels  36.9 us (19%)
  blocking collectives  19.3 us (10%)
  local copies, waits for them, and re-layouts  5.33 us (3%)
  other arithmetic  3.95 us (2%)
    ppermute x26, waiting for transfers between devices, shifted(): return lax.ppermute(shard, axis, [(i, (i + hops) % n) for i in range(n)])  57.3 us
    pallas_call x10, Pallas kernels, call(): pl.pallas_call(kernel, out_shape=out_shape, grid_spec=pltpu.PrefetchScala...  36.9 us
    all_to_all x5, starting transfers between devices, exchange(): return lax.all_to_all(blocks, axis, 0, 0, tiled=True)  30.7 us
    ppermute x26, starting transfers between devices, shifted(): return lax.ppermute(shard, axis, [(i, (i + hops) % n) for i in range(n)])  26.9 us
    all_to_all x1, blocking collectives, exchange(): return lax.all_to_all(blocks, axis, 0, 0, tiled=True)  19.3 us
    all_to_all x5, waiting for transfers between devices, exchange(): return lax.all_to_all(blocks, axis, 0, 0, tiled=True)  13.1 us
    unnamed x46, local copies, waits for them, and re-layouts  3.94 us
  transfers between devices with their start and end apart: 31, of which 18 were waited for; matrix products, arithmetic and copies ran while one was open for 2% of the time, Pallas kernels for 17%

profile of v2, /device:TPU:8, one launch (start us, length us, event | category | flops | bytes accessed | tf_op | source)
XLA Modules:
  0.0 193.8 jit_solution(16743317747078089200)
XLA Ops:
  0.0 2.0 %shard_map.83 = f32[32,8,512]{2,1,0:T(8,128)} custom-call(s32[1]{0:T(128)} %bitcast.me_ref, f32[32,28672]{1,0:T(8,128)} %basis_ref.3), custom_call_target="tpu_custom_call" | custom-call | tf_op jit(solution)/shard_map/pallas_call | solution.py:31
  2.0 11.3 %all-to-all-start.2 = ((f32[32,8,512]{2,1,0:T(8,128)}), f32[32,8,512]{2,1,0:T(8,128)S(1)}, u32[]{:S(2)}, u32[]{:S(2)}) async-start(f32[32,8,512]{2,1,0:T(8,128)} %shard_map.83), calls=%async_computation.2 | async-start | bytes 1048576 | tf_op jit(solution)/shard_map/all_to_all | solution.py:21
  13.3 2.9 %shard_map.82 = (f32[8,72,128]{2,1,0:T(8,128)}, f32[8,72,128]{2,1,0:T(8,128)}, f32[8,72,128]{2,1,0:T(8,128)}, f32[8,72,128]{2,1,0:T(8,128)}) custom-call(s32[1]{0:T(128)} %bitcast.me_ref, bf16[2048,256]{1,0:T(8,128)(2,1)} %acts_ref.1, bf16[256,256]{1,0:T(8,128)(2,1)} %query_ref.1, f32[128,8192]{1,0:T(8,128)} %basis_ref.2), custom_call_target="tpu_custom_call" | custom-call | tf_op jit(solution)/shard_map/pallas_call | solution.py:31
  16.3 3.3 %collective-permute-start = (f32[8,72,128]{2,1,0:T(8,128)}, f32[8,72,128]{2,1,0:T(8,128)S(1)}, u32[]{:S(2)}, u32[]{:S(2)}) collective-permute-start(f32[8,72,128]{2,1,0:T(8,128)} %get-tuple-element.19), channel_id=1, source_target_pairs={{0,2},{1,3},{2,0},{3,1},{4,6},{5,7},{6,4},{7,5},{8,10},{9,11},{10,... | collective-permute-start | bytes 884744 | tf_op jit(solution)/shard_map/ppermute | solution.py:26
  20.1 2.7 %collective-permute-start.2 = (f32[8,72,128]{2,1,0:T(8,128)}, f32[8,72,128]{2,1,0:T(8,128)S(1)}, u32[]{:S(2)}, u32[]{:S(2)}) collective-permute-start(f32[8,72,128]{2,1,0:T(8,128)} %get-tuple-element.21), channel_id=1, source_target_pairs={{0,3},{1,0},{2,1},{3,2},{4,7},{5,4},{6,5},{7,6},{8,11},{9,8},{10,9... | collective-permute-start | bytes 884744 | tf_op jit(solution)/shard_map/ppermute | solution.py:26
  22.8 8.4 %all-to-all-done.2 = f32[32,8,512]{2,1,0:T(8,128)S(1)} async-done(((f32[32,8,512]{2,1,0:T(8,128)}), f32[32,8,512]{2,1,0:T(8,128)S(1)}, u32[]{:S(2)}, u32[]{:S(2)}) %all-to-all-start.2) | async-done | bytes 524320 | tf_op jit(solution)/shard_map/all_to_all | solution.py:21
  31.2 1.6 collective-permute-start.8
  32.8 0.9 collective-permute-start.7
  33.7 2.4 %collective-permute-start.6 = (f32[8,4,8,512]{3,2,1,0:T(8,128)S(1)}, f32[8,4,8,512]{3,2,1,0:T(8,128)}, u32[]{:S(2)}, u32[]{:S(2)}) collective-permute-start(f32[8,4,8,512]{3,2,1,0:T(8,128)S(1)} %bitcast.4), channel_id=1, source_target_pairs={{0,192},{64,0},{128,64},{192,128},{1,193},{65,1},{129,65},{193,129... | collective-permute-start | bytes 1572872 | tf_op jit(solution)/shard_map/ppermute | solution.py:26
  36.1 1.1 collective-permute-done.1
  37.2 1.7 add_add_fusion.1
  39.0 5.6 %all-to-all-start = ((f32[8,72,128]{2,1,0:T(8,128)}), f32[8,72,128]{2,1,0:T(8,128)S(1)}, u32[]{:S(2)}, u32[]{:S(2)}) async-start(f32[8,72,128]{2,1,0:T(8,128)} %add_add_fusion.1), calls=%async_computation | async-start | bytes 589824 | tf_op jit(solution)/shard_map/all_to_all | solution.py:21
  44.6 1.4 collective-permute-done.8.refs_7_.refs_3_
  46.0 3.2 %collective-permute-done.7.refs_6_.refs_2_ = f32[8,4,8,512]{3,2,1,0:T(8,128)} collective-permute-done((f32[8,4,8,512]{3,2,1,0:T(8,128)S(1)}, f32[8,4,8,512]{3,2,1,0:T(8,128)}, u32[]{:S(2)}, u32[]{:S(2)}) %collective-permute-start.7) | collective-permute-done | bytes 524320 | tf_op jit(solution)/shard_map/ppermute | solution.py:26
  49.2 7.3 %collective-permute-done.6.refs_5_.refs_1_ = f32[8,4,8,512]{3,2,1,0:T(8,128)} collective-permute-done((f32[8,4,8,512]{3,2,1,0:T(8,128)S(1)}, f32[8,4,8,512]{3,2,1,0:T(8,128)}, u32[]{:S(2)}, u32[]{:S(2)}) %collective-permute-start.6) | collective-permute-done | bytes 524320 | tf_op jit(solution)/shard_map/ppermute | solution.py:26
  56.5 0.9 all-to-all-done
  58.1 3.4 %all-to-all-start.1 = ((f32[8,72,128]{2,1,0:T(8,128)}), f32[8,72,128]{2,1,0:T(8,128)S(1)}, u32[]{:S(2)}, u32[]{:S(2)}) async-start(f32[8,72,128]{2,1,0:T(8,128)} %broadcast_in_dim.2), calls=%async_computation.1 | async-start | bytes 589824 | tf_op jit(solution)/shard_map/all_to_all | solution.py:21
  61.6 3.4 %shard_map.87.refs_0_ = f32[8,4,4,8,256]{4,3,2,1,0:T(8,128)} custom-call(s32[1]{0:T(128)} %bitcast.me_ref, bf16[256,896]{1,0:T(8,128)(2,1)} %grads_ref.5, f32[8,4,8,512]{3,2,1,0:T(8,128)} %bitcast.6, f32[8,4,8,512]{3,2,1,0:T(8,128)} %collective-permute-done.6.refs_5_.refs_1_, f32[8,4,8,512]{3,2,1,0:T(8,128)} %collective-permute-done.7.refs_6_.refs_2_, ...), custom_call_target="tpu_custom_call" | custom-call | tf_op jit(solution)/shard_map/pallas_call | solution.py:31
  67.0 3.8 %shard_map.88 = f32[8,4,4,8,256]{4,3,2,1,0:T(8,128)} custom-call(s32[1]{0:T(128)} %bitcast.me_ref, bf16[256,896]{1,0:T(8,128)(2,1)} %grads_ref.5, f32[8,4,4,8,256]{4,3,2,1,0:T(8,128)} %shard_map.87.refs_0_, f32[8,4,8,512]{3,2,1,0:T(8,128)} %copy-done.1, f32[8,4,8,512]{3,2,1,0:T(8,128)} %copy-done.4, f32[8,4,8,512]{3,2,1,0:T(8,128)} %copy-done.3, ...), custom_call_target="tpu_custom_call" | custom-call | tf_op jit(solution)/shard_map/pallas_call | solution.py:31
  70.7 3.8 %all-to-all-done.1.refs_0_.refs_4_ = f32[8,72,128]{2,1,0:T(8,128)S(1)} async-done(((f32[8,72,128]{2,1,0:T(8,128)}), f32[8,72,128]{2,1,0:T(8,128)S(1)}, u32[]{:S(2)}, u32[]{:S(2)}) %all-to-all-start.1) | async-done | bytes 294944 | tf_op jit(solution)/shard_map/all_to_all | solution.py:21
  74.6 3.6 %all-to-all-start.4 = ((f32[8,4,4,8,256]{4,3,2,1,0:T(8,128)}), f32[8,4,4,8,256]{4,3,2,1,0:T(8,128)S(1)}, u32[]{:S(2)}, u32[]{:S(2)}) async-start(f32[8,4,4,8,256]{4,3,2,1,0:T(8,128)} %shard_map.88), calls=%async_computation.4 | async-start | bytes 2097152 | tf_op jit(solution)/shard_map/all_to_all | solution.py:21
  78.1 1.9 collective-permute-start.5
  80.0 1.1 collective-permute-start.4
  81.8 11.1 %collective-permute-done.5.refs_3_.refs_7_ = f32[8,72,128]{2,1,0:T(8,128)S(1)} collective-permute-done((f32[8,72,128]{2,1,0:T(8,128)S(1)}, f32[8,72,128]{2,1,0:T(8,128)S(1)}, u32[]{:S(2)}, u32[]{:S(2)}) %collective-permute-start.5) | collective-permute-done | bytes 294944 | tf_op jit(solution)/shard_map/ppermute | solution.py:26
  92.9 3.7 %collective-permute-done.3.refs_1_.refs_5_ = f32[8,72,128]{2,1,0:T(8,128)S(1)} collective-permute-done((f32[8,72,128]{2,1,0:T(8,128)S(1)}, f32[8,72,128]{2,1,0:T(8,128)S(1)}, u32[]{:S(2)}, u32[]{:S(2)}) %collective-permute-start.3) | collective-permute-done | bytes 294944 | tf_op jit(solution)/shard_map/ppermute | solution.py:26
  97.3 9.1 %shard_map.84 = (f32[8,32,512]{2,1,0:T(8,128)}, bf16[2,512,512]{2,1,0:T(8,128)(2,1)}, bf16[2,512,512]{2,1,0:T(8,128)(2,1)}) custom-call(s32[1]{0:T(128)} %bitcast.me_ref, s32[4]{0:T(128)} %len_ref.1, bf16[2048,896]{1,0:T(8,128)(2,1)} %grads_ref.3, f32[8,72,128]{2,1,0:T(8,128)} %copy-done.7, f32[8,72,128]{2,1,0:T(8,128)} %copy-done.11, ...), custom_call_target="tpu_custom_call" | custom-call | tf_op jit(solution)/shard_map/pallas_call | solution.py:31
  106.4 5.3 %shard_map.86 = (f32[8,32,512]{2,1,0:T(8,128)}, f32[8,32,512]{2,1,0:T(8,128)}) custom-call(s32[1]{0:T(128)} %bitcast.me_ref, bf16[2,512,512]{2,1,0:T(8,128)(2,1)} %get-tuple-element.22.high_ref, bf16[2,512,512]{2,1,0:T(8,128)(2,1)} %get-tuple-element.23.low_ref, f32[8,4,8,512]{3,2,1,0:T(8,128)} %bitcast.8, ...), custom_call_target="tpu_custom_call" | custom-call | tf_op jit(solution)/shard_map/pallas_call | solution.py:31
  111.7 3.2 %collective-permute-start.15 = (f32[8,32,512]{2,1,0:T(8,128)}, f32[8,32,512]{2,1,0:T(8,128)S(1)}, u32[]{:S(2)}, u32[]{:S(2)}) collective-permute-start(f32[8,32,512]{2,1,0:T(8,128)} %get-tuple-element.26), channel_id=1, source_target_pairs={{0,3},{1,0},{2,1},{3,2},{4,7},{5,4},{6,5},{7,6},{8,11},{9,8},{10,9... | collective-permute-start | bytes 1572872 | tf_op jit(solution)/shard_map/ppermute | solution.py:26
  114.9 3.6 %shard_map.85 = f32[8,32,512]{2,1,0:T(8,128)} custom-call(s32[1]{0:T(128)} %bitcast.me_ref, bf16[2,512,512]{2,1,0:T(8,128)(2,1)} %get-tuple-element.22.high_ref, bf16[2,512,512]{2,1,0:T(8,128)(2,1)} %get-tuple-element.23.low_ref, f32[8,4,8,512]{3,2,1,0:T(8,128)} %bitcast.9, f32[8,4,8,512]{3,2,1,0:T(8,128)} %collective-permute-done.6.refs_5_.refs_1_, ...), custom_call_target="tpu_custom_call" | custom-call | tf_op jit(solution)/shard_map/pallas_call | solution.py:31
  118.5 19.6 %collective-permute-done.13 = f32[8,32,512]{2,1,0:T(8,128)S(1)} collective-permute-done((f32[8,32,512]{2,1,0:T(8,128)}, f32[8,32,512]{2,1,0:T(8,128)S(1)}, u32[]{:S(2)}, u32[]{:S(2)}) %collective-permute-start.13) | collective-permute-done | bytes 524320 | tf_op jit(solution)/shard_map/ppermute | solution.py:26
  138.2 2.1 %add_add_fusion = f32[8,32,512]{2,1,0:T(8,128)} fusion(f32[8,32,512]{2,1,0:T(8,128)S(1)} %collective-permute-done.15, f32[8,32,512]{2,1,0:T(8,128)S(1)} %collective-permute-done.14, f32[8,32,512]{2,1,0:T(8,128)} %shard_map.85, f32[8,32,512]{2,1,0:T(8,128)S(1)} %collective-permute-done.13), kind=kLoop, calls=%fused_computation | loop fusion | flops 393216 | bytes 2621440 | tf_op jit(solution)/shard_map/add | solution.py:329
  140.3 6.8 %all-to-all-start.3 = ((f32[8,32,512]{2,1,0:T(8,128)}), f32[8,32,512]{2,1,0:T(8,128)S(1)}, u32[]{:S(2)}, u32[]{:S(2)}) async-start(f32[8,32,512]{2,1,0:T(8,128)} %add_add_fusion), calls=%async_computation.3 | async-start | bytes 1048576 | tf_op jit(solution)/shard_map/all_to_all | solution.py:21
  147.0 1.9 shard_map.89
  149.0 0.9 collective-permute-start.16
  149.8 3.6 %collective-permute-start.17 = (f32[4,8,256]{2,1,0:T(8,128)}, f32[4,8,256]{2,1,0:T(8,128)S(1)}, u32[]{:S(2)}, u32[]{:S(2)}) collective-permute-start(f32[4,8,256]{2,1,0:T(8,128)} %get-tuple-element.29), channel_id=1, source_target_pairs={{0,2},{1,3},{2,0},{3,1},{4,6},{5,7},{6,4},{7,5},{8,10},{9,11},{10,... | collective-permute-start | bytes 98312 | tf_op jit(solution)/shard_map/ppermute | solution.py:26
  153.4 0.9 collective-permute-done.16.refs_1_
  154.3 1.5 collective-permute-done.17.refs_2_
  155.8 1.7 collective-permute-done.18.refs_3_
  158.1 2.4 %shard_map.90.refs_0_ = f32[32,8,128]{2,1,0:T(8,128)} custom-call(s32[1]{0:T(128)} %bitcast.me_ref, f32[32,128]{1,0:T(8,128)} %eig_ref.1, f32[4,8,256]{2,1,0:T(8,128)} %get-tuple-element.27.refs_0_, f32[4,8,256]{2,1,0:T(8,128)} %copy-done.19, f32[4,8,256]{2,1,0:T(8,128)} %copy-done.20, f32[4,8,256]{2,1,0:T(8,128)} %copy-done.21, f32[8,72,128]{2,1,0:T(8,128)} %copy-done.7, ...), custom_call_target="tpu_custom_call" | custom-call | tf_op jit(solution)/shard_map/pallas_call | solution.py:31
  160.5 0.8 collective-permute-start.21
  161.3 2.0 %collective-permute-start.20 = (f32[32,8,128]{2,1,0:T(8,128)}, f32[32,8,128]{2,1,0:T(8,128)S(1)}, u32[]{:S(2)}, u32[]{:S(2)}) collective-permute-start(f32[32,8,128]{2,1,0:T(8,128)} %shard_map.90.refs_0_), channel_id=1, source_target_pairs={{0,128},{64,192},{128,0},{192,64},{1,129},{65,193},{129,1},{193,65... | collective-permute-start | bytes 393224 | tf_op jit(solution)/shard_map/ppermute | solution.py:26
  163.3 1.3 collective-permute-start.19
  164.6 1.1 collective-permute-done.21.refs_3_
  165.7 2.3 %collective-permute-done.20.refs_2_ = f32[32,8,128]{2,1,0:T(8,128)S(1)} collective-permute-done((f32[32,8,128]{2,1,0:T(8,128)}, f32[32,8,128]{2,1,0:T(8,128)S(1)}, u32[]{:S(2)}, u32[]{:S(2)}) %collective-permute-start.20) | collective-permute-done | bytes 131104 | tf_op jit(solution)/shard_map/ppermute | solution.py:26
  168.0 1.2 collective-permute-done.19.refs_1_
  169.3 1.2 collective-permute-done.23.refs_5_
  171.2 2.4 %shard_map.91 = f32[32,8,128]{2,1,0:T(8,128)} custom-call(s32[1]{0:T(128)} %bitcast.me_ref, f32[8,32,512]{2,1,0:T(8,128)} %copy-done.8, f32[32,8,128]{2,1,0:T(8,128)} %shard_map.90.refs_0_, f32[32,8,128]{2,1,0:T(8,128)} %copy-done.14, f32[32,8,128]{2,1,0:T(8,128)} %copy-done.13, f32[32,8,128]{2,1,0:T(8,128)} %copy-done.12, f32[32,8,128]{2,1,0:T(8,128)} %copy-done.15, ...), custom_call_target="tpu_custom_call" | custom-call | tf_op jit(solution)/shard_map/pallas_call | solution.py:31
  173.7 19.3 %all_to_all.30 = f32[32,8,128]{2,1,0:T(8,128)S(1)} all-to-all(f32[32,8,128]{2,1,0:T(8,128)} %shard_map.91), channel_id=1, replica_groups=mesh['y'=4,'core'=2,'z'=8,'x'=4] {'z','x'}, dimensions={0} | all-to-all | bytes 262144 | tf_op jit(solution)/shard_map/all_to_all | solution.py:21
  (77 shorter events, 6.9 us)
Async XLA Ops:
  2.0 29.2 %all-to-all-start.2 = ((f32[32,8,512]{2,1,0:T(8,128)}), f32[32,8,512]{2,1,0:T(8,128)S(1)}, u32[]{:S(2)}, u32[]{:S(2)}) async-start(f32[32,8,512]{2,1,0:T(8,128)} %shard_map.83), calls=%async_computation.2 | async-start | bytes 1048576 | tf_op jit(solution)/shard_map/all_to_all | solution.py:21
  16.3 17.4 %collective-permute-start = (f32[8,72,128]{2,1,0:T(8,128)}, f32[8,72,128]{2,1,0:T(8,128)S(1)}, u32[]{:S(2)}, u32[]{:S(2)}) collective-permute-start(f32[8,72,128]{2,1,0:T(8,128)} %get-tuple-element.19), channel_id=1, source_target_pairs={{0,2},{1,3},{2,0},{3,1},{4,6},{5,7},{6,4},{7,5},{8,10},{9,11},{10,... | collective-permute-start | bytes 884744 | tf_op jit(solution)/shard_map/ppermute | solution.py:26
  19.6 17.6 %collective-permute-start.1 = (f32[8,72,128]{2,1,0:T(8,128)}, f32[8,72,128]{2,1,0:T(8,128)S(1)}, u32[]{:S(2)}, u32[]{:S(2)}) collective-permute-start(f32[8,72,128]{2,1,0:T(8,128)} %get-tuple-element.20), channel_id=1, source_target_pairs={{0,1},{1,2},{2,3},{3,0},{4,5},{5,6},{6,7},{7,4},{8,9},{9,10},{10,1... | collective-permute-start | bytes 884744 | tf_op jit(solution)/shard_map/ppermute | solution.py:26
  20.1 17.1 %collective-permute-start.2 = (f32[8,72,128]{2,1,0:T(8,128)}, f32[8,72,128]{2,1,0:T(8,128)S(1)}, u32[]{:S(2)}, u32[]{:S(2)}) collective-permute-start(f32[8,72,128]{2,1,0:T(8,128)} %get-tuple-element.21), channel_id=1, source_target_pairs={{0,3},{1,0},{2,1},{3,2},{4,7},{5,4},{6,5},{7,6},{8,11},{9,8},{10,9... | collective-permute-start | bytes 884744 | tf_op jit(solution)/shard_map/ppermute | solution.py:26
  31.2 30.4 %copy-start = (f32[32,8,512]{2,1,0:T(8,128)}, f32[32,8,512]{2,1,0:T(8,128)S(1)}, u32[]{:S(2)}) copy-start(f32[32,8,512]{2,1,0:T(8,128)S(1)} %all-to-all-done.2) | copy-start | bytes 1572868
  31.2 14.8 %collective-permute-start.8 = (f32[8,4,8,512]{3,2,1,0:T(8,128)S(1)}, f32[8,4,8,512]{3,2,1,0:T(8,128)S(1)}, u32[]{:S(2)}, u32[]{:S(2)}) collective-permute-start(f32[8,4,8,512]{3,2,1,0:T(8,128)S(1)} %bitcast.2), channel_id=1, source_target_pairs={{0,64},{64,128},{128,192},{192,0},{1,65},{65,129},{129,193},{193,1... | collective-permute-start | bytes 1572872 | tf_op jit(solution)/shard_map/ppermute | solution.py:26
  32.8 16.4 %collective-permute-start.7 = (f32[8,4,8,512]{3,2,1,0:T(8,128)S(1)}, f32[8,4,8,512]{3,2,1,0:T(8,128)}, u32[]{:S(2)}, u32[]{:S(2)}) collective-permute-start(f32[8,4,8,512]{3,2,1,0:T(8,128)S(1)} %bitcast.3), channel_id=1, source_target_pairs={{0,128},{64,192},{128,0},{192,64},{1,129},{65,193},{129,1},{193,65... | collective-permute-start | bytes 1572872 | tf_op jit(solution)/shard_map/ppermute | solution.py:26
  33.7 22.8 %collective-permute-start.6 = (f32[8,4,8,512]{3,2,1,0:T(8,128)S(1)}, f32[8,4,8,512]{3,2,1,0:T(8,128)}, u32[]{:S(2)}, u32[]{:S(2)}) collective-permute-start(f32[8,4,8,512]{3,2,1,0:T(8,128)S(1)} %bitcast.4), channel_id=1, source_target_pairs={{0,192},{64,0},{128,64},{192,128},{1,193},{65,1},{129,65},{193,129... | collective-permute-start | bytes 1572872 | tf_op jit(solution)/shard_map/ppermute | solution.py:26
  39.0 18.4 %all-to-all-start = ((f32[8,72,128]{2,1,0:T(8,128)}), f32[8,72,128]{2,1,0:T(8,128)S(1)}, u32[]{:S(2)}, u32[]{:S(2)}) async-start(f32[8,72,128]{2,1,0:T(8,128)} %add_add_fusion.1), calls=%async_computation | async-start | bytes 589824 | tf_op jit(solution)/shard_map/all_to_all | solution.py:21
  44.6 20.4 %collective-permute-start.9 = (f32[8,4,8,512]{3,2,1,0:T(8,128)S(1)}, f32[8,4,8,512]{3,2,1,0:T(8,128)S(1)}, u32[]{:S(2)}, u32[]{:S(2)}) collective-permute-start(f32[8,4,8,512]{3,2,1,0:T(8,128)S(1)} %bitcast.5), channel_id=1, source_target_pairs={{0,32},{32,0},{1,33},{33,1},{2,34},{34,2},{3,35},{35,3},{4,36},{36... | collective-permute-start | bytes 1572872 | tf_op jit(solution)/shard_map/ppermute | solution.py:26
  46.0 15.6 %copy-start.5 = (f32[8,4,8,512]{3,2,1,0:T(8,128)}, f32[8,4,8,512]{3,2,1,0:T(8,128)S(1)}, u32[]{:S(2)}) copy-start(f32[8,4,8,512]{3,2,1,0:T(8,128)S(1)} %collective-permute-done.8.refs_7_.refs_3_) | copy-start | bytes 1572868
  46.0 19.0 %collective-permute-start.12 = (f32[8,4,8,512]{3,2,1,0:T(8,128)S(1)}, f32[8,4,8,512]{3,2,1,0:T(8,128)S(1)}, u32[]{:S(2)}, u32[]{:S(2)}) collective-permute-start(f32[8,4,8,512]{3,2,1,0:T(8,128)S(1)} %collective-permute-done.8.refs_7_.refs_3_), channel_id=1, source_target_pairs={{0,32},{32,0},{1,33},{33,1},{2,34},{34,2},{3,35},{35,3},{4,36},{36... | collective-permute-start | bytes 1572872 | tf_op jit(solution)/shard_map/ppermute | solution.py:26
  49.2 15.9 %collective-permute-start.11 = (f32[8,4,8,512]{3,2,1,0:T(8,128)}, f32[8,4,8,512]{3,2,1,0:T(8,128)S(1)}, u32[]{:S(2)}, u32[]{:S(2)}) collective-permute-start(f32[8,4,8,512]{3,2,1,0:T(8,128)} %collective-permute-done.7.refs_6_.refs_2_), channel_id=1, source_target_pairs={{0,32},{32,0},{1,33},{33,1},{2,34},{34,2},{3,35},{35,3},{4,36},{36... | collective-permute-start | bytes 1572872 | tf_op jit(solution)/shard_map/ppermute | solution.py:26
  56.5 8.6 %collective-permute-start.10 = (f32[8,4,8,512]{3,2,1,0:T(8,128)}, f32[8,4,8,512]{3,2,1,0:T(8,128)S(1)}, u32[]{:S(2)}, u32[]{:S(2)}) collective-permute-start(f32[8,4,8,512]{3,2,1,0:T(8,128)} %collective-permute-done.6.refs_5_.refs_1_), channel_id=1, source_target_pairs={{0,32},{32,0},{1,33},{33,1},{2,34},{34,2},{3,35},{35,3},{4,36},{36... | collective-permute-start | bytes 1572872 | tf_op jit(solution)/shard_map/ppermute | solution.py:26
  58.1 16.4 %all-to-all-start.1 = ((f32[8,72,128]{2,1,0:T(8,128)}), f32[8,72,128]{2,1,0:T(8,128)S(1)}, u32[]{:S(2)}, u32[]{:S(2)}) async-start(f32[8,72,128]{2,1,0:T(8,128)} %broadcast_in_dim.2), calls=%async_computation.1 | async-start | bytes 589824 | tf_op jit(solution)/shard_map/all_to_all | solution.py:21
  65.0 1.1 copy-start.3
  74.6 22.0 %copy-start.7 = (f32[8,72,128]{2,1,0:T(8,128)}, f32[8,72,128]{2,1,0:T(8,128)S(1)}, u32[]{:S(2)}) copy-start(f32[8,72,128]{2,1,0:T(8,128)S(1)} %all-to-all-done.1.refs_0_.refs_4_) | copy-start | bytes 884740
  74.6 65.7 %all-to-all-start.4 = ((f32[8,4,4,8,256]{4,3,2,1,0:T(8,128)}), f32[8,4,4,8,256]{4,3,2,1,0:T(8,128)S(1)}, u32[]{:S(2)}, u32[]{:S(2)}) async-start(f32[8,4,4,8,256]{4,3,2,1,0:T(8,128)} %shard_map.88), calls=%async_computation.4 | async-start | bytes 2097152 | tf_op jit(solution)/shard_map/all_to_all | solution.py:21
  78.1 14.7 %collective-permute-start.5 = (f32[8,72,128]{2,1,0:T(8,128)S(1)}, f32[8,72,128]{2,1,0:T(8,128)S(1)}, u32[]{:S(2)}, u32[]{:S(2)}) collective-permute-start(f32[8,72,128]{2,1,0:T(8,128)S(1)} %all-to-all-done.1.refs_0_.refs_4_), channel_id=1, source_target_pairs={{0,3},{1,0},{2,1},{3,2},{4,7},{5,4},{6,5},{7,6},{8,11},{9,8},{10,9... | collective-permute-start | bytes 884744 | tf_op jit(solution)/shard_map/ppermute | solution.py:26
  80.0 12.8 %collective-permute-start.4 = (f32[8,72,128]{2,1,0:T(8,128)S(1)}, f32[8,72,128]{2,1,0:T(8,128)S(1)}, u32[]{:S(2)}, u32[]{:S(2)}) collective-permute-start(f32[8,72,128]{2,1,0:T(8,128)S(1)} %all-to-all-done.1.refs_0_.refs_4_), channel_id=1, source_target_pairs={{0,2},{1,3},{2,0},{3,1},{4,6},{5,7},{6,4},{7,5},{8,10},{9,11},{10,... | collective-permute-start | bytes 884744 | tf_op jit(solution)/shard_map/ppermute | solution.py:26
  81.2 15.4 %collective-permute-start.3 = (f32[8,72,128]{2,1,0:T(8,128)S(1)}, f32[8,72,128]{2,1,0:T(8,128)S(1)}, u32[]{:S(2)}, u32[]{:S(2)}) collective-permute-start(f32[8,72,128]{2,1,0:T(8,128)S(1)} %all-to-all-done.1.refs_0_.refs_4_), channel_id=1, source_target_pairs={{0,1},{1,2},{2,3},{3,0},{4,5},{5,6},{6,7},{7,4},{8,9},{9,10},{10,1... | collective-permute-start | bytes 884744 | tf_op jit(solution)/shard_map/ppermute | solution.py:26
  92.9 3.7 %copy-start.9 = (f32[8,72,128]{2,1,0:T(8,128)}, f32[8,72,128]{2,1,0:T(8,128)S(1)}, u32[]{:S(2)}) copy-start(f32[8,72,128]{2,1,0:T(8,128)S(1)} %collective-permute-done.5.refs_3_.refs_7_) | copy-start | bytes 884740
  92.9 3.7 %copy-start.10 = (f32[8,72,128]{2,1,0:T(8,128)}, f32[8,72,128]{2,1,0:T(8,128)S(1)}, u32[]{:S(2)}) copy-start(f32[8,72,128]{2,1,0:T(8,128)S(1)} %collective-permute-done.4.refs_2_.refs_6_) | copy-start | bytes 884740
  106.4 8.6 %copy-start.22 = (f32[8,32,512]{2,1,0:T(8,128)S(1)}, f32[8,32,512]{2,1,0:T(8,128)}, u32[]{:S(2)}) copy-start(f32[8,32,512]{2,1,0:T(8,128)} %get-tuple-element.25) | copy-start | bytes 1572868
  111.7 26.5 %collective-permute-start.13 = (f32[8,32,512]{2,1,0:T(8,128)}, f32[8,32,512]{2,1,0:T(8,128)S(1)}, u32[]{:S(2)}, u32[]{:S(2)}) collective-permute-start(f32[8,32,512]{2,1,0:T(8,128)} %get-tuple-element.24), channel_id=1, source_target_pairs={{0,1},{1,2},{2,3},{3,0},{4,5},{5,6},{6,7},{7,4},{8,9},{9,10},{10,1... | collective-permute-start | bytes 1572872 | tf_op jit(solution)/shard_map/ppermute | solution.py:26
  111.7 26.5 %collective-permute-start.15 = (f32[8,32,512]{2,1,0:T(8,128)}, f32[8,32,512]{2,1,0:T(8,128)S(1)}, u32[]{:S(2)}, u32[]{:S(2)}) collective-permute-start(f32[8,32,512]{2,1,0:T(8,128)} %get-tuple-element.26), channel_id=1, source_target_pairs={{0,3},{1,0},{2,1},{3,2},{4,7},{5,4},{6,5},{7,6},{8,11},{9,8},{10,9... | collective-permute-start | bytes 1572872 | tf_op jit(solution)/shard_map/ppermute | solution.py:26
  114.9 23.3 %collective-permute-start.14 = (f32[8,32,512]{2,1,0:T(8,128)S(1)}, f32[8,32,512]{2,1,0:T(8,128)S(1)}, u32[]{:S(2)}, u32[]{:S(2)}) collective-permute-start(f32[8,32,512]{2,1,0:T(8,128)S(1)} %copy-done.22), channel_id=1, source_target_pairs={{0,2},{1,3},{2,0},{3,1},{4,6},{5,7},{6,4},{7,5},{8,10},{9,11},{10,... | collective-permute-start | bytes 1572872 | tf_op jit(solution)/shard_map/ppermute | solution.py:26
  140.3 6.8 %copy-start.6 = (f32[8,4,4,8,256]{4,3,2,1,0:T(8,128)}, f32[8,4,4,8,256]{4,3,2,1,0:T(8,128)S(1)}, u32[]{:S(2)}) copy-start(f32[8,4,4,8,256]{4,3,2,1,0:T(8,128)S(1)} %all-to-all-done.4.blocks_ref) | copy-start | bytes 3145732
  140.3 28.9 %all-to-all-start.3 = ((f32[8,32,512]{2,1,0:T(8,128)}), f32[8,32,512]{2,1,0:T(8,128)S(1)}, u32[]{:S(2)}, u32[]{:S(2)}) async-start(f32[8,32,512]{2,1,0:T(8,128)} %add_add_fusion), calls=%async_computation.3 | async-start | bytes 1048576 | tf_op jit(solution)/shard_map/all_to_all | solution.py:21
  149.0 5.3 %collective-permute-start.16 = (f32[4,8,256]{2,1,0:T(8,128)}, f32[4,8,256]{2,1,0:T(8,128)S(1)}, u32[]{:S(2)}, u32[]{:S(2)}) collective-permute-start(f32[4,8,256]{2,1,0:T(8,128)} %get-tuple-element.28), channel_id=1, source_target_pairs={{0,1},{1,2},{2,3},{3,0},{4,5},{5,6},{6,7},{7,4},{8,9},{9,10},{10,1... | collective-permute-start | bytes 98312 | tf_op jit(solution)/shard_map/ppermute | solution.py:26
  149.8 6.0 %collective-permute-start.17 = (f32[4,8,256]{2,1,0:T(8,128)}, f32[4,8,256]{2,1,0:T(8,128)S(1)}, u32[]{:S(2)}, u32[]{:S(2)}) collective-permute-start(f32[4,8,256]{2,1,0:T(8,128)} %get-tuple-element.29), channel_id=1, source_target_pairs={{0,2},{1,3},{2,0},{3,1},{4,6},{5,7},{6,4},{7,5},{8,10},{9,11},{10,... | collective-permute-start | bytes 98312 | tf_op jit(solution)/shard_map/ppermute | solution.py:26
  153.4 4.1 %collective-permute-start.18 = (f32[4,8,256]{2,1,0:T(8,128)}, f32[4,8,256]{2,1,0:T(8,128)S(1)}, u32[]{:S(2)}, u32[]{:S(2)}) collective-permute-start(f32[4,8,256]{2,1,0:T(8,128)} %get-tuple-element.30), channel_id=1, source_target_pairs={{0,3},{1,0},{2,1},{3,2},{4,7},{5,4},{6,5},{7,6},{8,11},{9,8},{10,9... | collective-permute-start | bytes 98312 | tf_op jit(solution)/shard_map/ppermute | solution.py:26
  154.3 3.2 %copy-start.19 = (f32[4,8,256]{2,1,0:T(8,128)}, f32[4,8,256]{2,1,0:T(8,128)S(1)}, u32[]{:S(2)}) copy-start(f32[4,8,256]{2,1,0:T(8,128)S(1)} %collective-permute-done.16.refs_1_) | copy-start | bytes 98308
  155.8 1.7 copy-start.20
  160.5 5.2 %collective-permute-start.21 = (f32[32,8,128]{2,1,0:T(8,128)}, f32[32,8,128]{2,1,0:T(8,128)S(1)}, u32[]{:S(2)}, u32[]{:S(2)}) collective-permute-start(f32[32,8,128]{2,1,0:T(8,128)} %shard_map.90.refs_0_), channel_id=1, source_target_pairs={{0,192},{64,0},{128,64},{192,128},{1,193},{65,1},{129,65},{193,129... | collective-permute-start | bytes 393224 | tf_op jit(solution)/shard_map/ppermute | solution.py:26
  161.3 6.7 %collective-permute-start.20 = (f32[32,8,128]{2,1,0:T(8,128)}, f32[32,8,128]{2,1,0:T(8,128)S(1)}, u32[]{:S(2)}, u32[]{:S(2)}) collective-permute-start(f32[32,8,128]{2,1,0:T(8,128)} %shard_map.90.refs_0_), channel_id=1, source_target_pairs={{0,128},{64,192},{128,0},{192,64},{1,129},{65,193},{129,1},{193,65... | collective-permute-start | bytes 393224 | tf_op jit(solution)/shard_map/ppermute | solution.py:26
  163.3 5.9 %collective-permute-start.19 = (f32[32,8,128]{2,1,0:T(8,128)}, f32[32,8,128]{2,1,0:T(8,128)S(1)}, u32[]{:S(2)}, u32[]{:S(2)}) collective-permute-start(f32[32,8,128]{2,1,0:T(8,128)} %shard_map.90.refs_0_), channel_id=1, source_target_pairs={{0,64},{64,128},{128,192},{192,0},{1,65},{65,129},{129,193},{193,1... | collective-permute-start | bytes 393224 | tf_op jit(solution)/shard_map/ppermute | solution.py:26
  164.6 4.6 %collective-permute-start.22 = (f32[32,8,128]{2,1,0:T(8,128)}, f32[32,8,128]{2,1,0:T(8,128)S(1)}, u32[]{:S(2)}, u32[]{:S(2)}) collective-permute-start(f32[32,8,128]{2,1,0:T(8,128)} %shard_map.90.refs_0_), channel_id=1, source_target_pairs={{0,32},{32,0},{1,33},{33,1},{2,34},{34,2},{3,35},{35,3},{4,36},{36... | collective-permute-start | bytes 393224 | tf_op jit(solution)/shard_map/ppermute | solution.py:26
  165.7 4.8 %copy-start.12 = (f32[32,8,128]{2,1,0:T(8,128)}, f32[32,8,128]{2,1,0:T(8,128)S(1)}, u32[]{:S(2)}) copy-start(f32[32,8,128]{2,1,0:T(8,128)S(1)} %collective-permute-done.21.refs_3_) | copy-start | bytes 393220
  165.7 3.5 %collective-permute-start.25 = (f32[32,8,128]{2,1,0:T(8,128)S(1)}, f32[32,8,128]{2,1,0:T(8,128)S(1)}, u32[]{:S(2)}, u32[]{:S(2)}) collective-permute-start(f32[32,8,128]{2,1,0:T(8,128)S(1)} %collective-permute-done.21.refs_3_), channel_id=1, source_target_pairs={{0,32},{32,0},{1,33},{33,1},{2,34},{34,2},{3,35},{35,3},{4,36},{36... | collective-permute-start | bytes 393224 | tf_op jit(solution)/shard_map/ppermute | solution.py:26
  168.0 2.5 %copy-start.13 = (f32[32,8,128]{2,1,0:T(8,128)}, f32[32,8,128]{2,1,0:T(8,128)S(1)}, u32[]{:S(2)}) copy-start(f32[32,8,128]{2,1,0:T(8,128)S(1)} %collective-permute-done.20.refs_2_) | copy-start | bytes 393220
  168.0 1.3 collective-permute-start.24
  169.1 1.4 copy-start.14
  169.1 1.3 collective-permute-start.23
  169.2 1.4 copy-start.8
  169.2 1.3 copy-start.15
  169.2 1.3 copy-start.16
  169.3 1.2 copy-start.17
  (6 other events, 4.6 us)

commit v3 on v2

--- a/solution.py
+++ b/solution.py
@@ -14,6 +14,7 @@
 
 HALF = 512
 VMEM = pl.BlockSpec(memory_space=pltpu.VMEM)
+HELD = pl.BlockSpec(memory_space=pltpu.VMEM)
 SMEM = pl.BlockSpec(memory_space=pltpu.SMEM)
 
 
@@ -26,8 +27,10 @@
     return lax.ppermute(shard, axis, [(i, (i + hops) % n) for i in range(n)])
 
 
-def call(kernel, outs, in_specs, me, *, args, grid=1, scratch=()):
-    out_shape = [jax.ShapeDtypeStruct(*o) for o in outs]
+def call(kernel, outs, in_specs, me, *, args, grid=1, scratch=(), held=True):
+    out_shape = [(pltpu.VMEM if held else pltpu.HBM)(*o) for o in outs]
+    spaces = [pltpu.VMEM if spec is HELD else None if spec.block_shape is None else pltpu.HBM for spec in in_specs]
+    args = [a if space is None else pltpu.with_memory_space_constraint(a, space) for a, space in zip(args, spaces)]
     return pl.pallas_call(
         kernel,
         out_shape=out_shape,
@@ -38,6 +41,7 @@
             out_specs=[VMEM] * len(out_shape),
             scratch_shapes=list(scratch),
         ),
+        compiler_params=pltpu.CompilerParams(vmem_limit_bytes=28 << 20),
     )(me, *args)
 
 
@@ -139,10 +143,12 @@
             out_ref[rows, q, :] = both[32 * q + 8 * slot : 32 * q + 8 * slot + 8] / eig
 
 
-def basis_product(core, slabs, high_ref, low_ref, out_ref):
+def basis_product(me_ref, hops, slabs, high_ref, low_ref, out_ref):
+    _, core, _, x = place(me_ref)
+    target = lax.rem(x + hops, 4)
     total = None
     for half, group in ((core, slabs[:4]), (1 - core, slabs[4:])):
-        value = jnp.concatenate([ref[...].reshape(64, HALF) for ref in group], 0)
+        value = jnp.concatenate([ref[:, target].reshape(64, HALF) for ref in group], 0)
         high, low = split(value)
         part = dot_nt(high, high_ref[half]) + dot_nt(high, low_ref[half]) + dot_nt(low, high_ref[half])
         total = part if total is None else total + part
@@ -152,7 +158,7 @@
 
 def train_kernel(me_ref, len_ref, grads_ref, *refs):
     blocks, slabs, (out_ref, high_ref, low_ref, total_ref) = refs[:4], refs[4:12], refs[12:]
-    _, core, _, x = place(me_ref)
+    _, _, _, x = place(me_ref)
     step = pl.program_id(0)
     cols = grads_ref.shape[1]
 
@@ -193,17 +199,13 @@
 
     @pl.when(step == 4)
     def _():
-        basis_product(core, slabs, high_ref, low_ref, out_ref)
-
-
-def product_kernel(me_ref, high_ref, low_ref, *refs):
+        basis_product(me_ref, 2, slabs, high_ref, low_ref, out_ref)
+
+
+def product_kernel(hops, me_ref, high_ref, low_ref, *refs):
     slabs, out_refs = refs[:8], refs[8:]
-    _, core, _, _ = place(me_ref)
-    for at, out_ref in enumerate(out_refs):
-
-        @pl.when(pl.program_id(0) == at)
-        def _(out_ref=out_ref):
-            basis_product(core, slabs, high_ref, low_ref, out_ref)
+    for k, out_ref in zip(hops, out_refs):
+        basis_product(me_ref, k, slabs, high_ref, low_ref, out_ref)
 
 
 def score_kernel(me_ref, blocks_ref, *refs):
@@ -265,7 +267,7 @@
         basis_pick_kernel,
         [((32, 8, HALF), f32)],
         [pl.BlockSpec((8, output_basis.shape[1]), lambda i, me: (me[0] // 64, 0))],
-        me, args=(output_basis,),
+        me, args=(output_basis,), held=False,
     )
     slab = exchange(picked, ZX).reshape(8, 4, 8, HALF)
     slabs = [slab]
@@ -277,17 +279,20 @@
     query_call = functools.partial(
         call, outs=[((8, 4, 4, 8, queries), f32)], me=me, scratch=[pltpu.VMEM((queries, HALF), bf16)]
     )
-    (rot,) = query_call(functools.partial(query_kernel, True), in_specs=[VMEM] * 5, args=(query_grads, *slabs[:4]))
+    (rot,) = query_call(functools.partial(query_kernel, True), in_specs=[VMEM] + [HELD] * 4, args=(query_grads, *slabs[:4]))
     (rot,) = query_call(
-        functools.partial(query_kernel, False), in_specs=[VMEM] * 6, args=(query_grads, rot, *slabs[4:])
+        functools.partial(query_kernel, False),
+        in_specs=[VMEM] + [HELD] * 5,
+        args=(query_grads, rot, *slabs[4:]),
+        held=False,
     )
     rot = exchange(rot, "z")
-    rots = call(query_sum_kernel, [((4, 8, queries), f32)] * 4, [VMEM], me, args=(rot,))
+    rots = call(query_sum_kernel, [((4, 8, queries), f32)] * 4, [HELD], me, args=(rot,))
     rots = [rots[0]] + [shifted(rots[k], "x", k) for k in (1, 2, 3)]
     (precond,) = call(
         precond_kernel,
         [((32, 8, 128), f32)],
-        [VMEM] * 9,
+        [VMEM] + [HELD] * 8,
         me, args=(eigenvalues, *rots, *blocks),
         scratch=[pltpu.VMEM((queries, 128), f32)],
     )
@@ -295,11 +300,6 @@
     for k in (1, 2, 3):
         preconds.append(shifted(precond, "y", k))
     preconds = preconds + [shifted(p, "core", 1) for p in preconds]
-
-    def slab_specs(first, stride=0):
-        return [
-            pl.BlockSpec((8, 1, 8, HALF), lambda i, me: (0, lax.rem(me[0] % 4 + first + stride * i, 4), 0, 0))
-        ] * 8
 
     block_shape, sum_shape = ((8, 32, 512), f32), ((2, 512, HALF), bf16)
     sent = [None] * 4
@@ -309,8 +309,7 @@
         [
             SMEM,
             pl.BlockSpec((512, out_grads.shape[1]), lambda i, me: (lax.rem(me[0] % 4 + 4 - jnp.minimum(i, 3), 4), 0)),
-            *[VMEM] * 4,
-            *slab_specs(2),
+            *[HELD] * 12,
         ],
         me,
         args=(doc_lengths, out_grads, *blocks, *slabs),
@@ -318,18 +317,18 @@
         scratch=[pltpu.VMEM((4, 128, out_grads.shape[1]), f32)],
     )
     sent[1], sent[3] = call(
-        product_kernel, [block_shape] * 2, [VMEM, VMEM, *slab_specs(1, 2)], me, args=(high, low, *slabs), grid=2
+        functools.partial(product_kernel, (1, 3)), [block_shape] * 2, [HELD] * 10, me, args=(high, low, *slabs)
     )
     sent[2] = shifted(sent[2], "x", 2)
     (sent[0],) = call(
-        product_kernel, [block_shape], [VMEM, VMEM, *slab_specs(0)], me, args=(high, low, *slabs)
+        functools.partial(product_kernel, (0,)), [block_shape], [HELD] * 10, me, args=(high, low, *slabs), held=False
     )
     for k in (1, 3):
         sent[k] = shifted(sent[k], "x", k)
     train = sent[0] + sent[1] + sent[2] + sent[3]
     train = exchange(train, "z")
 
-    (partial_scores,) = call(score_kernel, [((32, 8, 128), f32)], [VMEM] * 9, me, args=(train, *preconds))
+    (partial_scores,) = call(score_kernel, [((32, 8, 128), f32)], [HELD] * 9, me, args=(train, *preconds))
     return jnp.sum(exchange(partial_scores, ZX), axis=(0, 2)).reshape(2, 4)
 
 

time: 196 us -> 185 us (0.944)
  Pallas kernels: 36.9 us -> 22.8 us
  waiting for transfers between devices: 70.4 us -> 75.5 us
  local copies, waits for them, and re-layouts: 5.33 us -> 2.44 us
  starting transfers between devices: 57.6 us -> 60 us
    pallas_call x10, Pallas kernels: 36.9 us -> 22.8 us  [call(): pl.pallas_call(kernel, out_shape=out_shape, grid_spec=pltpu.PrefetchScala...]
    all_to_all x5, waiting for transfers between devices: 13.1 us -> 17.8 us  [exchange(): return lax.all_to_all(blocks, axis, 0, 0, tiled=True)]
    unnamed x46 -> x22, local copies, waits for them, and re-layouts: 3.94 us -> 1.05 us
  transfers between devices with their start and end apart: 31 -> 31, of which waited for: 18 -> 17; matrix products, arithmetic and copies ran while one was open for 2% -> 2% of each run, Pallas kernels for 17% -> 11%
where the time goes in v3:
time: 185 us; the launch traced here: 183 us
  waiting for transfers between devices  75.5 us (41%)
  starting transfers between devices  60 us (32%)
  Pallas kernels  22.8 us (12%)
  blocking collectives  19.1 us (10%)
  other arithmetic  2.99 us (2%)
  local copies, waits for them, and re-layouts  2.44 us (1%)
    ppermute x26, waiting for transfers between devices, shifted(): return lax.ppermute(shard, axis, [(i, (i + hops) % n) for i in range(n)])  57.7 us
    all_to_all x5, starting transfers between devices, exchange(): return lax.all_to_all(blocks, axis, 0, 0, tiled=True)  32.5 us
    ppermute x26, starting transfers between devices, shifted(): return lax.ppermute(shard, axis, [(i, (i + hops) % n) for i in range(n)])  27.5 us
    pallas_call x10, Pallas kernels, call(): pl.pallas_call(kernel, out_shape=out_shape, grid_spec=pltpu.PrefetchScala...  22.8 us
    all_to_all x1, blocking collectives, exchange(): return lax.all_to_all(blocks, axis, 0, 0, tiled=True)  19.1 us
    all_to_all x5, waiting for transfers between devices, exchange(): return lax.all_to_all(blocks, axis, 0, 0, tiled=True)  17.8 us
  transfers between devices with their start and end apart: 31, of which 17 were waited for; matrix products, arithmetic and copies ran while one was open for 2% of the time, Pallas kernels for 11%

profile of v3, /device:TPU:8, one launch (start us, length us, event | category | flops | bytes accessed | tf_op | source)
XLA Modules:
  0.0 183.1 jit_solution(1135441621098276470)
XLA Ops:
  0.0 2.1 %shard_map.83 = f32[32,8,512]{2,1,0:T(8,128)} custom-call(s32[1]{0:T(128)} %bitcast.me_ref, f32[32,28672]{1,0:T(8,128)} %basis_ref.3), custom_call_target="tpu_custom_call" | custom-call | tf_op jit(solution)/shard_map/pallas_call | solution.py:34
  2.1 11.3 %all-to-all-start.2 = ((f32[32,8,512]{2,1,0:T(8,128)}), f32[32,8,512]{2,1,0:T(8,128)S(1)}, u32[]{:S(2)}, u32[]{:S(2)}) async-start(f32[32,8,512]{2,1,0:T(8,128)} %shard_map.83), calls=%async_computation.2 | async-start | bytes 1048576 | tf_op jit(solution)/shard_map/all_to_all | solution.py:22
  13.5 1.8 shard_map.82
  15.2 3.4 %collective-permute-start = (f32[8,72,128]{2,1,0:T(8,128)S(1)}, f32[8,72,128]{2,1,0:T(8,128)S(1)}, u32[]{:S(2)}, u32[]{:S(2)}) collective-permute-start(f32[8,72,128]{2,1,0:T(8,128)S(1)} %get-tuple-element.19), channel_id=1, source_target_pairs={{0,2},{1,3},{2,0},{3,1},{4,6},{5,7},{6,4},{7,5},{8,10},{9,11},{10,... | collective-permute-start | bytes 884744 | tf_op jit(solution)/shard_map/ppermute | solution.py:27
  18.6 0.6 collective-permute-start.1
  19.2 2.7 %collective-permute-start.2 = (f32[8,72,128]{2,1,0:T(8,128)S(1)}, f32[8,72,128]{2,1,0:T(8,128)S(1)}, u32[]{:S(2)}, u32[]{:S(2)}) collective-permute-start(f32[8,72,128]{2,1,0:T(8,128)S(1)} %get-tuple-element.21), channel_id=1, source_target_pairs={{0,3},{1,0},{2,1},{3,2},{4,7},{5,4},{6,5},{7,6},{8,11},{9,8},{10,9... | collective-permute-start | bytes 884744 | tf_op jit(solution)/shard_map/ppermute | solution.py:27
  21.8 9.4 %all-to-all-done.2 = f32[32,8,512]{2,1,0:T(8,128)S(1)} async-done(((f32[32,8,512]{2,1,0:T(8,128)}), f32[32,8,512]{2,1,0:T(8,128)S(1)}, u32[]{:S(2)}, u32[]{:S(2)}) %all-to-all-start.2) | async-done | bytes 524320 | tf_op jit(solution)/shard_map/all_to_all | solution.py:22
  31.2 1.6 collective-permute-start.8
  32.8 0.9 collective-permute-start.7
  33.8 2.4 %collective-permute-start.6 = (f32[8,4,8,512]{3,2,1,0:T(8,128)S(1)}, f32[8,4,8,512]{3,2,1,0:T(8,128)}, u32[]{:S(2)}, u32[]{:S(2)}) collective-permute-start(f32[8,4,8,512]{3,2,1,0:T(8,128)S(1)} %bitcast.4), channel_id=1, source_target_pairs={{0,192},{64,0},{128,64},{192,128},{1,193},{65,1},{129,65},{193,129... | collective-permute-start | bytes 1572872 | tf_op jit(solution)/shard_map/ppermute | solution.py:27
  36.5 0.8 add_add_fusion.1
  37.3 6.1 %all-to-all-start = ((f32[8,72,128]{2,1,0:T(8,128)}), f32[8,72,128]{2,1,0:T(8,128)S(1)}, u32[]{:S(2)}, u32[]{:S(2)}) async-start(f32[8,72,128]{2,1,0:T(8,128)} %add_add_fusion.1), calls=%async_computation | async-start | bytes 589824 | tf_op jit(solution)/shard_map/all_to_all | solution.py:22
  43.4 2.6 %collective-permute-done.8.refs_7_.refs_3_ = f32[8,4,8,512]{3,2,1,0:T(8,128)S(1)} collective-permute-done((f32[8,4,8,512]{3,2,1,0:T(8,128)S(1)}, f32[8,4,8,512]{3,2,1,0:T(8,128)S(1)}, u32[]{:S(2)}, u32[]{:S(2)}) %collective-permute-start.8) | collective-permute-done | bytes 524320 | tf_op jit(solution)/shard_map/ppermute | solution.py:27
  46.0 3.2 %collective-permute-done.7.refs_6_.refs_2_ = f32[8,4,8,512]{3,2,1,0:T(8,128)} collective-permute-done((f32[8,4,8,512]{3,2,1,0:T(8,128)S(1)}, f32[8,4,8,512]{3,2,1,0:T(8,128)}, u32[]{:S(2)}, u32[]{:S(2)}) %collective-permute-start.7) | collective-permute-done | bytes 524320 | tf_op jit(solution)/shard_map/ppermute | solution.py:27
  49.2 7.3 %collective-permute-done.6.refs_5_.refs_1_ = f32[8,4,8,512]{3,2,1,0:T(8,128)} collective-permute-done((f32[8,4,8,512]{3,2,1,0:T(8,128)S(1)}, f32[8,4,8,512]{3,2,1,0:T(8,128)}, u32[]{:S(2)}, u32[]{:S(2)}) %collective-permute-start.6) | collective-permute-done | bytes 524320 | tf_op jit(solution)/shard_map/ppermute | solution.py:27
  56.6 0.7 broadcast_in_dim.2
  57.3 4.1 %all-to-all-start.1 = ((f32[8,72,128]{2,1,0:T(8,128)}), f32[8,72,128]{2,1,0:T(8,128)S(1)}, u32[]{:S(2)}, u32[]{:S(2)}) async-start(f32[8,72,128]{2,1,0:T(8,128)} %broadcast_in_dim.2), calls=%async_computation.1 | async-start | bytes 589824 | tf_op jit(solution)/shard_map/all_to_all | solution.py:22
  61.4 1.0 copy-done
  62.4 2.0 %shard_map.87.refs_0_ = f32[8,4,4,8,256]{4,3,2,1,0:T(8,128)S(1)} custom-call(s32[1]{0:T(128)} %bitcast.me_ref, bf16[256,896]{1,0:T(8,128)(2,1)S(1)} %copy-done, f32[8,4,8,512]{3,2,1,0:T(8,128)S(1)} %bitcast.6, f32[8,4,8,512]{3,2,1,0:T(8,128)} %collective-permute-done.6.refs_5_.refs_1_, f32[8,4,8,512]{3,2,1,0:T(8,128)} %collective-permute-done.7.refs_6_.refs_2_, ...), custom_call_target="tpu_custom_call" | custom-call | tf_op jit(solution)/shard_map/pallas_call | solution.py:34
  64.4 1.8 shard_map.88
  66.3 8.4 %all-to-all-done.1.refs_0_.refs_4_ = f32[8,72,128]{2,1,0:T(8,128)S(1)} async-done(((f32[8,72,128]{2,1,0:T(8,128)}), f32[8,72,128]{2,1,0:T(8,128)S(1)}, u32[]{:S(2)}, u32[]{:S(2)}) %all-to-all-start.1) | async-done | bytes 294944 | tf_op jit(solution)/shard_map/all_to_all | solution.py:22
  74.6 4.2 %all-to-all-start.4 = ((f32[8,4,4,8,256]{4,3,2,1,0:T(8,128)}), f32[8,4,4,8,256]{4,3,2,1,0:T(8,128)}, u32[]{:S(2)}, u32[]{:S(2)}) async-start(f32[8,4,4,8,256]{4,3,2,1,0:T(8,128)} %shard_map.88), calls=%async_computation.4 | async-start | bytes 2097152 | tf_op jit(solution)/shard_map/all_to_all | solution.py:22
  78.9 1.9 %collective-permute-start.5 = (f32[8,72,128]{2,1,0:T(8,128)S(1)}, f32[8,72,128]{2,1,0:T(8,128)S(1)}, u32[]{:S(2)}, u32[]{:S(2)}) collective-permute-start(f32[8,72,128]{2,1,0:T(8,128)S(1)} %all-to-all-done.1.refs_0_.refs_4_), channel_id=1, source_target_pairs={{0,3},{1,0},{2,1},{3,2},{4,7},{5,4},{6,5},{7,6},{8,11},{9,8},{10,9... | collective-permute-start | bytes 884744 | tf_op jit(solution)/shard_map/ppermute | solution.py:27
  80.8 1.0 collective-permute-start.4
  81.8 0.7 collective-permute-start.3
  82.5 11.1 %collective-permute-done.5.refs_3_.refs_7_ = f32[8,72,128]{2,1,0:T(8,128)S(1)} collective-permute-done((f32[8,72,128]{2,1,0:T(8,128)S(1)}, f32[8,72,128]{2,1,0:T(8,128)S(1)}, u32[]{:S(2)}, u32[]{:S(2)}) %collective-permute-start.5) | collective-permute-done | bytes 294944 | tf_op jit(solution)/shard_map/ppermute | solution.py:27
  93.7 3.7 %collective-permute-done.3.refs_1_.refs_5_ = f32[8,72,128]{2,1,0:T(8,128)S(1)} collective-permute-done((f32[8,72,128]{2,1,0:T(8,128)S(1)}, f32[8,72,128]{2,1,0:T(8,128)S(1)}, u32[]{:S(2)}, u32[]{:S(2)}) %collective-permute-start.3) | collective-permute-done | bytes 294944 | tf_op jit(solution)/shard_map/ppermute | solution.py:27
  97.3 7.1 %shard_map.84 = (f32[8,32,512]{2,1,0:T(8,128)S(1)}, bf16[2,512,512]{2,1,0:T(8,128)(2,1)S(1)}, bf16[2,512,512]{2,1,0:T(8,128)(2,1)S(1)}) custom-call(s32[1]{0:T(128)} %bitcast.me_ref, s32[4]{0:T(128)S(1)} %copy-done.10, bf16[2048,896]{1,0:T(8,128)(2,1)} %grads_ref.3, f32[8,72,128]{2,1,0:T(8,128)S(1)} %all-to-all-done.1.refs_0_.refs_4_, ...), custom_call_target="tpu_custom_call" | custom-call | tf_op jit(solution)/shard_map/pallas_call | solution.py:34
  104.5 3.0 %shard_map.86 = (f32[8,32,512]{2,1,0:T(8,128)S(1)}, f32[8,32,512]{2,1,0:T(8,128)S(1)}) custom-call(s32[1]{0:T(128)} %bitcast.me_ref, bf16[2,512,512]{2,1,0:T(8,128)(2,1)S(1)} %get-tuple-element.22.high_ref, bf16[2,512,512]{2,1,0:T(8,128)(2,1)S(1)} %get-tuple-element.23.low_ref, f32[8,4,8,512]{3,2,1,0:T(8,128)S(1)} %bitcast.8, ...), custom_call_target="tpu_custom_call" | custom-call | tf_op jit(solution)/shard_map/pallas_call | solution.py:34
  107.6 3.2 %collective-permute-start.15 = (f32[8,32,512]{2,1,0:T(8,128)S(1)}, f32[8,32,512]{2,1,0:T(8,128)S(1)}, u32[]{:S(2)}, u32[]{:S(2)}) collective-permute-start(f32[8,32,512]{2,1,0:T(8,128)S(1)} %get-tuple-element.26), channel_id=1, source_target_pairs={{0,3},{1,0},{2,1},{3,2},{4,7},{5,4},{6,5},{7,6},{8,11},{9,8},{10,9... | collective-permute-start | bytes 1572872 | tf_op jit(solution)/shard_map/ppermute | solution.py:27
  110.8 3.0 %shard_map.85 = f32[8,32,512]{2,1,0:T(8,128)} custom-call(s32[1]{0:T(128)} %bitcast.me_ref, bf16[2,512,512]{2,1,0:T(8,128)(2,1)S(1)} %get-tuple-element.22.high_ref, bf16[2,512,512]{2,1,0:T(8,128)(2,1)S(1)} %get-tuple-element.23.low_ref, f32[8,4,8,512]{3,2,1,0:T(8,128)S(1)} %bitcast.9, f32[8,4,8,512]{3,2,1,0:T(8,128)} %collective-permute-done.6.refs_5_.refs_1_, ...), custom_call_target="tpu_custom_call" | custom-call | tf_op jit(solution)/shard_map/pallas_call | solution.py:34
  113.8 20.2 %collective-permute-done.13 = f32[8,32,512]{2,1,0:T(8,128)S(1)} collective-permute-done((f32[8,32,512]{2,1,0:T(8,128)S(1)}, f32[8,32,512]{2,1,0:T(8,128)S(1)}, u32[]{:S(2)}, u32[]{:S(2)}) %collective-permute-start.13) | collective-permute-done | bytes 524320 | tf_op jit(solution)/shard_map/ppermute | solution.py:27
  134.0 2.0 %add_add_fusion = f32[8,32,512]{2,1,0:T(8,128)} fusion(f32[8,32,512]{2,1,0:T(8,128)S(1)} %collective-permute-done.15, f32[8,32,512]{2,1,0:T(8,128)S(1)} %collective-permute-done.14, f32[8,32,512]{2,1,0:T(8,128)} %shard_map.85, f32[8,32,512]{2,1,0:T(8,128)S(1)} %collective-permute-done.13), kind=kLoop, calls=%fused_computation | loop fusion | flops 393216 | bytes 2621440 | tf_op jit(solution)/shard_map/add | solution.py:328
  136.1 6.7 %all-to-all-start.3 = ((f32[8,32,512]{2,1,0:T(8,128)}), f32[8,32,512]{2,1,0:T(8,128)S(1)}, u32[]{:S(2)}, u32[]{:S(2)}) async-start(f32[8,32,512]{2,1,0:T(8,128)} %add_add_fusion), calls=%async_computation.3 | async-start | bytes 1048576 | tf_op jit(solution)/shard_map/all_to_all | solution.py:22
  142.8 1.3 shard_map.89
  144.1 0.9 collective-permute-start.16
  145.0 3.6 %collective-permute-start.17 = (f32[4,8,256]{2,1,0:T(8,128)S(1)}, f32[4,8,256]{2,1,0:T(8,128)S(1)}, u32[]{:S(2)}, u32[]{:S(2)}) collective-permute-start(f32[4,8,256]{2,1,0:T(8,128)S(1)} %get-tuple-element.29), channel_id=1, source_target_pairs={{0,2},{1,3},{2,0},{3,1},{4,6},{5,7},{6,4},{7,5},{8,10},{9,11},{10,... | collective-permute-start | bytes 98312 | tf_op jit(solution)/shard_map/ppermute | solution.py:27
  148.6 0.7 collective-permute-done.16.refs_1_
  149.3 1.5 collective-permute-done.17.refs_2_
  150.8 1.7 collective-permute-done.18.refs_3_
  153.0 0.9 collective-permute-start.21
  153.8 2.1 %collective-permute-start.20 = (f32[32,8,128]{2,1,0:T(8,128)S(1)}, f32[32,8,128]{2,1,0:T(8,128)S(1)}, u32[]{:S(2)}, u32[]{:S(2)}) collective-permute-start(f32[32,8,128]{2,1,0:T(8,128)S(1)} %shard_map.90.refs_0_), channel_id=1, source_target_pairs={{0,128},{64,192},{128,0},{192,64},{1,129},{65,193},{129,1},{193,65... | collective-permute-start | bytes 393224 | tf_op jit(solution)/shard_map/ppermute | solution.py:27
  155.9 1.6 collective-permute-start.19
  158.0 2.3 %collective-permute-done.20.refs_2_ = f32[32,8,128]{2,1,0:T(8,128)S(1)} collective-permute-done((f32[32,8,128]{2,1,0:T(8,128)S(1)}, f32[32,8,128]{2,1,0:T(8,128)S(1)}, u32[]{:S(2)}, u32[]{:S(2)}) %collective-permute-start.20) | collective-permute-done | bytes 131104 | tf_op jit(solution)/shard_map/ppermute | solution.py:27
  160.3 1.2 collective-permute-done.19.refs_1_
  161.6 1.2 collective-permute-done.23.refs_5_
  163.2 19.1 %all_to_all.30 = f32[32,8,128]{2,1,0:T(8,128)S(1)} all-to-all(f32[32,8,128]{2,1,0:T(8,128)S(1)} %shard_map.91), channel_id=1, replica_groups=mesh['y'=4,'core'=2,'z'=8,'x'=4] {'z','x'}, dimensions={0} | all-to-all | bytes 262144 | tf_op jit(solution)/shard_map/all_to_all | solution.py:22
  182.5 0.6 reshape.12
  (53 shorter events, 2.2 us)
Async XLA Ops:
  0.0 13.4 %copy-start.8 = (bf16[256,256]{1,0:T(8,128)(2,1)S(1)}, bf16[256,256]{1,0:T(8,128)(2,1)}, u32[]{:S(2)}) copy-start(bf16[256,256]{1,0:T(8,128)(2,1)} %query_ref.1) | copy-start | bytes 393220
  0.0 13.4 %copy-start.7 = (bf16[2048,256]{1,0:T(8,128)(2,1)S(1)}, bf16[2048,256]{1,0:T(8,128)(2,1)}, u32[]{:S(2)}) copy-start(bf16[2048,256]{1,0:T(8,128)(2,1)} %acts_ref.1) | copy-start | bytes 3145732
  2.1 29.1 %all-to-all-start.2 = ((f32[32,8,512]{2,1,0:T(8,128)}), f32[32,8,512]{2,1,0:T(8,128)S(1)}, u32[]{:S(2)}, u32[]{:S(2)}) async-start(f32[32,8,512]{2,1,0:T(8,128)} %shard_map.83), calls=%async_computation.2 | async-start | bytes 1048576 | tf_op jit(solution)/shard_map/all_to_all | solution.py:22
  15.2 18.5 %collective-permute-start = (f32[8,72,128]{2,1,0:T(8,128)S(1)}, f32[8,72,128]{2,1,0:T(8,128)S(1)}, u32[]{:S(2)}, u32[]{:S(2)}) collective-permute-start(f32[8,72,128]{2,1,0:T(8,128)S(1)} %get-tuple-element.19), channel_id=1, source_target_pairs={{0,2},{1,3},{2,0},{3,1},{4,6},{5,7},{6,4},{7,5},{8,10},{9,11},{10,... | collective-permute-start | bytes 884744 | tf_op jit(solution)/shard_map/ppermute | solution.py:27
  18.6 17.9 %collective-permute-start.1 = (f32[8,72,128]{2,1,0:T(8,128)S(1)}, f32[8,72,128]{2,1,0:T(8,128)S(1)}, u32[]{:S(2)}, u32[]{:S(2)}) collective-permute-start(f32[8,72,128]{2,1,0:T(8,128)S(1)} %get-tuple-element.20), channel_id=1, source_target_pairs={{0,1},{1,2},{2,3},{3,0},{4,5},{5,6},{6,7},{7,4},{8,9},{9,10},{10,1... | collective-permute-start | bytes 884744 | tf_op jit(solution)/shard_map/ppermute | solution.py:27
  19.2 17.4 %collective-permute-start.2 = (f32[8,72,128]{2,1,0:T(8,128)S(1)}, f32[8,72,128]{2,1,0:T(8,128)S(1)}, u32[]{:S(2)}, u32[]{:S(2)}) collective-permute-start(f32[8,72,128]{2,1,0:T(8,128)S(1)} %get-tuple-element.21), channel_id=1, source_target_pairs={{0,3},{1,0},{2,1},{3,2},{4,7},{5,4},{6,5},{7,6},{8,11},{9,8},{10,9... | collective-permute-start | bytes 884744 | tf_op jit(solution)/shard_map/ppermute | solution.py:27
  31.2 14.8 %collective-permute-start.8 = (f32[8,4,8,512]{3,2,1,0:T(8,128)S(1)}, f32[8,4,8,512]{3,2,1,0:T(8,128)S(1)}, u32[]{:S(2)}, u32[]{:S(2)}) collective-permute-start(f32[8,4,8,512]{3,2,1,0:T(8,128)S(1)} %bitcast.2), channel_id=1, source_target_pairs={{0,64},{64,128},{128,192},{192,0},{1,65},{65,129},{129,193},{193,1... | collective-permute-start | bytes 1572872 | tf_op jit(solution)/shard_map/ppermute | solution.py:27
  32.8 16.4 %collective-permute-start.7 = (f32[8,4,8,512]{3,2,1,0:T(8,128)S(1)}, f32[8,4,8,512]{3,2,1,0:T(8,128)}, u32[]{:S(2)}, u32[]{:S(2)}) collective-permute-start(f32[8,4,8,512]{3,2,1,0:T(8,128)S(1)} %bitcast.3), channel_id=1, source_target_pairs={{0,128},{64,192},{128,0},{192,64},{1,129},{65,193},{129,1},{193,65... | collective-permute-start | bytes 1572872 | tf_op jit(solution)/shard_map/ppermute | solution.py:27
  33.8 22.8 %collective-permute-start.6 = (f32[8,4,8,512]{3,2,1,0:T(8,128)S(1)}, f32[8,4,8,512]{3,2,1,0:T(8,128)}, u32[]{:S(2)}, u32[]{:S(2)}) collective-permute-start(f32[8,4,8,512]{3,2,1,0:T(8,128)S(1)} %bitcast.4), channel_id=1, source_target_pairs={{0,192},{64,0},{128,64},{192,128},{1,193},{65,1},{129,65},{193,129... | collective-permute-start | bytes 1572872 | tf_op jit(solution)/shard_map/ppermute | solution.py:27
  37.3 19.2 %all-to-all-start = ((f32[8,72,128]{2,1,0:T(8,128)}), f32[8,72,128]{2,1,0:T(8,128)S(1)}, u32[]{:S(2)}, u32[]{:S(2)}) async-start(f32[8,72,128]{2,1,0:T(8,128)} %add_add_fusion.1), calls=%async_computation | async-start | bytes 589824 | tf_op jit(solution)/shard_map/all_to_all | solution.py:22
  43.4 21.0 %collective-permute-start.9 = (f32[8,4,8,512]{3,2,1,0:T(8,128)S(1)}, f32[8,4,8,512]{3,2,1,0:T(8,128)S(1)}, u32[]{:S(2)}, u32[]{:S(2)}) collective-permute-start(f32[8,4,8,512]{3,2,1,0:T(8,128)S(1)} %bitcast.5), channel_id=1, source_target_pairs={{0,32},{32,0},{1,33},{33,1},{2,34},{34,2},{3,35},{35,3},{4,36},{36... | collective-permute-start | bytes 1572872 | tf_op jit(solution)/shard_map/ppermute | solution.py:27
  46.0 18.4 %collective-permute-start.12 = (f32[8,4,8,512]{3,2,1,0:T(8,128)S(1)}, f32[8,4,8,512]{3,2,1,0:T(8,128)S(1)}, u32[]{:S(2)}, u32[]{:S(2)}) collective-permute-start(f32[8,4,8,512]{3,2,1,0:T(8,128)S(1)} %collective-permute-done.8.refs_7_.refs_3_), channel_id=1, source_target_pairs={{0,32},{32,0},{1,33},{33,1},{2,34},{34,2},{3,35},{35,3},{4,36},{36... | collective-permute-start | bytes 1572872 | tf_op jit(solution)/shard_map/ppermute | solution.py:27
  49.2 15.2 %collective-permute-start.11 = (f32[8,4,8,512]{3,2,1,0:T(8,128)}, f32[8,4,8,512]{3,2,1,0:T(8,128)S(1)}, u32[]{:S(2)}, u32[]{:S(2)}) collective-permute-start(f32[8,4,8,512]{3,2,1,0:T(8,128)} %collective-permute-done.7.refs_6_.refs_2_), channel_id=1, source_target_pairs={{0,32},{32,0},{1,33},{33,1},{2,34},{34,2},{3,35},{35,3},{4,36},{36... | collective-permute-start | bytes 1572872 | tf_op jit(solution)/shard_map/ppermute | solution.py:27
  56.5 7.9 %collective-permute-start.10 = (f32[8,4,8,512]{3,2,1,0:T(8,128)}, f32[8,4,8,512]{3,2,1,0:T(8,128)S(1)}, u32[]{:S(2)}, u32[]{:S(2)}) collective-permute-start(f32[8,4,8,512]{3,2,1,0:T(8,128)} %collective-permute-done.6.refs_5_.refs_1_), channel_id=1, source_target_pairs={{0,32},{32,0},{1,33},{33,1},{2,34},{34,2},{3,35},{35,3},{4,36},{36... | collective-permute-start | bytes 1572872 | tf_op jit(solution)/shard_map/ppermute | solution.py:27
  57.3 17.3 %all-to-all-start.1 = ((f32[8,72,128]{2,1,0:T(8,128)}), f32[8,72,128]{2,1,0:T(8,128)S(1)}, u32[]{:S(2)}, u32[]{:S(2)}) async-start(f32[8,72,128]{2,1,0:T(8,128)} %broadcast_in_dim.2), calls=%async_computation.1 | async-start | bytes 589824 | tf_op jit(solution)/shard_map/all_to_all | solution.py:22
  61.4 1.0 copy-start
  64.4 32.9 %copy-start.10 = (s32[4]{0:T(128)S(1)}, s32[4]{0:T(128)}, u32[]{:S(2)}) copy-start(s32[4]{0:T(128)} %len_ref.1) | copy-start | bytes 52
  74.6 61.4 %all-to-all-start.4 = ((f32[8,4,4,8,256]{4,3,2,1,0:T(8,128)}), f32[8,4,4,8,256]{4,3,2,1,0:T(8,128)}, u32[]{:S(2)}, u32[]{:S(2)}) async-start(f32[8,4,4,8,256]{4,3,2,1,0:T(8,128)} %shard_map.88), calls=%async_computation.4 | async-start | bytes 2097152 | tf_op jit(solution)/shard_map/all_to_all | solution.py:22
  78.9 14.8 %collective-permute-start.5 = (f32[8,72,128]{2,1,0:T(8,128)S(1)}, f32[8,72,128]{2,1,0:T(8,128)S(1)}, u32[]{:S(2)}, u32[]{:S(2)}) collective-permute-start(f32[8,72,128]{2,1,0:T(8,128)S(1)} %all-to-all-done.1.refs_0_.refs_4_), channel_id=1, source_target_pairs={{0,3},{1,0},{2,1},{3,2},{4,7},{5,4},{6,5},{7,6},{8,11},{9,8},{10,9... | collective-permute-start | bytes 884744 | tf_op jit(solution)/shard_map/ppermute | solution.py:27
  80.8 12.9 %collective-permute-start.4 = (f32[8,72,128]{2,1,0:T(8,128)S(1)}, f32[8,72,128]{2,1,0:T(8,128)S(1)}, u32[]{:S(2)}, u32[]{:S(2)}) collective-permute-start(f32[8,72,128]{2,1,0:T(8,128)S(1)} %all-to-all-done.1.refs_0_.refs_4_), channel_id=1, source_target_pairs={{0,2},{1,3},{2,0},{3,1},{4,6},{5,7},{6,4},{7,5},{8,10},{9,11},{10,... | collective-permute-start | bytes 884744 | tf_op jit(solution)/shard_map/ppermute | solution.py:27
  81.8 15.5 %collective-permute-start.3 = (f32[8,72,128]{2,1,0:T(8,128)S(1)}, f32[8,72,128]{2,1,0:T(8,128)S(1)}, u32[]{:S(2)}, u32[]{:S(2)}) collective-permute-start(f32[8,72,128]{2,1,0:T(8,128)S(1)} %all-to-all-done.1.refs_0_.refs_4_), channel_id=1, source_target_pairs={{0,1},{1,2},{2,3},{3,0},{4,5},{5,6},{6,7},{7,4},{8,9},{9,10},{10,1... | collective-permute-start | bytes 884744 | tf_op jit(solution)/shard_map/ppermute | solution.py:27
  93.7 10.8 %copy-start.1 = (f32[8,72,128]{2,1,0:T(8,128)}, f32[8,72,128]{2,1,0:T(8,128)S(1)}, u32[]{:S(2)}) copy-start(f32[8,72,128]{2,1,0:T(8,128)S(1)} %collective-permute-done.5.refs_3_.refs_7_) | copy-start | bytes 884740
  93.7 10.8 %copy-start.3 = (f32[8,72,128]{2,1,0:T(8,128)}, f32[8,72,128]{2,1,0:T(8,128)S(1)}, u32[]{:S(2)}) copy-start(f32[8,72,128]{2,1,0:T(8,128)S(1)} %collective-permute-done.4.refs_2_.refs_6_) | copy-start | bytes 884740
  97.3 7.1 %copy-start.5 = (f32[8,72,128]{2,1,0:T(8,128)}, f32[8,72,128]{2,1,0:T(8,128)S(1)}, u32[]{:S(2)}) copy-start(f32[8,72,128]{2,1,0:T(8,128)S(1)} %collective-permute-done.3.refs_1_.refs_5_) | copy-start | bytes 884740
  107.5 26.5 %collective-permute-start.13 = (f32[8,32,512]{2,1,0:T(8,128)S(1)}, f32[8,32,512]{2,1,0:T(8,128)S(1)}, u32[]{:S(2)}, u32[]{:S(2)}) collective-permute-start(f32[8,32,512]{2,1,0:T(8,128)S(1)} %get-tuple-element.24), channel_id=1, source_target_pairs={{0,1},{1,2},{2,3},{3,0},{4,5},{5,6},{6,7},{7,4},{8,9},{9,10},{10,1... | collective-permute-start | bytes 1572872 | tf_op jit(solution)/shard_map/ppermute | solution.py:27
  107.6 26.4 %collective-permute-start.15 = (f32[8,32,512]{2,1,0:T(8,128)S(1)}, f32[8,32,512]{2,1,0:T(8,128)S(1)}, u32[]{:S(2)}, u32[]{:S(2)}) collective-permute-start(f32[8,32,512]{2,1,0:T(8,128)S(1)} %get-tuple-element.26), channel_id=1, source_target_pairs={{0,3},{1,0},{2,1},{3,2},{4,7},{5,4},{6,5},{7,6},{8,11},{9,8},{10,9... | collective-permute-start | bytes 1572872 | tf_op jit(solution)/shard_map/ppermute | solution.py:27
  110.8 23.2 %collective-permute-start.14 = (f32[8,32,512]{2,1,0:T(8,128)S(1)}, f32[8,32,512]{2,1,0:T(8,128)S(1)}, u32[]{:S(2)}, u32[]{:S(2)}) collective-permute-start(f32[8,32,512]{2,1,0:T(8,128)S(1)} %get-tuple-element.25), channel_id=1, source_target_pairs={{0,2},{1,3},{2,0},{3,1},{4,6},{5,7},{6,4},{7,5},{8,10},{9,11},{10,... | collective-permute-start | bytes 1572872 | tf_op jit(solution)/shard_map/ppermute | solution.py:27
  113.8 38.7 %copy-start.2 = (f32[8,72,128]{2,1,0:T(8,128)S(1)}, f32[8,72,128]{2,1,0:T(8,128)}, u32[]{:S(2)}) copy-start(f32[8,72,128]{2,1,0:T(8,128)} %copy-done.1) | copy-start | bytes 884740
  113.8 38.7 %copy-start.4 = (f32[8,72,128]{2,1,0:T(8,128)S(1)}, f32[8,72,128]{2,1,0:T(8,128)}, u32[]{:S(2)}) copy-start(f32[8,72,128]{2,1,0:T(8,128)} %copy-done.3) | copy-start | bytes 884740
  113.8 38.7 %copy-start.6 = (f32[8,72,128]{2,1,0:T(8,128)S(1)}, f32[8,72,128]{2,1,0:T(8,128)}, u32[]{:S(2)}) copy-start(f32[8,72,128]{2,1,0:T(8,128)} %copy-done.5) | copy-start | bytes 884740
  113.8 38.7 %copy-start.9 = (f32[32,128]{1,0:T(8,128)S(1)}, f32[32,128]{1,0:T(8,128)}, u32[]{:S(2)}) copy-start(f32[32,128]{1,0:T(8,128)} %eig_ref.1) | copy-start | bytes 49156
  136.1 25.4 %all-to-all-start.3 = ((f32[8,32,512]{2,1,0:T(8,128)}), f32[8,32,512]{2,1,0:T(8,128)S(1)}, u32[]{:S(2)}, u32[]{:S(2)}) async-start(f32[8,32,512]{2,1,0:T(8,128)} %add_add_fusion), calls=%async_computation.3 | async-start | bytes 1048576 | tf_op jit(solution)/shard_map/all_to_all | solution.py:22
  144.1 5.2 %collective-permute-start.16 = (f32[4,8,256]{2,1,0:T(8,128)S(1)}, f32[4,8,256]{2,1,0:T(8,128)S(1)}, u32[]{:S(2)}, u32[]{:S(2)}) collective-permute-start(f32[4,8,256]{2,1,0:T(8,128)S(1)} %get-tuple-element.28), channel_id=1, source_target_pairs={{0,1},{1,2},{2,3},{3,0},{4,5},{5,6},{6,7},{7,4},{8,9},{9,10},{10,1... | collective-permute-start | bytes 98312 | tf_op jit(solution)/shard_map/ppermute | solution.py:27
  145.0 5.8 %collective-permute-start.17 = (f32[4,8,256]{2,1,0:T(8,128)S(1)}, f32[4,8,256]{2,1,0:T(8,128)S(1)}, u32[]{:S(2)}, u32[]{:S(2)}) collective-permute-start(f32[4,8,256]{2,1,0:T(8,128)S(1)} %get-tuple-element.29), channel_id=1, source_target_pairs={{0,2},{1,3},{2,0},{3,1},{4,6},{5,7},{6,4},{7,5},{8,10},{9,11},{10,... | collective-permute-start | bytes 98312 | tf_op jit(solution)/shard_map/ppermute | solution.py:27
  148.6 3.9 %collective-permute-start.18 = (f32[4,8,256]{2,1,0:T(8,128)S(1)}, f32[4,8,256]{2,1,0:T(8,128)S(1)}, u32[]{:S(2)}, u32[]{:S(2)}) collective-permute-start(f32[4,8,256]{2,1,0:T(8,128)S(1)} %get-tuple-element.30), channel_id=1, source_target_pairs={{0,3},{1,0},{2,1},{3,2},{4,7},{5,4},{6,5},{7,6},{8,11},{9,8},{10,9... | collective-permute-start | bytes 98312 | tf_op jit(solution)/shard_map/ppermute | solution.py:27
  153.0 5.0 %collective-permute-start.21 = (f32[32,8,128]{2,1,0:T(8,128)S(1)}, f32[32,8,128]{2,1,0:T(8,128)S(1)}, u32[]{:S(2)}, u32[]{:S(2)}) collective-permute-start(f32[32,8,128]{2,1,0:T(8,128)S(1)} %shard_map.90.refs_0_), channel_id=1, source_target_pairs={{0,192},{64,0},{128,64},{192,128},{1,193},{65,1},{129,65},{193,129... | collective-permute-start | bytes 393224 | tf_op jit(solution)/shard_map/ppermute | solution.py:27
  153.8 6.5 %collective-permute-start.20 = (f32[32,8,128]{2,1,0:T(8,128)S(1)}, f32[32,8,128]{2,1,0:T(8,128)S(1)}, u32[]{:S(2)}, u32[]{:S(2)}) collective-permute-start(f32[32,8,128]{2,1,0:T(8,128)S(1)} %shard_map.90.refs_0_), channel_id=1, source_target_pairs={{0,128},{64,192},{128,0},{192,64},{1,129},{65,193},{129,1},{193,65... | collective-permute-start | bytes 393224 | tf_op jit(solution)/shard_map/ppermute | solution.py:27
  155.9 5.6 %collective-permute-start.19 = (f32[32,8,128]{2,1,0:T(8,128)S(1)}, f32[32,8,128]{2,1,0:T(8,128)S(1)}, u32[]{:S(2)}, u32[]{:S(2)}) collective-permute-start(f32[32,8,128]{2,1,0:T(8,128)S(1)} %shard_map.90.refs_0_), channel_id=1, source_target_pairs={{0,64},{64,128},{128,192},{192,0},{1,65},{65,129},{129,193},{193,1... | collective-permute-start | bytes 393224 | tf_op jit(solution)/shard_map/ppermute | solution.py:27
  157.4 4.0 %collective-permute-start.22 = (f32[32,8,128]{2,1,0:T(8,128)S(1)}, f32[32,8,128]{2,1,0:T(8,128)S(1)}, u32[]{:S(2)}, u32[]{:S(2)}) collective-permute-start(f32[32,8,128]{2,1,0:T(8,128)S(1)} %shard_map.90.refs_0_), channel_id=1, source_target_pairs={{0,32},{32,0},{1,33},{33,1},{2,34},{34,2},{3,35},{35,3},{4,36},{36... | collective-permute-start | bytes 393224 | tf_op jit(solution)/shard_map/ppermute | solution.py:27
  158.0 3.5 %collective-permute-start.25 = (f32[32,8,128]{2,1,0:T(8,128)S(1)}, f32[32,8,128]{2,1,0:T(8,128)S(1)}, u32[]{:S(2)}, u32[]{:S(2)}) collective-permute-start(f32[32,8,128]{2,1,0:T(8,128)S(1)} %collective-permute-done.21.refs_3_), channel_id=1, source_target_pairs={{0,32},{32,0},{1,33},{33,1},{2,34},{34,2},{3,35},{35,3},{4,36},{36... | collective-permute-start | bytes 393224 | tf_op jit(solution)/shard_map/ppermute | solution.py:27
  160.3 1.3 collective-permute-start.24
  161.5 1.3 collective-permute-start.23

commit v4 on v3

--- a/solution.py
+++ b/solution.py
@@ -16,6 +16,7 @@
 VMEM = pl.BlockSpec(memory_space=pltpu.VMEM)
 HELD = pl.BlockSpec(memory_space=pltpu.VMEM)
 SMEM = pl.BlockSpec(memory_space=pltpu.SMEM)
+ANY = pl.BlockSpec(memory_space=pl.ANY)
 
 
 def exchange(blocks, axis):
@@ -27,9 +28,9 @@
     return lax.ppermute(shard, axis, [(i, (i + hops) % n) for i in range(n)])
 
 
-def call(kernel, outs, in_specs, me, *, args, grid=1, scratch=(), held=True):
+def call(kernel, outs, in_specs, me, *, args, grid=1, scratch=(), held=True, out_spec=VMEM):
     out_shape = [(pltpu.VMEM if held else pltpu.HBM)(*o) for o in outs]
-    spaces = [pltpu.VMEM if spec is HELD else None if spec.block_shape is None else pltpu.HBM for spec in in_specs]
+    spaces = [pltpu.VMEM if spec is HELD else None if spec is SMEM else pltpu.HBM for spec in in_specs]
     args = [a if space is None else pltpu.with_memory_space_constraint(a, space) for a, space in zip(args, spaces)]
     return pl.pallas_call(
         kernel,
@@ -38,7 +39,7 @@
             num_scalar_prefetch=1,
             grid=(grid,),
             in_specs=in_specs,
-            out_specs=[VMEM] * len(out_shape),
+            out_specs=[out_spec] * len(out_shape),
             scratch_shapes=list(scratch),
         ),
         compiler_params=pltpu.CompilerParams(vmem_limit_bytes=28 << 20),
@@ -78,12 +79,17 @@
         out_ref[:, 64:, :] = (dot_nt(query, high) + dot_nt(query, low)).reshape(8, 8, 128)
 
 
-def basis_pick_kernel(me_ref, basis_ref, out_ref):
-    _, core, _, _ = place(me_ref)
+def basis_pick_kernel(me_ref, basis_ref, out_ref, sems):
+    y, core, _, _ = place(me_ref)
     cols = basis_ref.shape[1] // 32
+    rows = pl.ds(pl.multiple_of(8 * y, 8), 8)
+    copies = []
     for f in range(32):
         start = pl.multiple_of(f * cols + core * (cols - HALF), 128)
-        out_ref[f] = basis_ref[:, pl.ds(start, HALF)]
+        copies.append(pltpu.make_async_copy(basis_ref.at[rows, pl.ds(start, HALF)], out_ref.at[f], sems.at[f]))
+        copies[-1].start()
+    for copy in copies:
+        copy.wait()
 
 
 def query_kernel(own, me_ref, grads_ref, *refs):
@@ -108,23 +114,15 @@
         out_ref[:, :, slot] = total if own else so_far[:, :, slot] + total
 
 
-def query_sum_kernel(me_ref, blocks_ref, *out_refs):
-    _, _, _, x = place(me_ref)
-    for k, out_ref in enumerate(out_refs):
-        target = lax.rem(x + k, 4)
-        total = blocks_ref[0, target]
-        for sender in range(1, 8):
-            total = total + blocks_ref[sender, target]
-        out_ref[...] = total
-
-
 def precond_kernel(me_ref, eig_ref, *refs):
-    parts, blocks, out_ref, rot_in_ref = refs[:4], refs[4:8], refs[8], refs[9]
+    parts_ref, blocks, out_ref, rot_in_ref = refs[0], refs[1:5], refs[5], refs[6]
     y, _, _, x = place(me_ref)
     for k in range(4):
         source = lax.rem(x + 4 - k, 4)
         rot_in_ref[pl.ds(pl.multiple_of(source * 64, 64), 64), :] = blocks[k][:, 64:, :].reshape(64, 128)
-    rot = parts[0][...] + parts[1][...] + parts[2][...] + parts[3][...]
+    rot = parts_ref[0]
+    for sender in range(1, 32):
+        rot = rot + parts_ref[sender]
     rot = rot.reshape(32, rot.shape[-1])
     lane_query = lax.broadcasted_iota(jnp.int32, rot.shape, 1) // QLEN
     count = rot.shape[1] // QLEN
@@ -266,8 +264,9 @@
     (picked,) = call(
         basis_pick_kernel,
         [((32, 8, HALF), f32)],
-        [pl.BlockSpec((8, output_basis.shape[1]), lambda i, me: (me[0] // 64, 0))],
-        me, args=(output_basis,), held=False,
+        [ANY],
+        me, args=(output_basis,), held=False, out_spec=ANY,
+        scratch=[pltpu.SemaphoreType.DMA((32,))],
     )
     slab = exchange(picked, ZX).reshape(8, 4, 8, HALF)
     slabs = [slab]
@@ -279,21 +278,19 @@
     query_call = functools.partial(
         call, outs=[((8, 4, 4, 8, queries), f32)], me=me, scratch=[pltpu.VMEM((queries, HALF), bf16)]
     )
-    (rot,) = query_call(functools.partial(query_kernel, True), in_specs=[VMEM] + [HELD] * 4, args=(query_grads, *slabs[:4]))
+    (rot,) = query_call(functools.partial(query_kernel, True), in_specs=[VMEM] + [HELD] * 4, args=(query_grads, *slabs[:4]), held=False)
     (rot,) = query_call(
         functools.partial(query_kernel, False),
-        in_specs=[VMEM] + [HELD] * 5,
+        in_specs=[VMEM] * 2 + [HELD] * 4,
         args=(query_grads, rot, *slabs[4:]),
         held=False,
     )
-    rot = exchange(rot, "z")
-    rots = call(query_sum_kernel, [((4, 8, queries), f32)] * 4, [HELD], me, args=(rot,))
-    rots = [rots[0]] + [shifted(rots[k], "x", k) for k in (1, 2, 3)]
+    rot = exchange(rot.reshape(32, 4, 8, queries), ZX)
     (precond,) = call(
         precond_kernel,
         [((32, 8, 128), f32)],
-        [VMEM] + [HELD] * 8,
-        me, args=(eigenvalues, *rots, *blocks),
+        [VMEM] + [HELD] * 5,
+        me, args=(eigenvalues, rot, *blocks),
         scratch=[pltpu.VMEM((queries, 128), f32)],
     )
     preconds = [precond]

time: 185 us -> 207 us (1.12)
  Pallas kernels: 22.8 us -> 40.8 us
  waiting for transfers between devices: 75.5 us -> 82.4 us
  starting transfers between devices: 60 us -> 55.8 us
    pallas_call x10 -> x9, Pallas kernels: 22.8 us -> 40.8 us  [call(): pl.pallas_call(kernel, out_shape=out_shape, grid_spec=pltpu.PrefetchScala...]
    ppermute x26 -> x23, waiting for transfers between devices: 57.7 us -> 63.3 us  [shifted(): return lax.ppermute(shard, axis, [(i, (i + hops) % n) for i in range(n)])]
    ppermute x26 -> x23, starting transfers between devices: 27.5 us -> 23.7 us  [shifted(): return lax.ppermute(shard, axis, [(i, (i + hops) % n) for i in range(n)])]
  transfers between devices with their start and end apart: 31 -> 28, of which waited for: 17 -> 13; matrix products, arithmetic and copies ran while one was open for 2% -> 2% of each run, Pallas kernels for 11% -> 11%
where the time goes in v4:
time: 207 us; the launch traced here: 205 us
  waiting for transfers between devices  82.4 us (40%)
  starting transfers between devices  55.8 us (27%)
  Pallas kernels  40.8 us (20%)
  blocking collectives  18.3 us (9%)
  local copies, waits for them, and re-layouts  4.27 us (2%)
  other arithmetic  2.99 us (1%)
    ppermute x23, waiting for transfers between devices, shifted(): return lax.ppermute(shard, axis, [(i, (i + hops) % n) for i in range(n)])  63.3 us
    pallas_call x9, Pallas kernels, call(): pl.pallas_call(kernel, out_shape=out_shape, grid_spec=pltpu.PrefetchScala...  40.8 us
    all_to_all x5, starting transfers between devices, exchange(): return lax.all_to_all(blocks, axis, 0, 0, tiled=True)  32.1 us
    ppermute x23, starting transfers between devices, shifted(): return lax.ppermute(shard, axis, [(i, (i + hops) % n) for i in range(n)])  23.7 us
    all_to_all x5, waiting for transfers between devices, exchange(): return lax.all_to_all(blocks, axis, 0, 0, tiled=True)  19.1 us
    all_to_all x1, blocking collectives, exchange(): return lax.all_to_all(blocks, axis, 0, 0, tiled=True)  18.3 us
  transfers between devices with their start and end apart: 28, of which 13 were waited for; matrix products, arithmetic and copies ran while one was open for 2% of the time, Pallas kernels for 11%

profile of v4, /device:TPU:8, one launch (start us, length us, event | category | flops | bytes accessed | tf_op | source)
XLA Modules:
  0.0 204.7 jit_solution(2696727401791003228)
XLA Ops:
  0.0 17.3 %shard_map.83 = f32[32,8,512]{2,1,0:T(8,128)} custom-call(s32[1]{0:T(128)} %bitcast.me_ref, f32[32,28672]{1,0:T(8,128)} %basis_ref.3), custom_call_target="tpu_custom_call" | custom-call | tf_op jit(solution)/shard_map/pallas_call | solution.py:35
  17.3 11.3 %all-to-all-start.2 = ((f32[32,8,512]{2,1,0:T(8,128)}), f32[32,8,512]{2,1,0:T(8,128)S(1)}, u32[]{:S(2)}, u32[]{:S(2)}) async-start(f32[32,8,512]{2,1,0:T(8,128)} %shard_map.83), calls=%async_computation.2 | async-start | bytes 1048576 | tf_op jit(solution)/shard_map/all_to_all | solution.py:23
  28.6 2.2 %shard_map.82 = (f32[8,72,128]{2,1,0:T(8,128)S(1)}, f32[8,72,128]{2,1,0:T(8,128)S(1)}, f32[8,72,128]{2,1,0:T(8,128)S(1)}, f32[8,72,128]{2,1,0:T(8,128)S(1)}) custom-call(s32[1]{0:T(128)} %bitcast.me_ref, bf16[2048,256]{1,0:T(8,128)(2,1)} %acts_ref.1, bf16[256,256]{1,0:T(8,128)(2,1)} %query_ref.1, f32[128,8192]{1,0:T(8,128)} %basis_ref.2), custom_call_target="tpu_custom_call" | custom-call | tf_op jit(solution)/shard_map/pallas_call | solution.py:35
  30.8 3.4 %collective-permute-start = (f32[8,72,128]{2,1,0:T(8,128)S(1)}, f32[8,72,128]{2,1,0:T(8,128)S(1)}, u32[]{:S(2)}, u32[]{:S(2)}) collective-permute-start(f32[8,72,128]{2,1,0:T(8,128)S(1)} %get-tuple-element.15), channel_id=1, source_target_pairs={{0,2},{1,3},{2,0},{3,1},{4,6},{5,7},{6,4},{7,5},{8,10},{9,11},{10,... | collective-permute-start | bytes 884744 | tf_op jit(solution)/shard_map/ppermute | solution.py:28
  34.2 0.6 collective-permute-start.1
  34.7 2.7 %collective-permute-start.2 = (f32[8,72,128]{2,1,0:T(8,128)S(1)}, f32[8,72,128]{2,1,0:T(8,128)S(1)}, u32[]{:S(2)}, u32[]{:S(2)}) collective-permute-start(f32[8,72,128]{2,1,0:T(8,128)S(1)} %get-tuple-element.17), channel_id=1, source_target_pairs={{0,3},{1,0},{2,1},{3,2},{4,7},{5,4},{6,5},{7,6},{8,11},{9,8},{10,9... | collective-permute-start | bytes 884744 | tf_op jit(solution)/shard_map/ppermute | solution.py:28
  37.4 9.0 %all-to-all-done.2 = f32[32,8,512]{2,1,0:T(8,128)S(1)} async-done(((f32[32,8,512]{2,1,0:T(8,128)}), f32[32,8,512]{2,1,0:T(8,128)S(1)}, u32[]{:S(2)}, u32[]{:S(2)}) %all-to-all-start.2) | async-done | bytes 524320 | tf_op jit(solution)/shard_map/all_to_all | solution.py:23
  46.4 1.6 collective-permute-start.8
  48.0 0.9 collective-permute-start.7
  49.0 2.4 %collective-permute-start.6 = (f32[8,4,8,512]{3,2,1,0:T(8,128)S(1)}, f32[8,4,8,512]{3,2,1,0:T(8,128)}, u32[]{:S(2)}, u32[]{:S(2)}) collective-permute-start(f32[8,4,8,512]{3,2,1,0:T(8,128)S(1)} %bitcast.5), channel_id=1, source_target_pairs={{0,192},{64,0},{128,64},{192,128},{1,193},{65,1},{129,65},{193,129... | collective-permute-start | bytes 1572872 | tf_op jit(solution)/shard_map/ppermute | solution.py:28
  51.4 0.7 collective-permute-done.1
  52.1 0.8 add_add_fusion.1
  52.8 5.8 %all-to-all-start = ((f32[8,72,128]{2,1,0:T(8,128)}), f32[8,72,128]{2,1,0:T(8,128)S(1)}, u32[]{:S(2)}, u32[]{:S(2)}) async-start(f32[8,72,128]{2,1,0:T(8,128)} %add_add_fusion.1), calls=%async_computation | async-start | bytes 589824 | tf_op jit(solution)/shard_map/all_to_all | solution.py:23
  58.7 2.6 %collective-permute-done.8.refs_7_.refs_3_ = f32[8,4,8,512]{3,2,1,0:T(8,128)S(1)} collective-permute-done((f32[8,4,8,512]{3,2,1,0:T(8,128)S(1)}, f32[8,4,8,512]{3,2,1,0:T(8,128)S(1)}, u32[]{:S(2)}, u32[]{:S(2)}) %collective-permute-start.8) | collective-permute-done | bytes 524320 | tf_op jit(solution)/shard_map/ppermute | solution.py:28
  61.2 3.2 %collective-permute-done.7.refs_6_.refs_2_ = f32[8,4,8,512]{3,2,1,0:T(8,128)} collective-permute-done((f32[8,4,8,512]{3,2,1,0:T(8,128)S(1)}, f32[8,4,8,512]{3,2,1,0:T(8,128)}, u32[]{:S(2)}, u32[]{:S(2)}) %collective-permute-start.7) | collective-permute-done | bytes 524320 | tf_op jit(solution)/shard_map/ppermute | solution.py:28
  64.4 7.3 %collective-permute-done.6.refs_5_.refs_1_ = f32[8,4,8,512]{3,2,1,0:T(8,128)} collective-permute-done((f32[8,4,8,512]{3,2,1,0:T(8,128)S(1)}, f32[8,4,8,512]{3,2,1,0:T(8,128)}, u32[]{:S(2)}, u32[]{:S(2)}) %collective-permute-start.6) | collective-permute-done | bytes 524320 | tf_op jit(solution)/shard_map/ppermute | solution.py:28
  71.8 0.7 broadcast_in_dim.2
  72.5 4.1 %all-to-all-start.1 = ((f32[8,72,128]{2,1,0:T(8,128)}), f32[8,72,128]{2,1,0:T(8,128)S(1)}, u32[]{:S(2)}, u32[]{:S(2)}) async-start(f32[8,72,128]{2,1,0:T(8,128)} %broadcast_in_dim.2), calls=%async_computation.1 | async-start | bytes 589824 | tf_op jit(solution)/shard_map/all_to_all | solution.py:23
  76.6 3.1 %shard_map.87.refs_0_ = f32[8,4,4,8,256]{4,3,2,1,0:T(8,128)} custom-call(s32[1]{0:T(128)} %bitcast.me_ref, bf16[256,896]{1,0:T(8,128)(2,1)} %grads_ref.5, f32[8,4,8,512]{3,2,1,0:T(8,128)S(1)} %bitcast.7, f32[8,4,8,512]{3,2,1,0:T(8,128)} %collective-permute-done.6.refs_5_.refs_1_, f32[8,4,8,512]{3,2,1,0:T(8,128)} %collective-permute-done.7.refs_6_.refs_2_, ...), custom_call_target="tpu_custom_call" | custom-call | tf_op jit(solution)/shard_map/pallas_call | solution.py:35
  79.7 3.1 %shard_map.88 = f32[8,4,4,8,256]{4,3,2,1,0:T(8,128)} custom-call(s32[1]{0:T(128)} %bitcast.me_ref, bf16[256,896]{1,0:T(8,128)(2,1)} %grads_ref.5, f32[8,4,4,8,256]{4,3,2,1,0:T(8,128)} %shard_map.87.refs_0_, f32[8,4,8,512]{3,2,1,0:T(8,128)S(1)} %collective-permute-done.9.refs_8_.refs_4_.refs_1_, ...), custom_call_target="tpu_custom_call" | custom-call | tf_op jit(solution)/shard_map/pallas_call | solution.py:35
  82.8 7.0 %all-to-all-done.1.refs_0_.refs_1_ = f32[8,72,128]{2,1,0:T(8,128)S(1)} async-done(((f32[8,72,128]{2,1,0:T(8,128)}), f32[8,72,128]{2,1,0:T(8,128)S(1)}, u32[]{:S(2)}, u32[]{:S(2)}) %all-to-all-start.1) | async-done | bytes 294944 | tf_op jit(solution)/shard_map/all_to_all | solution.py:23
  89.8 4.7 %all-to-all-start.4 = ((f32[32,4,8,256]{3,2,1,0:T(8,128)}), f32[32,4,8,256]{3,2,1,0:T(8,128)}, u32[]{:S(2)}, u32[]{:S(2)}) async-start(f32[32,4,8,256]{3,2,1,0:T(8,128)} %bitcast.11), calls=%async_computation.4 | async-start | bytes 2097152 | tf_op jit(solution)/shard_map/all_to_all | solution.py:23
  94.5 2.9 %collective-permute-start.5 = (f32[8,72,128]{2,1,0:T(8,128)S(1)}, f32[8,72,128]{2,1,0:T(8,128)S(1)}, u32[]{:S(2)}, u32[]{:S(2)}) collective-permute-start(f32[8,72,128]{2,1,0:T(8,128)S(1)} %all-to-all-done.1.refs_0_.refs_1_), channel_id=1, source_target_pairs={{0,3},{1,0},{2,1},{3,2},{4,7},{5,4},{6,5},{7,6},{8,11},{9,8},{10,9... | collective-permute-start | bytes 884744 | tf_op jit(solution)/shard_map/ppermute | solution.py:28
  97.4 0.8 collective-permute-start.4
  98.2 0.9 collective-permute-start.3
  99.1 20.4 %collective-permute-done.5.refs_3_.refs_4_ = f32[8,72,128]{2,1,0:T(8,128)S(1)} collective-permute-done((f32[8,72,128]{2,1,0:T(8,128)S(1)}, f32[8,72,128]{2,1,0:T(8,128)S(1)}, u32[]{:S(2)}, u32[]{:S(2)}) %collective-permute-start.5) | collective-permute-done | bytes 294944 | tf_op jit(solution)/shard_map/ppermute | solution.py:28
  119.5 4.0 %collective-permute-done.3.refs_1_.refs_2_ = f32[8,72,128]{2,1,0:T(8,128)S(1)} collective-permute-done((f32[8,72,128]{2,1,0:T(8,128)S(1)}, f32[8,72,128]{2,1,0:T(8,128)S(1)}, u32[]{:S(2)}, u32[]{:S(2)}) %collective-permute-start.3) | collective-permute-done | bytes 294944 | tf_op jit(solution)/shard_map/ppermute | solution.py:28
  123.4 7.1 %shard_map.84 = (f32[8,32,512]{2,1,0:T(8,128)S(1)}, bf16[2,512,512]{2,1,0:T(8,128)(2,1)S(1)}, bf16[2,512,512]{2,1,0:T(8,128)(2,1)S(1)}) custom-call(s32[1]{0:T(128)} %bitcast.me_ref, s32[4]{0:T(128)S(1)} %copy-done.6, bf16[2048,896]{1,0:T(8,128)(2,1)} %grads_ref.3, f32[8,72,128]{2,1,0:T(8,128)S(1)} %all-to-all-done.1.refs_0_.refs_1_, ...), custom_call_target="tpu_custom_call" | custom-call | tf_op jit(solution)/shard_map/pallas_call | solution.py:35
  130.6 3.0 %shard_map.86 = (f32[8,32,512]{2,1,0:T(8,128)S(1)}, f32[8,32,512]{2,1,0:T(8,128)S(1)}) custom-call(s32[1]{0:T(128)} %bitcast.me_ref, bf16[2,512,512]{2,1,0:T(8,128)(2,1)S(1)} %get-tuple-element.18.high_ref, bf16[2,512,512]{2,1,0:T(8,128)(2,1)S(1)} %get-tuple-element.19.low_ref, f32[8,4,8,512]{3,2,1,0:T(8,128)S(1)} %bitcast.9, ...), custom_call_target="tpu_custom_call" | custom-call | tf_op jit(solution)/shard_map/pallas_call | solution.py:35
  133.7 3.2 %collective-permute-start.15 = (f32[8,32,512]{2,1,0:T(8,128)S(1)}, f32[8,32,512]{2,1,0:T(8,128)S(1)}, u32[]{:S(2)}, u32[]{:S(2)}) collective-permute-start(f32[8,32,512]{2,1,0:T(8,128)S(1)} %get-tuple-element.22), channel_id=1, source_target_pairs={{0,3},{1,0},{2,1},{3,2},{4,7},{5,4},{6,5},{7,6},{8,11},{9,8},{10,9... | collective-permute-start | bytes 1572872 | tf_op jit(solution)/shard_map/ppermute | solution.py:28
  136.9 3.0 %shard_map.85 = f32[8,32,512]{2,1,0:T(8,128)} custom-call(s32[1]{0:T(128)} %bitcast.me_ref, bf16[2,512,512]{2,1,0:T(8,128)(2,1)S(1)} %get-tuple-element.18.high_ref, bf16[2,512,512]{2,1,0:T(8,128)(2,1)S(1)} %get-tuple-element.19.low_ref, f32[8,4,8,512]{3,2,1,0:T(8,128)S(1)} %bitcast.10, f32[8,4,8,512]{3,2,1,0:T(8,128)} %collective-permute-done.6.refs_5_.refs_1_, ...), custom_call_target="tpu_custom_call" | custom-call | tf_op jit(solution)/shard_map/pallas_call | solution.py:35
  139.9 20.2 %collective-permute-done.13 = f32[8,32,512]{2,1,0:T(8,128)S(1)} collective-permute-done((f32[8,32,512]{2,1,0:T(8,128)S(1)}, f32[8,32,512]{2,1,0:T(8,128)S(1)}, u32[]{:S(2)}, u32[]{:S(2)}) %collective-permute-start.13) | collective-permute-done | bytes 524320 | tf_op jit(solution)/shard_map/ppermute | solution.py:28
  160.1 2.1 %add_add_fusion = f32[8,32,512]{2,1,0:T(8,128)} fusion(f32[8,32,512]{2,1,0:T(8,128)S(1)} %collective-permute-done.15, f32[8,32,512]{2,1,0:T(8,128)S(1)} %collective-permute-done.14, f32[8,32,512]{2,1,0:T(8,128)} %shard_map.85, f32[8,32,512]{2,1,0:T(8,128)S(1)} %collective-permute-done.13), kind=kLoop, calls=%fused_computation | loop fusion | flops 393216 | bytes 2621440 | tf_op jit(solution)/shard_map/add | solution.py:325
  162.2 6.2 %all-to-all-start.3 = ((f32[8,32,512]{2,1,0:T(8,128)}), f32[8,32,512]{2,1,0:T(8,128)S(1)}, u32[]{:S(2)}, u32[]{:S(2)}) async-start(f32[8,32,512]{2,1,0:T(8,128)} %add_add_fusion), calls=%async_computation.3 | async-start | bytes 1048576 | tf_op jit(solution)/shard_map/all_to_all | solution.py:23
  168.3 1.0 copy-done.1
  169.3 1.0 copy-done.3
  170.3 1.0 copy-done.5
  171.2 1.7 shard_map.89.refs_0_
  172.9 0.6 collective-permute-start.18
  173.5 2.1 %collective-permute-start.17 = (f32[32,8,128]{2,1,0:T(8,128)S(1)}, f32[32,8,128]{2,1,0:T(8,128)S(1)}, u32[]{:S(2)}, u32[]{:S(2)}) collective-permute-start(f32[32,8,128]{2,1,0:T(8,128)S(1)} %shard_map.89.refs_0_), channel_id=1, source_target_pairs={{0,128},{64,192},{128,0},{192,64},{1,129},{65,193},{129,1},{193,65... | collective-permute-start | bytes 393224 | tf_op jit(solution)/shard_map/ppermute | solution.py:28
  175.6 1.5 collective-permute-start.16
  177.1 2.2 %collective-permute-done.18.refs_3_ = f32[32,8,128]{2,1,0:T(8,128)S(1)} collective-permute-done((f32[32,8,128]{2,1,0:T(8,128)S(1)}, f32[32,8,128]{2,1,0:T(8,128)S(1)}, u32[]{:S(2)}, u32[]{:S(2)}) %collective-permute-start.18) | collective-permute-done | bytes 131104 | tf_op jit(solution)/shard_map/ppermute | solution.py:28
  179.4 1.4 collective-permute-done.17.refs_2_
  180.8 1.4 collective-permute-done.16.refs_1_
  182.2 3.1 %all-to-all-done.3.blocks_ref = f32[8,32,512]{2,1,0:T(8,128)S(1)} async-done(((f32[8,32,512]{2,1,0:T(8,128)}), f32[8,32,512]{2,1,0:T(8,128)S(1)}, u32[]{:S(2)}, u32[]{:S(2)}) %all-to-all-start.3) | async-done | bytes 524320 | tf_op jit(solution)/shard_map/all_to_all | solution.py:23
  185.3 0.4 shard_map.90
  185.7 18.3 %all_to_all.30 = f32[32,8,128]{2,1,0:T(8,128)S(1)} all-to-all(f32[32,8,128]{2,1,0:T(8,128)S(1)} %shard_map.90), channel_id=1, replica_groups=mesh['y'=4,'core'=2,'z'=8,'x'=4] {'z','x'}, dimensions={0} | all-to-all | bytes 262144 | tf_op jit(solution)/shard_map/all_to_all | solution.py:23
  204.1 0.6 reshape.16
  (38 shorter events, 0.3 us)
Async XLA Ops:
  17.3 29.2 %all-to-all-start.2 = ((f32[32,8,512]{2,1,0:T(8,128)}), f32[32,8,512]{2,1,0:T(8,128)S(1)}, u32[]{:S(2)}, u32[]{:S(2)}) async-start(f32[32,8,512]{2,1,0:T(8,128)} %shard_map.83), calls=%async_computation.2 | async-start | bytes 1048576 | tf_op jit(solution)/shard_map/all_to_all | solution.py:23
  30.8 18.2 %collective-permute-start = (f32[8,72,128]{2,1,0:T(8,128)S(1)}, f32[8,72,128]{2,1,0:T(8,128)S(1)}, u32[]{:S(2)}, u32[]{:S(2)}) collective-permute-start(f32[8,72,128]{2,1,0:T(8,128)S(1)} %get-tuple-element.15), channel_id=1, source_target_pairs={{0,2},{1,3},{2,0},{3,1},{4,6},{5,7},{6,4},{7,5},{8,10},{9,11},{10,... | collective-permute-start | bytes 884744 | tf_op jit(solution)/shard_map/ppermute | solution.py:28
  34.2 17.9 %collective-permute-start.1 = (f32[8,72,128]{2,1,0:T(8,128)S(1)}, f32[8,72,128]{2,1,0:T(8,128)S(1)}, u32[]{:S(2)}, u32[]{:S(2)}) collective-permute-start(f32[8,72,128]{2,1,0:T(8,128)S(1)} %get-tuple-element.16), channel_id=1, source_target_pairs={{0,1},{1,2},{2,3},{3,0},{4,5},{5,6},{6,7},{7,4},{8,9},{9,10},{10,1... | collective-permute-start | bytes 884744 | tf_op jit(solution)/shard_map/ppermute | solution.py:28
  34.7 17.3 %collective-permute-start.2 = (f32[8,72,128]{2,1,0:T(8,128)S(1)}, f32[8,72,128]{2,1,0:T(8,128)S(1)}, u32[]{:S(2)}, u32[]{:S(2)}) collective-permute-start(f32[8,72,128]{2,1,0:T(8,128)S(1)} %get-tuple-element.17), channel_id=1, source_target_pairs={{0,3},{1,0},{2,1},{3,2},{4,7},{5,4},{6,5},{7,6},{8,11},{9,8},{10,9... | collective-permute-start | bytes 884744 | tf_op jit(solution)/shard_map/ppermute | solution.py:28
  46.4 14.8 %collective-permute-start.8 = (f32[8,4,8,512]{3,2,1,0:T(8,128)S(1)}, f32[8,4,8,512]{3,2,1,0:T(8,128)S(1)}, u32[]{:S(2)}, u32[]{:S(2)}) collective-permute-start(f32[8,4,8,512]{3,2,1,0:T(8,128)S(1)} %bitcast.3), channel_id=1, source_target_pairs={{0,64},{64,128},{128,192},{192,0},{1,65},{65,129},{129,193},{193,1... | collective-permute-start | bytes 1572872 | tf_op jit(solution)/shard_map/ppermute | solution.py:28
  48.0 16.4 %collective-permute-start.7 = (f32[8,4,8,512]{3,2,1,0:T(8,128)S(1)}, f32[8,4,8,512]{3,2,1,0:T(8,128)}, u32[]{:S(2)}, u32[]{:S(2)}) collective-permute-start(f32[8,4,8,512]{3,2,1,0:T(8,128)S(1)} %bitcast.4), channel_id=1, source_target_pairs={{0,128},{64,192},{128,0},{192,64},{1,129},{65,193},{129,1},{193,65... | collective-permute-start | bytes 1572872 | tf_op jit(solution)/shard_map/ppermute | solution.py:28
  49.0 22.8 %collective-permute-start.6 = (f32[8,4,8,512]{3,2,1,0:T(8,128)S(1)}, f32[8,4,8,512]{3,2,1,0:T(8,128)}, u32[]{:S(2)}, u32[]{:S(2)}) collective-permute-start(f32[8,4,8,512]{3,2,1,0:T(8,128)S(1)} %bitcast.5), channel_id=1, source_target_pairs={{0,192},{64,0},{128,64},{192,128},{1,193},{65,1},{129,65},{193,129... | collective-permute-start | bytes 1572872 | tf_op jit(solution)/shard_map/ppermute | solution.py:28
  52.8 18.9 %all-to-all-start = ((f32[8,72,128]{2,1,0:T(8,128)}), f32[8,72,128]{2,1,0:T(8,128)S(1)}, u32[]{:S(2)}, u32[]{:S(2)}) async-start(f32[8,72,128]{2,1,0:T(8,128)} %add_add_fusion.1), calls=%async_computation | async-start | bytes 589824 | tf_op jit(solution)/shard_map/all_to_all | solution.py:23
  58.7 21.0 %collective-permute-start.9 = (f32[8,4,8,512]{3,2,1,0:T(8,128)S(1)}, f32[8,4,8,512]{3,2,1,0:T(8,128)S(1)}, u32[]{:S(2)}, u32[]{:S(2)}) collective-permute-start(f32[8,4,8,512]{3,2,1,0:T(8,128)S(1)} %bitcast.6), channel_id=1, source_target_pairs={{0,32},{32,0},{1,33},{33,1},{2,34},{34,2},{3,35},{35,3},{4,36},{36... | collective-permute-start | bytes 1572872 | tf_op jit(solution)/shard_map/ppermute | solution.py:28
  61.2 18.4 %collective-permute-start.12 = (f32[8,4,8,512]{3,2,1,0:T(8,128)S(1)}, f32[8,4,8,512]{3,2,1,0:T(8,128)S(1)}, u32[]{:S(2)}, u32[]{:S(2)}) collective-permute-start(f32[8,4,8,512]{3,2,1,0:T(8,128)S(1)} %collective-permute-done.8.refs_7_.refs_3_), channel_id=1, source_target_pairs={{0,32},{32,0},{1,33},{33,1},{2,34},{34,2},{3,35},{35,3},{4,36},{36... | collective-permute-start | bytes 1572872 | tf_op jit(solution)/shard_map/ppermute | solution.py:28
  64.4 15.2 %collective-permute-start.11 = (f32[8,4,8,512]{3,2,1,0:T(8,128)}, f32[8,4,8,512]{3,2,1,0:T(8,128)S(1)}, u32[]{:S(2)}, u32[]{:S(2)}) collective-permute-start(f32[8,4,8,512]{3,2,1,0:T(8,128)} %collective-permute-done.7.refs_6_.refs_2_), channel_id=1, source_target_pairs={{0,32},{32,0},{1,33},{33,1},{2,34},{34,2},{3,35},{35,3},{4,36},{36... | collective-permute-start | bytes 1572872 | tf_op jit(solution)/shard_map/ppermute | solution.py:28
  71.7 8.0 %collective-permute-start.10 = (f32[8,4,8,512]{3,2,1,0:T(8,128)}, f32[8,4,8,512]{3,2,1,0:T(8,128)S(1)}, u32[]{:S(2)}, u32[]{:S(2)}) collective-permute-start(f32[8,4,8,512]{3,2,1,0:T(8,128)} %collective-permute-done.6.refs_5_.refs_1_), channel_id=1, source_target_pairs={{0,32},{32,0},{1,33},{33,1},{2,34},{34,2},{3,35},{35,3},{4,36},{36... | collective-permute-start | bytes 1572872 | tf_op jit(solution)/shard_map/ppermute | solution.py:28
  72.5 17.3 %all-to-all-start.1 = ((f32[8,72,128]{2,1,0:T(8,128)}), f32[8,72,128]{2,1,0:T(8,128)S(1)}, u32[]{:S(2)}, u32[]{:S(2)}) async-start(f32[8,72,128]{2,1,0:T(8,128)} %broadcast_in_dim.2), calls=%async_computation.1 | async-start | bytes 589824 | tf_op jit(solution)/shard_map/all_to_all | solution.py:23
  79.7 43.8 %copy-start.6 = (s32[4]{0:T(128)S(1)}, s32[4]{0:T(128)}, u32[]{:S(2)}) copy-start(s32[4]{0:T(128)} %len_ref.1) | copy-start | bytes 52
  89.8 72.4 %all-to-all-start.4 = ((f32[32,4,8,256]{3,2,1,0:T(8,128)}), f32[32,4,8,256]{3,2,1,0:T(8,128)}, u32[]{:S(2)}, u32[]{:S(2)}) async-start(f32[32,4,8,256]{3,2,1,0:T(8,128)} %bitcast.11), calls=%async_computation.4 | async-start | bytes 2097152 | tf_op jit(solution)/shard_map/all_to_all | solution.py:23
  94.5 25.0 %collective-permute-start.5 = (f32[8,72,128]{2,1,0:T(8,128)S(1)}, f32[8,72,128]{2,1,0:T(8,128)S(1)}, u32[]{:S(2)}, u32[]{:S(2)}) collective-permute-start(f32[8,72,128]{2,1,0:T(8,128)S(1)} %all-to-all-done.1.refs_0_.refs_1_), channel_id=1, source_target_pairs={{0,3},{1,0},{2,1},{3,2},{4,7},{5,4},{6,5},{7,6},{8,11},{9,8},{10,9... | collective-permute-start | bytes 884744 | tf_op jit(solution)/shard_map/ppermute | solution.py:28
  97.4 22.1 %collective-permute-start.4 = (f32[8,72,128]{2,1,0:T(8,128)S(1)}, f32[8,72,128]{2,1,0:T(8,128)S(1)}, u32[]{:S(2)}, u32[]{:S(2)}) collective-permute-start(f32[8,72,128]{2,1,0:T(8,128)S(1)} %all-to-all-done.1.refs_0_.refs_1_), channel_id=1, source_target_pairs={{0,2},{1,3},{2,0},{3,1},{4,6},{5,7},{6,4},{7,5},{8,10},{9,11},{10,... | collective-permute-start | bytes 884744 | tf_op jit(solution)/shard_map/ppermute | solution.py:28
  98.2 25.2 %collective-permute-start.3 = (f32[8,72,128]{2,1,0:T(8,128)S(1)}, f32[8,72,128]{2,1,0:T(8,128)S(1)}, u32[]{:S(2)}, u32[]{:S(2)}) collective-permute-start(f32[8,72,128]{2,1,0:T(8,128)S(1)} %all-to-all-done.1.refs_0_.refs_1_), channel_id=1, source_target_pairs={{0,1},{1,2},{2,3},{3,0},{4,5},{5,6},{6,7},{7,4},{8,9},{9,10},{10,1... | collective-permute-start | bytes 884744 | tf_op jit(solution)/shard_map/ppermute | solution.py:28
  119.5 11.1 %copy-start = (f32[8,72,128]{2,1,0:T(8,128)}, f32[8,72,128]{2,1,0:T(8,128)S(1)}, u32[]{:S(2)}) copy-start(f32[8,72,128]{2,1,0:T(8,128)S(1)} %collective-permute-done.5.refs_3_.refs_4_) | copy-start | bytes 884740
  119.5 11.1 %copy-start.2 = (f32[8,72,128]{2,1,0:T(8,128)}, f32[8,72,128]{2,1,0:T(8,128)S(1)}, u32[]{:S(2)}) copy-start(f32[8,72,128]{2,1,0:T(8,128)S(1)} %collective-permute-done.4.refs_2_.refs_3_) | copy-start | bytes 884740
  123.4 7.1 %copy-start.4 = (f32[8,72,128]{2,1,0:T(8,128)}, f32[8,72,128]{2,1,0:T(8,128)S(1)}, u32[]{:S(2)}) copy-start(f32[8,72,128]{2,1,0:T(8,128)S(1)} %collective-permute-done.3.refs_1_.refs_2_) | copy-start | bytes 884740
  133.6 26.5 %collective-permute-start.13 = (f32[8,32,512]{2,1,0:T(8,128)S(1)}, f32[8,32,512]{2,1,0:T(8,128)S(1)}, u32[]{:S(2)}, u32[]{:S(2)}) collective-permute-start(f32[8,32,512]{2,1,0:T(8,128)S(1)} %get-tuple-element.20), channel_id=1, source_target_pairs={{0,1},{1,2},{2,3},{3,0},{4,5},{5,6},{6,7},{7,4},{8,9},{9,10},{10,1... | collective-permute-start | bytes 1572872 | tf_op jit(solution)/shard_map/ppermute | solution.py:28
  133.7 26.4 %collective-permute-start.15 = (f32[8,32,512]{2,1,0:T(8,128)S(1)}, f32[8,32,512]{2,1,0:T(8,128)S(1)}, u32[]{:S(2)}, u32[]{:S(2)}) collective-permute-start(f32[8,32,512]{2,1,0:T(8,128)S(1)} %get-tuple-element.22), channel_id=1, source_target_pairs={{0,3},{1,0},{2,1},{3,2},{4,7},{5,4},{6,5},{7,6},{8,11},{9,8},{10,9... | collective-permute-start | bytes 1572872 | tf_op jit(solution)/shard_map/ppermute | solution.py:28
  136.9 23.2 %collective-permute-start.14 = (f32[8,32,512]{2,1,0:T(8,128)S(1)}, f32[8,32,512]{2,1,0:T(8,128)S(1)}, u32[]{:S(2)}, u32[]{:S(2)}) collective-permute-start(f32[8,32,512]{2,1,0:T(8,128)S(1)} %get-tuple-element.21), channel_id=1, source_target_pairs={{0,2},{1,3},{2,0},{3,1},{4,6},{5,7},{6,4},{7,5},{8,10},{9,11},{10,... | collective-permute-start | bytes 1572872 | tf_op jit(solution)/shard_map/ppermute | solution.py:28
  162.2 23.1 %all-to-all-start.3 = ((f32[8,32,512]{2,1,0:T(8,128)}), f32[8,32,512]{2,1,0:T(8,128)S(1)}, u32[]{:S(2)}, u32[]{:S(2)}) async-start(f32[8,32,512]{2,1,0:T(8,128)} %add_add_fusion), calls=%async_computation.3 | async-start | bytes 1048576 | tf_op jit(solution)/shard_map/all_to_all | solution.py:23
  168.3 1.0 copy-start.1
  169.3 1.0 copy-start.3
  170.3 1.0 copy-start.5
  172.9 6.5 %collective-permute-start.18 = (f32[32,8,128]{2,1,0:T(8,128)S(1)}, f32[32,8,128]{2,1,0:T(8,128)S(1)}, u32[]{:S(2)}, u32[]{:S(2)}) collective-permute-start(f32[32,8,128]{2,1,0:T(8,128)S(1)} %shard_map.89.refs_0_), channel_id=1, source_target_pairs={{0,192},{64,0},{128,64},{192,128},{1,193},{65,1},{129,65},{193,129... | collective-permute-start | bytes 393224 | tf_op jit(solution)/shard_map/ppermute | solution.py:28
  173.5 7.2 %collective-permute-start.17 = (f32[32,8,128]{2,1,0:T(8,128)S(1)}, f32[32,8,128]{2,1,0:T(8,128)S(1)}, u32[]{:S(2)}, u32[]{:S(2)}) collective-permute-start(f32[32,8,128]{2,1,0:T(8,128)S(1)} %shard_map.89.refs_0_), channel_id=1, source_target_pairs={{0,128},{64,192},{128,0},{192,64},{1,129},{65,193},{129,1},{193,65... | collective-permute-start | bytes 393224 | tf_op jit(solution)/shard_map/ppermute | solution.py:28
  175.6 6.6 %collective-permute-start.16 = (f32[32,8,128]{2,1,0:T(8,128)S(1)}, f32[32,8,128]{2,1,0:T(8,128)S(1)}, u32[]{:S(2)}, u32[]{:S(2)}) collective-permute-start(f32[32,8,128]{2,1,0:T(8,128)S(1)} %shard_map.89.refs_0_), channel_id=1, source_target_pairs={{0,64},{64,128},{128,192},{192,0},{1,65},{65,129},{129,193},{193,1... | collective-permute-start | bytes 393224 | tf_op jit(solution)/shard_map/ppermute | solution.py:28
  177.1 8.1 %collective-permute-start.19 = (f32[32,8,128]{2,1,0:T(8,128)S(1)}, f32[32,8,128]{2,1,0:T(8,128)S(1)}, u32[]{:S(2)}, u32[]{:S(2)}) collective-permute-start(f32[32,8,128]{2,1,0:T(8,128)S(1)} %shard_map.89.refs_0_), channel_id=1, source_target_pairs={{0,32},{32,0},{1,33},{33,1},{2,34},{34,2},{3,35},{35,3},{4,36},{36... | collective-permute-start | bytes 393224 | tf_op jit(solution)/shard_map/ppermute | solution.py:28
  179.4 5.9 %collective-permute-start.22 = (f32[32,8,128]{2,1,0:T(8,128)S(1)}, f32[32,8,128]{2,1,0:T(8,128)S(1)}, u32[]{:S(2)}, u32[]{:S(2)}) collective-permute-start(f32[32,8,128]{2,1,0:T(8,128)S(1)} %collective-permute-done.18.refs_3_), channel_id=1, source_target_pairs={{0,32},{32,0},{1,33},{33,1},{2,34},{34,2},{3,35},{35,3},{4,36},{36... | collective-permute-start | bytes 393224 | tf_op jit(solution)/shard_map/ppermute | solution.py:28
  180.8 4.5 %collective-permute-start.21 = (f32[32,8,128]{2,1,0:T(8,128)S(1)}, f32[32,8,128]{2,1,0:T(8,128)S(1)}, u32[]{:S(2)}, u32[]{:S(2)}) collective-permute-start(f32[32,8,128]{2,1,0:T(8,128)S(1)} %collective-permute-done.17.refs_2_), channel_id=1, source_target_pairs={{0,32},{32,0},{1,33},{33,1},{2,34},{34,2},{3,35},{35,3},{4,36},{36... | collective-permute-start | bytes 393224 | tf_op jit(solution)/shard_map/ppermute | solution.py:28
  182.2 3.1 %collective-permute-start.20 = (f32[32,8,128]{2,1,0:T(8,128)S(1)}, f32[32,8,128]{2,1,0:T(8,128)S(1)}, u32[]{:S(2)}, u32[]{:S(2)}) collective-permute-start(f32[32,8,128]{2,1,0:T(8,128)S(1)} %collective-permute-done.16.refs_1_), channel_id=1, source_target_pairs={{0,32},{32,0},{1,33},{33,1},{2,34},{34,2},{3,35},{35,3},{4,36},{36... | collective-permute-start | bytes 393224 | tf_op jit(solution)/shard_map/ppermute | solution.py:28

commit v5 on v4

--- a/solution.py
+++ b/solution.py
@@ -28,7 +28,7 @@
     return lax.ppermute(shard, axis, [(i, (i + hops) % n) for i in range(n)])
 
 
-def call(kernel, outs, in_specs, me, *, args, grid=1, scratch=(), held=True, out_spec=VMEM):
+def call(kernel, outs, in_specs, me, *, args, grid=1, scratch=(), held=True):
     out_shape = [(pltpu.VMEM if held else pltpu.HBM)(*o) for o in outs]
     spaces = [pltpu.VMEM if spec is HELD else None if spec is SMEM else pltpu.HBM for spec in in_specs]
     args = [a if space is None else pltpu.with_memory_space_constraint(a, space) for a, space in zip(args, spaces)]
@@ -39,7 +39,7 @@
             num_scalar_prefetch=1,
             grid=(grid,),
             in_specs=in_specs,
-            out_specs=[out_spec] * len(out_shape),
+            out_specs=[VMEM] * len(out_shape),
             scratch_shapes=list(scratch),
         ),
         compiler_params=pltpu.CompilerParams(vmem_limit_bytes=28 << 20),
@@ -154,50 +154,55 @@
         out_ref[:, 8 * slot : 8 * slot + 8, :] = total[64 * slot : 64 * slot + 64].reshape(8, 8, 512)
 
 
-def train_kernel(me_ref, len_ref, grads_ref, *refs):
-    blocks, slabs, (out_ref, high_ref, low_ref, total_ref) = refs[:4], refs[4:12], refs[12:]
+def add_block(me_ref, len_ref, hops, grads_ref, block_ref, total_ref):
     _, _, _, x = place(me_ref)
-    step = pl.program_id(0)
+    first = lax.rem(x + 4 - hops, 4) * 512
+    high, low = split(block_ref[:, :64, :].reshape(512, 128).T)
+    pair = jnp.concatenate([high, low], 0)
+    token = first + lax.broadcasted_iota(jnp.int32, pair.shape, 1)
+    begin = jnp.int32(0)
+    for doc in range(4):
+        end = begin + len_ref[doc]
+
+        @pl.when((begin < first + 512) & (end > first))
+        def _(begin=begin, end=end, doc=doc):
+            masked = jnp.where((token >= begin) & (token < end), pair, jnp.zeros_like(pair))
+            both = dot_nn(masked, grads_ref[...])
+            total_ref[doc] += both[:128] + both[128:]
+
+        begin = end
+
+
+def outer_own_kernel(me_ref, len_ref, grads_ref, block_ref, total_ref):
+    total_ref[...] = jnp.zeros_like(total_ref)
+    add_block(me_ref, len_ref, 0, grads_ref, block_ref, total_ref)
+
+
+def outer_side_kernel(me_ref, len_ref, grads_ref, ahead_ref, behind_ref, so_far_ref, total_ref):
+    @pl.when(pl.program_id(0) == 0)
+    def _():
+        total_ref[...] = so_far_ref[...]
+        add_block(me_ref, len_ref, 1, grads_ref, ahead_ref, total_ref)
+
+    @pl.when(pl.program_id(0) == 1)
+    def _():
+        add_block(me_ref, len_ref, 3, grads_ref, behind_ref, total_ref)
+
+
+def train_kernel(me_ref, len_ref, grads_ref, block_ref, so_far_ref, *refs):
+    slabs, (out_ref, high_ref, low_ref, total_ref) = refs[:8], refs[8:]
     cols = grads_ref.shape[1]
-
-    @pl.when(step == 0)
-    def _():
-        total_ref[...] = jnp.zeros_like(total_ref)
-
-    for k in range(4):
-
-        @pl.when(step == k)
-        def _(k=k):
-            first = lax.rem(x + 4 - k, 4) * 512
-            high, low = split(blocks[k][:, :64, :].reshape(512, 128).T)
-            pair = jnp.concatenate([high, low], 0)
-            token = first + lax.broadcasted_iota(jnp.int32, pair.shape, 1)
-            begin = jnp.int32(0)
-            for doc in range(4):
-                end = begin + len_ref[doc]
-
-                @pl.when((begin < first + 512) & (end > first))
-                def _(begin=begin, end=end, doc=doc):
-                    masked = jnp.where((token >= begin) & (token < end), pair, jnp.zeros_like(pair))
-                    both = dot_nn(masked, grads_ref[...])
-                    total_ref[doc] += both[:128] + both[128:]
-
-                begin = end
-
-    @pl.when(step == 3)
-    def _():
-        for doc in range(4):
-            length = jnp.full((128, cols), len_ref[doc], jnp.int32).astype(jnp.float32)
-            high, low = split(total_ref[doc] / length)
-            rows = slice(128 * doc, 128 * doc + 128)
-            for ref, value in ((high_ref, high), (low_ref, low)):
-                ref[0, rows, :] = value[:, :HALF]
-                ref[1, rows, : 2 * HALF - cols] = jnp.zeros((128, 2 * HALF - cols), jnp.bfloat16)
-                ref[1, rows, 2 * HALF - cols :] = value[:, HALF:]
-
-    @pl.when(step == 4)
-    def _():
-        basis_product(me_ref, 2, slabs, high_ref, low_ref, out_ref)
+    total_ref[...] = so_far_ref[...]
+    add_block(me_ref, len_ref, 2, grads_ref, block_ref, total_ref)
+    for doc in range(4):
+        length = jnp.full((128, cols), len_ref[doc], jnp.int32).astype(jnp.float32)
+        high, low = split(total_ref[doc] / length)
+        rows = slice(128 * doc, 128 * doc + 128)
+        for ref, value in ((high_ref, high), (low_ref, low)):
+            ref[0, rows, :] = value[:, :HALF]
+            ref[1, rows, : 2 * HALF - cols] = jnp.zeros((128, 2 * HALF - cols), jnp.bfloat16)
+            ref[1, rows, 2 * HALF - cols :] = value[:, HALF:]
+    basis_product(me_ref, 2, slabs, high_ref, low_ref, out_ref)
 
 
 def product_kernel(hops, me_ref, high_ref, low_ref, *refs):
@@ -265,7 +270,7 @@
         basis_pick_kernel,
         [((32, 8, HALF), f32)],
         [ANY],
-        me, args=(output_basis,), held=False, out_spec=ANY,
+        me, args=(output_basis,), held=False,
         scratch=[pltpu.SemaphoreType.DMA((32,))],
     )
     slab = exchange(picked, ZX).reshape(8, 4, 8, HALF)
@@ -278,10 +283,10 @@
     query_call = functools.partial(
         call, outs=[((8, 4, 4, 8, queries), f32)], me=me, scratch=[pltpu.VMEM((queries, HALF), bf16)]
     )
-    (rot,) = query_call(functools.partial(query_kernel, True), in_specs=[VMEM] + [HELD] * 4, args=(query_grads, *slabs[:4]), held=False)
+    (rot,) = query_call(functools.partial(query_kernel, True), in_specs=[VMEM] + [HELD] * 4, args=(query_grads, *slabs[:4]))
     (rot,) = query_call(
         functools.partial(query_kernel, False),
-        in_specs=[VMEM] * 2 + [HELD] * 4,
+        in_specs=[VMEM] + [HELD] * 5,
         args=(query_grads, rot, *slabs[4:]),
         held=False,
     )
@@ -300,18 +305,32 @@
 
     block_shape, sum_shape = ((8, 32, 512), f32), ((2, 512, HALF), bf16)
     sent = [None] * 4
+    total_shape = ((4, 128, out_grads.shape[1]), f32)
+
+    def grads_spec(first, stride=0):
+        return pl.BlockSpec(
+            (512, out_grads.shape[1]), lambda i, me: (lax.rem(me[0] % 4 + 4 - first - stride * i, 4), 0)
+        )
+
+    (total,) = call(
+        outer_own_kernel,
+        [total_shape],
+        [SMEM, grads_spec(0), HELD],
+        me, args=(doc_lengths, out_grads, blocks[0]), held=False,
+    )
+    (total,) = call(
+        outer_side_kernel,
+        [total_shape],
+        [SMEM, grads_spec(1, 2), HELD, HELD, VMEM],
+        me, args=(doc_lengths, out_grads, blocks[1], blocks[3], total),
+        grid=2,
+    )
     sent[2], high, low = call(
         train_kernel,
         [block_shape, sum_shape, sum_shape],
-        [
-            SMEM,
-            pl.BlockSpec((512, out_grads.shape[1]), lambda i, me: (lax.rem(me[0] % 4 + 4 - jnp.minimum(i, 3), 4), 0)),
-            *[HELD] * 12,
-        ],
-        me,
-        args=(doc_lengths, out_grads, *blocks, *slabs),
-        grid=5,
-        scratch=[pltpu.VMEM((4, 128, out_grads.shape[1]), f32)],
+        [SMEM, grads_spec(2), *[HELD] * 10],
+        me, args=(doc_lengths, out_grads, blocks[2], total, *slabs),
+        scratch=[pltpu.VMEM(*total_shape)],
     )
     sent[1], sent[3] = call(
         functools.partial(product_kernel, (1, 3)), [block_shape] * 2, [HELD] * 10, me, args=(high, low, *slabs)

time: 207 us -> 188 us (0.908)
  Pallas kernels: 40.8 us -> 28 us
  waiting for transfers between devices: 82.4 us -> 76.7 us
    pallas_call x9 -> x11, Pallas kernels: 40.8 us -> 28 us  [call(): pl.pallas_call(kernel, out_shape=out_shape, grid_spec=pltpu.PrefetchScala...]
    ppermute x23, waiting for transfers between devices: 63.3 us -> 55.8 us  [shifted(): return lax.ppermute(shard, axis, [(i, (i + hops) % n) for i in range(n)])]
    ppermute x23, starting transfers between devices: 23.7 us -> 26 us  [shifted(): return lax.ppermute(shard, axis, [(i, (i + hops) % n) for i in range(n)])]
  transfers between devices with their start and end apart: 28 -> 28, of which waited for: 13 -> 16; matrix products, arithmetic and copies ran while one was open for 2% -> 2% of each run, Pallas kernels for 11% -> 14%
where the time goes in v5:
time: 188 us; the launch traced here: 186 us
  waiting for transfers between devices  76.7 us (41%)
  starting transfers between devices  56.1 us (30%)
  Pallas kernels  28 us (15%)
  blocking collectives  18 us (10%)
  local copies, waits for them, and re-layouts  4.27 us (2%)
  other arithmetic  2.98 us (2%)
    ppermute x23, waiting for transfers between devices, shifted(): return lax.ppermute(shard, axis, [(i, (i + hops) % n) for i in range(n)])  55.8 us
    all_to_all x5, starting transfers between devices, exchange(): return lax.all_to_all(blocks, axis, 0, 0, tiled=True)  30.1 us
    pallas_call x11, Pallas kernels, call(): pl.pallas_call(kernel, out_shape=out_shape, grid_spec=pltpu.PrefetchScala...  28 us
    ppermute x23, starting transfers between devices, shifted(): return lax.ppermute(shard, axis, [(i, (i + hops) % n) for i in range(n)])  26 us
    all_to_all x5, waiting for transfers between devices, exchange(): return lax.all_to_all(blocks, axis, 0, 0, tiled=True)  20.9 us
    all_to_all x1, blocking collectives, exchange(): return lax.all_to_all(blocks, axis, 0, 0, tiled=True)  18 us
  transfers between devices with their start and end apart: 28, of which 16 were waited for; matrix products, arithmetic and copies ran while one was open for 2% of the time, Pallas kernels for 14%

profile of v5, /device:TPU:8, one launch (start us, length us, event | category | flops | bytes accessed | tf_op | source)
XLA Modules:
  0.0 186.3 jit_solution(3220398133496034445)
XLA Ops:
  0.0 2.1 %shard_map.85 = f32[32,8,512]{2,1,0:T(8,128)} custom-call(s32[1]{0:T(128)} %bitcast.me_ref, f32[32,28672]{1,0:T(8,128)} %basis_ref.3), custom_call_target="tpu_custom_call" | custom-call | tf_op jit(solution)/shard_map/pallas_call | solution.py:35
  2.1 11.3 %all-to-all-start.2 = ((f32[32,8,512]{2,1,0:T(8,128)}), f32[32,8,512]{2,1,0:T(8,128)S(1)}, u32[]{:S(2)}, u32[]{:S(2)}) async-start(f32[32,8,512]{2,1,0:T(8,128)} %shard_map.85), calls=%async_computation.2 | async-start | bytes 1048576 | tf_op jit(solution)/shard_map/all_to_all | solution.py:23
  13.4 2.2 %shard_map.82 = (f32[8,72,128]{2,1,0:T(8,128)S(1)}, f32[8,72,128]{2,1,0:T(8,128)S(1)}, f32[8,72,128]{2,1,0:T(8,128)S(1)}, f32[8,72,128]{2,1,0:T(8,128)S(1)}) custom-call(s32[1]{0:T(128)} %bitcast.me_ref, bf16[2048,256]{1,0:T(8,128)(2,1)} %acts_ref.1, bf16[256,256]{1,0:T(8,128)(2,1)} %query_ref.1, f32[128,8192]{1,0:T(8,128)} %basis_ref.2), custom_call_target="tpu_custom_call" | custom-call | tf_op jit(solution)/shard_map/pallas_call | solution.py:35
  15.6 3.1 %collective-permute-start.2 = (f32[8,72,128]{2,1,0:T(8,128)S(1)}, f32[8,72,128]{2,1,0:T(8,128)S(1)}, u32[]{:S(2)}, u32[]{:S(2)}) collective-permute-start(f32[8,72,128]{2,1,0:T(8,128)S(1)} %get-tuple-element.17), channel_id=1, source_target_pairs={{0,3},{1,0},{2,1},{3,2},{4,7},{5,4},{6,5},{7,6},{8,11},{9,8},{10,9... | collective-permute-start | bytes 884744 | tf_op jit(solution)/shard_map/ppermute | solution.py:28
  18.7 2.3 %collective-permute-start = (f32[8,72,128]{2,1,0:T(8,128)S(1)}, f32[8,72,128]{2,1,0:T(8,128)S(1)}, u32[]{:S(2)}, u32[]{:S(2)}) collective-permute-start(f32[8,72,128]{2,1,0:T(8,128)S(1)} %get-tuple-element.15), channel_id=1, source_target_pairs={{0,2},{1,3},{2,0},{3,1},{4,6},{5,7},{6,4},{7,5},{8,10},{9,11},{10,... | collective-permute-start | bytes 884744 | tf_op jit(solution)/shard_map/ppermute | solution.py:28
  21.0 10.2 %all-to-all-done.2 = f32[32,8,512]{2,1,0:T(8,128)S(1)} async-done(((f32[32,8,512]{2,1,0:T(8,128)}), f32[32,8,512]{2,1,0:T(8,128)S(1)}, u32[]{:S(2)}, u32[]{:S(2)}) %all-to-all-start.2) | async-done | bytes 524320 | tf_op jit(solution)/shard_map/all_to_all | solution.py:23
  31.7 2.6 %collective-permute-start.7 = (f32[8,4,8,512]{3,2,1,0:T(8,128)S(1)}, f32[8,4,8,512]{3,2,1,0:T(8,128)}, u32[]{:S(2)}, u32[]{:S(2)}) collective-permute-start(f32[8,4,8,512]{3,2,1,0:T(8,128)S(1)} %bitcast.4), channel_id=1, source_target_pairs={{0,128},{64,192},{128,0},{192,64},{1,129},{65,193},{129,1},{193,65... | collective-permute-start | bytes 1572872 | tf_op jit(solution)/shard_map/ppermute | solution.py:28
  34.6 1.6 collective-permute-start.8
  36.2 1.7 collective-permute-done.1
  37.8 0.8 add_add_fusion.1
  38.6 5.8 %all-to-all-start = ((f32[8,72,128]{2,1,0:T(8,128)}), f32[8,72,128]{2,1,0:T(8,128)S(1)}, u32[]{:S(2)}, u32[]{:S(2)}) async-start(f32[8,72,128]{2,1,0:T(8,128)} %add_add_fusion.1), calls=%async_computation | async-start | bytes 589824 | tf_op jit(solution)/shard_map/all_to_all | solution.py:23
  44.5 0.6 collective-permute-done.6.refs_1_
  45.0 10.4 %collective-permute-done.7.refs_2_ = f32[8,4,8,512]{3,2,1,0:T(8,128)} collective-permute-done((f32[8,4,8,512]{3,2,1,0:T(8,128)S(1)}, f32[8,4,8,512]{3,2,1,0:T(8,128)}, u32[]{:S(2)}, u32[]{:S(2)}) %collective-permute-start.7) | collective-permute-done | bytes 524320 | tf_op jit(solution)/shard_map/ppermute | solution.py:28
  55.4 0.8 collective-permute-done.8.refs_3_
  56.3 0.7 broadcast_in_dim.2
  57.0 3.4 %all-to-all-start.1 = ((f32[8,72,128]{2,1,0:T(8,128)}), f32[8,72,128]{2,1,0:T(8,128)S(1)}, u32[]{:S(2)}, u32[]{:S(2)}) async-start(f32[8,72,128]{2,1,0:T(8,128)} %broadcast_in_dim.2), calls=%async_computation.1 | async-start | bytes 589824 | tf_op jit(solution)/shard_map/all_to_all | solution.py:23
  60.4 2.1 %shard_map.89.refs_0_ = f32[8,4,4,8,256]{4,3,2,1,0:T(8,128)S(1)} custom-call(s32[1]{0:T(128)} %bitcast.me_ref, bf16[256,896]{1,0:T(8,128)(2,1)} %grads_ref.9, f32[8,4,8,512]{3,2,1,0:T(8,128)S(1)} %bitcast.7, f32[8,4,8,512]{3,2,1,0:T(8,128)S(1)} %collective-permute-done.6.refs_1_, f32[8,4,8,512]{3,2,1,0:T(8,128)} %collective-permute-done.7.refs_2_, ...), custom_call_target="tpu_custom_call" | custom-call | tf_op jit(solution)/shard_map/pallas_call | solution.py:35
  62.6 2.8 %shard_map.90 = f32[8,4,4,8,256]{4,3,2,1,0:T(8,128)} custom-call(s32[1]{0:T(128)} %bitcast.me_ref, bf16[256,896]{1,0:T(8,128)(2,1)} %grads_ref.9, f32[8,4,4,8,256]{4,3,2,1,0:T(8,128)S(1)} %shard_map.89.refs_0_, f32[8,4,8,512]{3,2,1,0:T(8,128)S(1)} %collective-permute-done.9.refs_4_.refs_1_, f32[8,4,8,512]{3,2,1,0:T(8,128)S(1)} %collective-permute-done.10.refs_5_.refs_2_, ...), custom_call_target="tpu_custom_call" | custom-call | tf_op jit(solution)/shard_map/pallas_call | solution.py:35
  65.4 8.5 %all-to-all-done.1.block_ref.refs_1_ = f32[8,72,128]{2,1,0:T(8,128)S(1)} async-done(((f32[8,72,128]{2,1,0:T(8,128)}), f32[8,72,128]{2,1,0:T(8,128)S(1)}, u32[]{:S(2)}, u32[]{:S(2)}) %all-to-all-start.1) | async-done | bytes 294944 | tf_op jit(solution)/shard_map/all_to_all | solution.py:23
  73.9 4.7 %all-to-all-start.4 = ((f32[32,4,8,256]{3,2,1,0:T(8,128)}), f32[32,4,8,256]{3,2,1,0:T(8,128)}, u32[]{:S(2)}, u32[]{:S(2)}) async-start(f32[32,4,8,256]{3,2,1,0:T(8,128)} %bitcast.11), calls=%async_computation.4 | async-start | bytes 2097152 | tf_op jit(solution)/shard_map/all_to_all | solution.py:23
  78.5 1.7 collective-permute-start.4
  80.2 1.6 collective-permute-start.5
  81.9 1.9 %collective-permute-start.3 = (f32[8,72,128]{2,1,0:T(8,128)S(1)}, f32[8,72,128]{2,1,0:T(8,128)S(1)}, u32[]{:S(2)}, u32[]{:S(2)}) collective-permute-start(f32[8,72,128]{2,1,0:T(8,128)S(1)} %all-to-all-done.1.block_ref.refs_1_), channel_id=1, source_target_pairs={{0,2},{1,3},{2,0},{3,1},{4,6},{5,7},{6,4},{7,5},{8,10},{9,11},{10,... | collective-permute-start | bytes 884744 | tf_op jit(solution)/shard_map/ppermute | solution.py:28
  83.8 3.7 %shard_map.83.so_far_ref = f32[4,128,896]{2,1,0:T(8,128)} custom-call(s32[1]{0:T(128)} %bitcast.me_ref, s32[4]{0:T(128)S(1)} %copy-done.6, bf16[2048,896]{1,0:T(8,128)(2,1)} %grads_ref.7, f32[8,72,128]{2,1,0:T(8,128)S(1)} %all-to-all-done.1.block_ref.refs_1_), custom_call_target="tpu_custom_call" | custom-call | tf_op jit(solution)/shard_map/pallas_call | solution.py:35
  87.4 8.3 %collective-permute-done.4.ahead_ref.refs_2_ = f32[8,72,128]{2,1,0:T(8,128)S(1)} collective-permute-done((f32[8,72,128]{2,1,0:T(8,128)S(1)}, f32[8,72,128]{2,1,0:T(8,128)S(1)}, u32[]{:S(2)}, u32[]{:S(2)}) %collective-permute-start.4) | collective-permute-done | bytes 294944 | tf_op jit(solution)/shard_map/ppermute | solution.py:28
  95.8 7.7 %collective-permute-done.5.behind_ref.refs_4_ = f32[8,72,128]{2,1,0:T(8,128)S(1)} collective-permute-done((f32[8,72,128]{2,1,0:T(8,128)S(1)}, f32[8,72,128]{2,1,0:T(8,128)S(1)}, u32[]{:S(2)}, u32[]{:S(2)}) %collective-permute-start.5) | collective-permute-done | bytes 294944 | tf_op jit(solution)/shard_map/ppermute | solution.py:28
  103.5 3.2 %shard_map.84.so_far_ref = f32[4,128,896]{2,1,0:T(8,128)S(1)} custom-call(s32[1]{0:T(128)} %bitcast.me_ref, s32[4]{0:T(128)S(1)} %copy-done.6, bf16[2048,896]{1,0:T(8,128)(2,1)} %grads_ref.7, f32[8,72,128]{2,1,0:T(8,128)S(1)} %collective-permute-done.4.ahead_ref.refs_2_, f32[8,72,128]{2,1,0:T(8,128)S(1)} %collective-permute-done.5.behind_ref.refs_4_, ...), custom_call_target="tpu_custom_call" | custom-call | tf_op jit(solution)/shard_map/pallas_call | solution.py:35
  106.9 4.0 %shard_map.86 = (f32[8,32,512]{2,1,0:T(8,128)S(1)}, bf16[2,512,512]{2,1,0:T(8,128)(2,1)S(1)}, bf16[2,512,512]{2,1,0:T(8,128)(2,1)S(1)}) custom-call(s32[1]{0:T(128)} %bitcast.me_ref, s32[4]{0:T(128)S(1)} %copy-done.6, bf16[2048,896]{1,0:T(8,128)(2,1)} %grads_ref.7, f32[8,72,128]{2,1,0:T(8,128)S(1)} %collective-permute-done.3.block_ref.refs_3_, ...), custom_call_target="tpu_custom_call" | custom-call | tf_op jit(solution)/shard_map/pallas_call | solution.py:35
  111.0 3.0 %shard_map.88 = (f32[8,32,512]{2,1,0:T(8,128)S(1)}, f32[8,32,512]{2,1,0:T(8,128)S(1)}) custom-call(s32[1]{0:T(128)} %bitcast.me_ref, bf16[2,512,512]{2,1,0:T(8,128)(2,1)S(1)} %get-tuple-element.18.high_ref, bf16[2,512,512]{2,1,0:T(8,128)(2,1)S(1)} %get-tuple-element.19.low_ref, f32[8,4,8,512]{3,2,1,0:T(8,128)S(1)} %bitcast.9, ...), custom_call_target="tpu_custom_call" | custom-call | tf_op jit(solution)/shard_map/pallas_call | solution.py:35
  114.0 4.5 %collective-permute-start.15 = (f32[8,32,512]{2,1,0:T(8,128)S(1)}, f32[8,32,512]{2,1,0:T(8,128)S(1)}, u32[]{:S(2)}, u32[]{:S(2)}) collective-permute-start(f32[8,32,512]{2,1,0:T(8,128)S(1)} %get-tuple-element.22), channel_id=1, source_target_pairs={{0,3},{1,0},{2,1},{3,2},{4,7},{5,4},{6,5},{7,6},{8,11},{9,8},{10,9... | collective-permute-start | bytes 1572872 | tf_op jit(solution)/shard_map/ppermute | solution.py:28
  118.5 1.0 collective-permute-start.13
  119.5 3.0 %shard_map.87 = f32[8,32,512]{2,1,0:T(8,128)} custom-call(s32[1]{0:T(128)} %bitcast.me_ref, bf16[2,512,512]{2,1,0:T(8,128)(2,1)S(1)} %get-tuple-element.18.high_ref, bf16[2,512,512]{2,1,0:T(8,128)(2,1)S(1)} %get-tuple-element.19.low_ref, f32[8,4,8,512]{3,2,1,0:T(8,128)S(1)} %bitcast.10, f32[8,4,8,512]{3,2,1,0:T(8,128)S(1)} %collective-permute-done.6.refs_1_, ...), custom_call_target="tpu_custom_call" | custom-call | tf_op jit(solution)/shard_map/pallas_call | solution.py:35
  122.5 16.7 %collective-permute-done.15 = f32[8,32,512]{2,1,0:T(8,128)S(1)} collective-permute-done((f32[8,32,512]{2,1,0:T(8,128)S(1)}, f32[8,32,512]{2,1,0:T(8,128)S(1)}, u32[]{:S(2)}, u32[]{:S(2)}) %collective-permute-start.15) | collective-permute-done | bytes 524320 | tf_op jit(solution)/shard_map/ppermute | solution.py:28
  139.2 3.4 %collective-permute-done.13 = f32[8,32,512]{2,1,0:T(8,128)S(1)} collective-permute-done((f32[8,32,512]{2,1,0:T(8,128)S(1)}, f32[8,32,512]{2,1,0:T(8,128)S(1)}, u32[]{:S(2)}, u32[]{:S(2)}) %collective-permute-start.13) | collective-permute-done | bytes 524320 | tf_op jit(solution)/shard_map/ppermute | solution.py:28
  142.6 2.1 %add_add_fusion = f32[8,32,512]{2,1,0:T(8,128)} fusion(f32[8,32,512]{2,1,0:T(8,128)S(1)} %collective-permute-done.15, f32[8,32,512]{2,1,0:T(8,128)S(1)} %collective-permute-done.14, f32[8,32,512]{2,1,0:T(8,128)} %shard_map.87, f32[8,32,512]{2,1,0:T(8,128)S(1)} %collective-permute-done.13), kind=kLoop, calls=%fused_computation | loop fusion | flops 393216 | bytes 2621440 | tf_op jit(solution)/shard_map/add | solution.py:344
  144.6 4.8 %all-to-all-start.3 = ((f32[8,32,512]{2,1,0:T(8,128)}), f32[8,32,512]{2,1,0:T(8,128)S(1)}, u32[]{:S(2)}, u32[]{:S(2)}) async-start(f32[8,32,512]{2,1,0:T(8,128)} %add_add_fusion), calls=%async_computation.3 | async-start | bytes 1048576 | tf_op jit(solution)/shard_map/all_to_all | solution.py:23
  149.4 1.0 copy-done.1
  150.4 1.0 copy-done.3
  151.3 1.0 copy-done.5
  152.3 1.7 shard_map.91.refs_0_
  154.0 1.7 collective-permute-start.16
  155.7 3.1 %collective-permute-start.17 = (f32[32,8,128]{2,1,0:T(8,128)S(1)}, f32[32,8,128]{2,1,0:T(8,128)S(1)}, u32[]{:S(2)}, u32[]{:S(2)}) collective-permute-start(f32[32,8,128]{2,1,0:T(8,128)S(1)} %shard_map.91.refs_0_), channel_id=1, source_target_pairs={{0,128},{64,192},{128,0},{192,64},{1,129},{65,193},{129,1},{193,65... | collective-permute-start | bytes 393224 | tf_op jit(solution)/shard_map/ppermute | solution.py:28
  159.2 1.8 collective-permute-done.16.refs_1_
  161.0 2.5 %collective-permute-done.17.refs_2_ = f32[32,8,128]{2,1,0:T(8,128)S(1)} collective-permute-done((f32[32,8,128]{2,1,0:T(8,128)S(1)}, f32[32,8,128]{2,1,0:T(8,128)S(1)}, u32[]{:S(2)}, u32[]{:S(2)}) %collective-permute-start.17) | collective-permute-done | bytes 131104 | tf_op jit(solution)/shard_map/ppermute | solution.py:28
  163.5 1.4 collective-permute-done.18.refs_3_
  164.9 2.2 %all-to-all-done.3.blocks_ref = f32[8,32,512]{2,1,0:T(8,128)S(1)} async-done(((f32[8,32,512]{2,1,0:T(8,128)}), f32[8,32,512]{2,1,0:T(8,128)S(1)}, u32[]{:S(2)}, u32[]{:S(2)}) %all-to-all-start.3) | async-done | bytes 524320 | tf_op jit(solution)/shard_map/all_to_all | solution.py:23
  167.5 18.0 %all_to_all.30 = f32[32,8,128]{2,1,0:T(8,128)S(1)} all-to-all(f32[32,8,128]{2,1,0:T(8,128)S(1)} %shard_map.92), channel_id=1, replica_groups=mesh['y'=4,'core'=2,'z'=8,'x'=4] {'z','x'}, dimensions={0} | all-to-all | bytes 262144 | tf_op jit(solution)/shard_map/all_to_all | solution.py:23
  185.7 0.6 reshape.16
  (40 shorter events, 2.0 us)
Async XLA Ops:
  2.1 29.2 %all-to-all-start.2 = ((f32[32,8,512]{2,1,0:T(8,128)}), f32[32,8,512]{2,1,0:T(8,128)S(1)}, u32[]{:S(2)}, u32[]{:S(2)}) async-start(f32[32,8,512]{2,1,0:T(8,128)} %shard_map.85), calls=%async_computation.2 | async-start | bytes 1048576 | tf_op jit(solution)/shard_map/all_to_all | solution.py:23
  15.6 19.0 %collective-permute-start.2 = (f32[8,72,128]{2,1,0:T(8,128)S(1)}, f32[8,72,128]{2,1,0:T(8,128)S(1)}, u32[]{:S(2)}, u32[]{:S(2)}) collective-permute-start(f32[8,72,128]{2,1,0:T(8,128)S(1)} %get-tuple-element.17), channel_id=1, source_target_pairs={{0,3},{1,0},{2,1},{3,2},{4,7},{5,4},{6,5},{7,6},{8,11},{9,8},{10,9... | collective-permute-start | bytes 884744 | tf_op jit(solution)/shard_map/ppermute | solution.py:28
  18.7 19.2 %collective-permute-start.1 = (f32[8,72,128]{2,1,0:T(8,128)S(1)}, f32[8,72,128]{2,1,0:T(8,128)S(1)}, u32[]{:S(2)}, u32[]{:S(2)}) collective-permute-start(f32[8,72,128]{2,1,0:T(8,128)S(1)} %get-tuple-element.16), channel_id=1, source_target_pairs={{0,1},{1,2},{2,3},{3,0},{4,5},{5,6},{6,7},{7,4},{8,9},{9,10},{10,1... | collective-permute-start | bytes 884744 | tf_op jit(solution)/shard_map/ppermute | solution.py:28
  18.7 19.2 %collective-permute-start = (f32[8,72,128]{2,1,0:T(8,128)S(1)}, f32[8,72,128]{2,1,0:T(8,128)S(1)}, u32[]{:S(2)}, u32[]{:S(2)}) collective-permute-start(f32[8,72,128]{2,1,0:T(8,128)S(1)} %get-tuple-element.15), channel_id=1, source_target_pairs={{0,2},{1,3},{2,0},{3,1},{4,6},{5,7},{6,4},{7,5},{8,10},{9,11},{10,... | collective-permute-start | bytes 884744 | tf_op jit(solution)/shard_map/ppermute | solution.py:28
  31.2 13.8 %collective-permute-start.6 = (f32[8,4,8,512]{3,2,1,0:T(8,128)S(1)}, f32[8,4,8,512]{3,2,1,0:T(8,128)S(1)}, u32[]{:S(2)}, u32[]{:S(2)}) collective-permute-start(f32[8,4,8,512]{3,2,1,0:T(8,128)S(1)} %bitcast.3), channel_id=1, source_target_pairs={{0,192},{64,0},{128,64},{192,128},{1,193},{65,1},{129,65},{193,129... | collective-permute-start | bytes 1572872 | tf_op jit(solution)/shard_map/ppermute | solution.py:28
  31.7 23.7 %collective-permute-start.7 = (f32[8,4,8,512]{3,2,1,0:T(8,128)S(1)}, f32[8,4,8,512]{3,2,1,0:T(8,128)}, u32[]{:S(2)}, u32[]{:S(2)}) collective-permute-start(f32[8,4,8,512]{3,2,1,0:T(8,128)S(1)} %bitcast.4), channel_id=1, source_target_pairs={{0,128},{64,192},{128,0},{192,64},{1,129},{65,193},{129,1},{193,65... | collective-permute-start | bytes 1572872 | tf_op jit(solution)/shard_map/ppermute | solution.py:28
  34.6 21.7 %collective-permute-start.8 = (f32[8,4,8,512]{3,2,1,0:T(8,128)S(1)}, f32[8,4,8,512]{3,2,1,0:T(8,128)}, u32[]{:S(2)}, u32[]{:S(2)}) collective-permute-start(f32[8,4,8,512]{3,2,1,0:T(8,128)S(1)} %bitcast.5), channel_id=1, source_target_pairs={{0,64},{64,128},{128,192},{192,0},{1,65},{65,129},{129,193},{193,1... | collective-permute-start | bytes 1572872 | tf_op jit(solution)/shard_map/ppermute | solution.py:28
  38.6 17.6 %all-to-all-start = ((f32[8,72,128]{2,1,0:T(8,128)}), f32[8,72,128]{2,1,0:T(8,128)S(1)}, u32[]{:S(2)}, u32[]{:S(2)}) async-start(f32[8,72,128]{2,1,0:T(8,128)} %add_add_fusion.1), calls=%async_computation | async-start | bytes 589824 | tf_op jit(solution)/shard_map/all_to_all | solution.py:23
  44.5 18.1 %collective-permute-start.9 = (f32[8,4,8,512]{3,2,1,0:T(8,128)S(1)}, f32[8,4,8,512]{3,2,1,0:T(8,128)S(1)}, u32[]{:S(2)}, u32[]{:S(2)}) collective-permute-start(f32[8,4,8,512]{3,2,1,0:T(8,128)S(1)} %bitcast.6), channel_id=1, source_target_pairs={{0,32},{32,0},{1,33},{33,1},{2,34},{34,2},{3,35},{35,3},{4,36},{36... | collective-permute-start | bytes 1572872 | tf_op jit(solution)/shard_map/ppermute | solution.py:28
  45.0 17.6 %collective-permute-start.10 = (f32[8,4,8,512]{3,2,1,0:T(8,128)S(1)}, f32[8,4,8,512]{3,2,1,0:T(8,128)S(1)}, u32[]{:S(2)}, u32[]{:S(2)}) collective-permute-start(f32[8,4,8,512]{3,2,1,0:T(8,128)S(1)} %collective-permute-done.6.refs_1_), channel_id=1, source_target_pairs={{0,32},{32,0},{1,33},{33,1},{2,34},{34,2},{3,35},{35,3},{4,36},{36... | collective-permute-start | bytes 1572872 | tf_op jit(solution)/shard_map/ppermute | solution.py:28
  55.4 7.2 %collective-permute-start.11 = (f32[8,4,8,512]{3,2,1,0:T(8,128)}, f32[8,4,8,512]{3,2,1,0:T(8,128)S(1)}, u32[]{:S(2)}, u32[]{:S(2)}) collective-permute-start(f32[8,4,8,512]{3,2,1,0:T(8,128)} %collective-permute-done.7.refs_2_), channel_id=1, source_target_pairs={{0,32},{32,0},{1,33},{33,1},{2,34},{34,2},{3,35},{35,3},{4,36},{36... | collective-permute-start | bytes 1572872 | tf_op jit(solution)/shard_map/ppermute | solution.py:28
  56.2 6.4 %collective-permute-start.12 = (f32[8,4,8,512]{3,2,1,0:T(8,128)}, f32[8,4,8,512]{3,2,1,0:T(8,128)S(1)}, u32[]{:S(2)}, u32[]{:S(2)}) collective-permute-start(f32[8,4,8,512]{3,2,1,0:T(8,128)} %collective-permute-done.8.refs_3_), channel_id=1, source_target_pairs={{0,32},{32,0},{1,33},{33,1},{2,34},{34,2},{3,35},{35,3},{4,36},{36... | collective-permute-start | bytes 1572872 | tf_op jit(solution)/shard_map/ppermute | solution.py:28
  57.0 16.9 %all-to-all-start.1 = ((f32[8,72,128]{2,1,0:T(8,128)}), f32[8,72,128]{2,1,0:T(8,128)S(1)}, u32[]{:S(2)}, u32[]{:S(2)}) async-start(f32[8,72,128]{2,1,0:T(8,128)} %broadcast_in_dim.2), calls=%async_computation.1 | async-start | bytes 589824 | tf_op jit(solution)/shard_map/all_to_all | solution.py:23
  62.6 21.2 %copy-start.6 = (s32[4]{0:T(128)S(1)}, s32[4]{0:T(128)}, u32[]{:S(2)}) copy-start(s32[4]{0:T(128)} %len_ref.5) | copy-start | bytes 52
  73.9 70.7 %all-to-all-start.4 = ((f32[32,4,8,256]{3,2,1,0:T(8,128)}), f32[32,4,8,256]{3,2,1,0:T(8,128)}, u32[]{:S(2)}, u32[]{:S(2)}) async-start(f32[32,4,8,256]{3,2,1,0:T(8,128)} %bitcast.11), calls=%async_computation.4 | async-start | bytes 2097152 | tf_op jit(solution)/shard_map/all_to_all | solution.py:23
  78.5 17.2 %collective-permute-start.4 = (f32[8,72,128]{2,1,0:T(8,128)S(1)}, f32[8,72,128]{2,1,0:T(8,128)S(1)}, u32[]{:S(2)}, u32[]{:S(2)}) collective-permute-start(f32[8,72,128]{2,1,0:T(8,128)S(1)} %all-to-all-done.1.block_ref.refs_1_), channel_id=1, source_target_pairs={{0,1},{1,2},{2,3},{3,0},{4,5},{5,6},{6,7},{7,4},{8,9},{9,10},{10,1... | collective-permute-start | bytes 884744 | tf_op jit(solution)/shard_map/ppermute | solution.py:28
  80.2 23.3 %collective-permute-start.5 = (f32[8,72,128]{2,1,0:T(8,128)S(1)}, f32[8,72,128]{2,1,0:T(8,128)S(1)}, u32[]{:S(2)}, u32[]{:S(2)}) collective-permute-start(f32[8,72,128]{2,1,0:T(8,128)S(1)} %all-to-all-done.1.block_ref.refs_1_), channel_id=1, source_target_pairs={{0,3},{1,0},{2,1},{3,2},{4,7},{5,4},{6,5},{7,6},{8,11},{9,8},{10,9... | collective-permute-start | bytes 884744 | tf_op jit(solution)/shard_map/ppermute | solution.py:28
  81.9 25.1 %collective-permute-start.3 = (f32[8,72,128]{2,1,0:T(8,128)S(1)}, f32[8,72,128]{2,1,0:T(8,128)S(1)}, u32[]{:S(2)}, u32[]{:S(2)}) collective-permute-start(f32[8,72,128]{2,1,0:T(8,128)S(1)} %all-to-all-done.1.block_ref.refs_1_), channel_id=1, source_target_pairs={{0,2},{1,3},{2,0},{3,1},{4,6},{5,7},{6,4},{7,5},{8,10},{9,11},{10,... | collective-permute-start | bytes 884744 | tf_op jit(solution)/shard_map/ppermute | solution.py:28
  95.8 10.9 %copy-start = (f32[8,72,128]{2,1,0:T(8,128)}, f32[8,72,128]{2,1,0:T(8,128)S(1)}, u32[]{:S(2)}) copy-start(f32[8,72,128]{2,1,0:T(8,128)S(1)} %collective-permute-done.4.ahead_ref.refs_2_) | copy-start | bytes 884740
  103.5 3.2 %copy-start.2 = (f32[8,72,128]{2,1,0:T(8,128)}, f32[8,72,128]{2,1,0:T(8,128)S(1)}, u32[]{:S(2)}) copy-start(f32[8,72,128]{2,1,0:T(8,128)S(1)} %collective-permute-done.5.behind_ref.refs_4_) | copy-start | bytes 884740
  106.9 4.0 %copy-start.4 = (f32[8,72,128]{2,1,0:T(8,128)}, f32[8,72,128]{2,1,0:T(8,128)S(1)}, u32[]{:S(2)}) copy-start(f32[8,72,128]{2,1,0:T(8,128)S(1)} %collective-permute-done.3.block_ref.refs_3_) | copy-start | bytes 884740
  114.0 25.2 %collective-permute-start.15 = (f32[8,32,512]{2,1,0:T(8,128)S(1)}, f32[8,32,512]{2,1,0:T(8,128)S(1)}, u32[]{:S(2)}, u32[]{:S(2)}) collective-permute-start(f32[8,32,512]{2,1,0:T(8,128)S(1)} %get-tuple-element.22), channel_id=1, source_target_pairs={{0,3},{1,0},{2,1},{3,2},{4,7},{5,4},{6,5},{7,6},{8,11},{9,8},{10,9... | collective-permute-start | bytes 1572872 | tf_op jit(solution)/shard_map/ppermute | solution.py:28
  118.5 20.6 %collective-permute-start.14 = (f32[8,32,512]{2,1,0:T(8,128)S(1)}, f32[8,32,512]{2,1,0:T(8,128)S(1)}, u32[]{:S(2)}, u32[]{:S(2)}) collective-permute-start(f32[8,32,512]{2,1,0:T(8,128)S(1)} %get-tuple-element.21), channel_id=1, source_target_pairs={{0,2},{1,3},{2,0},{3,1},{4,6},{5,7},{6,4},{7,5},{8,10},{9,11},{10,... | collective-permute-start | bytes 1572872 | tf_op jit(solution)/shard_map/ppermute | solution.py:28
  118.5 24.0 %collective-permute-start.13 = (f32[8,32,512]{2,1,0:T(8,128)S(1)}, f32[8,32,512]{2,1,0:T(8,128)S(1)}, u32[]{:S(2)}, u32[]{:S(2)}) collective-permute-start(f32[8,32,512]{2,1,0:T(8,128)S(1)} %get-tuple-element.20), channel_id=1, source_target_pairs={{0,1},{1,2},{2,3},{3,0},{4,5},{5,6},{6,7},{7,4},{8,9},{9,10},{10,1... | collective-permute-start | bytes 1572872 | tf_op jit(solution)/shard_map/ppermute | solution.py:28
  144.6 22.5 %all-to-all-start.3 = ((f32[8,32,512]{2,1,0:T(8,128)}), f32[8,32,512]{2,1,0:T(8,128)S(1)}, u32[]{:S(2)}, u32[]{:S(2)}) async-start(f32[8,32,512]{2,1,0:T(8,128)} %add_add_fusion), calls=%async_computation.3 | async-start | bytes 1048576 | tf_op jit(solution)/shard_map/all_to_all | solution.py:23
  149.4 1.0 copy-start.1
  150.4 1.0 copy-start.3
  151.3 1.0 copy-start.5
  154.0 7.0 %collective-permute-start.16 = (f32[32,8,128]{2,1,0:T(8,128)S(1)}, f32[32,8,128]{2,1,0:T(8,128)S(1)}, u32[]{:S(2)}, u32[]{:S(2)}) collective-permute-start(f32[32,8,128]{2,1,0:T(8,128)S(1)} %shard_map.91.refs_0_), channel_id=1, source_target_pairs={{0,64},{64,128},{128,192},{192,0},{1,65},{65,129},{129,193},{193,1... | collective-permute-start | bytes 393224 | tf_op jit(solution)/shard_map/ppermute | solution.py:28
  155.7 7.8 %collective-permute-start.17 = (f32[32,8,128]{2,1,0:T(8,128)S(1)}, f32[32,8,128]{2,1,0:T(8,128)S(1)}, u32[]{:S(2)}, u32[]{:S(2)}) collective-permute-start(f32[32,8,128]{2,1,0:T(8,128)S(1)} %shard_map.91.refs_0_), channel_id=1, source_target_pairs={{0,128},{64,192},{128,0},{192,64},{1,129},{65,193},{129,1},{193,65... | collective-permute-start | bytes 393224 | tf_op jit(solution)/shard_map/ppermute | solution.py:28
  158.8 6.1 %collective-permute-start.18 = (f32[32,8,128]{2,1,0:T(8,128)S(1)}, f32[32,8,128]{2,1,0:T(8,128)S(1)}, u32[]{:S(2)}, u32[]{:S(2)}) collective-permute-start(f32[32,8,128]{2,1,0:T(8,128)S(1)} %shard_map.91.refs_0_), channel_id=1, source_target_pairs={{0,192},{64,0},{128,64},{192,128},{1,193},{65,1},{129,65},{193,129... | collective-permute-start | bytes 393224 | tf_op jit(solution)/shard_map/ppermute | solution.py:28
  159.2 7.9 %collective-permute-start.19 = (f32[32,8,128]{2,1,0:T(8,128)S(1)}, f32[32,8,128]{2,1,0:T(8,128)S(1)}, u32[]{:S(2)}, u32[]{:S(2)}) collective-permute-start(f32[32,8,128]{2,1,0:T(8,128)S(1)} %shard_map.91.refs_0_), channel_id=1, source_target_pairs={{0,32},{32,0},{1,33},{33,1},{2,34},{34,2},{3,35},{35,3},{4,36},{36... | collective-permute-start | bytes 393224 | tf_op jit(solution)/shard_map/ppermute | solution.py:28
  161.0 6.1 %collective-permute-start.20 = (f32[32,8,128]{2,1,0:T(8,128)S(1)}, f32[32,8,128]{2,1,0:T(8,128)S(1)}, u32[]{:S(2)}, u32[]{:S(2)}) collective-permute-start(f32[32,8,128]{2,1,0:T(8,128)S(1)} %collective-permute-done.16.refs_1_), channel_id=1, source_target_pairs={{0,32},{32,0},{1,33},{33,1},{2,34},{34,2},{3,35},{35,3},{4,36},{36... | collective-permute-start | bytes 393224 | tf_op jit(solution)/shard_map/ppermute | solution.py:28
  163.5 3.6 %collective-permute-start.21 = (f32[32,8,128]{2,1,0:T(8,128)S(1)}, f32[32,8,128]{2,1,0:T(8,128)S(1)}, u32[]{:S(2)}, u32[]{:S(2)}) collective-permute-start(f32[32,8,128]{2,1,0:T(8,128)S(1)} %collective-permute-done.17.refs_2_), channel_id=1, source_target_pairs={{0,32},{32,0},{1,33},{33,1},{2,34},{34,2},{3,35},{35,3},{4,36},{36... | collective-permute-start | bytes 393224 | tf_op jit(solution)/shard_map/ppermute | solution.py:28
  164.9 2.2 %collective-permute-start.22 = (f32[32,8,128]{2,1,0:T(8,128)S(1)}, f32[32,8,128]{2,1,0:T(8,128)S(1)}, u32[]{:S(2)}, u32[]{:S(2)}) collective-permute-start(f32[32,8,128]{2,1,0:T(8,128)S(1)} %collective-permute-done.18.refs_3_), channel_id=1, source_target_pairs={{0,32},{32,0},{1,33},{33,1},{2,34},{34,2},{3,35},{35,3},{4,36},{36... | collective-permute-start | bytes 393224 | tf_op jit(solution)/shard_map/ppermute | solution.py:28

commit v6 on v5

--- a/solution.py
+++ b/solution.py
@@ -114,15 +114,23 @@
         out_ref[:, :, slot] = total if own else so_far[:, :, slot] + total
 
 
+def query_sum_kernel(me_ref, blocks_ref, *out_refs):
+    _, _, _, x = place(me_ref)
+    for k, out_ref in enumerate(out_refs):
+        target = lax.rem(x + k, 4)
+        total = blocks_ref[0, target]
+        for sender in range(1, 8):
+            total = total + blocks_ref[sender, target]
+        out_ref[...] = total
+
+
 def precond_kernel(me_ref, eig_ref, *refs):
-    parts_ref, blocks, out_ref, rot_in_ref = refs[0], refs[1:5], refs[5], refs[6]
+    parts, blocks, out_ref, rot_in_ref = refs[:4], refs[4:8], refs[8], refs[9]
     y, _, _, x = place(me_ref)
     for k in range(4):
         source = lax.rem(x + 4 - k, 4)
         rot_in_ref[pl.ds(pl.multiple_of(source * 64, 64), 64), :] = blocks[k][:, 64:, :].reshape(64, 128)
-    rot = parts_ref[0]
-    for sender in range(1, 32):
-        rot = rot + parts_ref[sender]
+    rot = parts[0][...] + parts[1][...] + parts[2][...] + parts[3][...]
     rot = rot.reshape(32, rot.shape[-1])
     lane_query = lax.broadcasted_iota(jnp.int32, rot.shape, 1) // QLEN
     count = rot.shape[1] // QLEN
@@ -290,12 +298,16 @@
         args=(query_grads, rot, *slabs[4:]),
         held=False,
     )
-    rot = exchange(rot.reshape(32, 4, 8, queries), ZX)
+    rot = exchange(rot, "z")
+    rots = call(query_sum_kernel, [((4, 8, queries), f32)] * 4, [HELD], me, args=(rot,))
+    rots = [rots[0], *rots[1:]]
+    for k in (1, 2, 3):
+        rots[k] = shifted(rots[k], "x", k)
     (precond,) = call(
         precond_kernel,
         [((32, 8, 128), f32)],
-        [VMEM] + [HELD] * 5,
-        me, args=(eigenvalues, rot, *blocks),
+        [VMEM] + [HELD] * 8,
+        me, args=(eigenvalues, *rots, *blocks),
         scratch=[pltpu.VMEM((queries, 128), f32)],
     )
     preconds = [precond]

time: 188 us -> 181 us (0.963)
  waiting for transfers between devices: 76.7 us -> 65.5 us
  starting transfers between devices: 56.1 us -> 60.2 us
  local copies, waits for them, and re-layouts: 4.27 us -> 1.42 us
  blocking collectives: 18 us -> 20.7 us
    ppermute x23 -> x26, waiting for transfers between devices: 55.8 us -> 46.8 us  [shifted(): return lax.ppermute(shard, axis, [(i, (i + hops) % n) for i in range(n)])]
    ppermute x23 -> x26, starting transfers between devices: 26 us -> 28.9 us  [shifted(): return lax.ppermute(shard, axis, [(i, (i + hops) % n) for i in range(n)])]
    unnamed x14, local copies, waits for them, and re-layouts: 2.9 us -> 0.03 us
    all_to_all x1, blocking collectives: 18 us -> 20.7 us  [exchange(): return lax.all_to_all(blocks, axis, 0, 0, tiled=True)]
    all_to_all x5, waiting for transfers between devices: 20.9 us -> 18.7 us  [exchange(): return lax.all_to_all(blocks, axis, 0, 0, tiled=True)]
    pallas_call x11 -> x12, Pallas kernels: 28 us -> 28.8 us  [call(): pl.pallas_call(kernel, out_shape=out_shape, grid_spec=pltpu.PrefetchScala...]
  transfers between devices with their start and end apart: 28 -> 31, of which waited for: 16 -> 18; matrix products, arithmetic and copies ran while one was open for 2% -> 2% of each run, Pallas kernels for 14% -> 15%
where the time goes in v6:
time: 181 us; the launch traced here: 180 us
  waiting for transfers between devices  65.5 us (36%)
  starting transfers between devices  60.2 us (33%)
  Pallas kernels  28.8 us (16%)
  blocking collectives  20.7 us (11%)
  other arithmetic  2.97 us (2%)
    ppermute x26, waiting for transfers between devices, shifted(): return lax.ppermute(shard, axis, [(i, (i + hops) % n) for i in range(n)])  46.8 us
    all_to_all x5, starting transfers between devices, exchange(): return lax.all_to_all(blocks, axis, 0, 0, tiled=True)  31.3 us
    ppermute x26, starting transfers between devices, shifted(): return lax.ppermute(shard, axis, [(i, (i + hops) % n) for i in range(n)])  28.9 us
    pallas_call x12, Pallas kernels, call(): pl.pallas_call(kernel, out_shape=out_shape, grid_spec=pltpu.PrefetchScala...  28.8 us
    all_to_all x1, blocking collectives, exchange(): return lax.all_to_all(blocks, axis, 0, 0, tiled=True)  20.7 us
    all_to_all x5, waiting for transfers between devices, exchange(): return lax.all_to_all(blocks, axis, 0, 0, tiled=True)  18.7 us
  transfers between devices with their start and end apart: 31, of which 18 were waited for; matrix products, arithmetic and copies ran while one was open for 2% of the time, Pallas kernels for 15%

profile of v6, /device:TPU:8, one launch (start us, length us, event | category | flops | bytes accessed | tf_op | source)
XLA Modules:
  0.0 179.9 jit_solution(1476985036012597398)
XLA Ops:
  0.0 2.0 %shard_map.85 = f32[32,8,512]{2,1,0:T(8,128)} custom-call(s32[1]{0:T(128)} %bitcast.me_ref, f32[32,28672]{1,0:T(8,128)} %basis_ref.3), custom_call_target="tpu_custom_call" | custom-call | tf_op jit(solution)/shard_map/pallas_call | solution.py:35
  2.1 11.3 %all-to-all-start.2 = ((f32[32,8,512]{2,1,0:T(8,128)}), f32[32,8,512]{2,1,0:T(8,128)S(1)}, u32[]{:S(2)}, u32[]{:S(2)}) async-start(f32[32,8,512]{2,1,0:T(8,128)} %shard_map.85), calls=%async_computation.2 | async-start | bytes 1048576 | tf_op jit(solution)/shard_map/all_to_all | solution.py:23
  13.4 2.2 %shard_map.82 = (f32[8,72,128]{2,1,0:T(8,128)S(1)}, f32[8,72,128]{2,1,0:T(8,128)S(1)}, f32[8,72,128]{2,1,0:T(8,128)S(1)}, f32[8,72,128]{2,1,0:T(8,128)S(1)}) custom-call(s32[1]{0:T(128)} %bitcast.me_ref, bf16[2048,256]{1,0:T(8,128)(2,1)} %acts_ref.1, bf16[256,256]{1,0:T(8,128)(2,1)} %query_ref.1, f32[128,8192]{1,0:T(8,128)} %basis_ref.2), custom_call_target="tpu_custom_call" | custom-call | tf_op jit(solution)/shard_map/pallas_call | solution.py:35
  15.6 3.1 %collective-permute-start.2 = (f32[8,72,128]{2,1,0:T(8,128)S(1)}, f32[8,72,128]{2,1,0:T(8,128)S(1)}, u32[]{:S(2)}, u32[]{:S(2)}) collective-permute-start(f32[8,72,128]{2,1,0:T(8,128)S(1)} %get-tuple-element.21), channel_id=1, source_target_pairs={{0,3},{1,0},{2,1},{3,2},{4,7},{5,4},{6,5},{7,6},{8,11},{9,8},{10,9... | collective-permute-start | bytes 884744 | tf_op jit(solution)/shard_map/ppermute | solution.py:28
  18.6 2.3 %collective-permute-start = (f32[8,72,128]{2,1,0:T(8,128)S(1)}, f32[8,72,128]{2,1,0:T(8,128)S(1)}, u32[]{:S(2)}, u32[]{:S(2)}) collective-permute-start(f32[8,72,128]{2,1,0:T(8,128)S(1)} %get-tuple-element.19), channel_id=1, source_target_pairs={{0,2},{1,3},{2,0},{3,1},{4,6},{5,7},{6,4},{7,5},{8,10},{9,11},{10,... | collective-permute-start | bytes 884744 | tf_op jit(solution)/shard_map/ppermute | solution.py:28
  21.0 10.3 %all-to-all-done.2 = f32[32,8,512]{2,1,0:T(8,128)S(1)} async-done(((f32[32,8,512]{2,1,0:T(8,128)}), f32[32,8,512]{2,1,0:T(8,128)S(1)}, u32[]{:S(2)}, u32[]{:S(2)}) %all-to-all-start.2) | async-done | bytes 524320 | tf_op jit(solution)/shard_map/all_to_all | solution.py:23
  31.7 2.6 %collective-permute-start.7 = (f32[8,4,8,512]{3,2,1,0:T(8,128)S(1)}, f32[8,4,8,512]{3,2,1,0:T(8,128)}, u32[]{:S(2)}, u32[]{:S(2)}) collective-permute-start(f32[8,4,8,512]{3,2,1,0:T(8,128)S(1)} %bitcast.3), channel_id=1, source_target_pairs={{0,128},{64,192},{128,0},{192,64},{1,129},{65,193},{129,1},{193,65... | collective-permute-start | bytes 1572872 | tf_op jit(solution)/shard_map/ppermute | solution.py:28
  34.6 1.6 collective-permute-start.8
  36.2 1.7 collective-permute-done.1
  37.8 0.8 add_add_fusion.1
  38.6 5.8 %all-to-all-start = ((f32[8,72,128]{2,1,0:T(8,128)}), f32[8,72,128]{2,1,0:T(8,128)S(1)}, u32[]{:S(2)}, u32[]{:S(2)}) async-start(f32[8,72,128]{2,1,0:T(8,128)} %add_add_fusion.1), calls=%async_computation | async-start | bytes 589824 | tf_op jit(solution)/shard_map/all_to_all | solution.py:23
  45.0 10.4 %collective-permute-done.7.refs_2_ = f32[8,4,8,512]{3,2,1,0:T(8,128)} collective-permute-done((f32[8,4,8,512]{3,2,1,0:T(8,128)S(1)}, f32[8,4,8,512]{3,2,1,0:T(8,128)}, u32[]{:S(2)}, u32[]{:S(2)}) %collective-permute-start.7) | collective-permute-done | bytes 524320 | tf_op jit(solution)/shard_map/ppermute | solution.py:28
  55.4 0.8 collective-permute-done.8.refs_3_
  56.3 0.7 broadcast_in_dim.2
  57.0 3.4 %all-to-all-start.1 = ((f32[8,72,128]{2,1,0:T(8,128)}), f32[8,72,128]{2,1,0:T(8,128)S(1)}, u32[]{:S(2)}, u32[]{:S(2)}) async-start(f32[8,72,128]{2,1,0:T(8,128)} %broadcast_in_dim.2), calls=%async_computation.1 | async-start | bytes 589824 | tf_op jit(solution)/shard_map/all_to_all | solution.py:23
  60.5 2.1 %shard_map.89.refs_0_ = f32[8,4,4,8,256]{4,3,2,1,0:T(8,128)S(1)} custom-call(s32[1]{0:T(128)} %bitcast.me_ref, bf16[256,896]{1,0:T(8,128)(2,1)} %grads_ref.9, f32[8,4,8,512]{3,2,1,0:T(8,128)S(1)} %bitcast.6, f32[8,4,8,512]{3,2,1,0:T(8,128)S(1)} %collective-permute-done.6.refs_1_, f32[8,4,8,512]{3,2,1,0:T(8,128)} %collective-permute-done.7.refs_2_, ...), custom_call_target="tpu_custom_call" | custom-call | tf_op jit(solution)/shard_map/pallas_call | solution.py:35
  62.6 2.8 %shard_map.90 = f32[8,4,4,8,256]{4,3,2,1,0:T(8,128)} custom-call(s32[1]{0:T(128)} %bitcast.me_ref, bf16[256,896]{1,0:T(8,128)(2,1)} %grads_ref.9, f32[8,4,4,8,256]{4,3,2,1,0:T(8,128)S(1)} %shard_map.89.refs_0_, f32[8,4,8,512]{3,2,1,0:T(8,128)S(1)} %collective-permute-done.9.refs_4_.refs_1_, f32[8,4,8,512]{3,2,1,0:T(8,128)S(1)} %collective-permute-done.10.refs_5_.refs_2_, ...), custom_call_target="tpu_custom_call" | custom-call | tf_op jit(solution)/shard_map/pallas_call | solution.py:35
  65.4 8.5 %all-to-all-done.1.block_ref.refs_4_ = f32[8,72,128]{2,1,0:T(8,128)S(1)} async-done(((f32[8,72,128]{2,1,0:T(8,128)}), f32[8,72,128]{2,1,0:T(8,128)S(1)}, u32[]{:S(2)}, u32[]{:S(2)}) %all-to-all-start.1) | async-done | bytes 294944 | tf_op jit(solution)/shard_map/all_to_all | solution.py:23
  73.9 4.2 %all-to-all-start.4 = ((f32[8,4,4,8,256]{4,3,2,1,0:T(8,128)}), f32[8,4,4,8,256]{4,3,2,1,0:T(8,128)}, u32[]{:S(2)}, u32[]{:S(2)}) async-start(f32[8,4,4,8,256]{4,3,2,1,0:T(8,128)} %shard_map.90), calls=%async_computation.4 | async-start | bytes 2097152 | tf_op jit(solution)/shard_map/all_to_all | solution.py:23
  78.1 1.4 collective-permute-start.4
  79.5 1.9 %collective-permute-start.5 = (f32[8,72,128]{2,1,0:T(8,128)S(1)}, f32[8,72,128]{2,1,0:T(8,128)S(1)}, u32[]{:S(2)}, u32[]{:S(2)}) collective-permute-start(f32[8,72,128]{2,1,0:T(8,128)S(1)} %all-to-all-done.1.block_ref.refs_4_), channel_id=1, source_target_pairs={{0,3},{1,0},{2,1},{3,2},{4,7},{5,4},{6,5},{7,6},{8,11},{9,8},{10,9... | collective-permute-start | bytes 884744 | tf_op jit(solution)/shard_map/ppermute | solution.py:28
  81.4 1.5 collective-permute-start.3
  82.9 3.7 %shard_map.83.so_far_ref = f32[4,128,896]{2,1,0:T(8,128)} custom-call(s32[1]{0:T(128)} %bitcast.me_ref, s32[4]{0:T(128)S(1)} %copy-done.6, bf16[2048,896]{1,0:T(8,128)(2,1)} %grads_ref.7, f32[8,72,128]{2,1,0:T(8,128)S(1)} %all-to-all-done.1.block_ref.refs_4_), custom_call_target="tpu_custom_call" | custom-call | tf_op jit(solution)/shard_map/pallas_call | solution.py:35
  86.6 2.1 %collective-permute-done.4.ahead_ref.refs_5_ = f32[8,72,128]{2,1,0:T(8,128)S(1)} collective-permute-done((f32[8,72,128]{2,1,0:T(8,128)S(1)}, f32[8,72,128]{2,1,0:T(8,128)S(1)}, u32[]{:S(2)}, u32[]{:S(2)}) %collective-permute-start.4) | collective-permute-done | bytes 294944 | tf_op jit(solution)/shard_map/ppermute | solution.py:28
  88.7 5.3 %collective-permute-done.5.behind_ref.refs_7_ = f32[8,72,128]{2,1,0:T(8,128)S(1)} collective-permute-done((f32[8,72,128]{2,1,0:T(8,128)S(1)}, f32[8,72,128]{2,1,0:T(8,128)S(1)}, u32[]{:S(2)}, u32[]{:S(2)}) %collective-permute-start.5) | collective-permute-done | bytes 294944 | tf_op jit(solution)/shard_map/ppermute | solution.py:28
  94.0 3.2 %shard_map.84.so_far_ref = f32[4,128,896]{2,1,0:T(8,128)S(1)} custom-call(s32[1]{0:T(128)} %bitcast.me_ref, s32[4]{0:T(128)S(1)} %copy-done.6, bf16[2048,896]{1,0:T(8,128)(2,1)} %grads_ref.7, f32[8,72,128]{2,1,0:T(8,128)S(1)} %collective-permute-done.4.ahead_ref.refs_5_, f32[8,72,128]{2,1,0:T(8,128)S(1)} %collective-permute-done.5.behind_ref.refs_7_, ...), custom_call_target="tpu_custom_call" | custom-call | tf_op jit(solution)/shard_map/pallas_call | solution.py:35
  97.2 4.0 %shard_map.86 = (f32[8,32,512]{2,1,0:T(8,128)S(1)}, bf16[2,512,512]{2,1,0:T(8,128)(2,1)S(1)}, bf16[2,512,512]{2,1,0:T(8,128)(2,1)S(1)}) custom-call(s32[1]{0:T(128)} %bitcast.me_ref, s32[4]{0:T(128)S(1)} %copy-done.6, bf16[2048,896]{1,0:T(8,128)(2,1)} %grads_ref.7, f32[8,72,128]{2,1,0:T(8,128)S(1)} %collective-permute-done.3.block_ref.refs_6_, ...), custom_call_target="tpu_custom_call" | custom-call | tf_op jit(solution)/shard_map/pallas_call | solution.py:35
  101.3 3.0 %shard_map.88 = (f32[8,32,512]{2,1,0:T(8,128)S(1)}, f32[8,32,512]{2,1,0:T(8,128)S(1)}) custom-call(s32[1]{0:T(128)} %bitcast.me_ref, bf16[2,512,512]{2,1,0:T(8,128)(2,1)S(1)} %get-tuple-element.22.high_ref, bf16[2,512,512]{2,1,0:T(8,128)(2,1)S(1)} %get-tuple-element.23.low_ref, f32[8,4,8,512]{3,2,1,0:T(8,128)S(1)} %bitcast.8, ...), custom_call_target="tpu_custom_call" | custom-call | tf_op jit(solution)/shard_map/pallas_call | solution.py:35
  104.3 4.2 %collective-permute-start.15 = (f32[8,32,512]{2,1,0:T(8,128)S(1)}, f32[8,32,512]{2,1,0:T(8,128)S(1)}, u32[]{:S(2)}, u32[]{:S(2)}) collective-permute-start(f32[8,32,512]{2,1,0:T(8,128)S(1)} %get-tuple-element.26), channel_id=1, source_target_pairs={{0,3},{1,0},{2,1},{3,2},{4,7},{5,4},{6,5},{7,6},{8,11},{9,8},{10,9... | collective-permute-start | bytes 1572872 | tf_op jit(solution)/shard_map/ppermute | solution.py:28
  108.5 1.0 collective-permute-start.13
  109.4 3.0 %shard_map.87 = f32[8,32,512]{2,1,0:T(8,128)} custom-call(s32[1]{0:T(128)} %bitcast.me_ref, bf16[2,512,512]{2,1,0:T(8,128)(2,1)S(1)} %get-tuple-element.22.high_ref, bf16[2,512,512]{2,1,0:T(8,128)(2,1)S(1)} %get-tuple-element.23.low_ref, f32[8,4,8,512]{3,2,1,0:T(8,128)S(1)} %bitcast.9, f32[8,4,8,512]{3,2,1,0:T(8,128)S(1)} %collective-permute-done.6.refs_1_, ...), custom_call_target="tpu_custom_call" | custom-call | tf_op jit(solution)/shard_map/pallas_call | solution.py:35
  112.4 14.0 %collective-permute-done.15 = f32[8,32,512]{2,1,0:T(8,128)S(1)} collective-permute-done((f32[8,32,512]{2,1,0:T(8,128)S(1)}, f32[8,32,512]{2,1,0:T(8,128)S(1)}, u32[]{:S(2)}, u32[]{:S(2)}) %collective-permute-start.15) | collective-permute-done | bytes 524320 | tf_op jit(solution)/shard_map/ppermute | solution.py:28
  126.4 3.3 %collective-permute-done.13 = f32[8,32,512]{2,1,0:T(8,128)S(1)} collective-permute-done((f32[8,32,512]{2,1,0:T(8,128)S(1)}, f32[8,32,512]{2,1,0:T(8,128)S(1)}, u32[]{:S(2)}, u32[]{:S(2)}) %collective-permute-start.13) | collective-permute-done | bytes 524320 | tf_op jit(solution)/shard_map/ppermute | solution.py:28
  129.8 2.0 %add_add_fusion = f32[8,32,512]{2,1,0:T(8,128)} fusion(f32[8,32,512]{2,1,0:T(8,128)S(1)} %collective-permute-done.15, f32[8,32,512]{2,1,0:T(8,128)S(1)} %collective-permute-done.14, f32[8,32,512]{2,1,0:T(8,128)} %shard_map.87, f32[8,32,512]{2,1,0:T(8,128)S(1)} %collective-permute-done.13), kind=kLoop, calls=%fused_computation | loop fusion | flops 393216 | bytes 2621440 | tf_op jit(solution)/shard_map/add | solution.py:356
  131.8 6.5 %all-to-all-start.3 = ((f32[8,32,512]{2,1,0:T(8,128)}), f32[8,32,512]{2,1,0:T(8,128)S(1)}, u32[]{:S(2)}, u32[]{:S(2)}) async-start(f32[8,32,512]{2,1,0:T(8,128)} %add_add_fusion), calls=%async_computation.3 | async-start | bytes 1048576 | tf_op jit(solution)/shard_map/all_to_all | solution.py:23
  138.3 1.3 shard_map.91
  139.6 2.1 %collective-permute-start.17 = (f32[4,8,256]{2,1,0:T(8,128)S(1)}, f32[4,8,256]{2,1,0:T(8,128)S(1)}, u32[]{:S(2)}, u32[]{:S(2)}) collective-permute-start(f32[4,8,256]{2,1,0:T(8,128)S(1)} %get-tuple-element.29), channel_id=1, source_target_pairs={{0,2},{1,3},{2,0},{3,1},{4,6},{5,7},{6,4},{7,5},{8,10},{9,11},{10,... | collective-permute-start | bytes 98312 | tf_op jit(solution)/shard_map/ppermute | solution.py:28
  141.7 1.8 %collective-permute-start.18 = (f32[4,8,256]{2,1,0:T(8,128)S(1)}, f32[4,8,256]{2,1,0:T(8,128)S(1)}, u32[]{:S(2)}, u32[]{:S(2)}) collective-permute-start(f32[4,8,256]{2,1,0:T(8,128)S(1)} %get-tuple-element.30), channel_id=1, source_target_pairs={{0,3},{1,0},{2,1},{3,2},{4,7},{5,4},{6,5},{7,6},{8,11},{9,8},{10,9... | collective-permute-start | bytes 98312 | tf_op jit(solution)/shard_map/ppermute | solution.py:28
  143.5 1.2 collective-permute-done.16.refs_1_
  145.1 0.8 collective-permute-done.18.refs_3_
  146.0 1.2 shard_map.92.refs_0_
  147.1 1.5 collective-permute-start.19
  148.6 3.1 %collective-permute-start.20 = (f32[32,8,128]{2,1,0:T(8,128)S(1)}, f32[32,8,128]{2,1,0:T(8,128)S(1)}, u32[]{:S(2)}, u32[]{:S(2)}) collective-permute-start(f32[32,8,128]{2,1,0:T(8,128)S(1)} %shard_map.92.refs_0_), channel_id=1, source_target_pairs={{0,128},{64,192},{128,0},{192,64},{1,129},{65,193},{129,1},{193,65... | collective-permute-start | bytes 393224 | tf_op jit(solution)/shard_map/ppermute | solution.py:28
  152.1 1.2 collective-permute-done.19.refs_1_
  153.3 1.9 %collective-permute-done.20.refs_2_ = f32[32,8,128]{2,1,0:T(8,128)S(1)} collective-permute-done((f32[32,8,128]{2,1,0:T(8,128)S(1)}, f32[32,8,128]{2,1,0:T(8,128)S(1)}, u32[]{:S(2)}, u32[]{:S(2)}) %collective-permute-start.20) | collective-permute-done | bytes 131104 | tf_op jit(solution)/shard_map/ppermute | solution.py:28
  155.2 1.5 collective-permute-done.21.refs_3_
  156.7 1.3 collective-permute-done.25.refs_7_
  158.4 20.7 %all_to_all.30 = f32[32,8,128]{2,1,0:T(8,128)S(1)} all-to-all(f32[32,8,128]{2,1,0:T(8,128)S(1)} %shard_map.93), channel_id=1, replica_groups=mesh['y'=4,'core'=2,'z'=8,'x'=4] {'z','x'}, dimensions={0} | all-to-all | bytes 262144 | tf_op jit(solution)/shard_map/all_to_all | solution.py:23
  (47 shorter events, 3.4 us)
Async XLA Ops:
  2.1 29.2 %all-to-all-start.2 = ((f32[32,8,512]{2,1,0:T(8,128)}), f32[32,8,512]{2,1,0:T(8,128)S(1)}, u32[]{:S(2)}, u32[]{:S(2)}) async-start(f32[32,8,512]{2,1,0:T(8,128)} %shard_map.85), calls=%async_computation.2 | async-start | bytes 1048576 | tf_op jit(solution)/shard_map/all_to_all | solution.py:23
  15.6 19.0 %collective-permute-start.2 = (f32[8,72,128]{2,1,0:T(8,128)S(1)}, f32[8,72,128]{2,1,0:T(8,128)S(1)}, u32[]{:S(2)}, u32[]{:S(2)}) collective-permute-start(f32[8,72,128]{2,1,0:T(8,128)S(1)} %get-tuple-element.21), channel_id=1, source_target_pairs={{0,3},{1,0},{2,1},{3,2},{4,7},{5,4},{6,5},{7,6},{8,11},{9,8},{10,9... | collective-permute-start | bytes 884744 | tf_op jit(solution)/shard_map/ppermute | solution.py:28
  18.6 19.2 %collective-permute-start.1 = (f32[8,72,128]{2,1,0:T(8,128)S(1)}, f32[8,72,128]{2,1,0:T(8,128)S(1)}, u32[]{:S(2)}, u32[]{:S(2)}) collective-permute-start(f32[8,72,128]{2,1,0:T(8,128)S(1)} %get-tuple-element.20), channel_id=1, source_target_pairs={{0,1},{1,2},{2,3},{3,0},{4,5},{5,6},{6,7},{7,4},{8,9},{9,10},{10,1... | collective-permute-start | bytes 884744 | tf_op jit(solution)/shard_map/ppermute | solution.py:28
  18.6 19.2 %collective-permute-start = (f32[8,72,128]{2,1,0:T(8,128)S(1)}, f32[8,72,128]{2,1,0:T(8,128)S(1)}, u32[]{:S(2)}, u32[]{:S(2)}) collective-permute-start(f32[8,72,128]{2,1,0:T(8,128)S(1)} %get-tuple-element.19), channel_id=1, source_target_pairs={{0,2},{1,3},{2,0},{3,1},{4,6},{5,7},{6,4},{7,5},{8,10},{9,11},{10,... | collective-permute-start | bytes 884744 | tf_op jit(solution)/shard_map/ppermute | solution.py:28
  31.2 13.8 %collective-permute-start.6 = (f32[8,4,8,512]{3,2,1,0:T(8,128)S(1)}, f32[8,4,8,512]{3,2,1,0:T(8,128)S(1)}, u32[]{:S(2)}, u32[]{:S(2)}) collective-permute-start(f32[8,4,8,512]{3,2,1,0:T(8,128)S(1)} %bitcast.2), channel_id=1, source_target_pairs={{0,192},{64,0},{128,64},{192,128},{1,193},{65,1},{129,65},{193,129... | collective-permute-start | bytes 1572872 | tf_op jit(solution)/shard_map/ppermute | solution.py:28
  31.7 23.7 %collective-permute-start.7 = (f32[8,4,8,512]{3,2,1,0:T(8,128)S(1)}, f32[8,4,8,512]{3,2,1,0:T(8,128)}, u32[]{:S(2)}, u32[]{:S(2)}) collective-permute-start(f32[8,4,8,512]{3,2,1,0:T(8,128)S(1)} %bitcast.3), channel_id=1, source_target_pairs={{0,128},{64,192},{128,0},{192,64},{1,129},{65,193},{129,1},{193,65... | collective-permute-start | bytes 1572872 | tf_op jit(solution)/shard_map/ppermute | solution.py:28
  34.6 21.7 %collective-permute-start.8 = (f32[8,4,8,512]{3,2,1,0:T(8,128)S(1)}, f32[8,4,8,512]{3,2,1,0:T(8,128)}, u32[]{:S(2)}, u32[]{:S(2)}) collective-permute-start(f32[8,4,8,512]{3,2,1,0:T(8,128)S(1)} %bitcast.4), channel_id=1, source_target_pairs={{0,64},{64,128},{128,192},{192,0},{1,65},{65,129},{129,193},{193,1... | collective-permute-start | bytes 1572872 | tf_op jit(solution)/shard_map/ppermute | solution.py:28
  38.6 17.6 %all-to-all-start = ((f32[8,72,128]{2,1,0:T(8,128)}), f32[8,72,128]{2,1,0:T(8,128)S(1)}, u32[]{:S(2)}, u32[]{:S(2)}) async-start(f32[8,72,128]{2,1,0:T(8,128)} %add_add_fusion.1), calls=%async_computation | async-start | bytes 589824 | tf_op jit(solution)/shard_map/all_to_all | solution.py:23
  44.4 18.1 %collective-permute-start.9 = (f32[8,4,8,512]{3,2,1,0:T(8,128)S(1)}, f32[8,4,8,512]{3,2,1,0:T(8,128)S(1)}, u32[]{:S(2)}, u32[]{:S(2)}) collective-permute-start(f32[8,4,8,512]{3,2,1,0:T(8,128)S(1)} %bitcast.5), channel_id=1, source_target_pairs={{0,32},{32,0},{1,33},{33,1},{2,34},{34,2},{3,35},{35,3},{4,36},{36... | collective-permute-start | bytes 1572872 | tf_op jit(solution)/shard_map/ppermute | solution.py:28
  45.0 17.6 %collective-permute-start.10 = (f32[8,4,8,512]{3,2,1,0:T(8,128)S(1)}, f32[8,4,8,512]{3,2,1,0:T(8,128)S(1)}, u32[]{:S(2)}, u32[]{:S(2)}) collective-permute-start(f32[8,4,8,512]{3,2,1,0:T(8,128)S(1)} %collective-permute-done.6.refs_1_), channel_id=1, source_target_pairs={{0,32},{32,0},{1,33},{33,1},{2,34},{34,2},{3,35},{35,3},{4,36},{36... | collective-permute-start | bytes 1572872 | tf_op jit(solution)/shard_map/ppermute | solution.py:28
  55.4 7.2 %collective-permute-start.11 = (f32[8,4,8,512]{3,2,1,0:T(8,128)}, f32[8,4,8,512]{3,2,1,0:T(8,128)S(1)}, u32[]{:S(2)}, u32[]{:S(2)}) collective-permute-start(f32[8,4,8,512]{3,2,1,0:T(8,128)} %collective-permute-done.7.refs_2_), channel_id=1, source_target_pairs={{0,32},{32,0},{1,33},{33,1},{2,34},{34,2},{3,35},{35,3},{4,36},{36... | collective-permute-start | bytes 1572872 | tf_op jit(solution)/shard_map/ppermute | solution.py:28
  56.2 6.4 %collective-permute-start.12 = (f32[8,4,8,512]{3,2,1,0:T(8,128)}, f32[8,4,8,512]{3,2,1,0:T(8,128)S(1)}, u32[]{:S(2)}, u32[]{:S(2)}) collective-permute-start(f32[8,4,8,512]{3,2,1,0:T(8,128)} %collective-permute-done.8.refs_3_), channel_id=1, source_target_pairs={{0,32},{32,0},{1,33},{33,1},{2,34},{34,2},{3,35},{35,3},{4,36},{36... | collective-permute-start | bytes 1572872 | tf_op jit(solution)/shard_map/ppermute | solution.py:28
  57.0 16.9 %all-to-all-start.1 = ((f32[8,72,128]{2,1,0:T(8,128)}), f32[8,72,128]{2,1,0:T(8,128)S(1)}, u32[]{:S(2)}, u32[]{:S(2)}) async-start(f32[8,72,128]{2,1,0:T(8,128)} %broadcast_in_dim.2), calls=%async_computation.1 | async-start | bytes 589824 | tf_op jit(solution)/shard_map/all_to_all | solution.py:23
  62.6 20.4 %copy-start.6 = (s32[4]{0:T(128)S(1)}, s32[4]{0:T(128)}, u32[]{:S(2)}) copy-start(s32[4]{0:T(128)} %len_ref.5) | copy-start | bytes 52
  73.9 57.9 %all-to-all-start.4 = ((f32[8,4,4,8,256]{4,3,2,1,0:T(8,128)}), f32[8,4,4,8,256]{4,3,2,1,0:T(8,128)}, u32[]{:S(2)}, u32[]{:S(2)}) async-start(f32[8,4,4,8,256]{4,3,2,1,0:T(8,128)} %shard_map.90), calls=%async_computation.4 | async-start | bytes 2097152 | tf_op jit(solution)/shard_map/all_to_all | solution.py:23
  78.1 10.6 %collective-permute-start.4 = (f32[8,72,128]{2,1,0:T(8,128)S(1)}, f32[8,72,128]{2,1,0:T(8,128)S(1)}, u32[]{:S(2)}, u32[]{:S(2)}) collective-permute-start(f32[8,72,128]{2,1,0:T(8,128)S(1)} %all-to-all-done.1.block_ref.refs_4_), channel_id=1, source_target_pairs={{0,1},{1,2},{2,3},{3,0},{4,5},{5,6},{6,7},{7,4},{8,9},{9,10},{10,1... | collective-permute-start | bytes 884744 | tf_op jit(solution)/shard_map/ppermute | solution.py:28
  79.5 14.5 %collective-permute-start.5 = (f32[8,72,128]{2,1,0:T(8,128)S(1)}, f32[8,72,128]{2,1,0:T(8,128)S(1)}, u32[]{:S(2)}, u32[]{:S(2)}) collective-permute-start(f32[8,72,128]{2,1,0:T(8,128)S(1)} %all-to-all-done.1.block_ref.refs_4_), channel_id=1, source_target_pairs={{0,3},{1,0},{2,1},{3,2},{4,7},{5,4},{6,5},{7,6},{8,11},{9,8},{10,9... | collective-permute-start | bytes 884744 | tf_op jit(solution)/shard_map/ppermute | solution.py:28
  81.4 15.8 %collective-permute-start.3 = (f32[8,72,128]{2,1,0:T(8,128)S(1)}, f32[8,72,128]{2,1,0:T(8,128)S(1)}, u32[]{:S(2)}, u32[]{:S(2)}) collective-permute-start(f32[8,72,128]{2,1,0:T(8,128)S(1)} %all-to-all-done.1.block_ref.refs_4_), channel_id=1, source_target_pairs={{0,2},{1,3},{2,0},{3,1},{4,6},{5,7},{6,4},{7,5},{8,10},{9,11},{10,... | collective-permute-start | bytes 884744 | tf_op jit(solution)/shard_map/ppermute | solution.py:28
  88.7 8.5 %copy-start = (f32[8,72,128]{2,1,0:T(8,128)}, f32[8,72,128]{2,1,0:T(8,128)S(1)}, u32[]{:S(2)}) copy-start(f32[8,72,128]{2,1,0:T(8,128)S(1)} %collective-permute-done.4.ahead_ref.refs_5_) | copy-start | bytes 884740
  94.0 3.2 %copy-start.2 = (f32[8,72,128]{2,1,0:T(8,128)}, f32[8,72,128]{2,1,0:T(8,128)S(1)}, u32[]{:S(2)}) copy-start(f32[8,72,128]{2,1,0:T(8,128)S(1)} %collective-permute-done.5.behind_ref.refs_7_) | copy-start | bytes 884740
  97.2 4.0 %copy-start.4 = (f32[8,72,128]{2,1,0:T(8,128)}, f32[8,72,128]{2,1,0:T(8,128)S(1)}, u32[]{:S(2)}) copy-start(f32[8,72,128]{2,1,0:T(8,128)S(1)} %collective-permute-done.3.block_ref.refs_6_) | copy-start | bytes 884740
  104.3 22.1 %collective-permute-start.15 = (f32[8,32,512]{2,1,0:T(8,128)S(1)}, f32[8,32,512]{2,1,0:T(8,128)S(1)}, u32[]{:S(2)}, u32[]{:S(2)}) collective-permute-start(f32[8,32,512]{2,1,0:T(8,128)S(1)} %get-tuple-element.26), channel_id=1, source_target_pairs={{0,3},{1,0},{2,1},{3,2},{4,7},{5,4},{6,5},{7,6},{8,11},{9,8},{10,9... | collective-permute-start | bytes 1572872 | tf_op jit(solution)/shard_map/ppermute | solution.py:28
  108.5 18.0 %collective-permute-start.14 = (f32[8,32,512]{2,1,0:T(8,128)S(1)}, f32[8,32,512]{2,1,0:T(8,128)S(1)}, u32[]{:S(2)}, u32[]{:S(2)}) collective-permute-start(f32[8,32,512]{2,1,0:T(8,128)S(1)} %get-tuple-element.25), channel_id=1, source_target_pairs={{0,2},{1,3},{2,0},{3,1},{4,6},{5,7},{6,4},{7,5},{8,10},{9,11},{10,... | collective-permute-start | bytes 1572872 | tf_op jit(solution)/shard_map/ppermute | solution.py:28
  108.5 21.3 %collective-permute-start.13 = (f32[8,32,512]{2,1,0:T(8,128)S(1)}, f32[8,32,512]{2,1,0:T(8,128)S(1)}, u32[]{:S(2)}, u32[]{:S(2)}) collective-permute-start(f32[8,32,512]{2,1,0:T(8,128)S(1)} %get-tuple-element.24), channel_id=1, source_target_pairs={{0,1},{1,2},{2,3},{3,0},{4,5},{5,6},{6,7},{7,4},{8,9},{9,10},{10,1... | collective-permute-start | bytes 1572872 | tf_op jit(solution)/shard_map/ppermute | solution.py:28
  112.4 33.5 %copy-start.1 = (f32[8,72,128]{2,1,0:T(8,128)S(1)}, f32[8,72,128]{2,1,0:T(8,128)}, u32[]{:S(2)}) copy-start(f32[8,72,128]{2,1,0:T(8,128)} %copy-done) | copy-start | bytes 884740
  112.4 33.5 %copy-start.3 = (f32[8,72,128]{2,1,0:T(8,128)S(1)}, f32[8,72,128]{2,1,0:T(8,128)}, u32[]{:S(2)}) copy-start(f32[8,72,128]{2,1,0:T(8,128)} %copy-done.2) | copy-start | bytes 884740
  112.4 33.5 %copy-start.5 = (f32[8,72,128]{2,1,0:T(8,128)S(1)}, f32[8,72,128]{2,1,0:T(8,128)}, u32[]{:S(2)}) copy-start(f32[8,72,128]{2,1,0:T(8,128)} %copy-done.4) | copy-start | bytes 884740
  131.8 24.9 %all-to-all-start.3 = ((f32[8,32,512]{2,1,0:T(8,128)}), f32[8,32,512]{2,1,0:T(8,128)S(1)}, u32[]{:S(2)}, u32[]{:S(2)}) async-start(f32[8,32,512]{2,1,0:T(8,128)} %add_add_fusion), calls=%async_computation.3 | async-start | bytes 1048576 | tf_op jit(solution)/shard_map/all_to_all | solution.py:23
  139.5 5.2 %collective-permute-start.16 = (f32[4,8,256]{2,1,0:T(8,128)S(1)}, f32[4,8,256]{2,1,0:T(8,128)S(1)}, u32[]{:S(2)}, u32[]{:S(2)}) collective-permute-start(f32[4,8,256]{2,1,0:T(8,128)S(1)} %get-tuple-element.28), channel_id=1, source_target_pairs={{0,1},{1,2},{2,3},{3,0},{4,5},{5,6},{6,7},{7,4},{8,9},{9,10},{10,1... | collective-permute-start | bytes 98312 | tf_op jit(solution)/shard_map/ppermute | solution.py:28
  139.6 5.5 %collective-permute-start.17 = (f32[4,8,256]{2,1,0:T(8,128)S(1)}, f32[4,8,256]{2,1,0:T(8,128)S(1)}, u32[]{:S(2)}, u32[]{:S(2)}) collective-permute-start(f32[4,8,256]{2,1,0:T(8,128)S(1)} %get-tuple-element.29), channel_id=1, source_target_pairs={{0,2},{1,3},{2,0},{3,1},{4,6},{5,7},{6,4},{7,5},{8,10},{9,11},{10,... | collective-permute-start | bytes 98312 | tf_op jit(solution)/shard_map/ppermute | solution.py:28
  141.7 4.3 %collective-permute-start.18 = (f32[4,8,256]{2,1,0:T(8,128)S(1)}, f32[4,8,256]{2,1,0:T(8,128)S(1)}, u32[]{:S(2)}, u32[]{:S(2)}) collective-permute-start(f32[4,8,256]{2,1,0:T(8,128)S(1)} %get-tuple-element.30), channel_id=1, source_target_pairs={{0,3},{1,0},{2,1},{3,2},{4,7},{5,4},{6,5},{7,6},{8,11},{9,8},{10,9... | collective-permute-start | bytes 98312 | tf_op jit(solution)/shard_map/ppermute | solution.py:28
  147.1 6.2 %collective-permute-start.19 = (f32[32,8,128]{2,1,0:T(8,128)S(1)}, f32[32,8,128]{2,1,0:T(8,128)S(1)}, u32[]{:S(2)}, u32[]{:S(2)}) collective-permute-start(f32[32,8,128]{2,1,0:T(8,128)S(1)} %shard_map.92.refs_0_), channel_id=1, source_target_pairs={{0,64},{64,128},{128,192},{192,0},{1,65},{65,129},{129,193},{193,1... | collective-permute-start | bytes 393224 | tf_op jit(solution)/shard_map/ppermute | solution.py:28
  148.6 6.5 %collective-permute-start.20 = (f32[32,8,128]{2,1,0:T(8,128)S(1)}, f32[32,8,128]{2,1,0:T(8,128)S(1)}, u32[]{:S(2)}, u32[]{:S(2)}) collective-permute-start(f32[32,8,128]{2,1,0:T(8,128)S(1)} %shard_map.92.refs_0_), channel_id=1, source_target_pairs={{0,128},{64,192},{128,0},{192,64},{1,129},{65,193},{129,1},{193,65... | collective-permute-start | bytes 393224 | tf_op jit(solution)/shard_map/ppermute | solution.py:28
  151.7 5.0 %collective-permute-start.21 = (f32[32,8,128]{2,1,0:T(8,128)S(1)}, f32[32,8,128]{2,1,0:T(8,128)S(1)}, u32[]{:S(2)}, u32[]{:S(2)}) collective-permute-start(f32[32,8,128]{2,1,0:T(8,128)S(1)} %shard_map.92.refs_0_), channel_id=1, source_target_pairs={{0,192},{64,0},{128,64},{192,128},{1,193},{65,1},{129,65},{193,129... | collective-permute-start | bytes 393224 | tf_op jit(solution)/shard_map/ppermute | solution.py:28
  152.1 4.6 %collective-permute-start.22 = (f32[32,8,128]{2,1,0:T(8,128)S(1)}, f32[32,8,128]{2,1,0:T(8,128)S(1)}, u32[]{:S(2)}, u32[]{:S(2)}) collective-permute-start(f32[32,8,128]{2,1,0:T(8,128)S(1)} %shard_map.92.refs_0_), channel_id=1, source_target_pairs={{0,32},{32,0},{1,33},{33,1},{2,34},{34,2},{3,35},{35,3},{4,36},{36... | collective-permute-start | bytes 393224 | tf_op jit(solution)/shard_map/ppermute | solution.py:28
  153.3 3.4 %collective-permute-start.23 = (f32[32,8,128]{2,1,0:T(8,128)S(1)}, f32[32,8,128]{2,1,0:T(8,128)S(1)}, u32[]{:S(2)}, u32[]{:S(2)}) collective-permute-start(f32[32,8,128]{2,1,0:T(8,128)S(1)} %collective-permute-done.19.refs_1_), channel_id=1, source_target_pairs={{0,32},{32,0},{1,33},{33,1},{2,34},{34,2},{3,35},{35,3},{4,36},{36... | collective-permute-start | bytes 393224 | tf_op jit(solution)/shard_map/ppermute | solution.py:28
  155.2 1.5 collective-permute-start.24
  156.7 1.3 collective-permute-start.25

commit v7 on v6

--- a/solution.py
+++ b/solution.py
@@ -28,7 +28,7 @@
     return lax.ppermute(shard, axis, [(i, (i + hops) % n) for i in range(n)])
 
 
-def call(kernel, outs, in_specs, me, *, args, grid=1, scratch=(), held=True):
+def call(kernel, outs, in_specs, me, *, args, grid=1, scratch=(), held=True, out_spec=VMEM):
     out_shape = [(pltpu.VMEM if held else pltpu.HBM)(*o) for o in outs]
     spaces = [pltpu.VMEM if spec is HELD else None if spec is SMEM else pltpu.HBM for spec in in_specs]
     args = [a if space is None else pltpu.with_memory_space_constraint(a, space) for a, space in zip(args, spaces)]
@@ -39,7 +39,7 @@
             num_scalar_prefetch=1,
             grid=(grid,),
             in_specs=in_specs,
-            out_specs=[VMEM] * len(out_shape),
+            out_specs=[out_spec] * len(out_shape),
             scratch_shapes=list(scratch),
         ),
         compiler_params=pltpu.CompilerParams(vmem_limit_bytes=28 << 20),
@@ -167,18 +167,20 @@
     first = lax.rem(x + 4 - hops, 4) * 512
     high, low = split(block_ref[:, :64, :].reshape(512, 128).T)
     pair = jnp.concatenate([high, low], 0)
-    token = first + lax.broadcasted_iota(jnp.int32, pair.shape, 1)
-    begin = jnp.int32(0)
-    for doc in range(4):
-        end = begin + len_ref[doc]
-
-        @pl.when((begin < first + 512) & (end > first))
-        def _(begin=begin, end=end, doc=doc):
-            masked = jnp.where((token >= begin) & (token < end), pair, jnp.zeros_like(pair))
-            both = dot_nn(masked, grads_ref[...])
-            total_ref[doc] += both[:128] + both[128:]
-
-        begin = end
+    for part in (0, 256):
+        half = pair[:, part : part + 256]
+        token = first + part + lax.broadcasted_iota(jnp.int32, half.shape, 1)
+        begin = jnp.int32(0)
+        for doc in range(4):
+            end = begin + len_ref[doc]
+
+            @pl.when((begin < first + part + 256) & (end > first + part))
+            def _(begin=begin, end=end, doc=doc, part=part, half=half, token=token):
+                masked = jnp.where((token >= begin) & (token < end), half, jnp.zeros_like(half))
+                both = dot_nn(masked, grads_ref[part : part + 256, :])
+                total_ref[doc] += both[:128] + both[128:]
+
+            begin = end
 
 
 def outer_own_kernel(me_ref, len_ref, grads_ref, block_ref, total_ref):
@@ -220,7 +222,7 @@
 
 
 def score_kernel(me_ref, blocks_ref, *refs):
-    preconds, out_ref = refs[:8], refs[8]
+    preconds, out_ref, sums_ref = refs[:8], refs[8], refs[9]
     y, core, _, _ = place(me_ref)
     train = blocks_ref[0]
     for sender in range(1, 8):
@@ -237,9 +239,17 @@
                 for doc in range(4):
                     product = value * row[:, 128 * doc : 128 * doc + 128]
                     sums[doc] = product if sums[doc] is None else sums[doc] + product
-        for q in range(8):
-            for doc in range(4):
-                out_ref[4 * owner + q // 2, 4 * (q % 2) + doc : 4 * (q % 2) + doc + 1, :] = sums[doc][q : q + 1]
+        for doc in range(4):
+            sums_ref[doc, pl.ds(pl.multiple_of(8 * owner, 8), 8), :] = sums[doc]
+    lane = lax.broadcasted_iota(jnp.int32, out_ref.shape, 1)
+    scores = jnp.zeros(out_ref.shape, jnp.float32)
+    for doc in range(4):
+        scores = jnp.where(lane == doc, jnp.sum(sums_ref[doc], axis=1, keepdims=True), scores)
+    out_ref[...] = scores
+
+
+def train_sum_kernel(me_ref, *refs):
+    refs[4][...] = refs[0][...] + refs[1][...] + refs[2][...] + refs[3][...]
 
 
 def local(
@@ -353,11 +363,20 @@
     )
     for k in (1, 3):
         sent[k] = shifted(sent[k], "x", k)
-    train = sent[0] + sent[1] + sent[2] + sent[3]
+    part_spec = pl.BlockSpec((2, 32, 512), lambda i, me: (i, 0, 0))
+    (train,) = call(
+        train_sum_kernel, [block_shape], [part_spec] * 4, me, args=sent, grid=4, held=False, out_spec=part_spec
+    )
     train = exchange(train, "z")
 
-    (partial_scores,) = call(score_kernel, [((32, 8, 128), f32)], [HELD] * 9, me, args=(train, *preconds))
-    return jnp.sum(exchange(partial_scores, ZX), axis=(0, 2)).reshape(2, 4)
+    (partial_scores,) = call(
+        score_kernel,
+        [((64, 128), f32)],
+        [HELD] * 9,
+        me, args=(train, *preconds),
+        scratch=[pltpu.VMEM((4, 64, 128), f32)],
+    )
+    return jnp.sum(exchange(partial_scores.reshape(32, 2, 128), ZX), axis=0)[:, :4]
 
 
 def solution(mesh):

time: 181 us -> 182 us (level)
  Pallas kernels: 28.8 us -> 32.6 us
  blocking collectives: 20.7 us -> 18.2 us
    pallas_call x12 -> x13, Pallas kernels: 28.8 us -> 32.6 us  [call(): pl.pallas_call(kernel, out_shape=out_shape, grid_spec=pltpu.PrefetchScala...]
    all_to_all x1, blocking collectives: 20.7 us -> 18.2 us  [exchange(): return lax.all_to_all(blocks, axis, 0, 0, tiled=True)]
    add x1 -> x0, other arithmetic: 2.04 us -> none  [local(): train = sent[0] + sent[1] + sent[2] + sent[3]]
  transfers between devices with their start and end apart: 31 -> 31, of which waited for: 18 -> 19; matrix products, arithmetic and copies ran while one was open for 2% -> 1% of each run, Pallas kernels for 15% -> 17%
where the time goes in v7:
time: 182 us; the launch traced here: 180 us
  waiting for transfers between devices  65.4 us (36%)
  starting transfers between devices  60.6 us (33%)
  Pallas kernels  32.6 us (18%)
  blocking collectives  18.2 us (10%)
  local copies, waits for them, and re-layouts  1.95 us (1%)
    ppermute x26, waiting for transfers between devices, shifted(): return lax.ppermute(shard, axis, [(i, (i + hops) % n) for i in range(n)])  46.7 us
    pallas_call x13, Pallas kernels, call(): pl.pallas_call(kernel, out_shape=out_shape, grid_spec=pltpu.PrefetchScala...  32.6 us
    all_to_all x5, starting transfers between devices, exchange(): return lax.all_to_all(blocks, axis, 0, 0, tiled=True)  31.3 us
    ppermute x26, starting transfers between devices, shifted(): return lax.ppermute(shard, axis, [(i, (i + hops) % n) for i in range(n)])  29.2 us
    all_to_all x5, waiting for transfers between devices, exchange(): return lax.all_to_all(blocks, axis, 0, 0, tiled=True)  18.7 us
    all_to_all x1, blocking collectives, exchange(): return lax.all_to_all(blocks, axis, 0, 0, tiled=True)  18.2 us
  transfers between devices with their start and end apart: 31, of which 19 were waited for; matrix products, arithmetic and copies ran while one was open for 1% of the time, Pallas kernels for 17%

profile of v7, /device:TPU:8, one launch (start us, length us, event | category | flops | bytes accessed | tf_op | source)
XLA Modules:
  0.0 180.4 jit_solution(3102859247263425358)
XLA Ops:
  0.0 2.1 %shard_map.85 = f32[32,8,512]{2,1,0:T(8,128)} custom-call(s32[1]{0:T(128)} %bitcast.me_ref, f32[32,28672]{1,0:T(8,128)} %basis_ref.3), custom_call_target="tpu_custom_call" | custom-call | tf_op jit(solution)/shard_map/pallas_call | solution.py:35
  2.1 11.3 %all-to-all-start.2 = ((f32[32,8,512]{2,1,0:T(8,128)}), f32[32,8,512]{2,1,0:T(8,128)S(1)}, u32[]{:S(2)}, u32[]{:S(2)}) async-start(f32[32,8,512]{2,1,0:T(8,128)} %shard_map.85), calls=%async_computation.2 | async-start | bytes 1048576 | tf_op jit(solution)/shard_map/all_to_all | solution.py:23
  13.4 2.2 %shard_map.82 = (f32[8,72,128]{2,1,0:T(8,128)S(1)}, f32[8,72,128]{2,1,0:T(8,128)S(1)}, f32[8,72,128]{2,1,0:T(8,128)S(1)}, f32[8,72,128]{2,1,0:T(8,128)S(1)}) custom-call(s32[1]{0:T(128)} %bitcast.me_ref, bf16[2048,256]{1,0:T(8,128)(2,1)} %acts_ref.1, bf16[256,256]{1,0:T(8,128)(2,1)} %query_ref.1, f32[128,8192]{1,0:T(8,128)} %basis_ref.2), custom_call_target="tpu_custom_call" | custom-call | tf_op jit(solution)/shard_map/pallas_call | solution.py:35
  15.6 3.1 %collective-permute-start.2 = (f32[8,72,128]{2,1,0:T(8,128)S(1)}, f32[8,72,128]{2,1,0:T(8,128)S(1)}, u32[]{:S(2)}, u32[]{:S(2)}) collective-permute-start(f32[8,72,128]{2,1,0:T(8,128)S(1)} %get-tuple-element.21), channel_id=1, source_target_pairs={{0,3},{1,0},{2,1},{3,2},{4,7},{5,4},{6,5},{7,6},{8,11},{9,8},{10,9... | collective-permute-start | bytes 884744 | tf_op jit(solution)/shard_map/ppermute | solution.py:28
  18.7 2.3 %collective-permute-start = (f32[8,72,128]{2,1,0:T(8,128)S(1)}, f32[8,72,128]{2,1,0:T(8,128)S(1)}, u32[]{:S(2)}, u32[]{:S(2)}) collective-permute-start(f32[8,72,128]{2,1,0:T(8,128)S(1)} %get-tuple-element.19), channel_id=1, source_target_pairs={{0,2},{1,3},{2,0},{3,1},{4,6},{5,7},{6,4},{7,5},{8,10},{9,11},{10,... | collective-permute-start | bytes 884744 | tf_op jit(solution)/shard_map/ppermute | solution.py:28
  21.0 10.3 %all-to-all-done.2 = f32[32,8,512]{2,1,0:T(8,128)S(1)} async-done(((f32[32,8,512]{2,1,0:T(8,128)}), f32[32,8,512]{2,1,0:T(8,128)S(1)}, u32[]{:S(2)}, u32[]{:S(2)}) %all-to-all-start.2) | async-done | bytes 524320 | tf_op jit(solution)/shard_map/all_to_all | solution.py:23
  31.7 2.6 %collective-permute-start.7 = (f32[8,4,8,512]{3,2,1,0:T(8,128)S(1)}, f32[8,4,8,512]{3,2,1,0:T(8,128)}, u32[]{:S(2)}, u32[]{:S(2)}) collective-permute-start(f32[8,4,8,512]{3,2,1,0:T(8,128)S(1)} %bitcast.5), channel_id=1, source_target_pairs={{0,128},{64,192},{128,0},{192,64},{1,129},{65,193},{129,1},{193,65... | collective-permute-start | bytes 1572872 | tf_op jit(solution)/shard_map/ppermute | solution.py:28
  34.6 1.6 collective-permute-start.8
  36.2 1.7 collective-permute-done.1
  37.9 0.8 add_add_fusion
  38.6 5.8 %all-to-all-start = ((f32[8,72,128]{2,1,0:T(8,128)}), f32[8,72,128]{2,1,0:T(8,128)S(1)}, u32[]{:S(2)}, u32[]{:S(2)}) async-start(f32[8,72,128]{2,1,0:T(8,128)} %add_add_fusion), calls=%async_computation | async-start | bytes 589824 | tf_op jit(solution)/shard_map/all_to_all | solution.py:23
  45.0 10.4 %collective-permute-done.7.refs_2_ = f32[8,4,8,512]{3,2,1,0:T(8,128)} collective-permute-done((f32[8,4,8,512]{3,2,1,0:T(8,128)S(1)}, f32[8,4,8,512]{3,2,1,0:T(8,128)}, u32[]{:S(2)}, u32[]{:S(2)}) %collective-permute-start.7) | collective-permute-done | bytes 524320 | tf_op jit(solution)/shard_map/ppermute | solution.py:28
  55.4 0.8 collective-permute-done.8.refs_3_
  56.3 0.7 broadcast_in_dim.2
  57.0 3.4 %all-to-all-start.1 = ((f32[8,72,128]{2,1,0:T(8,128)}), f32[8,72,128]{2,1,0:T(8,128)S(1)}, u32[]{:S(2)}, u32[]{:S(2)}) async-start(f32[8,72,128]{2,1,0:T(8,128)} %broadcast_in_dim.2), calls=%async_computation.1 | async-start | bytes 589824 | tf_op jit(solution)/shard_map/all_to_all | solution.py:23
  60.5 2.1 %shard_map.90.refs_0_ = f32[8,4,4,8,256]{4,3,2,1,0:T(8,128)S(1)} custom-call(s32[1]{0:T(128)} %bitcast.me_ref, bf16[256,896]{1,0:T(8,128)(2,1)} %grads_ref.9, f32[8,4,8,512]{3,2,1,0:T(8,128)S(1)} %bitcast.8, f32[8,4,8,512]{3,2,1,0:T(8,128)S(1)} %collective-permute-done.6.refs_1_, f32[8,4,8,512]{3,2,1,0:T(8,128)} %collective-permute-done.7.refs_2_, ...), custom_call_target="tpu_custom_call" | custom-call | tf_op jit(solution)/shard_map/pallas_call | solution.py:35
  62.6 2.8 %shard_map.91 = f32[8,4,4,8,256]{4,3,2,1,0:T(8,128)} custom-call(s32[1]{0:T(128)} %bitcast.me_ref, bf16[256,896]{1,0:T(8,128)(2,1)} %grads_ref.9, f32[8,4,4,8,256]{4,3,2,1,0:T(8,128)S(1)} %shard_map.90.refs_0_, f32[8,4,8,512]{3,2,1,0:T(8,128)S(1)} %collective-permute-done.9.refs_4_.refs_1_, f32[8,4,8,512]{3,2,1,0:T(8,128)S(1)} %collective-permute-done.10.refs_5_.refs_2_, ...), custom_call_target="tpu_custom_call" | custom-call | tf_op jit(solution)/shard_map/pallas_call | solution.py:35
  65.4 8.5 %all-to-all-done.1.block_ref.refs_4_ = f32[8,72,128]{2,1,0:T(8,128)S(1)} async-done(((f32[8,72,128]{2,1,0:T(8,128)}), f32[8,72,128]{2,1,0:T(8,128)S(1)}, u32[]{:S(2)}, u32[]{:S(2)}) %all-to-all-start.1) | async-done | bytes 294944 | tf_op jit(solution)/shard_map/all_to_all | solution.py:23
  73.9 4.2 %all-to-all-start.4 = ((f32[8,4,4,8,256]{4,3,2,1,0:T(8,128)}), f32[8,4,4,8,256]{4,3,2,1,0:T(8,128)}, u32[]{:S(2)}, u32[]{:S(2)}) async-start(f32[8,4,4,8,256]{4,3,2,1,0:T(8,128)} %shard_map.91), calls=%async_computation.4 | async-start | bytes 2097152 | tf_op jit(solution)/shard_map/all_to_all | solution.py:23
  78.1 1.4 collective-permute-start.4
  79.5 1.9 %collective-permute-start.5 = (f32[8,72,128]{2,1,0:T(8,128)S(1)}, f32[8,72,128]{2,1,0:T(8,128)S(1)}, u32[]{:S(2)}, u32[]{:S(2)}) collective-permute-start(f32[8,72,128]{2,1,0:T(8,128)S(1)} %all-to-all-done.1.block_ref.refs_4_), channel_id=1, source_target_pairs={{0,3},{1,0},{2,1},{3,2},{4,7},{5,4},{6,5},{7,6},{8,11},{9,8},{10,9... | collective-permute-start | bytes 884744 | tf_op jit(solution)/shard_map/ppermute | solution.py:28
  81.4 1.5 collective-permute-start.3
  82.9 3.8 %shard_map.83.so_far_ref = f32[4,128,896]{2,1,0:T(8,128)} custom-call(s32[1]{0:T(128)} %bitcast.me_ref, s32[4]{0:T(128)S(1)} %copy-done.6, bf16[2048,896]{1,0:T(8,128)(2,1)} %grads_ref.7, f32[8,72,128]{2,1,0:T(8,128)S(1)} %all-to-all-done.1.block_ref.refs_4_), custom_call_target="tpu_custom_call" | custom-call | tf_op jit(solution)/shard_map/pallas_call | solution.py:35
  86.7 2.0 %collective-permute-done.4.ahead_ref.refs_5_ = f32[8,72,128]{2,1,0:T(8,128)S(1)} collective-permute-done((f32[8,72,128]{2,1,0:T(8,128)S(1)}, f32[8,72,128]{2,1,0:T(8,128)S(1)}, u32[]{:S(2)}, u32[]{:S(2)}) %collective-permute-start.4) | collective-permute-done | bytes 294944 | tf_op jit(solution)/shard_map/ppermute | solution.py:28
  88.7 5.3 %collective-permute-done.5.behind_ref.refs_7_ = f32[8,72,128]{2,1,0:T(8,128)S(1)} collective-permute-done((f32[8,72,128]{2,1,0:T(8,128)S(1)}, f32[8,72,128]{2,1,0:T(8,128)S(1)}, u32[]{:S(2)}, u32[]{:S(2)}) %collective-permute-start.5) | collective-permute-done | bytes 294944 | tf_op jit(solution)/shard_map/ppermute | solution.py:28
  94.0 3.6 %shard_map.84.so_far_ref = f32[4,128,896]{2,1,0:T(8,128)S(1)} custom-call(s32[1]{0:T(128)} %bitcast.me_ref, s32[4]{0:T(128)S(1)} %copy-done.6, bf16[2048,896]{1,0:T(8,128)(2,1)} %grads_ref.7, f32[8,72,128]{2,1,0:T(8,128)S(1)} %collective-permute-done.4.ahead_ref.refs_5_, f32[8,72,128]{2,1,0:T(8,128)S(1)} %collective-permute-done.5.behind_ref.refs_7_, ...), custom_call_target="tpu_custom_call" | custom-call | tf_op jit(solution)/shard_map/pallas_call | solution.py:35
  97.6 3.8 %shard_map.86 = (f32[8,32,512]{2,1,0:T(8,128)S(1)}, bf16[2,512,512]{2,1,0:T(8,128)(2,1)S(1)}, bf16[2,512,512]{2,1,0:T(8,128)(2,1)S(1)}) custom-call(s32[1]{0:T(128)} %bitcast.me_ref, s32[4]{0:T(128)S(1)} %copy-done.6, bf16[2048,896]{1,0:T(8,128)(2,1)} %grads_ref.7, f32[8,72,128]{2,1,0:T(8,128)S(1)} %collective-permute-done.3.block_ref.refs_6_, ...), custom_call_target="tpu_custom_call" | custom-call | tf_op jit(solution)/shard_map/pallas_call | solution.py:35
  101.4 3.0 %shard_map.88 = (f32[8,32,512]{2,1,0:T(8,128)S(1)}, f32[8,32,512]{2,1,0:T(8,128)S(1)}) custom-call(s32[1]{0:T(128)} %bitcast.me_ref, bf16[2,512,512]{2,1,0:T(8,128)(2,1)S(1)} %get-tuple-element.22.high_ref, bf16[2,512,512]{2,1,0:T(8,128)(2,1)S(1)} %get-tuple-element.23.low_ref, f32[8,4,8,512]{3,2,1,0:T(8,128)S(1)} %bitcast.10, ...), custom_call_target="tpu_custom_call" | custom-call | tf_op jit(solution)/shard_map/pallas_call | solution.py:35
  104.5 5.4 %collective-permute-start.14 = (f32[8,32,512]{2,1,0:T(8,128)S(1)}, f32[8,32,512]{2,1,0:T(8,128)S(1)}, u32[]{:S(2)}, u32[]{:S(2)}) collective-permute-start(f32[8,32,512]{2,1,0:T(8,128)S(1)} %get-tuple-element.25), channel_id=1, source_target_pairs={{0,2},{1,3},{2,0},{3,1},{4,6},{5,7},{6,4},{7,5},{8,10},{9,11},{10,... | collective-permute-start | bytes 1572872 | tf_op jit(solution)/shard_map/ppermute | solution.py:28
  109.9 3.0 %shard_map.87.refs_0_ = f32[8,32,512]{2,1,0:T(8,128)} custom-call(s32[1]{0:T(128)} %bitcast.me_ref, bf16[2,512,512]{2,1,0:T(8,128)(2,1)S(1)} %get-tuple-element.22.high_ref, bf16[2,512,512]{2,1,0:T(8,128)(2,1)S(1)} %get-tuple-element.23.low_ref, f32[8,4,8,512]{3,2,1,0:T(8,128)S(1)} %bitcast.11, f32[8,4,8,512]{3,2,1,0:T(8,128)S(1)} %collective-permute-done.6.refs_1_, ...), custom_call_target="tpu_custom_call" | custom-call | tf_op jit(solution)/shard_map/pallas_call | solution.py:35
  113.0 9.2 %collective-permute-done.13.refs_1_ = f32[8,32,512]{2,1,0:T(8,128)S(1)} collective-permute-done((f32[8,32,512]{2,1,0:T(8,128)S(1)}, f32[8,32,512]{2,1,0:T(8,128)S(1)}, u32[]{:S(2)}, u32[]{:S(2)}) %collective-permute-start.13) | collective-permute-done | bytes 524320 | tf_op jit(solution)/shard_map/ppermute | solution.py:28
  122.2 5.8 %collective-permute-done.14.refs_2_ = f32[8,32,512]{2,1,0:T(8,128)S(1)} collective-permute-done((f32[8,32,512]{2,1,0:T(8,128)S(1)}, f32[8,32,512]{2,1,0:T(8,128)S(1)}, u32[]{:S(2)}, u32[]{:S(2)}) %collective-permute-start.14) | collective-permute-done | bytes 524320 | tf_op jit(solution)/shard_map/ppermute | solution.py:28
  128.8 0.8 copy-done.9
  129.6 3.5 %shard_map.89 = f32[8,32,512]{2,1,0:T(8,128)} custom-call(s32[1]{0:T(128)} %bitcast.me_ref, f32[8,32,512]{2,1,0:T(8,128)} %shard_map.87.refs_0_, f32[8,32,512]{2,1,0:T(8,128)} %copy-done.7, f32[8,32,512]{2,1,0:T(8,128)} %copy-done.8, f32[8,32,512]{2,1,0:T(8,128)} %copy-done.9), custom_call_target="tpu_custom_call" | custom-call | tf_op jit(solution)/shard_map/pallas_call | solution.py:35
  133.1 6.5 %all-to-all-start.3 = ((f32[8,32,512]{2,1,0:T(8,128)}), f32[8,32,512]{2,1,0:T(8,128)S(1)}, u32[]{:S(2)}, u32[]{:S(2)}) async-start(f32[8,32,512]{2,1,0:T(8,128)} %shard_map.89), calls=%async_computation.3 | async-start | bytes 1048576 | tf_op jit(solution)/shard_map/all_to_all | solution.py:23
  139.6 1.3 shard_map.92
  141.4 3.3 %collective-permute-start.17 = (f32[4,8,256]{2,1,0:T(8,128)S(1)}, f32[4,8,256]{2,1,0:T(8,128)S(1)}, u32[]{:S(2)}, u32[]{:S(2)}) collective-permute-start(f32[4,8,256]{2,1,0:T(8,128)S(1)} %get-tuple-element.29), channel_id=1, source_target_pairs={{0,2},{1,3},{2,0},{3,1},{4,6},{5,7},{6,4},{7,5},{8,10},{9,11},{10,... | collective-permute-start | bytes 98312 | tf_op jit(solution)/shard_map/ppermute | solution.py:28
  144.8 1.5 collective-permute-done.16.refs_1_
  146.3 0.7 collective-permute-done.17.refs_2_
  147.0 1.7 collective-permute-done.18.refs_3_
  148.7 1.1 shard_map.93.refs_0_
  149.9 1.5 collective-permute-start.19
  151.4 3.5 %collective-permute-start.20 = (f32[32,8,128]{2,1,0:T(8,128)S(1)}, f32[32,8,128]{2,1,0:T(8,128)S(1)}, u32[]{:S(2)}, u32[]{:S(2)}) collective-permute-start(f32[32,8,128]{2,1,0:T(8,128)S(1)} %shard_map.93.refs_0_), channel_id=1, source_target_pairs={{0,128},{64,192},{128,0},{192,64},{1,129},{65,193},{129,1},{193,65... | collective-permute-start | bytes 393224 | tf_op jit(solution)/shard_map/ppermute | solution.py:28
  154.9 1.3 collective-permute-done.19.refs_1_
  156.1 1.8 collective-permute-done.20.refs_2_
  157.9 1.9 %collective-permute-done.21.refs_3_ = f32[32,8,128]{2,1,0:T(8,128)S(1)} collective-permute-done((f32[32,8,128]{2,1,0:T(8,128)S(1)}, f32[32,8,128]{2,1,0:T(8,128)S(1)}, u32[]{:S(2)}, u32[]{:S(2)}) %collective-permute-start.21) | collective-permute-done | bytes 131104 | tf_op jit(solution)/shard_map/ppermute | solution.py:28
  159.9 1.3 collective-permute-done.25.refs_7_
  161.6 18.2 %all_to_all.30 = f32[32,2,128]{2,1,0:T(2,128)S(1)} all-to-all(f32[32,2,128]{2,1,0:T(2,128)S(1)} %bitcast.12), channel_id=1, replica_groups=mesh['y'=4,'core'=2,'z'=8,'x'=4] {'z','x'}, dimensions={0} | all-to-all | bytes 65536 | tf_op jit(solution)/shard_map/all_to_all | solution.py:23
  (52 shorter events, 3.8 us)
Async XLA Ops:
  2.1 29.2 %all-to-all-start.2 = ((f32[32,8,512]{2,1,0:T(8,128)}), f32[32,8,512]{2,1,0:T(8,128)S(1)}, u32[]{:S(2)}, u32[]{:S(2)}) async-start(f32[32,8,512]{2,1,0:T(8,128)} %shard_map.85), calls=%async_computation.2 | async-start | bytes 1048576 | tf_op jit(solution)/shard_map/all_to_all | solution.py:23
  15.6 19.0 %collective-permute-start.2 = (f32[8,72,128]{2,1,0:T(8,128)S(1)}, f32[8,72,128]{2,1,0:T(8,128)S(1)}, u32[]{:S(2)}, u32[]{:S(2)}) collective-permute-start(f32[8,72,128]{2,1,0:T(8,128)S(1)} %get-tuple-element.21), channel_id=1, source_target_pairs={{0,3},{1,0},{2,1},{3,2},{4,7},{5,4},{6,5},{7,6},{8,11},{9,8},{10,9... | collective-permute-start | bytes 884744 | tf_op jit(solution)/shard_map/ppermute | solution.py:28
  18.7 19.2 %collective-permute-start.1 = (f32[8,72,128]{2,1,0:T(8,128)S(1)}, f32[8,72,128]{2,1,0:T(8,128)S(1)}, u32[]{:S(2)}, u32[]{:S(2)}) collective-permute-start(f32[8,72,128]{2,1,0:T(8,128)S(1)} %get-tuple-element.20), channel_id=1, source_target_pairs={{0,1},{1,2},{2,3},{3,0},{4,5},{5,6},{6,7},{7,4},{8,9},{9,10},{10,1... | collective-permute-start | bytes 884744 | tf_op jit(solution)/shard_map/ppermute | solution.py:28
  18.7 19.2 %collective-permute-start = (f32[8,72,128]{2,1,0:T(8,128)S(1)}, f32[8,72,128]{2,1,0:T(8,128)S(1)}, u32[]{:S(2)}, u32[]{:S(2)}) collective-permute-start(f32[8,72,128]{2,1,0:T(8,128)S(1)} %get-tuple-element.19), channel_id=1, source_target_pairs={{0,2},{1,3},{2,0},{3,1},{4,6},{5,7},{6,4},{7,5},{8,10},{9,11},{10,... | collective-permute-start | bytes 884744 | tf_op jit(solution)/shard_map/ppermute | solution.py:28
  31.2 13.8 %collective-permute-start.6 = (f32[8,4,8,512]{3,2,1,0:T(8,128)S(1)}, f32[8,4,8,512]{3,2,1,0:T(8,128)S(1)}, u32[]{:S(2)}, u32[]{:S(2)}) collective-permute-start(f32[8,4,8,512]{3,2,1,0:T(8,128)S(1)} %bitcast.4), channel_id=1, source_target_pairs={{0,192},{64,0},{128,64},{192,128},{1,193},{65,1},{129,65},{193,129... | collective-permute-start | bytes 1572872 | tf_op jit(solution)/shard_map/ppermute | solution.py:28
  31.7 23.7 %collective-permute-start.7 = (f32[8,4,8,512]{3,2,1,0:T(8,128)S(1)}, f32[8,4,8,512]{3,2,1,0:T(8,128)}, u32[]{:S(2)}, u32[]{:S(2)}) collective-permute-start(f32[8,4,8,512]{3,2,1,0:T(8,128)S(1)} %bitcast.5), channel_id=1, source_target_pairs={{0,128},{64,192},{128,0},{192,64},{1,129},{65,193},{129,1},{193,65... | collective-permute-start | bytes 1572872 | tf_op jit(solution)/shard_map/ppermute | solution.py:28
  34.6 21.7 %collective-permute-start.8 = (f32[8,4,8,512]{3,2,1,0:T(8,128)S(1)}, f32[8,4,8,512]{3,2,1,0:T(8,128)}, u32[]{:S(2)}, u32[]{:S(2)}) collective-permute-start(f32[8,4,8,512]{3,2,1,0:T(8,128)S(1)} %bitcast.6), channel_id=1, source_target_pairs={{0,64},{64,128},{128,192},{192,0},{1,65},{65,129},{129,193},{193,1... | collective-permute-start | bytes 1572872 | tf_op jit(solution)/shard_map/ppermute | solution.py:28
  38.6 17.6 %all-to-all-start = ((f32[8,72,128]{2,1,0:T(8,128)}), f32[8,72,128]{2,1,0:T(8,128)S(1)}, u32[]{:S(2)}, u32[]{:S(2)}) async-start(f32[8,72,128]{2,1,0:T(8,128)} %add_add_fusion), calls=%async_computation | async-start | bytes 589824 | tf_op jit(solution)/shard_map/all_to_all | solution.py:23
  44.5 18.1 %collective-permute-start.9 = (f32[8,4,8,512]{3,2,1,0:T(8,128)S(1)}, f32[8,4,8,512]{3,2,1,0:T(8,128)S(1)}, u32[]{:S(2)}, u32[]{:S(2)}) collective-permute-start(f32[8,4,8,512]{3,2,1,0:T(8,128)S(1)} %bitcast.7), channel_id=1, source_target_pairs={{0,32},{32,0},{1,33},{33,1},{2,34},{34,2},{3,35},{35,3},{4,36},{36... | collective-permute-start | bytes 1572872 | tf_op jit(solution)/shard_map/ppermute | solution.py:28
  45.0 17.6 %collective-permute-start.10 = (f32[8,4,8,512]{3,2,1,0:T(8,128)S(1)}, f32[8,4,8,512]{3,2,1,0:T(8,128)S(1)}, u32[]{:S(2)}, u32[]{:S(2)}) collective-permute-start(f32[8,4,8,512]{3,2,1,0:T(8,128)S(1)} %collective-permute-done.6.refs_1_), channel_id=1, source_target_pairs={{0,32},{32,0},{1,33},{33,1},{2,34},{34,2},{3,35},{35,3},{4,36},{36... | collective-permute-start | bytes 1572872 | tf_op jit(solution)/shard_map/ppermute | solution.py:28
  55.4 7.2 %collective-permute-start.11 = (f32[8,4,8,512]{3,2,1,0:T(8,128)}, f32[8,4,8,512]{3,2,1,0:T(8,128)S(1)}, u32[]{:S(2)}, u32[]{:S(2)}) collective-permute-start(f32[8,4,8,512]{3,2,1,0:T(8,128)} %collective-permute-done.7.refs_2_), channel_id=1, source_target_pairs={{0,32},{32,0},{1,33},{33,1},{2,34},{34,2},{3,35},{35,3},{4,36},{36... | collective-permute-start | bytes 1572872 | tf_op jit(solution)/shard_map/ppermute | solution.py:28
  56.3 6.4 %collective-permute-start.12 = (f32[8,4,8,512]{3,2,1,0:T(8,128)}, f32[8,4,8,512]{3,2,1,0:T(8,128)S(1)}, u32[]{:S(2)}, u32[]{:S(2)}) collective-permute-start(f32[8,4,8,512]{3,2,1,0:T(8,128)} %collective-permute-done.8.refs_3_), channel_id=1, source_target_pairs={{0,32},{32,0},{1,33},{33,1},{2,34},{34,2},{3,35},{35,3},{4,36},{36... | collective-permute-start | bytes 1572872 | tf_op jit(solution)/shard_map/ppermute | solution.py:28
  57.0 16.9 %all-to-all-start.1 = ((f32[8,72,128]{2,1,0:T(8,128)}), f32[8,72,128]{2,1,0:T(8,128)S(1)}, u32[]{:S(2)}, u32[]{:S(2)}) async-start(f32[8,72,128]{2,1,0:T(8,128)} %broadcast_in_dim.2), calls=%async_computation.1 | async-start | bytes 589824 | tf_op jit(solution)/shard_map/all_to_all | solution.py:23
  62.6 20.4 %copy-start.6 = (s32[4]{0:T(128)S(1)}, s32[4]{0:T(128)}, u32[]{:S(2)}) copy-start(s32[4]{0:T(128)} %len_ref.5) | copy-start | bytes 52
  73.9 59.3 %all-to-all-start.4 = ((f32[8,4,4,8,256]{4,3,2,1,0:T(8,128)}), f32[8,4,4,8,256]{4,3,2,1,0:T(8,128)}, u32[]{:S(2)}, u32[]{:S(2)}) async-start(f32[8,4,4,8,256]{4,3,2,1,0:T(8,128)} %shard_map.91), calls=%async_computation.4 | async-start | bytes 2097152 | tf_op jit(solution)/shard_map/all_to_all | solution.py:23
  78.1 10.6 %collective-permute-start.4 = (f32[8,72,128]{2,1,0:T(8,128)S(1)}, f32[8,72,128]{2,1,0:T(8,128)S(1)}, u32[]{:S(2)}, u32[]{:S(2)}) collective-permute-start(f32[8,72,128]{2,1,0:T(8,128)S(1)} %all-to-all-done.1.block_ref.refs_4_), channel_id=1, source_target_pairs={{0,1},{1,2},{2,3},{3,0},{4,5},{5,6},{6,7},{7,4},{8,9},{9,10},{10,1... | collective-permute-start | bytes 884744 | tf_op jit(solution)/shard_map/ppermute | solution.py:28
  79.5 14.5 %collective-permute-start.5 = (f32[8,72,128]{2,1,0:T(8,128)S(1)}, f32[8,72,128]{2,1,0:T(8,128)S(1)}, u32[]{:S(2)}, u32[]{:S(2)}) collective-permute-start(f32[8,72,128]{2,1,0:T(8,128)S(1)} %all-to-all-done.1.block_ref.refs_4_), channel_id=1, source_target_pairs={{0,3},{1,0},{2,1},{3,2},{4,7},{5,4},{6,5},{7,6},{8,11},{9,8},{10,9... | collective-permute-start | bytes 884744 | tf_op jit(solution)/shard_map/ppermute | solution.py:28
  81.4 16.2 %collective-permute-start.3 = (f32[8,72,128]{2,1,0:T(8,128)S(1)}, f32[8,72,128]{2,1,0:T(8,128)S(1)}, u32[]{:S(2)}, u32[]{:S(2)}) collective-permute-start(f32[8,72,128]{2,1,0:T(8,128)S(1)} %all-to-all-done.1.block_ref.refs_4_), channel_id=1, source_target_pairs={{0,2},{1,3},{2,0},{3,1},{4,6},{5,7},{6,4},{7,5},{8,10},{9,11},{10,... | collective-permute-start | bytes 884744 | tf_op jit(solution)/shard_map/ppermute | solution.py:28
  88.7 8.9 %copy-start = (f32[8,72,128]{2,1,0:T(8,128)}, f32[8,72,128]{2,1,0:T(8,128)S(1)}, u32[]{:S(2)}) copy-start(f32[8,72,128]{2,1,0:T(8,128)S(1)} %collective-permute-done.4.ahead_ref.refs_5_) | copy-start | bytes 884740
  94.0 3.6 %copy-start.2 = (f32[8,72,128]{2,1,0:T(8,128)}, f32[8,72,128]{2,1,0:T(8,128)S(1)}, u32[]{:S(2)}) copy-start(f32[8,72,128]{2,1,0:T(8,128)S(1)} %collective-permute-done.5.behind_ref.refs_7_) | copy-start | bytes 884740
  97.6 3.8 %copy-start.4 = (f32[8,72,128]{2,1,0:T(8,128)}, f32[8,72,128]{2,1,0:T(8,128)S(1)}, u32[]{:S(2)}) copy-start(f32[8,72,128]{2,1,0:T(8,128)S(1)} %collective-permute-done.3.block_ref.refs_6_) | copy-start | bytes 884740
  104.4 17.8 %collective-permute-start.13 = (f32[8,32,512]{2,1,0:T(8,128)S(1)}, f32[8,32,512]{2,1,0:T(8,128)S(1)}, u32[]{:S(2)}, u32[]{:S(2)}) collective-permute-start(f32[8,32,512]{2,1,0:T(8,128)S(1)} %get-tuple-element.24), channel_id=1, source_target_pairs={{0,1},{1,2},{2,3},{3,0},{4,5},{5,6},{6,7},{7,4},{8,9},{9,10},{10,1... | collective-permute-start | bytes 1572872 | tf_op jit(solution)/shard_map/ppermute | solution.py:28
  104.5 23.5 %collective-permute-start.14 = (f32[8,32,512]{2,1,0:T(8,128)S(1)}, f32[8,32,512]{2,1,0:T(8,128)S(1)}, u32[]{:S(2)}, u32[]{:S(2)}) collective-permute-start(f32[8,32,512]{2,1,0:T(8,128)S(1)} %get-tuple-element.25), channel_id=1, source_target_pairs={{0,2},{1,3},{2,0},{3,1},{4,6},{5,7},{6,4},{7,5},{8,10},{9,11},{10,... | collective-permute-start | bytes 1572872 | tf_op jit(solution)/shard_map/ppermute | solution.py:28
  109.9 18.5 %collective-permute-start.15 = (f32[8,32,512]{2,1,0:T(8,128)S(1)}, f32[8,32,512]{2,1,0:T(8,128)S(1)}, u32[]{:S(2)}, u32[]{:S(2)}) collective-permute-start(f32[8,32,512]{2,1,0:T(8,128)S(1)} %get-tuple-element.26), channel_id=1, source_target_pairs={{0,3},{1,0},{2,1},{3,2},{4,7},{5,4},{6,5},{7,6},{8,11},{9,8},{10,9... | collective-permute-start | bytes 1572872 | tf_op jit(solution)/shard_map/ppermute | solution.py:28
  113.0 35.7 %copy-start.1 = (f32[8,72,128]{2,1,0:T(8,128)S(1)}, f32[8,72,128]{2,1,0:T(8,128)}, u32[]{:S(2)}) copy-start(f32[8,72,128]{2,1,0:T(8,128)} %copy-done) | copy-start | bytes 884740
  113.0 35.7 %copy-start.3 = (f32[8,72,128]{2,1,0:T(8,128)S(1)}, f32[8,72,128]{2,1,0:T(8,128)}, u32[]{:S(2)}) copy-start(f32[8,72,128]{2,1,0:T(8,128)} %copy-done.2) | copy-start | bytes 884740
  113.0 35.7 %copy-start.5 = (f32[8,72,128]{2,1,0:T(8,128)S(1)}, f32[8,72,128]{2,1,0:T(8,128)}, u32[]{:S(2)}) copy-start(f32[8,72,128]{2,1,0:T(8,128)} %copy-done.4) | copy-start | bytes 884740
  122.2 6.2 %copy-start.7 = (f32[8,32,512]{2,1,0:T(8,128)}, f32[8,32,512]{2,1,0:T(8,128)S(1)}, u32[]{:S(2)}) copy-start(f32[8,32,512]{2,1,0:T(8,128)S(1)} %collective-permute-done.13.refs_1_) | copy-start | bytes 1572868
  128.0 0.8 copy-start.8
  128.8 0.8 copy-start.9
  133.1 26.7 %all-to-all-start.3 = ((f32[8,32,512]{2,1,0:T(8,128)}), f32[8,32,512]{2,1,0:T(8,128)S(1)}, u32[]{:S(2)}, u32[]{:S(2)}) async-start(f32[8,32,512]{2,1,0:T(8,128)} %shard_map.89), calls=%async_computation.3 | async-start | bytes 1048576 | tf_op jit(solution)/shard_map/all_to_all | solution.py:23
  140.9 5.4 %collective-permute-start.16 = (f32[4,8,256]{2,1,0:T(8,128)S(1)}, f32[4,8,256]{2,1,0:T(8,128)S(1)}, u32[]{:S(2)}, u32[]{:S(2)}) collective-permute-start(f32[4,8,256]{2,1,0:T(8,128)S(1)} %get-tuple-element.28), channel_id=1, source_target_pairs={{0,1},{1,2},{2,3},{3,0},{4,5},{5,6},{6,7},{7,4},{8,9},{9,10},{10,1... | collective-permute-start | bytes 98312 | tf_op jit(solution)/shard_map/ppermute | solution.py:28
  141.4 5.6 %collective-permute-start.17 = (f32[4,8,256]{2,1,0:T(8,128)S(1)}, f32[4,8,256]{2,1,0:T(8,128)S(1)}, u32[]{:S(2)}, u32[]{:S(2)}) collective-permute-start(f32[4,8,256]{2,1,0:T(8,128)S(1)} %get-tuple-element.29), channel_id=1, source_target_pairs={{0,2},{1,3},{2,0},{3,1},{4,6},{5,7},{6,4},{7,5},{8,10},{9,11},{10,... | collective-permute-start | bytes 98312 | tf_op jit(solution)/shard_map/ppermute | solution.py:28
  144.8 3.9 %collective-permute-start.18 = (f32[4,8,256]{2,1,0:T(8,128)S(1)}, f32[4,8,256]{2,1,0:T(8,128)S(1)}, u32[]{:S(2)}, u32[]{:S(2)}) collective-permute-start(f32[4,8,256]{2,1,0:T(8,128)S(1)} %get-tuple-element.30), channel_id=1, source_target_pairs={{0,3},{1,0},{2,1},{3,2},{4,7},{5,4},{6,5},{7,6},{8,11},{9,8},{10,9... | collective-permute-start | bytes 98312 | tf_op jit(solution)/shard_map/ppermute | solution.py:28
  149.9 6.3 %collective-permute-start.19 = (f32[32,8,128]{2,1,0:T(8,128)S(1)}, f32[32,8,128]{2,1,0:T(8,128)S(1)}, u32[]{:S(2)}, u32[]{:S(2)}) collective-permute-start(f32[32,8,128]{2,1,0:T(8,128)S(1)} %shard_map.93.refs_0_), channel_id=1, source_target_pairs={{0,64},{64,128},{128,192},{192,0},{1,65},{65,129},{129,193},{193,1... | collective-permute-start | bytes 393224 | tf_op jit(solution)/shard_map/ppermute | solution.py:28
  151.4 6.5 %collective-permute-start.20 = (f32[32,8,128]{2,1,0:T(8,128)S(1)}, f32[32,8,128]{2,1,0:T(8,128)S(1)}, u32[]{:S(2)}, u32[]{:S(2)}) collective-permute-start(f32[32,8,128]{2,1,0:T(8,128)S(1)} %shard_map.93.refs_0_), channel_id=1, source_target_pairs={{0,128},{64,192},{128,0},{192,64},{1,129},{65,193},{129,1},{193,65... | collective-permute-start | bytes 393224 | tf_op jit(solution)/shard_map/ppermute | solution.py:28
  154.9 5.0 %collective-permute-start.21 = (f32[32,8,128]{2,1,0:T(8,128)S(1)}, f32[32,8,128]{2,1,0:T(8,128)S(1)}, u32[]{:S(2)}, u32[]{:S(2)}) collective-permute-start(f32[32,8,128]{2,1,0:T(8,128)S(1)} %shard_map.93.refs_0_), channel_id=1, source_target_pairs={{0,192},{64,0},{128,64},{192,128},{1,193},{65,1},{129,65},{193,129... | collective-permute-start | bytes 393224 | tf_op jit(solution)/shard_map/ppermute | solution.py:28
  154.9 5.0 %collective-permute-start.22 = (f32[32,8,128]{2,1,0:T(8,128)S(1)}, f32[32,8,128]{2,1,0:T(8,128)S(1)}, u32[]{:S(2)}, u32[]{:S(2)}) collective-permute-start(f32[32,8,128]{2,1,0:T(8,128)S(1)} %shard_map.93.refs_0_), channel_id=1, source_target_pairs={{0,32},{32,0},{1,33},{33,1},{2,34},{34,2},{3,35},{35,3},{4,36},{36... | collective-permute-start | bytes 393224 | tf_op jit(solution)/shard_map/ppermute | solution.py:28
  156.1 3.7 %collective-permute-start.23 = (f32[32,8,128]{2,1,0:T(8,128)S(1)}, f32[32,8,128]{2,1,0:T(8,128)S(1)}, u32[]{:S(2)}, u32[]{:S(2)}) collective-permute-start(f32[32,8,128]{2,1,0:T(8,128)S(1)} %collective-permute-done.19.refs_1_), channel_id=1, source_target_pairs={{0,32},{32,0},{1,33},{33,1},{2,34},{34,2},{3,35},{35,3},{4,36},{36... | collective-permute-start | bytes 393224 | tf_op jit(solution)/shard_map/ppermute | solution.py:28
  157.9 1.9 %collective-permute-start.24 = (f32[32,8,128]{2,1,0:T(8,128)S(1)}, f32[32,8,128]{2,1,0:T(8,128)S(1)}, u32[]{:S(2)}, u32[]{:S(2)}) collective-permute-start(f32[32,8,128]{2,1,0:T(8,128)S(1)} %collective-permute-done.20.refs_2_), channel_id=1, source_target_pairs={{0,32},{32,0},{1,33},{33,1},{2,34},{34,2},{3,35},{35,3},{4,36},{36... | collective-permute-start | bytes 393224 | tf_op jit(solution)/shard_map/ppermute | solution.py:28
  159.8 1.3 collective-permute-start.25

commit v8 on v6

--- a/solution.py
+++ b/solution.py
@@ -12,6 +12,7 @@
 DAMPING = 1.0
 ZX = ("z", "x")
 
+PEERS = (1, 3, 2)
 HALF = 512
 VMEM = pl.BlockSpec(memory_space=pltpu.VMEM)
 HELD = pl.BlockSpec(memory_space=pltpu.VMEM)
@@ -186,31 +187,32 @@
     add_block(me_ref, len_ref, 0, grads_ref, block_ref, total_ref)
 
 
-def outer_side_kernel(me_ref, len_ref, grads_ref, ahead_ref, behind_ref, so_far_ref, total_ref):
-    @pl.when(pl.program_id(0) == 0)
+def train_kernel(me_ref, len_ref, grads_ref, *refs):
+    blocks, so_far_ref, slabs, (out_ref, high_ref, low_ref, total_ref) = refs[:3], refs[3], refs[4:12], refs[12:]
+    cols = grads_ref.shape[1]
+    step = pl.program_id(0)
+
+    @pl.when(step == 0)
     def _():
         total_ref[...] = so_far_ref[...]
-        add_block(me_ref, len_ref, 1, grads_ref, ahead_ref, total_ref)
-
-    @pl.when(pl.program_id(0) == 1)
+
+    for at, hops in enumerate(PEERS):
+
+        @pl.when(step == at)
+        def _(at=at, hops=hops):
+            add_block(me_ref, len_ref, hops, grads_ref, blocks[at], total_ref)
+
+    @pl.when(step == len(PEERS) - 1)
     def _():
-        add_block(me_ref, len_ref, 3, grads_ref, behind_ref, total_ref)
-
-
-def train_kernel(me_ref, len_ref, grads_ref, block_ref, so_far_ref, *refs):
-    slabs, (out_ref, high_ref, low_ref, total_ref) = refs[:8], refs[8:]
-    cols = grads_ref.shape[1]
-    total_ref[...] = so_far_ref[...]
-    add_block(me_ref, len_ref, 2, grads_ref, block_ref, total_ref)
-    for doc in range(4):
-        length = jnp.full((128, cols), len_ref[doc], jnp.int32).astype(jnp.float32)
-        high, low = split(total_ref[doc] / length)
-        rows = slice(128 * doc, 128 * doc + 128)
-        for ref, value in ((high_ref, high), (low_ref, low)):
-            ref[0, rows, :] = value[:, :HALF]
-            ref[1, rows, : 2 * HALF - cols] = jnp.zeros((128, 2 * HALF - cols), jnp.bfloat16)
-            ref[1, rows, 2 * HALF - cols :] = value[:, HALF:]
-    basis_product(me_ref, 2, slabs, high_ref, low_ref, out_ref)
+        for doc in range(4):
+            length = jnp.full((128, cols), len_ref[doc], jnp.int32).astype(jnp.float32)
+            high, low = split(total_ref[doc] / length)
+            rows = slice(128 * doc, 128 * doc + 128)
+            for ref, value in ((high_ref, high), (low_ref, low)):
+                ref[0, rows, :] = value[:, :HALF]
+                ref[1, rows, : 2 * HALF - cols] = jnp.zeros((128, 2 * HALF - cols), jnp.bfloat16)
+                ref[1, rows, 2 * HALF - cols :] = value[:, HALF:]
+        basis_product(me_ref, 2, slabs, high_ref, low_ref, out_ref)
 
 
 def product_kernel(hops, me_ref, high_ref, low_ref, *refs):
@@ -220,7 +222,7 @@
 
 
 def score_kernel(me_ref, blocks_ref, *refs):
-    preconds, out_ref = refs[:8], refs[8]
+    preconds, out_ref, sums_ref = refs[:8], refs[8], refs[9]
     y, core, _, _ = place(me_ref)
     train = blocks_ref[0]
     for sender in range(1, 8):
@@ -237,9 +239,13 @@
                 for doc in range(4):
                     product = value * row[:, 128 * doc : 128 * doc + 128]
                     sums[doc] = product if sums[doc] is None else sums[doc] + product
-        for q in range(8):
-            for doc in range(4):
-                out_ref[4 * owner + q // 2, 4 * (q % 2) + doc : 4 * (q % 2) + doc + 1, :] = sums[doc][q : q + 1]
+        for doc in range(4):
+            sums_ref[doc, pl.ds(pl.multiple_of(8 * owner, 8), 8), :] = sums[doc]
+    lane = lax.broadcasted_iota(jnp.int32, out_ref.shape, 1)
+    scores = jnp.zeros(out_ref.shape, jnp.float32)
+    for doc in range(4):
+        scores = jnp.where(lane == doc, jnp.sum(sums_ref[doc], axis=1, keepdims=True), scores)
+    out_ref[...] = scores
 
 
 def local(
@@ -319,29 +325,22 @@
     sent = [None] * 4
     total_shape = ((4, 128, out_grads.shape[1]), f32)
 
-    def grads_spec(first, stride=0):
-        return pl.BlockSpec(
-            (512, out_grads.shape[1]), lambda i, me: (lax.rem(me[0] % 4 + 4 - first - stride * i, 4), 0)
-        )
-
+    def grads_index(step, me):
+        return (lax.rem(me[0] % 4 + 4 - jnp.where(step == 2, 2, 1 + 2 * step), 4), 0)
+
+    grads_block = (512, out_grads.shape[1])
     (total,) = call(
         outer_own_kernel,
         [total_shape],
-        [SMEM, grads_spec(0), HELD],
-        me, args=(doc_lengths, out_grads, blocks[0]), held=False,
-    )
-    (total,) = call(
-        outer_side_kernel,
-        [total_shape],
-        [SMEM, grads_spec(1, 2), HELD, HELD, VMEM],
-        me, args=(doc_lengths, out_grads, blocks[1], blocks[3], total),
-        grid=2,
+        [SMEM, pl.BlockSpec(grads_block, lambda i, me: (me[0] % 4, 0)), HELD],
+        me, args=(doc_lengths, out_grads, blocks[0]),
     )
     sent[2], high, low = call(
         train_kernel,
         [block_shape, sum_shape, sum_shape],
-        [SMEM, grads_spec(2), *[HELD] * 10],
-        me, args=(doc_lengths, out_grads, blocks[2], total, *slabs),
+        [SMEM, pl.BlockSpec(grads_block, grads_index), *[HELD] * 12],
+        me, args=(doc_lengths, out_grads, *[blocks[k] for k in PEERS], total, *slabs),
+        grid=3,
         scratch=[pltpu.VMEM(*total_shape)],
     )
     sent[1], sent[3] = call(
@@ -356,8 +355,14 @@
     train = sent[0] + sent[1] + sent[2] + sent[3]
     train = exchange(train, "z")
 
-    (partial_scores,) = call(score_kernel, [((32, 8, 128), f32)], [HELD] * 9, me, args=(train, *preconds))
-    return jnp.sum(exchange(partial_scores, ZX), axis=(0, 2)).reshape(2, 4)
+    (partial_scores,) = call(
+        score_kernel,
+        [((64, 128), f32)],
+        [HELD] * 9,
+        me, args=(train, *preconds),
+        scratch=[pltpu.VMEM((4, 64, 128), f32)],
+    )
+    return jnp.sum(exchange(partial_scores.reshape(32, 2, 128), ZX), axis=0)[:, :4]
 
 
 def solution(mesh):

time: 181 us -> 182 us (level)
  waiting for transfers between devices: 65.5 us -> 71.6 us
  Pallas kernels: 28.8 us -> 26.2 us
    ppermute x26, waiting for transfers between devices: 46.8 us -> 52.9 us  [shifted(): return lax.ppermute(shard, axis, [(i, (i + hops) % n) for i in range(n)])]
    pallas_call x12 -> x11, Pallas kernels: 28.8 us -> 26.2 us  [call(): pl.pallas_call(kernel, out_shape=out_shape, grid_spec=pltpu.PrefetchScala...]
  transfers between devices with their start and end apart: 31 -> 31, of which waited for: 18 -> 20; matrix products, arithmetic and copies ran while one was open for 2% -> 2% of each run, Pallas kernels for 15% -> 13%
where the time goes in v8:
time: 182 us; the launch traced here: 181 us
  waiting for transfers between devices  71.6 us (39%)
  starting transfers between devices  58.6 us (32%)
  Pallas kernels  26.2 us (14%)
  blocking collectives  19.8 us (11%)
  other arithmetic  3.44 us (2%)
    ppermute x26, waiting for transfers between devices, shifted(): return lax.ppermute(shard, axis, [(i, (i + hops) % n) for i in range(n)])  52.9 us
    all_to_all x5, starting transfers between devices, exchange(): return lax.all_to_all(blocks, axis, 0, 0, tiled=True)  31.3 us
    ppermute x26, starting transfers between devices, shifted(): return lax.ppermute(shard, axis, [(i, (i + hops) % n) for i in range(n)])  27.3 us
    pallas_call x11, Pallas kernels, call(): pl.pallas_call(kernel, out_shape=out_shape, grid_spec=pltpu.PrefetchScala...  26.2 us
    all_to_all x1, blocking collectives, exchange(): return lax.all_to_all(blocks, axis, 0, 0, tiled=True)  19.8 us
    all_to_all x5, waiting for transfers between devices, exchange(): return lax.all_to_all(blocks, axis, 0, 0, tiled=True)  18.7 us
  transfers between devices with their start and end apart: 31, of which 20 were waited for; matrix products, arithmetic and copies ran while one was open for 2% of the time, Pallas kernels for 13%

profile of v8, /device:TPU:8, one launch (start us, length us, event | category | flops | bytes accessed | tf_op | source)
XLA Modules:
  0.0 180.7 jit_solution(4187828721448185008)
XLA Ops:
  0.0 2.0 %shard_map.84 = f32[32,8,512]{2,1,0:T(8,128)} custom-call(s32[1]{0:T(128)} %bitcast.me_ref, f32[32,28672]{1,0:T(8,128)} %basis_ref.3), custom_call_target="tpu_custom_call" | custom-call | tf_op jit(solution)/shard_map/pallas_call | solution.py:36
  2.1 11.3 %all-to-all-start.2 = ((f32[32,8,512]{2,1,0:T(8,128)}), f32[32,8,512]{2,1,0:T(8,128)S(1)}, u32[]{:S(2)}, u32[]{:S(2)}) async-start(f32[32,8,512]{2,1,0:T(8,128)} %shard_map.84), calls=%async_computation.2 | async-start | bytes 1048576 | tf_op jit(solution)/shard_map/all_to_all | solution.py:24
  13.4 2.2 %shard_map.82 = (f32[8,72,128]{2,1,0:T(8,128)S(1)}, f32[8,72,128]{2,1,0:T(8,128)S(1)}, f32[8,72,128]{2,1,0:T(8,128)S(1)}, f32[8,72,128]{2,1,0:T(8,128)S(1)}) custom-call(s32[1]{0:T(128)} %bitcast.me_ref, bf16[2048,256]{1,0:T(8,128)(2,1)} %acts_ref.1, bf16[256,256]{1,0:T(8,128)(2,1)} %query_ref.1, f32[128,8192]{1,0:T(8,128)} %basis_ref.2), custom_call_target="tpu_custom_call" | custom-call | tf_op jit(solution)/shard_map/pallas_call | solution.py:36
  15.6 3.1 %collective-permute-start.2 = (f32[8,72,128]{2,1,0:T(8,128)S(1)}, f32[8,72,128]{2,1,0:T(8,128)S(1)}, u32[]{:S(2)}, u32[]{:S(2)}) collective-permute-start(f32[8,72,128]{2,1,0:T(8,128)S(1)} %get-tuple-element.21), channel_id=1, source_target_pairs={{0,3},{1,0},{2,1},{3,2},{4,7},{5,4},{6,5},{7,6},{8,11},{9,8},{10,9... | collective-permute-start | bytes 884744 | tf_op jit(solution)/shard_map/ppermute | solution.py:29
  18.6 2.3 %collective-permute-start = (f32[8,72,128]{2,1,0:T(8,128)S(1)}, f32[8,72,128]{2,1,0:T(8,128)S(1)}, u32[]{:S(2)}, u32[]{:S(2)}) collective-permute-start(f32[8,72,128]{2,1,0:T(8,128)S(1)} %get-tuple-element.19), channel_id=1, source_target_pairs={{0,2},{1,3},{2,0},{3,1},{4,6},{5,7},{6,4},{7,5},{8,10},{9,11},{10,... | collective-permute-start | bytes 884744 | tf_op jit(solution)/shard_map/ppermute | solution.py:29
  21.0 10.3 %all-to-all-done.2 = f32[32,8,512]{2,1,0:T(8,128)S(1)} async-done(((f32[32,8,512]{2,1,0:T(8,128)}), f32[32,8,512]{2,1,0:T(8,128)S(1)}, u32[]{:S(2)}, u32[]{:S(2)}) %all-to-all-start.2) | async-done | bytes 524320 | tf_op jit(solution)/shard_map/all_to_all | solution.py:24
  31.7 2.6 %collective-permute-start.7 = (f32[8,4,8,512]{3,2,1,0:T(8,128)S(1)}, f32[8,4,8,512]{3,2,1,0:T(8,128)}, u32[]{:S(2)}, u32[]{:S(2)}) collective-permute-start(f32[8,4,8,512]{3,2,1,0:T(8,128)S(1)} %bitcast.5), channel_id=1, source_target_pairs={{0,128},{64,192},{128,0},{192,64},{1,129},{65,193},{129,1},{193,65... | collective-permute-start | bytes 1572872 | tf_op jit(solution)/shard_map/ppermute | solution.py:29
  34.6 1.6 collective-permute-start.8
  36.2 1.7 collective-permute-done.1
  37.8 0.8 add_add_fusion.1
  38.6 5.8 %all-to-all-start = ((f32[8,72,128]{2,1,0:T(8,128)}), f32[8,72,128]{2,1,0:T(8,128)S(1)}, u32[]{:S(2)}, u32[]{:S(2)}) async-start(f32[8,72,128]{2,1,0:T(8,128)} %add_add_fusion.1), calls=%async_computation | async-start | bytes 589824 | tf_op jit(solution)/shard_map/all_to_all | solution.py:24
  45.0 10.4 %collective-permute-done.7.refs_6_.refs_2_ = f32[8,4,8,512]{3,2,1,0:T(8,128)} collective-permute-done((f32[8,4,8,512]{3,2,1,0:T(8,128)S(1)}, f32[8,4,8,512]{3,2,1,0:T(8,128)}, u32[]{:S(2)}, u32[]{:S(2)}) %collective-permute-start.7) | collective-permute-done | bytes 524320 | tf_op jit(solution)/shard_map/ppermute | solution.py:29
  55.4 0.8 collective-permute-done.8.refs_7_.refs_3_
  57.0 3.4 %all-to-all-start.1 = ((f32[8,72,128]{2,1,0:T(8,128)}), f32[8,72,128]{2,1,0:T(8,128)S(1)}, u32[]{:S(2)}, u32[]{:S(2)}) async-start(f32[8,72,128]{2,1,0:T(8,128)} %broadcast_in_dim.2), calls=%async_computation.1 | async-start | bytes 589824 | tf_op jit(solution)/shard_map/all_to_all | solution.py:24
  60.4 2.1 %shard_map.88.refs_0_ = f32[8,4,4,8,256]{4,3,2,1,0:T(8,128)S(1)} custom-call(s32[1]{0:T(128)} %bitcast.me_ref, bf16[256,896]{1,0:T(8,128)(2,1)} %grads_ref.7, f32[8,4,8,512]{3,2,1,0:T(8,128)S(1)} %bitcast.8, f32[8,4,8,512]{3,2,1,0:T(8,128)S(1)} %collective-permute-done.6.refs_5_.refs_1_, f32[8,4,8,512]{3,2,1,0:T(8,128)} %collective-permute-done.7.refs_6_.refs_2_, ...), custom_call_target="tpu_custom_call" | custom-call | tf_op jit(solution)/shard_map/pallas_call | solution.py:36
  62.6 2.8 %shard_map.89 = f32[8,4,4,8,256]{4,3,2,1,0:T(8,128)} custom-call(s32[1]{0:T(128)} %bitcast.me_ref, bf16[256,896]{1,0:T(8,128)(2,1)} %grads_ref.7, f32[8,4,4,8,256]{4,3,2,1,0:T(8,128)S(1)} %shard_map.88.refs_0_, f32[8,4,8,512]{3,2,1,0:T(8,128)S(1)} %collective-permute-done.9.refs_8_.refs_4_.refs_1_, ...), custom_call_target="tpu_custom_call" | custom-call | tf_op jit(solution)/shard_map/pallas_call | solution.py:36
  65.4 8.5 %all-to-all-done.1.block_ref.refs_4_ = f32[8,72,128]{2,1,0:T(8,128)S(1)} async-done(((f32[8,72,128]{2,1,0:T(8,128)}), f32[8,72,128]{2,1,0:T(8,128)S(1)}, u32[]{:S(2)}, u32[]{:S(2)}) %all-to-all-start.1) | async-done | bytes 294944 | tf_op jit(solution)/shard_map/all_to_all | solution.py:24
  73.9 4.2 %all-to-all-start.4 = ((f32[8,4,4,8,256]{4,3,2,1,0:T(8,128)}), f32[8,4,4,8,256]{4,3,2,1,0:T(8,128)}, u32[]{:S(2)}, u32[]{:S(2)}) async-start(f32[8,4,4,8,256]{4,3,2,1,0:T(8,128)} %shard_map.89), calls=%async_computation.4 | async-start | bytes 2097152 | tf_op jit(solution)/shard_map/all_to_all | solution.py:24
  78.1 1.4 collective-permute-start.3
  79.5 1.9 %collective-permute-start.4 = (f32[8,72,128]{2,1,0:T(8,128)S(1)}, f32[8,72,128]{2,1,0:T(8,128)S(1)}, u32[]{:S(2)}, u32[]{:S(2)}) collective-permute-start(f32[8,72,128]{2,1,0:T(8,128)S(1)} %all-to-all-done.1.block_ref.refs_4_), channel_id=1, source_target_pairs={{0,3},{1,0},{2,1},{3,2},{4,7},{5,4},{6,5},{7,6},{8,11},{9,8},{10,9... | collective-permute-start | bytes 884744 | tf_op jit(solution)/shard_map/ppermute | solution.py:29
  81.4 1.5 collective-permute-start.5
  82.9 2.4 %shard_map.83.refs_3_ = f32[4,128,896]{2,1,0:T(8,128)S(1)} custom-call(s32[1]{0:T(128)} %bitcast.me_ref, s32[4]{0:T(128)S(1)} %copy-done.6, bf16[2048,896]{1,0:T(8,128)(2,1)} %grads_ref.5, f32[8,72,128]{2,1,0:T(8,128)S(1)} %all-to-all-done.1.block_ref.refs_4_), custom_call_target="tpu_custom_call" | custom-call | tf_op jit(solution)/shard_map/pallas_call | solution.py:36
  85.4 3.3 %collective-permute-done.3.refs_0_.refs_5_ = f32[8,72,128]{2,1,0:T(8,128)S(1)} collective-permute-done((f32[8,72,128]{2,1,0:T(8,128)S(1)}, f32[8,72,128]{2,1,0:T(8,128)S(1)}, u32[]{:S(2)}, u32[]{:S(2)}) %collective-permute-start.3) | collective-permute-done | bytes 294944 | tf_op jit(solution)/shard_map/ppermute | solution.py:29
  88.7 5.3 %collective-permute-done.4.refs_1_.refs_7_ = f32[8,72,128]{2,1,0:T(8,128)S(1)} collective-permute-done((f32[8,72,128]{2,1,0:T(8,128)S(1)}, f32[8,72,128]{2,1,0:T(8,128)S(1)}, u32[]{:S(2)}, u32[]{:S(2)}) %collective-permute-start.4) | collective-permute-done | bytes 294944 | tf_op jit(solution)/shard_map/ppermute | solution.py:29
  94.0 1.3 collective-permute-done.5.refs_2_.refs_6_
  95.3 5.9 %shard_map.85 = (f32[8,32,512]{2,1,0:T(8,128)S(1)}, bf16[2,512,512]{2,1,0:T(8,128)(2,1)S(1)}, bf16[2,512,512]{2,1,0:T(8,128)(2,1)S(1)}) custom-call(s32[1]{0:T(128)} %bitcast.me_ref, s32[4]{0:T(128)S(1)} %copy-done.6, bf16[2048,896]{1,0:T(8,128)(2,1)} %grads_ref.5, f32[8,72,128]{2,1,0:T(8,128)S(1)} %collective-permute-done.3.refs_0_.refs_5_, ...), custom_call_target="tpu_custom_call" | custom-call | tf_op jit(solution)/shard_map/pallas_call | solution.py:36
  101.2 3.0 %shard_map.87 = (f32[8,32,512]{2,1,0:T(8,128)S(1)}, f32[8,32,512]{2,1,0:T(8,128)S(1)}) custom-call(s32[1]{0:T(128)} %bitcast.me_ref, bf16[2,512,512]{2,1,0:T(8,128)(2,1)S(1)} %get-tuple-element.22.high_ref, bf16[2,512,512]{2,1,0:T(8,128)(2,1)S(1)} %get-tuple-element.23.low_ref, f32[8,4,8,512]{3,2,1,0:T(8,128)S(1)} %bitcast.10, ...), custom_call_target="tpu_custom_call" | custom-call | tf_op jit(solution)/shard_map/pallas_call | solution.py:36
  104.2 2.5 %collective-permute-start.15 = (f32[8,32,512]{2,1,0:T(8,128)S(1)}, f32[8,32,512]{2,1,0:T(8,128)S(1)}, u32[]{:S(2)}, u32[]{:S(2)}) collective-permute-start(f32[8,32,512]{2,1,0:T(8,128)S(1)} %get-tuple-element.26), channel_id=1, source_target_pairs={{0,3},{1,0},{2,1},{3,2},{4,7},{5,4},{6,5},{7,6},{8,11},{9,8},{10,9... | collective-permute-start | bytes 1572872 | tf_op jit(solution)/shard_map/ppermute | solution.py:29
  106.8 0.8 collective-permute-start.14
  107.7 3.0 %shard_map.86 = f32[8,32,512]{2,1,0:T(8,128)} custom-call(s32[1]{0:T(128)} %bitcast.me_ref, bf16[2,512,512]{2,1,0:T(8,128)(2,1)S(1)} %get-tuple-element.22.high_ref, bf16[2,512,512]{2,1,0:T(8,128)(2,1)S(1)} %get-tuple-element.23.low_ref, f32[8,4,8,512]{3,2,1,0:T(8,128)S(1)} %bitcast.11, f32[8,4,8,512]{3,2,1,0:T(8,128)S(1)} %collective-permute-done.6.refs_5_.refs_1_, ...), custom_call_target="tpu_custom_call" | custom-call | tf_op jit(solution)/shard_map/pallas_call | solution.py:36
  110.7 8.4 %collective-permute-done.15 = f32[8,32,512]{2,1,0:T(8,128)S(1)} collective-permute-done((f32[8,32,512]{2,1,0:T(8,128)S(1)}, f32[8,32,512]{2,1,0:T(8,128)S(1)}, u32[]{:S(2)}, u32[]{:S(2)}) %collective-permute-start.15) | collective-permute-done | bytes 524320 | tf_op jit(solution)/shard_map/ppermute | solution.py:29
  119.1 4.0 %collective-permute-done.14 = f32[8,32,512]{2,1,0:T(8,128)S(1)} collective-permute-done((f32[8,32,512]{2,1,0:T(8,128)S(1)}, f32[8,32,512]{2,1,0:T(8,128)S(1)}, u32[]{:S(2)}, u32[]{:S(2)}) %collective-permute-start.14) | collective-permute-done | bytes 524320 | tf_op jit(solution)/shard_map/ppermute | solution.py:29
  123.1 8.6 %collective-permute-done.13 = f32[8,32,512]{2,1,0:T(8,128)S(1)} collective-permute-done((f32[8,32,512]{2,1,0:T(8,128)S(1)}, f32[8,32,512]{2,1,0:T(8,128)S(1)}, u32[]{:S(2)}, u32[]{:S(2)}) %collective-permute-start.13) | collective-permute-done | bytes 524320 | tf_op jit(solution)/shard_map/ppermute | solution.py:29
  131.6 2.0 %add_add_fusion = f32[8,32,512]{2,1,0:T(8,128)} fusion(f32[8,32,512]{2,1,0:T(8,128)S(1)} %collective-permute-done.15, f32[8,32,512]{2,1,0:T(8,128)S(1)} %collective-permute-done.14, f32[8,32,512]{2,1,0:T(8,128)} %shard_map.86, f32[8,32,512]{2,1,0:T(8,128)S(1)} %collective-permute-done.13), kind=kLoop, calls=%fused_computation | loop fusion | flops 393216 | bytes 2621440 | tf_op jit(solution)/shard_map/add | solution.py:355
  133.7 6.5 %all-to-all-start.3 = ((f32[8,32,512]{2,1,0:T(8,128)}), f32[8,32,512]{2,1,0:T(8,128)S(1)}, u32[]{:S(2)}, u32[]{:S(2)}) async-start(f32[8,32,512]{2,1,0:T(8,128)} %add_add_fusion), calls=%async_computation.3 | async-start | bytes 1048576 | tf_op jit(solution)/shard_map/all_to_all | solution.py:24
  140.1 1.3 shard_map.90
  141.5 2.1 %collective-permute-start.17 = (f32[4,8,256]{2,1,0:T(8,128)S(1)}, f32[4,8,256]{2,1,0:T(8,128)S(1)}, u32[]{:S(2)}, u32[]{:S(2)}) collective-permute-start(f32[4,8,256]{2,1,0:T(8,128)S(1)} %get-tuple-element.29), channel_id=1, source_target_pairs={{0,2},{1,3},{2,0},{3,1},{4,6},{5,7},{6,4},{7,5},{8,10},{9,11},{10,... | collective-permute-start | bytes 98312 | tf_op jit(solution)/shard_map/ppermute | solution.py:29
  143.6 1.8 %collective-permute-start.18 = (f32[4,8,256]{2,1,0:T(8,128)S(1)}, f32[4,8,256]{2,1,0:T(8,128)S(1)}, u32[]{:S(2)}, u32[]{:S(2)}) collective-permute-start(f32[4,8,256]{2,1,0:T(8,128)S(1)} %get-tuple-element.30), channel_id=1, source_target_pairs={{0,3},{1,0},{2,1},{3,2},{4,7},{5,4},{6,5},{7,6},{8,11},{9,8},{10,9... | collective-permute-start | bytes 98312 | tf_op jit(solution)/shard_map/ppermute | solution.py:29
  145.4 1.2 collective-permute-done.16.refs_1_
  147.0 0.8 collective-permute-done.18.refs_3_
  147.8 1.2 shard_map.91.refs_0_
  149.0 1.5 collective-permute-start.19
  150.5 3.1 %collective-permute-start.20 = (f32[32,8,128]{2,1,0:T(8,128)S(1)}, f32[32,8,128]{2,1,0:T(8,128)S(1)}, u32[]{:S(2)}, u32[]{:S(2)}) collective-permute-start(f32[32,8,128]{2,1,0:T(8,128)S(1)} %shard_map.91.refs_0_), channel_id=1, source_target_pairs={{0,128},{64,192},{128,0},{192,64},{1,129},{65,193},{129,1},{193,65... | collective-permute-start | bytes 393224 | tf_op jit(solution)/shard_map/ppermute | solution.py:29
  154.0 1.7 collective-permute-done.19.refs_1_
  155.7 1.4 collective-permute-done.20.refs_2_
  157.1 1.4 collective-permute-done.21.refs_3_
  158.6 1.3 collective-permute-done.25.refs_7_
  160.3 19.8 %all_to_all.30 = f32[32,2,128]{2,1,0:T(2,128)S(1)} all-to-all(f32[32,2,128]{2,1,0:T(2,128)S(1)} %bitcast.12), channel_id=1, replica_groups=mesh['y'=4,'core'=2,'z'=8,'x'=4] {'z','x'}, dimensions={0} | all-to-all | bytes 65536 | tf_op jit(solution)/shard_map/all_to_all | solution.py:24
  (45 shorter events, 4.3 us)
Async XLA Ops:
  2.1 29.2 %all-to-all-start.2 = ((f32[32,8,512]{2,1,0:T(8,128)}), f32[32,8,512]{2,1,0:T(8,128)S(1)}, u32[]{:S(2)}, u32[]{:S(2)}) async-start(f32[32,8,512]{2,1,0:T(8,128)} %shard_map.84), calls=%async_computation.2 | async-start | bytes 1048576 | tf_op jit(solution)/shard_map/all_to_all | solution.py:24
  15.6 19.0 %collective-permute-start.2 = (f32[8,72,128]{2,1,0:T(8,128)S(1)}, f32[8,72,128]{2,1,0:T(8,128)S(1)}, u32[]{:S(2)}, u32[]{:S(2)}) collective-permute-start(f32[8,72,128]{2,1,0:T(8,128)S(1)} %get-tuple-element.21), channel_id=1, source_target_pairs={{0,3},{1,0},{2,1},{3,2},{4,7},{5,4},{6,5},{7,6},{8,11},{9,8},{10,9... | collective-permute-start | bytes 884744 | tf_op jit(solution)/shard_map/ppermute | solution.py:29
  18.6 19.2 %collective-permute-start.1 = (f32[8,72,128]{2,1,0:T(8,128)S(1)}, f32[8,72,128]{2,1,0:T(8,128)S(1)}, u32[]{:S(2)}, u32[]{:S(2)}) collective-permute-start(f32[8,72,128]{2,1,0:T(8,128)S(1)} %get-tuple-element.20), channel_id=1, source_target_pairs={{0,1},{1,2},{2,3},{3,0},{4,5},{5,6},{6,7},{7,4},{8,9},{9,10},{10,1... | collective-permute-start | bytes 884744 | tf_op jit(solution)/shard_map/ppermute | solution.py:29
  18.6 19.2 %collective-permute-start = (f32[8,72,128]{2,1,0:T(8,128)S(1)}, f32[8,72,128]{2,1,0:T(8,128)S(1)}, u32[]{:S(2)}, u32[]{:S(2)}) collective-permute-start(f32[8,72,128]{2,1,0:T(8,128)S(1)} %get-tuple-element.19), channel_id=1, source_target_pairs={{0,2},{1,3},{2,0},{3,1},{4,6},{5,7},{6,4},{7,5},{8,10},{9,11},{10,... | collective-permute-start | bytes 884744 | tf_op jit(solution)/shard_map/ppermute | solution.py:29
  31.2 13.8 %collective-permute-start.6 = (f32[8,4,8,512]{3,2,1,0:T(8,128)S(1)}, f32[8,4,8,512]{3,2,1,0:T(8,128)S(1)}, u32[]{:S(2)}, u32[]{:S(2)}) collective-permute-start(f32[8,4,8,512]{3,2,1,0:T(8,128)S(1)} %bitcast.4), channel_id=1, source_target_pairs={{0,192},{64,0},{128,64},{192,128},{1,193},{65,1},{129,65},{193,129... | collective-permute-start | bytes 1572872 | tf_op jit(solution)/shard_map/ppermute | solution.py:29
  31.7 23.7 %collective-permute-start.7 = (f32[8,4,8,512]{3,2,1,0:T(8,128)S(1)}, f32[8,4,8,512]{3,2,1,0:T(8,128)}, u32[]{:S(2)}, u32[]{:S(2)}) collective-permute-start(f32[8,4,8,512]{3,2,1,0:T(8,128)S(1)} %bitcast.5), channel_id=1, source_target_pairs={{0,128},{64,192},{128,0},{192,64},{1,129},{65,193},{129,1},{193,65... | collective-permute-start | bytes 1572872 | tf_op jit(solution)/shard_map/ppermute | solution.py:29
  34.6 21.7 %collective-permute-start.8 = (f32[8,4,8,512]{3,2,1,0:T(8,128)S(1)}, f32[8,4,8,512]{3,2,1,0:T(8,128)}, u32[]{:S(2)}, u32[]{:S(2)}) collective-permute-start(f32[8,4,8,512]{3,2,1,0:T(8,128)S(1)} %bitcast.6), channel_id=1, source_target_pairs={{0,64},{64,128},{128,192},{192,0},{1,65},{65,129},{129,193},{193,1... | collective-permute-start | bytes 1572872 | tf_op jit(solution)/shard_map/ppermute | solution.py:29
  38.6 17.6 %all-to-all-start = ((f32[8,72,128]{2,1,0:T(8,128)}), f32[8,72,128]{2,1,0:T(8,128)S(1)}, u32[]{:S(2)}, u32[]{:S(2)}) async-start(f32[8,72,128]{2,1,0:T(8,128)} %add_add_fusion.1), calls=%async_computation | async-start | bytes 589824 | tf_op jit(solution)/shard_map/all_to_all | solution.py:24
  44.4 18.1 %collective-permute-start.9 = (f32[8,4,8,512]{3,2,1,0:T(8,128)S(1)}, f32[8,4,8,512]{3,2,1,0:T(8,128)S(1)}, u32[]{:S(2)}, u32[]{:S(2)}) collective-permute-start(f32[8,4,8,512]{3,2,1,0:T(8,128)S(1)} %bitcast.7), channel_id=1, source_target_pairs={{0,32},{32,0},{1,33},{33,1},{2,34},{34,2},{3,35},{35,3},{4,36},{36... | collective-permute-start | bytes 1572872 | tf_op jit(solution)/shard_map/ppermute | solution.py:29
  45.0 17.6 %collective-permute-start.10 = (f32[8,4,8,512]{3,2,1,0:T(8,128)S(1)}, f32[8,4,8,512]{3,2,1,0:T(8,128)S(1)}, u32[]{:S(2)}, u32[]{:S(2)}) collective-permute-start(f32[8,4,8,512]{3,2,1,0:T(8,128)S(1)} %collective-permute-done.6.refs_5_.refs_1_), channel_id=1, source_target_pairs={{0,32},{32,0},{1,33},{33,1},{2,34},{34,2},{3,35},{35,3},{4,36},{36... | collective-permute-start | bytes 1572872 | tf_op jit(solution)/shard_map/ppermute | solution.py:29
  55.4 7.2 %collective-permute-start.11 = (f32[8,4,8,512]{3,2,1,0:T(8,128)}, f32[8,4,8,512]{3,2,1,0:T(8,128)S(1)}, u32[]{:S(2)}, u32[]{:S(2)}) collective-permute-start(f32[8,4,8,512]{3,2,1,0:T(8,128)} %collective-permute-done.7.refs_6_.refs_2_), channel_id=1, source_target_pairs={{0,32},{32,0},{1,33},{33,1},{2,34},{34,2},{3,35},{35,3},{4,36},{36... | collective-permute-start | bytes 1572872 | tf_op jit(solution)/shard_map/ppermute | solution.py:29
  56.2 6.4 %collective-permute-start.12 = (f32[8,4,8,512]{3,2,1,0:T(8,128)}, f32[8,4,8,512]{3,2,1,0:T(8,128)S(1)}, u32[]{:S(2)}, u32[]{:S(2)}) collective-permute-start(f32[8,4,8,512]{3,2,1,0:T(8,128)} %collective-permute-done.8.refs_7_.refs_3_), channel_id=1, source_target_pairs={{0,32},{32,0},{1,33},{33,1},{2,34},{34,2},{3,35},{35,3},{4,36},{36... | collective-permute-start | bytes 1572872 | tf_op jit(solution)/shard_map/ppermute | solution.py:29
  57.0 16.9 %all-to-all-start.1 = ((f32[8,72,128]{2,1,0:T(8,128)}), f32[8,72,128]{2,1,0:T(8,128)S(1)}, u32[]{:S(2)}, u32[]{:S(2)}) async-start(f32[8,72,128]{2,1,0:T(8,128)} %broadcast_in_dim.2), calls=%async_computation.1 | async-start | bytes 589824 | tf_op jit(solution)/shard_map/all_to_all | solution.py:24
  62.5 20.4 %copy-start.6 = (s32[4]{0:T(128)S(1)}, s32[4]{0:T(128)}, u32[]{:S(2)}) copy-start(s32[4]{0:T(128)} %len_ref.3) | copy-start | bytes 52
  73.9 59.8 %all-to-all-start.4 = ((f32[8,4,4,8,256]{4,3,2,1,0:T(8,128)}), f32[8,4,4,8,256]{4,3,2,1,0:T(8,128)}, u32[]{:S(2)}, u32[]{:S(2)}) async-start(f32[8,4,4,8,256]{4,3,2,1,0:T(8,128)} %shard_map.89), calls=%async_computation.4 | async-start | bytes 2097152 | tf_op jit(solution)/shard_map/all_to_all | solution.py:24
  78.1 10.6 %collective-permute-start.3 = (f32[8,72,128]{2,1,0:T(8,128)S(1)}, f32[8,72,128]{2,1,0:T(8,128)S(1)}, u32[]{:S(2)}, u32[]{:S(2)}) collective-permute-start(f32[8,72,128]{2,1,0:T(8,128)S(1)} %all-to-all-done.1.block_ref.refs_4_), channel_id=1, source_target_pairs={{0,1},{1,2},{2,3},{3,0},{4,5},{5,6},{6,7},{7,4},{8,9},{9,10},{10,1... | collective-permute-start | bytes 884744 | tf_op jit(solution)/shard_map/ppermute | solution.py:29
  79.5 14.5 %collective-permute-start.4 = (f32[8,72,128]{2,1,0:T(8,128)S(1)}, f32[8,72,128]{2,1,0:T(8,128)S(1)}, u32[]{:S(2)}, u32[]{:S(2)}) collective-permute-start(f32[8,72,128]{2,1,0:T(8,128)S(1)} %all-to-all-done.1.block_ref.refs_4_), channel_id=1, source_target_pairs={{0,3},{1,0},{2,1},{3,2},{4,7},{5,4},{6,5},{7,6},{8,11},{9,8},{10,9... | collective-permute-start | bytes 884744 | tf_op jit(solution)/shard_map/ppermute | solution.py:29
  81.4 13.9 %collective-permute-start.5 = (f32[8,72,128]{2,1,0:T(8,128)S(1)}, f32[8,72,128]{2,1,0:T(8,128)S(1)}, u32[]{:S(2)}, u32[]{:S(2)}) collective-permute-start(f32[8,72,128]{2,1,0:T(8,128)S(1)} %all-to-all-done.1.block_ref.refs_4_), channel_id=1, source_target_pairs={{0,2},{1,3},{2,0},{3,1},{4,6},{5,7},{6,4},{7,5},{8,10},{9,11},{10,... | collective-permute-start | bytes 884744 | tf_op jit(solution)/shard_map/ppermute | solution.py:29
  88.7 12.5 %copy-start = (f32[8,72,128]{2,1,0:T(8,128)}, f32[8,72,128]{2,1,0:T(8,128)S(1)}, u32[]{:S(2)}) copy-start(f32[8,72,128]{2,1,0:T(8,128)S(1)} %collective-permute-done.3.refs_0_.refs_5_) | copy-start | bytes 884740
  94.0 7.2 %copy-start.2 = (f32[8,72,128]{2,1,0:T(8,128)}, f32[8,72,128]{2,1,0:T(8,128)S(1)}, u32[]{:S(2)}) copy-start(f32[8,72,128]{2,1,0:T(8,128)S(1)} %collective-permute-done.4.refs_1_.refs_7_) | copy-start | bytes 884740
  95.3 5.9 %copy-start.4 = (f32[8,72,128]{2,1,0:T(8,128)}, f32[8,72,128]{2,1,0:T(8,128)S(1)}, u32[]{:S(2)}) copy-start(f32[8,72,128]{2,1,0:T(8,128)S(1)} %collective-permute-done.5.refs_2_.refs_6_) | copy-start | bytes 884740
  104.2 14.9 %collective-permute-start.15 = (f32[8,32,512]{2,1,0:T(8,128)S(1)}, f32[8,32,512]{2,1,0:T(8,128)S(1)}, u32[]{:S(2)}, u32[]{:S(2)}) collective-permute-start(f32[8,32,512]{2,1,0:T(8,128)S(1)} %get-tuple-element.26), channel_id=1, source_target_pairs={{0,3},{1,0},{2,1},{3,2},{4,7},{5,4},{6,5},{7,6},{8,11},{9,8},{10,9... | collective-permute-start | bytes 1572872 | tf_op jit(solution)/shard_map/ppermute | solution.py:29
  106.8 16.3 %collective-permute-start.14 = (f32[8,32,512]{2,1,0:T(8,128)S(1)}, f32[8,32,512]{2,1,0:T(8,128)S(1)}, u32[]{:S(2)}, u32[]{:S(2)}) collective-permute-start(f32[8,32,512]{2,1,0:T(8,128)S(1)} %get-tuple-element.25), channel_id=1, source_target_pairs={{0,2},{1,3},{2,0},{3,1},{4,6},{5,7},{6,4},{7,5},{8,10},{9,11},{10,... | collective-permute-start | bytes 1572872 | tf_op jit(solution)/shard_map/ppermute | solution.py:29
  107.5 24.1 %collective-permute-start.13 = (f32[8,32,512]{2,1,0:T(8,128)S(1)}, f32[8,32,512]{2,1,0:T(8,128)S(1)}, u32[]{:S(2)}, u32[]{:S(2)}) collective-permute-start(f32[8,32,512]{2,1,0:T(8,128)S(1)} %get-tuple-element.24), channel_id=1, source_target_pairs={{0,1},{1,2},{2,3},{3,0},{4,5},{5,6},{6,7},{7,4},{8,9},{9,10},{10,1... | collective-permute-start | bytes 1572872 | tf_op jit(solution)/shard_map/ppermute | solution.py:29
  110.7 37.1 %copy-start.1 = (f32[8,72,128]{2,1,0:T(8,128)S(1)}, f32[8,72,128]{2,1,0:T(8,128)}, u32[]{:S(2)}) copy-start(f32[8,72,128]{2,1,0:T(8,128)} %copy-done) | copy-start | bytes 884740
  110.7 37.1 %copy-start.3 = (f32[8,72,128]{2,1,0:T(8,128)S(1)}, f32[8,72,128]{2,1,0:T(8,128)}, u32[]{:S(2)}) copy-start(f32[8,72,128]{2,1,0:T(8,128)} %copy-done.2) | copy-start | bytes 884740
  110.7 37.1 %copy-start.5 = (f32[8,72,128]{2,1,0:T(8,128)S(1)}, f32[8,72,128]{2,1,0:T(8,128)}, u32[]{:S(2)}) copy-start(f32[8,72,128]{2,1,0:T(8,128)} %copy-done.4) | copy-start | bytes 884740
  133.7 24.9 %all-to-all-start.3 = ((f32[8,32,512]{2,1,0:T(8,128)}), f32[8,32,512]{2,1,0:T(8,128)S(1)}, u32[]{:S(2)}, u32[]{:S(2)}) async-start(f32[8,32,512]{2,1,0:T(8,128)} %add_add_fusion), calls=%async_computation.3 | async-start | bytes 1048576 | tf_op jit(solution)/shard_map/all_to_all | solution.py:24
  141.4 5.2 %collective-permute-start.16 = (f32[4,8,256]{2,1,0:T(8,128)S(1)}, f32[4,8,256]{2,1,0:T(8,128)S(1)}, u32[]{:S(2)}, u32[]{:S(2)}) collective-permute-start(f32[4,8,256]{2,1,0:T(8,128)S(1)} %get-tuple-element.28), channel_id=1, source_target_pairs={{0,1},{1,2},{2,3},{3,0},{4,5},{5,6},{6,7},{7,4},{8,9},{9,10},{10,1... | collective-permute-start | bytes 98312 | tf_op jit(solution)/shard_map/ppermute | solution.py:29
  141.5 5.5 %collective-permute-start.17 = (f32[4,8,256]{2,1,0:T(8,128)S(1)}, f32[4,8,256]{2,1,0:T(8,128)S(1)}, u32[]{:S(2)}, u32[]{:S(2)}) collective-permute-start(f32[4,8,256]{2,1,0:T(8,128)S(1)} %get-tuple-element.29), channel_id=1, source_target_pairs={{0,2},{1,3},{2,0},{3,1},{4,6},{5,7},{6,4},{7,5},{8,10},{9,11},{10,... | collective-permute-start | bytes 98312 | tf_op jit(solution)/shard_map/ppermute | solution.py:29
  143.6 4.3 %collective-permute-start.18 = (f32[4,8,256]{2,1,0:T(8,128)S(1)}, f32[4,8,256]{2,1,0:T(8,128)S(1)}, u32[]{:S(2)}, u32[]{:S(2)}) collective-permute-start(f32[4,8,256]{2,1,0:T(8,128)S(1)} %get-tuple-element.30), channel_id=1, source_target_pairs={{0,3},{1,0},{2,1},{3,2},{4,7},{5,4},{6,5},{7,6},{8,11},{9,8},{10,9... | collective-permute-start | bytes 98312 | tf_op jit(solution)/shard_map/ppermute | solution.py:29
  149.0 6.7 %collective-permute-start.19 = (f32[32,8,128]{2,1,0:T(8,128)S(1)}, f32[32,8,128]{2,1,0:T(8,128)S(1)}, u32[]{:S(2)}, u32[]{:S(2)}) collective-permute-start(f32[32,8,128]{2,1,0:T(8,128)S(1)} %shard_map.91.refs_0_), channel_id=1, source_target_pairs={{0,64},{64,128},{128,192},{192,0},{1,65},{65,129},{129,193},{193,1... | collective-permute-start | bytes 393224 | tf_op jit(solution)/shard_map/ppermute | solution.py:29
  150.5 6.6 %collective-permute-start.20 = (f32[32,8,128]{2,1,0:T(8,128)S(1)}, f32[32,8,128]{2,1,0:T(8,128)S(1)}, u32[]{:S(2)}, u32[]{:S(2)}) collective-permute-start(f32[32,8,128]{2,1,0:T(8,128)S(1)} %shard_map.91.refs_0_), channel_id=1, source_target_pairs={{0,128},{64,192},{128,0},{192,64},{1,129},{65,193},{129,1},{193,65... | collective-permute-start | bytes 393224 | tf_op jit(solution)/shard_map/ppermute | solution.py:29
  153.6 5.0 %collective-permute-start.21 = (f32[32,8,128]{2,1,0:T(8,128)S(1)}, f32[32,8,128]{2,1,0:T(8,128)S(1)}, u32[]{:S(2)}, u32[]{:S(2)}) collective-permute-start(f32[32,8,128]{2,1,0:T(8,128)S(1)} %shard_map.91.refs_0_), channel_id=1, source_target_pairs={{0,192},{64,0},{128,64},{192,128},{1,193},{65,1},{129,65},{193,129... | collective-permute-start | bytes 393224 | tf_op jit(solution)/shard_map/ppermute | solution.py:29
  154.0 4.5 %collective-permute-start.22 = (f32[32,8,128]{2,1,0:T(8,128)S(1)}, f32[32,8,128]{2,1,0:T(8,128)S(1)}, u32[]{:S(2)}, u32[]{:S(2)}) collective-permute-start(f32[32,8,128]{2,1,0:T(8,128)S(1)} %shard_map.91.refs_0_), channel_id=1, source_target_pairs={{0,32},{32,0},{1,33},{33,1},{2,34},{34,2},{3,35},{35,3},{4,36},{36... | collective-permute-start | bytes 393224 | tf_op jit(solution)/shard_map/ppermute | solution.py:29
  155.7 2.8 %collective-permute-start.23 = (f32[32,8,128]{2,1,0:T(8,128)S(1)}, f32[32,8,128]{2,1,0:T(8,128)S(1)}, u32[]{:S(2)}, u32[]{:S(2)}) collective-permute-start(f32[32,8,128]{2,1,0:T(8,128)S(1)} %collective-permute-done.19.refs_1_), channel_id=1, source_target_pairs={{0,32},{32,0},{1,33},{33,1},{2,34},{34,2},{3,35},{35,3},{4,36},{36... | collective-permute-start | bytes 393224 | tf_op jit(solution)/shard_map/ppermute | solution.py:29
  157.1 1.4 collective-permute-start.24
  158.5 1.3 collective-permute-start.25
